TPU v7x, 128 devices: a whole 4x4x4 slice. The times are simulated.
128 devices in a mesh: read: 16 (over x_lo, z, core), tm: 8 (over y, x_hi).
Axes of the slice: x: 4 (x_hi: 2, x_lo: 2; x = x_hi * 2 + x_lo), y: 4, z: 4, core: 2. Of those that a mesh axis runs over, the one named last changes fastest.
Arguments:
- student_in: bfloat16 [16, 4096, 512], P('read', 'tm'), may hold values from -6 to 6
- teacher_rows: bfloat16 [16, 4096, 768], P('read', 'tm'), may hold values from -6 to 6
- valid: int32 [16], P('read'), may hold values from 1024 to 4096, as said below
- conv_weight: bfloat16 [4, 3, 512, 512], replicated, may hold values from -0.15625 to 0.15625
- head_weight: bfloat16 [512, 5120], replicated, may hold values from -0.25 to 0.25
- teacher_head_weight: bfloat16 [768, 5120], replicated, may hold values from -0.21875 to 0.21875
Outputs:
- grad_conv: float32 [4, 3, 512, 512], P(None, None, 'read', 'tm')
- grad_head: float32 [512, 5120], P('read', 'tm')
Inputs may be any that keep to these rules, and one draw needn't show every extreme that they name: One read of each draw has all 4096 frames valid.
All inputs are finite; a program needn't handle non-finite values.
Results may differ from a plain program's by a relative error of at most 0.002.
Values may be sent and summed in bfloat16 or wider, within the bound.
No kernel may reach another device: no remote copies, remote signals or barrier semaphores. Data moves between devices by JAX's collectives and lax.ppermute only.
A program may use at most 192 MiB of HBM per device.

v0:
```python
import functools
import math

import jax
import jax.numpy as jnp
from jax import lax
from jax.experimental import pallas as pl
from jax.experimental.pallas import tpu as pltpu
from jax.sharding import PartitionSpec as P

LAYERS, TAPS = 4, 3
BASE_DILATION = 32
AXES = ("read", "tm")
READ, TM = 16, 8
CLASSES = BASE_DILATION // TM
PAD = CLASSES * 2 ** (LAYERS - 1)
BITS = [(a, b, c) for a in range(2) for b in range(2) for c in range(2)]
F32, BF16 = jnp.float32, jnp.bfloat16


def near_of(core, v):
    return (v // 2) ^ (v % 2) if core == 0 else v // 2


def far_of(core, v):
    return v // 2 if core == 0 else (v // 2) ^ (v % 2)


def high_low(core, near, far):
    return (far if core == 0 else near, near ^ far)


def device_index(x, y, z, core):
    return (((x % 2) * 4 + z) * 2 + core) * TM + y * 2 + x // 2


def groups_of(fixed, order):
    groups = {}
    for core in range(2):
        for x in range(4):
            for y in range(4):
                for z in range(4):
                    key = (core, fixed(core, x), fixed(core, y), fixed(core, z))
                    place = order(core, x) * 4 + order(core, y) * 2 + order(core, z)
                    groups.setdefault(key, [0] * 8)[place] = device_index(x, y, z, core)
    return list(groups.values())


def near_groups():
    def cube(core, v):
        return (v + core) % 4 // 2

    return groups_of(cube, near_of)


def far_groups():
    return groups_of(near_of, far_of)


def other_core():
    return [(d, d ^ TM) for d in range(READ * TM)]


def frame_groups():
    return [[r * TM + t for t in range(TM)] for r in range(READ)]


def exchange(x, groups):
    return lax.all_to_all(x, AXES, 0, 0, tiled=True, axis_index_groups=groups)


def encode(x):
    return (x * jnp.abs(x)).astype(BF16)


def decode(y):
    y = y.astype(F32)
    return y * lax.rsqrt(jnp.maximum(jnp.abs(y), 1e-37))


def low_lanes(shape):
    return lax.broadcasted_iota(jnp.int32, shape, len(shape) - 1) < 64


def dot(a, b):
    return jnp.dot(a, b, preferred_element_type=F32)


def dot_nt(a, b):
    return lax.dot_general(a, b, (((1,), (1,)), ((), ())), preferred_element_type=F32)


def params(*kinds):
    return pltpu.CompilerParams(dimension_semantics=kinds, vmem_limit_bytes=62 * 1024 * 1024)


def whole():
    return pl.BlockSpec(memory_space=pltpu.VMEM)


def frame_mask(sc_ref, frames):
    row = lax.broadcasted_iota(jnp.int32, (frames, 1), 0)
    position = row // CLASSES * BASE_DILATION + sc_ref[1] * CLASSES + row % CLASSES
    return (position < sc_ref[0]).astype(F32)


def regroup_kernel(x_ref, out_ref):
    frames = x_ref.shape[0]
    row = lax.broadcasted_iota(jnp.int32, (frames, frames), 0)
    col = lax.broadcasted_iota(jnp.int32, (frames, frames), 1)
    per = frames // TM
    source = (row % per) // CLASSES * BASE_DILATION + row // per * CLASSES + row % CLASSES
    select = jnp.where(col == source, 1.0, 0.0).astype(BF16)
    out_ref[...] = dot(select, x_ref[...]).astype(BF16)


def regroup(x):
    return pl.pallas_call(
        regroup_kernel,
        out_shape=jax.ShapeDtypeStruct(x.shape, BF16),
        in_specs=[whole()],
        out_specs=whole(),
        name="regroup",
    )(x)


def conv_kernel(sc_ref, x_ref, w_ref, saved_ref, pre_ref, last_ref, pad_s, tap_s):
    layer = pl.program_id(0)
    frames = x_ref.shape[0]

    @pl.when(layer == 0)
    def _():
        pad_s[...] = jnp.zeros_like(pad_s)
        pad_s[PAD : PAD + frames] = x_ref[...].astype(F32)

    for at in range(LAYERS):

        @pl.when(layer == at)
        def _():
            reach = CLASSES * 2**at
            tap_s[0] = pad_s[PAD - reach : PAD - reach + frames].astype(BF16)
            tap_s[1] = pad_s[PAD + reach : PAD + reach + frames].astype(BF16)

    hidden = pad_s[PAD : PAD + frames]
    middle = hidden.astype(BF16)
    saved_ref[0] = middle
    pre = dot(tap_s[0], w_ref[0, 0]) + dot(middle, w_ref[0, 1]) + dot(tap_s[1], w_ref[0, 2])
    pre_ref[0] = pre
    new = (frame_mask(sc_ref, frames) * (hidden + jax.nn.silu(pre))).astype(BF16)
    last_ref[...] = new
    pad_s[PAD : PAD + frames] = new.astype(F32)


def convolve(sc, x, weight):
    frames, width = x.shape
    one = pl.BlockSpec((1, frames, width), lambda i: (i, 0, 0))
    flat = pl.BlockSpec((frames, width), lambda i: (0, 0))
    return pl.pallas_call(
        conv_kernel,
        grid=(LAYERS,),
        in_specs=[
            pl.BlockSpec(memory_space=pltpu.SMEM),
            flat,
            pl.BlockSpec((1, TAPS, width, width), lambda i: (i, 0, 0, 0)),
        ],
        out_specs=[one, one, flat],
        out_shape=[
            jax.ShapeDtypeStruct((LAYERS, frames, width), BF16),
            jax.ShapeDtypeStruct((LAYERS, frames, width), F32),
            jax.ShapeDtypeStruct((frames, width), BF16),
        ],
        scratch_shapes=[
            pltpu.VMEM((frames + 2 * PAD, width), F32),
            pltpu.VMEM((2, frames, width), BF16),
        ],
        compiler_params=params("arbitrary"),
        cost_estimate=pl.CostEstimate(
            flops=2 * LAYERS * TAPS * frames * width * width,
            bytes_accessed=LAYERS * (TAPS * width * width * 2 + frames * width * 6),
            transcendentals=LAYERS * frames * width,
        ),
        name="convolve",
    )(sc, x, weight)


def head_kernel(scale, tiles, sc_ref, h_ref, t_ref, ws_ref, wt_ref, mine_ref, other_ref, g_ref,
                sq_s, es_s, et_s, sum_s, ht_s, gs_s, res_s):
    step = pl.program_id(0)
    frames, width = h_ref.shape
    tile = ws_ref.shape[1]
    sub = 256

    @pl.when(step == 0)
    def _():
        sum_s[...] = jnp.zeros_like(sum_s)

    @pl.when(step < tiles)
    def _():
        for c in range(tile // sub):
            cols = slice(c * sub, (c + 1) * sub)
            squash = jnp.tanh(dot(h_ref[...], ws_ref[:, cols]))
            exp_s = jnp.exp(5.0 * squash)
            sq_s[step, :, cols] = squash
            es_s[step, :, cols] = exp_s
            sum_s[0] += exp_s[:, :128] + exp_s[:, 128:]
            exp_t = jnp.exp(5.0 * jnp.tanh(dot(t_ref[...], wt_ref[:, cols])))
            et_s[step, :, cols] = exp_t
            sum_s[1] += exp_t[:, :128] + exp_t[:, 128:]

    @pl.when(step == tiles)
    def _():
        factor = scale * frame_mask(sc_ref, frames)
        for i in range(2):
            inverse = factor / jnp.sum(sum_s[i], axis=1, keepdims=True)
            sum_s[i] = jnp.broadcast_to(inverse, (frames, 128))
        ht_s[...] = h_ref[...].T
        g_ref[...] = jnp.zeros_like(g_ref)

    @pl.when(step >= tiles)
    def _():
        at = step - tiles
        for c in range(tile // 128):
            cols = slice(c * 128, (c + 1) * 128)
            squash = sq_s[at, :, cols]
            p = es_s[at, :, cols] * sum_s[0] - et_s[at, :, cols] * sum_s[1]
            gs_s[:, cols] = (p * (1.0 - squash * squash)).astype(BF16)
        res_s[...] = dot(ht_s[...], gs_s[...])
        g_ref[...] += dot_nt(gs_s[...], ws_ref[...])
        first = sc_ref[2] == 0
        half = tile // 2
        for nx, nz, fz in BITS:
            for fx in range(2):
                found = []
                for core in range(2):
                    xh, xl = high_low(core, nx, fx)
                    zh, zl = high_low(core, nz, fz)
                    r = ((xl * 4 + zh * 2 + zl) * 2 + core) * 32
                    found.append(res_s[r : r + 32, xh * half : (xh + 1) * half])
                to = slice(fx * half, (fx + 1) * half)
                mine_ref[nx, 0, nz, fz, 0, :, to] = jnp.where(first, found[0], found[1])
                other_ref[nx, 0, nz, fz, 0, :, to] = encode(jnp.where(first, found[1], found[0]))


def heads(sc, hidden, teacher_in, head_weight, teacher_head_weight, loss_scale):
    frames, width = hidden.shape
    wide = teacher_in.shape[1]
    scores = head_weight.shape[1]
    tiles = 4
    tile = scores // tiles

    def place(i, core):
        y = jnp.maximum(i - tiles, 0)
        high, low = y // 2, y % 2
        even = core == 0
        near = jnp.where(even, high ^ low, high)
        far = jnp.where(even, high, high ^ low)
        return (0, near, 0, 0, far, 0, 0)

    block = (2, 1, 2, 2, 1, 32, tile)
    shape = (2, 2, 2, 2, 2, 32, tile)
    kernel = functools.partial(head_kernel, 5.0 * loss_scale, tiles)
    big = pltpu.VMEM((tiles, frames, tile), F32)
    return pl.pallas_call(
        kernel,
        grid_spec=pltpu.PrefetchScalarGridSpec(
            num_scalar_prefetch=1,
            grid=(2 * tiles,),
            in_specs=[
                pl.BlockSpec((frames, width), lambda i, sc: (0, 0)),
                pl.BlockSpec((frames, wide), lambda i, sc: (0, 0)),
                pl.BlockSpec((width, tile), lambda i, sc: (0, i % tiles)),
                pl.BlockSpec((wide, tile), lambda i, sc: (0, jnp.minimum(i, tiles - 1))),
            ],
            out_specs=[
                pl.BlockSpec(block, lambda i, sc: place(i, sc[2])),
                pl.BlockSpec(block, lambda i, sc: place(i, 1 - sc[2])),
                pl.BlockSpec((frames, width), lambda i, sc: (0, 0)),
            ],
            scratch_shapes=[
                big,
                big,
                big,
                pltpu.VMEM((2, frames, 128), F32),
                pltpu.VMEM((width, frames), BF16),
                pltpu.VMEM((frames, tile), BF16),
                pltpu.VMEM((width, tile), F32),
            ],
        ),
        out_shape=[
            jax.ShapeDtypeStruct(shape, F32),
            jax.ShapeDtypeStruct(shape, BF16),
            jax.ShapeDtypeStruct((frames, width), F32),
        ],
        compiler_params=params("arbitrary"),
        cost_estimate=pl.CostEstimate(
            flops=2 * frames * scores * (3 * width + wide),
            bytes_accessed=scores * (6 * width + 2 * wide),
            transcendentals=4 * frames * scores,
        ),
        name="heads",
    )(sc, hidden, teacher_in, head_weight, teacher_head_weight)


def back_kernel(sc_ref, g4_ref, h_ref, pre_ref, w_ref, mine_ref, other_ref, g_s, pad_s, tap_s, ht_s, res_s):
    step = pl.program_id(0)
    frames, width = g4_ref.shape

    @pl.when(step == 0)
    def _():
        g_s[...] = g4_ref[...]
        pad_s[...] = jnp.zeros_like(pad_s)

    g_act = frame_mask(sc_ref, frames) * g_s[...]
    pre = pre_ref[0]
    sigma = jax.nn.sigmoid(pre)
    g_pre = (g_act * sigma * (1.0 + pre * (1.0 - sigma))).astype(BF16)
    pad_s[PAD : PAD + frames] = g_pre.astype(F32)
    tap_s[1] = g_pre
    for at in range(LAYERS):

        @pl.when(step == LAYERS - 1 - at)
        def _():
            reach = CLASSES * 2**at
            tap_s[0] = pad_s[PAD + reach : PAD + reach + frames].astype(BF16)
            tap_s[2] = pad_s[PAD - reach : PAD - reach + frames].astype(BF16)

    ht_s[...] = h_ref[0].T
    first = sc_ref[2] == 0
    low = low_lanes((32, 128))
    for tap in range(TAPS):
        res_s[...] = dot(ht_s[...], tap_s[tap])
        for nz, fz in ((0, 0), (0, 1), (1, 0), (1, 1)):
            for ny, fy in ((0, 0), (0, 1), (1, 0), (1, 1)):
                found = []
                for core in range(2):
                    zh, zl = high_low(core, nz, fz)
                    yh, yl = high_low(core, ny, fy)
                    cols = slice((yh * 2 + yl) * 128, (yh * 2 + yl + 1) * 128)
                    rows = [((xl * 4 + zh * 2 + zl) * 2 + core) * 32 for xl in range(2)]
                    a, b = (res_s[r : r + 32, cols] for r in rows)
                    if core == 1:
                        b = pltpu.roll(b, 64, 1)
                    found.append((jnp.where(low, a, b), jnp.where(low, b, a)))
                for nx in range(2):
                    mine = jnp.where(first, found[0][nx], found[1][nx])
                    other = jnp.where(first, found[1][nx], found[0][nx])
                    mine_ref[nx, ny, nz, tap, fz, fy] = mine
                    other_ref[nx, ny, nz, tap, fz, fy] = encode(other)

    @pl.when(step < LAYERS - 1)
    def _():
        g_s[...] = (
            g_act
            + dot_nt(tap_s[0], w_ref[0, 0])
            + dot_nt(tap_s[1], w_ref[0, 1])
            + dot_nt(tap_s[2], w_ref[0, 2])
        )


def back(sc, g4, saved, pre, weight):
    frames, width = g4.shape
    one = pl.BlockSpec((1, frames, width), lambda i: (LAYERS - 1 - i, 0, 0))
    block = (2, 2, 2, TAPS, 2, 2, 32, width // 4)
    shape = (2, 2, 2, LAYERS * TAPS, 2, 2, 32, width // 4)
    out = pl.BlockSpec(block, lambda i: (0, 0, 0, LAYERS - 1 - i, 0, 0, 0, 0))
    return pl.pallas_call(
        back_kernel,
        grid=(LAYERS,),
        in_specs=[
            pl.BlockSpec(memory_space=pltpu.SMEM),
            pl.BlockSpec((frames, width), lambda i: (0, 0)),
            one,
            one,
            pl.BlockSpec((1, TAPS, width, width), lambda i: (LAYERS - 1 - i, 0, 0, 0)),
        ],
        out_specs=[out, out],
        out_shape=[jax.ShapeDtypeStruct(shape, F32), jax.ShapeDtypeStruct(shape, BF16)],
        scratch_shapes=[
            pltpu.VMEM((frames, width), F32),
            pltpu.VMEM((frames + 2 * PAD, width), F32),
            pltpu.VMEM((TAPS, frames, width), BF16),
            pltpu.VMEM((width, frames), BF16),
            pltpu.VMEM((width, width), F32),
        ],
        compiler_params=params("arbitrary"),
        cost_estimate=pl.CostEstimate(
            flops=2 * (2 * LAYERS - 1) * TAPS * frames * width * width,
            bytes_accessed=LAYERS * (TAPS * width * width * 8 + frames * width * 6),
            transcendentals=LAYERS * frames * width,
        ),
        name="back",
    )(sc, g4, saved, pre, weight)


def total_of(ref, *at):
    total = decode(ref[(0, *at)])
    for i in range(1, 8):
        total = total + decode(ref[(i, *at)])
    return total


def head_far_kernel(got_ref, out_ref):
    half = got_ref.shape[-1] // 2
    for fz in range(2):
        for fy in range(2):
            for fx in range(2):
                for c in range(half // 128):
                    lanes = slice(fx * half + c * 128, fx * half + (c + 1) * 128)
                    total = total_of(got_ref, fz, fy, slice(None), lanes)
                    out_ref[fx * 4 + fy * 2 + fz, c * 32 : (c + 1) * 32] = encode(total)


def head_far(got):
    tile = got.shape[-1]
    return pl.pallas_call(
        head_far_kernel,
        out_shape=jax.ShapeDtypeStruct((8, 32 * tile // 256, 128), BF16),
        in_specs=[whole()],
        out_specs=whole(),
        compiler_params=params(),
        cost_estimate=pl.CostEstimate(
            flops=8 * got.size, bytes_accessed=3 * got.size, transcendentals=got.size
        ),
        name="head_far",
    )(got)


def conv_far_kernel(got_ref, head_ref, out_ref):
    cut = head_ref.shape[1]
    out_ref[:, :cut] = head_ref[...]
    low = low_lanes((32, 128))
    half = LAYERS * TAPS // 2
    for t in range(half):
        for fz in range(2):
            for fy in range(2):
                a = total_of(got_ref, t, fz, fy)
                b = total_of(got_ref, t + half, fz, fy)
                rows = slice(cut + t * 32, cut + (t + 1) * 32)
                out_ref[fy * 2 + fz, rows] = encode(jnp.where(low, a, pltpu.roll(b, 64, 1)))
                out_ref[4 + fy * 2 + fz, rows] = encode(jnp.where(low, pltpu.roll(a, 64, 1), b))


def conv_far(got, head):
    return pl.pallas_call(
        conv_far_kernel,
        out_shape=jax.ShapeDtypeStruct((8, head.shape[1] + LAYERS * TAPS * 16, 128), BF16),
        in_specs=[whole(), whole()],
        out_specs=whole(),
        compiler_params=params(),
        name="conv_far",
    )(got, head)


def finish_kernel(got_ref, conv_ref, head_ref):
    blocks = head_ref.shape[1] // 128
    for c in range(blocks):
        head_ref[:, c * 128 : (c + 1) * 128] = total_of(got_ref, slice(c * 32, (c + 1) * 32))
    half = LAYERS * TAPS // 2
    for t in range(half):
        total = total_of(got_ref, slice((blocks + t) * 32, (blocks + t + 1) * 32))
        for tap, value in ((t, total), (t + half, pltpu.roll(total, 64, 1))):
            conv_ref[tap // TAPS, tap % TAPS] = value[:, :64]


def finish(got, scores):
    return pl.pallas_call(
        finish_kernel,
        out_shape=[
            jax.ShapeDtypeStruct((LAYERS, TAPS, 32, 64), F32),
            jax.ShapeDtypeStruct((32, scores // 8), F32),
        ],
        in_specs=[whole()],
        out_specs=[whole(), whole()],
        compiler_params=params(),
        name="finish",
    )(got)


def pair_sum(mine, other):
    return encode(mine + decode(lax.ppermute(other, AXES, other_core())))


def on_device(student_in, teacher_rows, valid, conv_weight, head_weight, teacher_head_weight):
    _, frames, width = student_in.shape
    scores = head_weight.shape[1]
    loss_scale = scores / (3.0 * math.sqrt(READ * TM * frames))
    sc = jnp.stack([valid[0], lax.axis_index("tm"), lax.axis_index("read") % 2])
    regrouped = regroup(student_in[0]).reshape(TM, frames // TM, width)
    student = exchange(regrouped, frame_groups()).reshape(frames, width)
    teacher = regroup(teacher_rows[0]).reshape(TM, frames // TM, -1)
    teacher = exchange(teacher, frame_groups()).reshape(frames, -1)

    saved, pre, hidden = convolve(sc, student, conv_weight)
    mine, other, g4 = heads(sc, hidden, teacher, head_weight, teacher_head_weight, loss_scale)
    near = pair_sum(mine, other)
    near, g4 = lax.optimization_barrier((near, g4))
    head_got = exchange(near.reshape(8, 4 * 32, scores // 4), near_groups())

    mine, other = back(sc, g4, saved, pre, conv_weight)
    near = pair_sum(mine, other)
    conv_got = exchange(near.reshape(8, LAYERS * TAPS * 4 * 32, width // 4), near_groups())

    far = head_far(head_got.reshape(8, 2, 2, 32, scores // 4))
    far = conv_far(conv_got.reshape(8, LAYERS * TAPS, 2, 2, 32, width // 4), far)
    return tuple(finish(exchange(far, far_groups()), scores))


def solution(mesh):
    return jax.shard_map(
        on_device,
        mesh=mesh,
        in_specs=(P("read", "tm", None), P("read", "tm", None), P("read"), P(), P(), P()),
        out_specs=(P(None, None, "read", "tm"), P("read", "tm")),
        check_vma=False,
    )
```

profile of v0, /device:TPU:0, one launch (start us, length us, event | category | flops | bytes accessed | tf_op | source)
XLA Modules:
  0.0 164.0 jit_solution(9002155271683968674)
XLA Ops:
  0.6 2.3 %regroup.2 = bf16[512,512]{1,0:T(8,128)(2,1)} custom-call(bf16[512,512]{1,0:T(8,128)(2,1)} %bitcast.17), custom_call_target="tpu_custom_call" | custom-call | tf_op jit(solution)/shard_map/regroup/pallas_call | solution.py:118
  2.9 7.0 %all-to-all-start = ((bf16[8,64,512]{2,1,0:T(8,128)(2,1)}), bf16[8,64,512]{2,1,0:T(8,128)(2,1)S(1)}, u32[]{:S(2)}, u32[]{:S(2)}) async-start(bf16[8,64,512]{2,1,0:T(8,128)(2,1)} %bitcast.14), calls=%async_computation | async-start | bytes 1048576 | tf_op jit(solution)/shard_map/all_to_all | solution.py:69
  9.9 2.6 %regroup.3 = bf16[512,768]{1,0:T(8,128)(2,1)} custom-call(bf16[512,768]{1,0:T(8,128)(2,1)} %bitcast.15), custom_call_target="tpu_custom_call" | custom-call | tf_op jit(solution)/shard_map/regroup/pallas_call | solution.py:118
  12.6 9.0 %all-to-all-done = bf16[8,64,512]{2,1,0:T(8,128)(2,1)S(1)} async-done(((bf16[8,64,512]{2,1,0:T(8,128)(2,1)}), bf16[8,64,512]{2,1,0:T(8,128)(2,1)S(1)}, u32[]{:S(2)}, u32[]{:S(2)}) %all-to-all-start) | async-done | bytes 524320 | tf_op jit(solution)/shard_map/all_to_all | solution.py:69
  21.5 0.0 copy-start.1
  21.5 3.5 %all-to-all-start.1 = ((bf16[8,64,768]{2,1,0:T(8,128)(2,1)}), bf16[8,64,768]{2,1,0:T(8,128)(2,1)S(1)}, u32[]{:S(2)}, u32[]{:S(2)}) async-start(bf16[8,64,768]{2,1,0:T(8,128)(2,1)} %bitcast.13), calls=%async_computation.1 | async-start | bytes 1572864 | tf_op jit(solution)/shard_map/all_to_all | solution.py:69
  25.7 0.6 pad_add_fusion.sc_ref
  26.3 0.0 copy-done.1
  26.3 8.5 %convolve.1 = (bf16[4,512,512]{2,1,0:T(8,128)(2,1)}, f32[4,512,512]{2,1,0:T(8,128)}, bf16[512,512]{1,0:T(8,128)(2,1)}) custom-call(s32[3]{0:T(128)} %pad_add_fusion.sc_ref, bf16[512,512]{1,0:T(8,128)(2,1)} %bitcast.18, bf16[4,3,512,512]{3,2,1,0:T(8,128)(2,1)} %w_ref.3), custom_call_target="tpu_custom_call" | custom-call | flops 3221225472 | bytes 12582912 | tf_op jit(solution)/shard_map/convolve/pallas_call | solution.py:158
  34.8 3.7 %all-to-all-done.1 = bf16[8,64,768]{2,1,0:T(8,128)(2,1)S(1)} async-done(((bf16[8,64,768]{2,1,0:T(8,128)(2,1)}), bf16[8,64,768]{2,1,0:T(8,128)(2,1)S(1)}, u32[]{:S(2)}, u32[]{:S(2)}) %all-to-all-start.1) | async-done | bytes 786464 | tf_op jit(solution)/shard_map/all_to_all | solution.py:69
  38.5 0.0 copy-start
  38.5 0.9 copy-done
  39.4 22.5 %heads.1 = (f32[2,2,2,2,2,32,1280]{6,5,4,3,2,1,0:T(8,128)}, bf16[2,2,2,2,2,32,1280]{6,5,4,3,2,1,0:T(8,128)(2,1)}, f32[512,512]{1,0:T(8,128)}) custom-call(s32[3]{0:T(128)} %pad_add_fusion.sc_ref, bf16[512,512]{1,0:T(8,128)(2,1)} %get-tuple-element.12.h_ref, bf16[512,768]{1,0:T(8,128)(2,1)} %bitcast.16, bf16[512,5120]{1,0:T(8,128)(2,1)} %ws_ref.1, ...), custom_call_target="tpu_custom_call" | custom-call | flops 12079595520 | bytes 23592960 | tf_op jit(solution)/shard_map/heads/pallas_call | solution.py:263
  62.0 0.1 collective-permute-start
  62.1 5.1 %collective-permute-done = bf16[2,2,2,2,2,32,1280]{6,5,4,3,2,1,0:T(8,128)(2,1)S(1)} collective-permute-done((bf16[2,2,2,2,2,32,1280]{6,5,4,3,2,1,0:T(8,128)(2,1)}, bf16[2,2,2,2,2,32,1280]{6,5,4,3,2,1,0:T(8,128)(2,1)S(1)}, u32[]{:S(2)}, u32[]{:S(2)}) %collective-permute-start) | collective-permute-done | bytes 2621472 | tf_op jit(solution)/shard_map/ppermute | solution.py:480
  67.2 5.6 %fusion.7 = bf16[2,2,2,2,2,32,1280]{6,5,4,3,2,1,0:T(8,128)(2,1)} fusion(f32[2,2,2,2,2,32,1280]{6,5,4,3,2,1,0:T(8,128)} %get-tuple-element.13, bf16[2,2,2,2,2,32,1280]{6,5,4,3,2,1,0:T(8,128)(2,1)S(1)} %collective-permute-done), kind=kLoop, calls=%fused_computation.13 | loop fusion | flops 10485760 | bytes 10485760 | tf_op jit(solution)/shard_map/convert_element_type | solution.py:73
  72.8 14.1 %back.1 = (f32[2,2,2,12,2,2,32,128]{7,6,5,4,3,2,1,0:T(8,128)}, bf16[2,2,2,12,2,2,32,128]{7,6,5,4,3,2,1,0:T(8,128)(2,1)}) custom-call(s32[3]{0:T(128)} %pad_add_fusion.sc_ref, f32[512,512]{1,0:T(8,128)} %get-tuple-element.16.g4_ref, bf16[4,512,512]{2,1,0:T(8,128)(2,1)} %get-tuple-element.17.h_ref, f32[4,512,512]{2,1,0:T(8,128)} %get-tuple-element.18.pre_ref, ...), custom_call_target="tpu_custom_call" | custom-call | flops 5637144576 | bytes 31457280 | tf_op jit(solution)/shard_map/back/pallas_call | solution.py:366
  86.9 0.1 collective-permute-start.1
  87.0 4.6 %all-to-all-start.3 = ((bf16[8,128,1280]{2,1,0:T(8,128)(2,1)}), bf16[8,128,1280]{2,1,0:T(8,128)(2,1)}, u32[]{:S(2)}, u32[]{:S(2)}) async-start(bf16[8,128,1280]{2,1,0:T(8,128)(2,1)} %bitcast.12), calls=%async_computation.3 | async-start | bytes 5242880 | tf_op jit(solution)/shard_map/all_to_all | solution.py:69
  91.6 1.1 collective-permute-done.1
  92.7 6.4 %fusion.3 = bf16[2,2,2,12,2,2,32,128]{7,6,5,4,3,2,1,0:T(8,128)(2,1)} fusion(f32[2,2,2,12,2,2,32,128]{7,6,5,4,3,2,1,0:T(8,128)} %get-tuple-element.19, bf16[2,2,2,12,2,2,32,128]{7,6,5,4,3,2,1,0:T(8,128)(2,1)S(1)} %collective-permute-done.1), kind=kLoop, calls=%fused_computation.9 | loop fusion | flops 12582912 | bytes 12582912 | tf_op jit(solution)/shard_map/convert_element_type | solution.py:73
  99.1 11.8 %all-to-all-done.3 = bf16[8,128,1280]{2,1,0:T(8,128)(2,1)} async-done(((bf16[8,128,1280]{2,1,0:T(8,128)(2,1)}), bf16[8,128,1280]{2,1,0:T(8,128)(2,1)}, u32[]{:S(2)}, u32[]{:S(2)}) %all-to-all-start.3) | async-done | bytes 2621472 | tf_op jit(solution)/shard_map/all_to_all | solution.py:69
  110.8 4.4 %all-to-all-start.2 = ((bf16[8,1536,128]{2,1,0:T(8,128)(2,1)}), bf16[8,1536,128]{2,1,0:T(8,128)(2,1)}, u32[]{:S(2)}, u32[]{:S(2)}) async-start(bf16[8,1536,128]{2,1,0:T(8,128)(2,1)} %bitcast.8), calls=%async_computation.2 | async-start | bytes 6291456 | tf_op jit(solution)/shard_map/all_to_all | solution.py:69
  115.3 3.5 %head_far.1.head_ref = bf16[8,160,128]{2,1,0:T(8,128)(2,1)} custom-call(bf16[8,2,2,32,1280]{4,3,2,1,0:T(8,128)(2,1)} %bitcast.11.got_ref), custom_call_target="tpu_custom_call" | custom-call | flops 10485760 | bytes 3932160 | tf_op jit(solution)/shard_map/head_far/pallas_call | solution.py:415
  118.8 19.7 %all-to-all-done.2 = bf16[8,1536,128]{2,1,0:T(8,128)(2,1)} async-done(((bf16[8,1536,128]{2,1,0:T(8,128)(2,1)}), bf16[8,1536,128]{2,1,0:T(8,128)(2,1)}, u32[]{:S(2)}, u32[]{:S(2)}) %all-to-all-start.2) | async-done | bytes 3145760 | tf_op jit(solution)/shard_map/all_to_all | solution.py:69
  138.5 4.2 %conv_far.1 = bf16[8,352,128]{2,1,0:T(8,128)(2,1)} custom-call(bf16[8,12,2,2,32,128]{5,4,3,2,1,0:T(8,128)(2,1)} %bitcast.9.got_ref, bf16[8,160,128]{2,1,0:T(8,128)(2,1)} %head_far.1.head_ref), custom_call_target="tpu_custom_call" | custom-call | tf_op jit(solution)/shard_map/conv_far/pallas_call | solution.py:444
  142.7 19.2 %all_to_all.25.got_ref = bf16[8,352,128]{2,1,0:T(8,128)(2,1)} all-to-all(bf16[8,352,128]{2,1,0:T(8,128)(2,1)} %conv_far.1), channel_id=1, replica_groups={{0,48,6,54,65,113,71,119},{16,32,22,38,81,97,87,103},{2,50,4,52,67,115,..., dimensions={0} | all-to-all | bytes 1441792 | tf_op jit(solution)/shard_map/all_to_all | solution.py:69
  161.9 2.0 %finish.1 = (f32[4,3,32,64]{3,2,1,0:T(8,128)}, f32[32,640]{1,0:T(8,128)}) custom-call(bf16[8,352,128]{2,1,0:T(8,128)(2,1)} %all_to_all.25.got_ref), custom_call_target="tpu_custom_call" | custom-call | tf_op jit(solution)/shard_map/finish/pallas_call | solution.py:466
Async XLA Ops:
  2.9 18.6 %all-to-all-start = ((bf16[8,64,512]{2,1,0:T(8,128)(2,1)}), bf16[8,64,512]{2,1,0:T(8,128)(2,1)S(1)}, u32[]{:S(2)}, u32[]{:S(2)}) async-start(bf16[8,64,512]{2,1,0:T(8,128)(2,1)} %bitcast.14), calls=%async_computation | async-start | bytes 1048576 | tf_op jit(solution)/shard_map/all_to_all | solution.py:69
  21.5 4.8 %copy-start.1 = (bf16[8,64,512]{2,1,0:T(8,128)(2,1)}, bf16[8,64,512]{2,1,0:T(8,128)(2,1)S(1)}, u32[]{:S(2)}) copy-start(bf16[8,64,512]{2,1,0:T(8,128)(2,1)S(1)} %all-to-all-done) | copy-start | bytes 1572868
  21.5 17.0 %all-to-all-start.1 = ((bf16[8,64,768]{2,1,0:T(8,128)(2,1)}), bf16[8,64,768]{2,1,0:T(8,128)(2,1)S(1)}, u32[]{:S(2)}, u32[]{:S(2)}) async-start(bf16[8,64,768]{2,1,0:T(8,128)(2,1)} %bitcast.13), calls=%async_computation.1 | async-start | bytes 1572864 | tf_op jit(solution)/shard_map/all_to_all | solution.py:69
  38.5 0.9 copy-start
  62.0 5.2 %collective-permute-start = (bf16[2,2,2,2,2,32,1280]{6,5,4,3,2,1,0:T(8,128)(2,1)}, bf16[2,2,2,2,2,32,1280]{6,5,4,3,2,1,0:T(8,128)(2,1)S(1)}, u32[]{:S(2)}, u32[]{:S(2)}) collective-permute-start(bf16[2,2,2,2,2,32,1280]{6,5,4,3,2,1,0:T(8,128)(2,1)} %get-tuple-element.14), channel_id=1, source_target_pairs={{0,8},{1,9},{2,10},{3,11},{4,12},{5,13},{6,14},{7,15},{8,0},{9,1},... | collective-permute-start | bytes 7864328 | tf_op jit(solution)/shard_map/ppermute | solution.py:480
  86.9 5.9 %collective-permute-start.1 = (bf16[2,2,2,12,2,2,32,128]{7,6,5,4,3,2,1,0:T(8,128)(2,1)}, bf16[2,2,2,12,2,2,32,128]{7,6,5,4,3,2,1,0:T(8,128)(2,1)S(1)}, u32[]{:S(2)}, u32[]{:S(2)}) collective-permute-start(bf16[2,2,2,12,2,2,32,128]{7,6,5,4,3,2,1,0:T(8,128)(2,1)} %get-tuple-element.20), channel_id=1, source_target_pairs={{0,8},{1,9},{2,10},{3,11},{4,12},{5,13},{6,14},{7,15},{8,0},{9,1},... | collective-permute-start | bytes 9437192 | tf_op jit(solution)/shard_map/ppermute | solution.py:480
  87.0 23.8 %all-to-all-start.3 = ((bf16[8,128,1280]{2,1,0:T(8,128)(2,1)}), bf16[8,128,1280]{2,1,0:T(8,128)(2,1)}, u32[]{:S(2)}, u32[]{:S(2)}) async-start(bf16[8,128,1280]{2,1,0:T(8,128)(2,1)} %bitcast.12), calls=%async_computation.3 | async-start | bytes 5242880 | tf_op jit(solution)/shard_map/all_to_all | solution.py:69
  110.8 27.6 %all-to-all-start.2 = ((bf16[8,1536,128]{2,1,0:T(8,128)(2,1)}), bf16[8,1536,128]{2,1,0:T(8,128)(2,1)}, u32[]{:S(2)}, u32[]{:S(2)}) async-start(bf16[8,1536,128]{2,1,0:T(8,128)(2,1)} %bitcast.8), calls=%async_computation.2 | async-start | bytes 6291456 | tf_op jit(solution)/shard_map/all_to_all | solution.py:69
where the time goes:
time: 165 us; the launch traced here: 164 us
  Pallas kernels  59.8 us (36%)
  waiting for transfers between devices  50.4 us (31%)
  starting transfers between devices  19.8 us (12%)
  blocking collectives  19.2 us (12%)
  other arithmetic  12.5 us (8%)
    all_to_all x4, waiting for transfers between devices, exchange(): return lax.all_to_all(x, AXES, 0, 0, tiled=True, axis_index_groups=groups)  44.1 us
    pallas_call x1, Pallas kernels, heads(): pl.pallas_call(kernel, grid_spec=pltpu.PrefetchScalarGridSpec(num_scalar_...  22.5 us
    all_to_all x4, starting transfers between devices, exchange(): return lax.all_to_all(x, AXES, 0, 0, tiled=True, axis_index_groups=groups)  19.6 us
    all_to_all x1, blocking collectives, exchange(): return lax.all_to_all(x, AXES, 0, 0, tiled=True, axis_index_groups=groups)  19.2 us
    pallas_call x1, Pallas kernels, back(): pl.pallas_call(back_kernel, grid=(LAYERS,), in_specs=[pl.BlockSpec(memory...  14.1 us
    convert_element_type x2, other arithmetic, encode(): return (x * jnp.abs(x)).astype(BF16)  12 us
    pallas_call x1, Pallas kernels, convolve(): pl.pallas_call(conv_kernel, grid=(LAYERS,), in_specs=[pl.BlockSpec(memory...  8.46 us
    ppermute x2, waiting for transfers between devices, pair_sum(): return encode(mine + decode(lax.ppermute(other, AXES, other_core())))  6.23 us
  transfers between devices with their start and end apart: 6, of which 6 were waited for; matrix products, arithmetic and copies ran while one was open for 4% of the time, Pallas kernels for 9%

commit v1 on v0

--- a/solution.py
+++ b/solution.py
@@ -301,7 +301,8 @@
     )(sc, hidden, teacher_in, head_weight, teacher_head_weight)
 
 
-def back_kernel(sc_ref, g4_ref, h_ref, pre_ref, w_ref, mine_ref, other_ref, g_s, pad_s, tap_s, ht_s, res_s):
+def back_kernel(top, count, sc_ref, g4_ref, h_ref, pre_ref, w_ref, *refs):
+    *out_g, mine_ref, other_ref, g_s, pad_s, tap_s, ht_s, res_s = refs
     step = pl.program_id(0)
     frames, width = g4_ref.shape
 
@@ -316,9 +317,9 @@
     g_pre = (g_act * sigma * (1.0 + pre * (1.0 - sigma))).astype(BF16)
     pad_s[PAD : PAD + frames] = g_pre.astype(F32)
     tap_s[1] = g_pre
-    for at in range(LAYERS):
-
-        @pl.when(step == LAYERS - 1 - at)
+    for at in range(top, top - count, -1):
+
+        @pl.when(step == top - at)
         def _():
             reach = CLASSES * 2**at
             tap_s[0] = pad_s[PAD + reach : PAD + reach + frames].astype(BF16)
@@ -347,34 +348,47 @@
                     mine_ref[nx, ny, nz, tap, fz, fy] = mine
                     other_ref[nx, ny, nz, tap, fz, fy] = encode(other)
 
-    @pl.when(step < LAYERS - 1)
-    def _():
-        g_s[...] = (
+    def through():
+        return (
             g_act
             + dot_nt(tap_s[0], w_ref[0, 0])
             + dot_nt(tap_s[1], w_ref[0, 1])
             + dot_nt(tap_s[2], w_ref[0, 2])
         )
 
-
-def back(sc, g4, saved, pre, weight):
-    frames, width = g4.shape
-    one = pl.BlockSpec((1, frames, width), lambda i: (LAYERS - 1 - i, 0, 0))
+    @pl.when(step < count - 1)
+    def _():
+        g_s[...] = through()
+
+    if out_g:
+
+        @pl.when(step == count - 1)
+        def _():
+            out_g[0][...] = through()
+
+
+def back(sc, g, saved, pre, weight, top, count):
+    frames, width = g.shape
+    more = top - count + 1 > 0
+    one = pl.BlockSpec((1, frames, width), lambda i: (top - i, 0, 0))
+    flat = pl.BlockSpec((frames, width), lambda i: (0, 0))
     block = (2, 2, 2, TAPS, 2, 2, 32, width // 4)
-    shape = (2, 2, 2, LAYERS * TAPS, 2, 2, 32, width // 4)
-    out = pl.BlockSpec(block, lambda i: (0, 0, 0, LAYERS - 1 - i, 0, 0, 0, 0))
-    return pl.pallas_call(
-        back_kernel,
-        grid=(LAYERS,),
+    shape = (2, 2, 2, count * TAPS, 2, 2, 32, width // 4)
+    out = pl.BlockSpec(block, lambda i: (0, 0, 0, count - 1 - i, 0, 0, 0, 0))
+    dots = 2 * count - (not more)
+    return pl.pallas_call(
+        functools.partial(back_kernel, top, count),
+        grid=(count,),
         in_specs=[
             pl.BlockSpec(memory_space=pltpu.SMEM),
-            pl.BlockSpec((frames, width), lambda i: (0, 0)),
+            flat,
             one,
             one,
-            pl.BlockSpec((1, TAPS, width, width), lambda i: (LAYERS - 1 - i, 0, 0, 0)),
-        ],
-        out_specs=[out, out],
-        out_shape=[jax.ShapeDtypeStruct(shape, F32), jax.ShapeDtypeStruct(shape, BF16)],
+            pl.BlockSpec((1, TAPS, width, width), lambda i: (top - i, 0, 0, 0)),
+        ],
+        out_specs=[flat] * more + [out, out],
+        out_shape=[jax.ShapeDtypeStruct((frames, width), F32)] * more
+        + [jax.ShapeDtypeStruct(shape, F32), jax.ShapeDtypeStruct(shape, BF16)],
         scratch_shapes=[
             pltpu.VMEM((frames, width), F32),
             pltpu.VMEM((frames + 2 * PAD, width), F32),
@@ -384,12 +398,43 @@
         ],
         compiler_params=params("arbitrary"),
         cost_estimate=pl.CostEstimate(
-            flops=2 * (2 * LAYERS - 1) * TAPS * frames * width * width,
-            bytes_accessed=LAYERS * (TAPS * width * width * 8 + frames * width * 6),
-            transcendentals=LAYERS * frames * width,
+            flops=2 * dots * TAPS * frames * width * width,
+            bytes_accessed=count * (TAPS * width * width * 5 + frames * width * 6),
+            transcendentals=count * frames * width,
         ),
         name="back",
-    )(sc, g4, saved, pre, weight)
+    )(sc, g, saved, pre, weight)
+
+
+def pair_kernel(*refs):
+    *ins, out_ref = refs
+    at = 0
+    for mine, other in zip(ins[::2], ins[1::2]):
+        rows = mine.shape[1]
+        out_ref[0, at : at + rows] = encode(mine[0] + decode(other[0]))
+        at += rows
+
+
+def pair_sum(pieces):
+    lanes = pieces[0][0].shape[2]
+    rows = sum(mine.shape[1] for mine, _ in pieces)
+    specs = [
+        pl.BlockSpec((1, mine.shape[1], lanes), lambda i: (i, 0, 0))
+        for mine, _ in pieces
+        for _ in range(2)
+    ]
+    return pl.pallas_call(
+        pair_kernel,
+        grid=(8,),
+        in_specs=specs,
+        out_specs=pl.BlockSpec((1, rows, lanes), lambda i: (i, 0, 0)),
+        out_shape=jax.ShapeDtypeStruct((8, rows, lanes), BF16),
+        compiler_params=params("arbitrary"),
+        cost_estimate=pl.CostEstimate(
+            flops=64 * rows * lanes, bytes_accessed=64 * rows * lanes, transcendentals=8 * rows * lanes
+        ),
+        name="pair_sum",
+    )(*[x for piece in pieces for x in piece])
 
 
 def total_of(ref, *at):
@@ -401,20 +446,17 @@
 
 def head_far_kernel(got_ref, out_ref):
     half = got_ref.shape[-1] // 2
-    for fz in range(2):
-        for fy in range(2):
-            for fx in range(2):
-                for c in range(half // 128):
-                    lanes = slice(fx * half + c * 128, fx * half + (c + 1) * 128)
-                    total = total_of(got_ref, fz, fy, slice(None), lanes)
-                    out_ref[fx * 4 + fy * 2 + fz, c * 32 : (c + 1) * 32] = encode(total)
+    for fz, fy, fx in BITS:
+        for c in range(half // 128):
+            lanes = slice(fx * half + c * 128, fx * half + (c + 1) * 128)
+            out_ref[fx * 4 + fy * 2 + fz, c] = encode(total_of(got_ref, fz, fy, slice(None), lanes))
 
 
 def head_far(got):
     tile = got.shape[-1]
     return pl.pallas_call(
         head_far_kernel,
-        out_shape=jax.ShapeDtypeStruct((8, 32 * tile // 256, 128), BF16),
+        out_shape=jax.ShapeDtypeStruct((8, tile // 256, 32, 128), BF16),
         in_specs=[whole()],
         out_specs=whole(),
         compiler_params=params(),
@@ -425,39 +467,55 @@
     )(got)
 
 
-def conv_far_kernel(got_ref, head_ref, out_ref):
-    cut = head_ref.shape[1]
-    out_ref[:, :cut] = head_ref[...]
+def conv_far_kernel(a_ref, b_ref, head_ref, out_ref):
+    step = pl.program_id(0)
+    blocks, each = head_ref.shape[1], a_ref.shape[1]
     low = low_lanes((32, 128))
-    half = LAYERS * TAPS // 2
-    for t in range(half):
+
+    @pl.when(step == 0)
+    def _():
+        out_ref[:, :blocks] = head_ref[...]
+
+    for t in range(each):
+        at = blocks + step * each + t
         for fz in range(2):
             for fy in range(2):
-                a = total_of(got_ref, t, fz, fy)
-                b = total_of(got_ref, t + half, fz, fy)
-                rows = slice(cut + t * 32, cut + (t + 1) * 32)
-                out_ref[fy * 2 + fz, rows] = encode(jnp.where(low, a, pltpu.roll(b, 64, 1)))
-                out_ref[4 + fy * 2 + fz, rows] = encode(jnp.where(low, pltpu.roll(a, 64, 1), b))
+                a = total_of(a_ref, t, fz, fy)
+                b = total_of(b_ref, t, fz, fy)
+                out_ref[fy * 2 + fz, at] = encode(jnp.where(low, a, pltpu.roll(b, 64, 1)))
+                out_ref[4 + fy * 2 + fz, at] = encode(jnp.where(low, pltpu.roll(a, 64, 1), b))
 
 
 def conv_far(got, head):
+    half = LAYERS * TAPS // 2
+    steps = 3
+    block = (8, half // steps, 2, 2, 32, 128)
+    shape = (8, head.shape[1] + half, 32, 128)
     return pl.pallas_call(
         conv_far_kernel,
-        out_shape=jax.ShapeDtypeStruct((8, head.shape[1] + LAYERS * TAPS * 16, 128), BF16),
-        in_specs=[whole(), whole()],
-        out_specs=whole(),
-        compiler_params=params(),
+        grid=(steps,),
+        out_shape=jax.ShapeDtypeStruct(shape, BF16),
+        in_specs=[
+            pl.BlockSpec(block, lambda i: (0, i, 0, 0, 0, 0)),
+            pl.BlockSpec(block, lambda i: (0, i + steps, 0, 0, 0, 0)),
+            pl.BlockSpec(head.shape, lambda i: (0, 0, 0, 0)),
+        ],
+        out_specs=pl.BlockSpec(shape, lambda i: (0, 0, 0, 0)),
+        compiler_params=params("arbitrary"),
+        cost_estimate=pl.CostEstimate(
+            flops=8 * got.size, bytes_accessed=3 * got.size, transcendentals=got.size
+        ),
         name="conv_far",
-    )(got, head)
+    )(got, got, head)
 
 
 def finish_kernel(got_ref, conv_ref, head_ref):
     blocks = head_ref.shape[1] // 128
     for c in range(blocks):
-        head_ref[:, c * 128 : (c + 1) * 128] = total_of(got_ref, slice(c * 32, (c + 1) * 32))
+        head_ref[:, c * 128 : (c + 1) * 128] = total_of(got_ref, c)
     half = LAYERS * TAPS // 2
     for t in range(half):
-        total = total_of(got_ref, slice((blocks + t) * 32, (blocks + t + 1) * 32))
+        total = total_of(got_ref, blocks + t)
         for tap, value in ((t, total), (t + half, pltpu.roll(total, 64, 1))):
             conv_ref[tap // TAPS, tap % TAPS] = value[:, :64]
 
@@ -476,8 +534,8 @@
     )(got)
 
 
-def pair_sum(mine, other):
-    return encode(mine + decode(lax.ppermute(other, AXES, other_core())))
+def swap(x):
+    return lax.ppermute(x, AXES, other_core())
 
 
 def on_device(student_in, teacher_rows, valid, conv_weight, head_weight, teacher_head_weight):
@@ -491,14 +549,23 @@
     teacher = exchange(teacher, frame_groups()).reshape(frames, -1)
 
     saved, pre, hidden = convolve(sc, student, conv_weight)
-    mine, other, g4 = heads(sc, hidden, teacher, head_weight, teacher_head_weight, loss_scale)
-    near = pair_sum(mine, other)
-    near, g4 = lax.optimization_barrier((near, g4))
-    head_got = exchange(near.reshape(8, 4 * 32, scores // 4), near_groups())
-
-    mine, other = back(sc, g4, saved, pre, conv_weight)
-    near = pair_sum(mine, other)
-    conv_got = exchange(near.reshape(8, LAYERS * TAPS * 4 * 32, width // 4), near_groups())
+    mine, other, g = heads(sc, hidden, teacher, head_weight, teacher_head_weight, loss_scale)
+    other = swap(other)
+    g, mine_hi, other_hi = back(sc, g, saved, pre, conv_weight, LAYERS - 1, 2)
+    other_hi = swap(other_hi)
+    mine, other, g = lax.optimization_barrier((mine, other, g))
+    shape = (8, 4 * 32, scores // 4)
+    near = pair_sum([(mine.reshape(shape), other.reshape(shape))])
+    near, g = lax.optimization_barrier((near, g))
+    head_got = exchange(near, near_groups())
+
+    mine_lo, other_lo = back(sc, g, saved, pre, conv_weight, LAYERS - 3, 2)
+    other_lo = swap(other_lo)
+    other_lo, head_got = lax.optimization_barrier((other_lo, head_got))
+    shape = (8, LAYERS * TAPS * 2 * 32, width // 4)
+    low = (mine_lo.reshape(shape), other_lo.reshape(shape))
+    high = (mine_hi.reshape(shape), other_hi.reshape(shape))
+    conv_got = exchange(pair_sum([low, high]), near_groups())
 
     far = head_far(head_got.reshape(8, 2, 2, 32, scores // 4))
     far = conv_far(conv_got.reshape(8, LAYERS * TAPS, 2, 2, 32, width // 4), far)

time: 165 us -> 166 us (level)
  Pallas kernels: 59.8 us -> 79.9 us
  other arithmetic: 12.5 us -> 0.56 us
  waiting for transfers between devices: 50.4 us -> 41 us
  starting transfers between devices: 19.8 us -> 21.7 us
    pallas_call x3 -> x6, Pallas kernels: 21.8 us -> 41.8 us  [the longest x2 18.4 us: back(): pl.pallas_call(functools.partial(back_kernel, top, count), grid=(count,),...]
    convert_element_type x2 -> x0, other arithmetic: 12 us -> none  [encode(): return (x * jnp.abs(x)).astype(BF16)]
    all_to_all x4, waiting for transfers between devices: 44.1 us -> 36.3 us  [exchange(): return lax.all_to_all(x, AXES, 0, 0, tiled=True, axis_index_groups=groups)]
    ppermute x2 -> x3, starting transfers between devices: 0.22 us -> 2.09 us  [swap(): return lax.ppermute(x, AXES, other_core())]
    ppermute x2 -> x3, waiting for transfers between devices: 6.23 us -> 4.64 us  [swap(): return lax.ppermute(x, AXES, other_core())]
  transfers between devices with their start and end apart: 6 -> 7, of which waited for: 6 -> 5; matrix products, arithmetic and copies ran while one was open for 4% -> 0% of each run, Pallas kernels for 9% -> 20%
where the time goes in v1:
time: 166 us; the launch traced here: 165 us
  Pallas kernels  79.9 us (48%)
  waiting for transfers between devices  41 us (25%)
  starting transfers between devices  21.7 us (13%)
  blocking collectives  19.2 us (12%)
    all_to_all x4, waiting for transfers between devices, exchange(): return lax.all_to_all(x, AXES, 0, 0, tiled=True, axis_index_groups=groups)  36.3 us
    pallas_call x1, Pallas kernels, heads(): pl.pallas_call(kernel, grid_spec=pltpu.PrefetchScalarGridSpec(num_scalar_...  22.6 us
    all_to_all x4, starting transfers between devices, exchange(): return lax.all_to_all(x, AXES, 0, 0, tiled=True, axis_index_groups=groups)  19.6 us
    all_to_all x1, blocking collectives, exchange(): return lax.all_to_all(x, AXES, 0, 0, tiled=True, axis_index_groups=groups)  19.2 us
    pallas_call x2, Pallas kernels, back(): pl.pallas_call(functools.partial(back_kernel, top, count), grid=(count,),...  18.4 us
    pallas_call x2, Pallas kernels, pair_sum(): pl.pallas_call(pair_kernel, grid=(8,), in_specs=specs, out_specs=pl.Block...  15.5 us
    pallas_call x1, Pallas kernels, convolve(): pl.pallas_call(conv_kernel, grid=(LAYERS,), in_specs=[pl.BlockSpec(memory...  8.5 us
    pallas_call x2, Pallas kernels, regroup(): pl.pallas_call(regroup_kernel, out_shape=jax.ShapeDtypeStruct(x.shape, BF...  4.95 us
  transfers between devices with their start and end apart: 7, of which 5 were waited for; matrix products, arithmetic and copies ran while one was open for 0% of the time, Pallas kernels for 20%

profile of v1, /device:TPU:0, one launch (start us, length us, event | category | flops | bytes accessed | tf_op | source)
XLA Modules:
  0.0 164.6 jit_solution(14964434512319912043)
XLA Ops:
  0.6 2.3 %regroup.2 = bf16[512,512]{1,0:T(8,128)(2,1)} custom-call(bf16[512,512]{1,0:T(8,128)(2,1)} %bitcast.24), custom_call_target="tpu_custom_call" | custom-call | tf_op jit(solution)/shard_map/regroup/pallas_call | solution.py:118
  2.9 7.0 %all-to-all-start = ((bf16[8,64,512]{2,1,0:T(8,128)(2,1)}), bf16[8,64,512]{2,1,0:T(8,128)(2,1)S(1)}, u32[]{:S(2)}, u32[]{:S(2)}) async-start(bf16[8,64,512]{2,1,0:T(8,128)(2,1)} %bitcast.20), calls=%async_computation | async-start | bytes 1048576 | tf_op jit(solution)/shard_map/all_to_all | solution.py:69
  9.9 2.6 %regroup.3 = bf16[512,768]{1,0:T(8,128)(2,1)} custom-call(bf16[512,768]{1,0:T(8,128)(2,1)} %bitcast.22), custom_call_target="tpu_custom_call" | custom-call | tf_op jit(solution)/shard_map/regroup/pallas_call | solution.py:118
  12.6 9.0 %all-to-all-done = bf16[8,64,512]{2,1,0:T(8,128)(2,1)S(1)} async-done(((bf16[8,64,512]{2,1,0:T(8,128)(2,1)}), bf16[8,64,512]{2,1,0:T(8,128)(2,1)S(1)}, u32[]{:S(2)}, u32[]{:S(2)}) %all-to-all-start) | async-done | bytes 524320 | tf_op jit(solution)/shard_map/all_to_all | solution.py:69
  21.5 0.0 copy-start.2
  21.5 3.5 %all-to-all-start.1 = ((bf16[8,64,768]{2,1,0:T(8,128)(2,1)}), bf16[8,64,768]{2,1,0:T(8,128)(2,1)S(1)}, u32[]{:S(2)}, u32[]{:S(2)}) async-start(bf16[8,64,768]{2,1,0:T(8,128)(2,1)} %bitcast.17), calls=%async_computation.1 | async-start | bytes 1572864 | tf_op jit(solution)/shard_map/all_to_all | solution.py:69
  25.8 0.6 pad_add_fusion.sc_ref
  26.3 0.0 copy-done.2
  26.3 8.5 %convolve.1 = (bf16[4,512,512]{2,1,0:T(8,128)(2,1)}, f32[4,512,512]{2,1,0:T(8,128)}, bf16[512,512]{1,0:T(8,128)(2,1)}) custom-call(s32[3]{0:T(128)} %pad_add_fusion.sc_ref, bf16[512,512]{1,0:T(8,128)(2,1)} %bitcast.25, bf16[4,3,512,512]{3,2,1,0:T(8,128)(2,1)} %w_ref.5), custom_call_target="tpu_custom_call" | custom-call | flops 3221225472 | bytes 12582912 | tf_op jit(solution)/shard_map/convolve/pallas_call | solution.py:158
  34.8 3.7 %all-to-all-done.1 = bf16[8,64,768]{2,1,0:T(8,128)(2,1)S(1)} async-done(((bf16[8,64,768]{2,1,0:T(8,128)(2,1)}), bf16[8,64,768]{2,1,0:T(8,128)(2,1)S(1)}, u32[]{:S(2)}, u32[]{:S(2)}) %all-to-all-start.1) | async-done | bytes 786464 | tf_op jit(solution)/shard_map/all_to_all | solution.py:69
  38.5 0.0 copy-start.1
  38.5 0.9 copy-done.1
  39.4 22.6 %heads.1 = (f32[2,2,2,2,2,32,1280]{6,5,4,3,2,1,0:T(8,128)}, bf16[2,2,2,2,2,32,1280]{6,5,4,3,2,1,0:T(8,128)(2,1)}, f32[512,512]{1,0:T(8,128)}) custom-call(s32[3]{0:T(128)} %pad_add_fusion.sc_ref, bf16[512,512]{1,0:T(8,128)(2,1)} %get-tuple-element.20.h_ref, bf16[512,768]{1,0:T(8,128)(2,1)} %bitcast.23, bf16[512,5120]{1,0:T(8,128)(2,1)} %ws_ref.1, ...), custom_call_target="tpu_custom_call" | custom-call | flops 12079595520 | bytes 23592960 | tf_op jit(solution)/shard_map/heads/pallas_call | solution.py:263
  62.0 0.1 collective-permute-start
  62.1 9.8 %back.2 = (f32[512,512]{1,0:T(8,128)}, f32[2,2,2,6,2,2,32,128]{7,6,5,4,3,2,1,0:T(8,128)}, bf16[2,2,2,6,2,2,32,128]{7,6,5,4,3,2,1,0:T(8,128)(2,1)}) custom-call(s32[3]{0:T(128)} %pad_add_fusion.sc_ref, f32[512,512]{1,0:T(8,128)} %get-tuple-element.23.g4_ref, bf16[4,512,512]{2,1,0:T(8,128)(2,1)} %get-tuple-element.24.h_ref, ...), custom_call_target="tpu_custom_call" | custom-call | flops 3221225472 | bytes 11010048 | tf_op jit(solution)/shard_map/back/pallas_call | solution.py:379
  71.9 0.0 collective-permute-done
  71.9 7.5 %pair_sum.2 = bf16[8,128,1280]{2,1,0:T(8,128)(2,1)} custom-call(f32[8,128,1280]{2,1,0:T(8,128)} %bitcast.16, bf16[8,128,1280]{2,1,0:T(8,128)(2,1)} %bitcast.9.refs_1_), custom_call_target="tpu_custom_call" | custom-call | flops 10485760 | bytes 10485760 | tf_op jit(solution)/shard_map/pair_sum/pallas_call | solution.py:426
  79.4 4.6 %all-to-all-start.2 = ((bf16[8,128,1280]{2,1,0:T(8,128)(2,1)}), bf16[8,128,1280]{2,1,0:T(8,128)(2,1)}, u32[]{:S(2)}, u32[]{:S(2)}) async-start(bf16[8,128,1280]{2,1,0:T(8,128)(2,1)} %pair_sum.2), calls=%async_computation.2 | async-start | bytes 5242880 | tf_op jit(solution)/shard_map/all_to_all | solution.py:69
  84.0 8.5 %back.3 = (f32[2,2,2,6,2,2,32,128]{7,6,5,4,3,2,1,0:T(8,128)}, bf16[2,2,2,6,2,2,32,128]{7,6,5,4,3,2,1,0:T(8,128)(2,1)}) custom-call(s32[3]{0:T(128)} %pad_add_fusion.sc_ref, f32[512,512]{1,0:T(8,128)} %get-tuple-element.30.g4_ref, bf16[4,512,512]{2,1,0:T(8,128)(2,1)} %get-tuple-element.24.h_ref, f32[4,512,512]{2,1,0:T(8,128)} %get-tuple-element.25.pre_ref, ...), custom_call_target="tpu_custom_call" | custom-call | flops 2415919104 | bytes 11010048 | tf_op jit(solution)/shard_map/back/pallas_call | solution.py:379
  92.6 1.9 %collective-permute-start.1 = (bf16[2,2,2,6,2,2,32,128]{7,6,5,4,3,2,1,0:T(8,128)(2,1)}, bf16[2,2,2,6,2,2,32,128]{7,6,5,4,3,2,1,0:T(8,128)(2,1)S(1)}, u32[]{:S(2)}, u32[]{:S(2)}) collective-permute-start(bf16[2,2,2,6,2,2,32,128]{7,6,5,4,3,2,1,0:T(8,128)(2,1)} %get-tuple-element.32), channel_id=1, source_target_pairs={{0,8},{1,9},{2,10},{3,11},{4,12},{5,13},{6,14},{7,15},{8,0},{9,1},... | collective-permute-start | bytes 4718600 | tf_op jit(solution)/shard_map/ppermute | solution.py:538
  94.5 0.1 collective-permute-start.2
  94.6 4.6 %collective-permute-done.1 = bf16[2,2,2,6,2,2,32,128]{7,6,5,4,3,2,1,0:T(8,128)(2,1)S(1)} collective-permute-done((bf16[2,2,2,6,2,2,32,128]{7,6,5,4,3,2,1,0:T(8,128)(2,1)}, bf16[2,2,2,6,2,2,32,128]{7,6,5,4,3,2,1,0:T(8,128)(2,1)S(1)}, u32[]{:S(2)}, u32[]{:S(2)}) %collective-permute-start.1) | collective-permute-done | bytes 1572896 | tf_op jit(solution)/shard_map/ppermute | solution.py:538
  99.2 0.0 copy-start
  99.2 4.1 %all-to-all-done.2 = bf16[8,128,1280]{2,1,0:T(8,128)(2,1)} async-done(((bf16[8,128,1280]{2,1,0:T(8,128)(2,1)}), bf16[8,128,1280]{2,1,0:T(8,128)(2,1)}, u32[]{:S(2)}, u32[]{:S(2)}) %all-to-all-start.2) | async-done | bytes 2621472 | tf_op jit(solution)/shard_map/all_to_all | solution.py:69
  103.3 0.0 collective-permute-done.2
  103.3 0.0 copy-done
  103.3 8.0 %pair_sum.3 = bf16[8,1536,128]{2,1,0:T(8,128)(2,1)} custom-call(f32[8,768,128]{2,1,0:T(8,128)} %bitcast.19, bf16[8,768,128]{2,1,0:T(8,128)(2,1)} %bitcast.21, f32[8,768,128]{2,1,0:T(8,128)} %bitcast.18, bf16[8,768,128]{2,1,0:T(8,128)(2,1)} %bitcast.13.refs_3_), custom_call_target="tpu_custom_call" | custom-call | flops 12582912 | bytes 12582912 | tf_op jit(solution)/shard_map/pair_sum/pallas_call | solution.py:426
  111.3 4.5 %all-to-all-start.3 = ((bf16[8,1536,128]{2,1,0:T(8,128)(2,1)}), bf16[8,1536,128]{2,1,0:T(8,128)(2,1)}, u32[]{:S(2)}, u32[]{:S(2)}) async-start(bf16[8,1536,128]{2,1,0:T(8,128)(2,1)} %pair_sum.3), calls=%async_computation.3 | async-start | bytes 6291456 | tf_op jit(solution)/shard_map/all_to_all | solution.py:69
  115.7 3.5 %head_far.1.head_ref = bf16[8,5,32,128]{3,2,1,0:T(8,128)(2,1)} custom-call(bf16[8,2,2,32,1280]{4,3,2,1,0:T(8,128)(2,1)} %bitcast.15.got_ref), custom_call_target="tpu_custom_call" | custom-call | flops 10485760 | bytes 3932160 | tf_op jit(solution)/shard_map/head_far/pallas_call | solution.py:457
  119.3 19.6 %all-to-all-done.3 = bf16[8,1536,128]{2,1,0:T(8,128)(2,1)} async-done(((bf16[8,1536,128]{2,1,0:T(8,128)(2,1)}), bf16[8,1536,128]{2,1,0:T(8,128)(2,1)}, u32[]{:S(2)}, u32[]{:S(2)}) %all-to-all-start.3) | async-done | bytes 3145760 | tf_op jit(solution)/shard_map/all_to_all | solution.py:69
  138.9 4.4 %conv_far.1 = bf16[8,11,32,128]{3,2,1,0:T(8,128)(2,1)} custom-call(bf16[8,12,2,2,32,128]{5,4,3,2,1,0:T(8,128)(2,1)} %bitcast.14.a_ref.b_ref, bf16[8,12,2,2,32,128]{5,4,3,2,1,0:T(8,128)(2,1)} %bitcast.14.a_ref.b_ref, bf16[8,5,32,128]{3,2,1,0:T(8,128)(2,1)} %head_far.1.head_ref), custom_call_target="tpu_custom_call" | custom-call | flops 12582912 | bytes 4718592 | tf_op jit(solution)/shard_map/conv_far/pallas_call | solution.py:494
  143.3 19.2 %all_to_all.25.got_ref = bf16[8,11,32,128]{3,2,1,0:T(8,128)(2,1)} all-to-all(bf16[8,11,32,128]{3,2,1,0:T(8,128)(2,1)} %conv_far.1), channel_id=1, replica_groups={{0,48,6,54,65,113,71,119},{16,32,22,38,81,97,87,103},{2,50,4,52,67,115,..., dimensions={0} | all-to-all | bytes 1441792 | tf_op jit(solution)/shard_map/all_to_all | solution.py:69
  162.5 2.0 %finish.1 = (f32[4,3,32,64]{3,2,1,0:T(8,128)}, f32[32,640]{1,0:T(8,128)}) custom-call(bf16[8,11,32,128]{3,2,1,0:T(8,128)(2,1)} %all_to_all.25.got_ref), custom_call_target="tpu_custom_call" | custom-call | tf_op jit(solution)/shard_map/finish/pallas_call | solution.py:524
Async XLA Ops:
  2.9 18.6 %all-to-all-start = ((bf16[8,64,512]{2,1,0:T(8,128)(2,1)}), bf16[8,64,512]{2,1,0:T(8,128)(2,1)S(1)}, u32[]{:S(2)}, u32[]{:S(2)}) async-start(bf16[8,64,512]{2,1,0:T(8,128)(2,1)} %bitcast.20), calls=%async_computation | async-start | bytes 1048576 | tf_op jit(solution)/shard_map/all_to_all | solution.py:69
  21.5 4.8 %copy-start.2 = (bf16[8,64,512]{2,1,0:T(8,128)(2,1)}, bf16[8,64,512]{2,1,0:T(8,128)(2,1)S(1)}, u32[]{:S(2)}) copy-start(bf16[8,64,512]{2,1,0:T(8,128)(2,1)S(1)} %all-to-all-done) | copy-start | bytes 1572868
  21.5 17.0 %all-to-all-start.1 = ((bf16[8,64,768]{2,1,0:T(8,128)(2,1)}), bf16[8,64,768]{2,1,0:T(8,128)(2,1)S(1)}, u32[]{:S(2)}, u32[]{:S(2)}) async-start(bf16[8,64,768]{2,1,0:T(8,128)(2,1)} %bitcast.17), calls=%async_computation.1 | async-start | bytes 1572864 | tf_op jit(solution)/shard_map/all_to_all | solution.py:69
  38.5 0.9 copy-start.1
  62.0 9.9 %collective-permute-start = (bf16[2,2,2,2,2,32,1280]{6,5,4,3,2,1,0:T(8,128)(2,1)}, bf16[2,2,2,2,2,32,1280]{6,5,4,3,2,1,0:T(8,128)(2,1)}, u32[]{:S(2)}, u32[]{:S(2)}) collective-permute-start(bf16[2,2,2,2,2,32,1280]{6,5,4,3,2,1,0:T(8,128)(2,1)} %get-tuple-element.22), channel_id=1, source_target_pairs={{0,8},{1,9},{2,10},{3,11},{4,12},{5,13},{6,14},{7,15},{8,0},{9,1},... | collective-permute-start | bytes 7864328 | tf_op jit(solution)/shard_map/ppermute | solution.py:538
  79.4 23.9 %all-to-all-start.2 = ((bf16[8,128,1280]{2,1,0:T(8,128)(2,1)}), bf16[8,128,1280]{2,1,0:T(8,128)(2,1)}, u32[]{:S(2)}, u32[]{:S(2)}) async-start(bf16[8,128,1280]{2,1,0:T(8,128)(2,1)} %pair_sum.2), calls=%async_computation.2 | async-start | bytes 5242880 | tf_op jit(solution)/shard_map/all_to_all | solution.py:69
  92.6 6.6 %collective-permute-start.1 = (bf16[2,2,2,6,2,2,32,128]{7,6,5,4,3,2,1,0:T(8,128)(2,1)}, bf16[2,2,2,6,2,2,32,128]{7,6,5,4,3,2,1,0:T(8,128)(2,1)S(1)}, u32[]{:S(2)}, u32[]{:S(2)}) collective-permute-start(bf16[2,2,2,6,2,2,32,128]{7,6,5,4,3,2,1,0:T(8,128)(2,1)} %get-tuple-element.32), channel_id=1, source_target_pairs={{0,8},{1,9},{2,10},{3,11},{4,12},{5,13},{6,14},{7,15},{8,0},{9,1},... | collective-permute-start | bytes 4718600 | tf_op jit(solution)/shard_map/ppermute | solution.py:538
  94.5 8.8 %collective-permute-start.2 = (bf16[2,2,2,6,2,2,32,128]{7,6,5,4,3,2,1,0:T(8,128)(2,1)}, bf16[2,2,2,6,2,2,32,128]{7,6,5,4,3,2,1,0:T(8,128)(2,1)}, u32[]{:S(2)}, u32[]{:S(2)}) collective-permute-start(bf16[2,2,2,6,2,2,32,128]{7,6,5,4,3,2,1,0:T(8,128)(2,1)} %get-tuple-element.36), channel_id=1, source_target_pairs={{0,8},{1,9},{2,10},{3,11},{4,12},{5,13},{6,14},{7,15},{8,0},{9,1},... | collective-permute-start | bytes 4718600 | tf_op jit(solution)/shard_map/ppermute | solution.py:538
  99.2 4.1 %copy-start = (bf16[2,2,2,6,2,2,32,128]{7,6,5,4,3,2,1,0:T(8,128)(2,1)}, bf16[2,2,2,6,2,2,32,128]{7,6,5,4,3,2,1,0:T(8,128)(2,1)S(1)}, u32[]{:S(2)}) copy-start(bf16[2,2,2,6,2,2,32,128]{7,6,5,4,3,2,1,0:T(8,128)(2,1)S(1)} %collective-permute-done.1) | copy-start | bytes 4718596
  111.3 27.6 %all-to-all-start.3 = ((bf16[8,1536,128]{2,1,0:T(8,128)(2,1)}), bf16[8,1536,128]{2,1,0:T(8,128)(2,1)}, u32[]{:S(2)}, u32[]{:S(2)}) async-start(bf16[8,1536,128]{2,1,0:T(8,128)(2,1)} %pair_sum.3), calls=%async_computation.3 | async-start | bytes 6291456 | tf_op jit(solution)/shard_map/all_to_all | solution.py:69

commit v2 on v1

--- a/solution.py
+++ b/solution.py
@@ -183,8 +183,16 @@
     )(sc, x, weight)
 
 
-def head_kernel(scale, tiles, sc_ref, h_ref, t_ref, ws_ref, wt_ref, mine_ref, other_ref, g_ref,
-                sq_s, es_s, et_s, sum_s, ht_s, gs_s, res_s):
+def split_rows(core, ht_s, mine_ref, other_ref):
+    for ref, owner in ((mine_ref, core), (other_ref, 1 - core)):
+        for at, (nz, fz, xl) in enumerate(BITS):
+            high = jnp.where(owner == 0, fz, nz)
+            row = ((xl * 4 + high * 2 + (nz ^ fz)) * 2 + owner) * 32
+            ref[at * 32 : (at + 1) * 32] = ht_s[pl.ds(pl.multiple_of(row, 32), 32)]
+
+
+def head_kernel(scale, tiles, sc_ref, h_ref, t_ref, ws_ref, wt_ref, score_ref, g_ref, mine_ref, other_ref,
+                sq_s, es_s, et_s, sum_s, ht_s):
     step = pl.program_id(0)
     frames, width = h_ref.shape
     tile = ws_ref.shape[1]
@@ -214,6 +222,7 @@
             inverse = factor / jnp.sum(sum_s[i], axis=1, keepdims=True)
             sum_s[i] = jnp.broadcast_to(inverse, (frames, 128))
         ht_s[...] = h_ref[...].T
+        split_rows(sc_ref[2], ht_s, mine_ref, other_ref)
         g_ref[...] = jnp.zeros_like(g_ref)
 
     @pl.when(step >= tiles)
@@ -223,22 +232,8 @@
             cols = slice(c * 128, (c + 1) * 128)
             squash = sq_s[at, :, cols]
             p = es_s[at, :, cols] * sum_s[0] - et_s[at, :, cols] * sum_s[1]
-            gs_s[:, cols] = (p * (1.0 - squash * squash)).astype(BF16)
-        res_s[...] = dot(ht_s[...], gs_s[...])
-        g_ref[...] += dot_nt(gs_s[...], ws_ref[...])
-        first = sc_ref[2] == 0
-        half = tile // 2
-        for nx, nz, fz in BITS:
-            for fx in range(2):
-                found = []
-                for core in range(2):
-                    xh, xl = high_low(core, nx, fx)
-                    zh, zl = high_low(core, nz, fz)
-                    r = ((xl * 4 + zh * 2 + zl) * 2 + core) * 32
-                    found.append(res_s[r : r + 32, xh * half : (xh + 1) * half])
-                to = slice(fx * half, (fx + 1) * half)
-                mine_ref[nx, 0, nz, fz, 0, :, to] = jnp.where(first, found[0], found[1])
-                other_ref[nx, 0, nz, fz, 0, :, to] = encode(jnp.where(first, found[1], found[0]))
+            score_ref[:, cols] = (p * (1.0 - squash * squash)).astype(BF16)
+        g_ref[...] += dot_nt(score_ref[...], ws_ref[...])
 
 
 def heads(sc, hidden, teacher_in, head_weight, teacher_head_weight, loss_scale):
@@ -247,62 +242,94 @@
     scores = head_weight.shape[1]
     tiles = 4
     tile = scores // tiles
-
-    def place(i, core):
-        y = jnp.maximum(i - tiles, 0)
-        high, low = y // 2, y % 2
-        even = core == 0
-        near = jnp.where(even, high ^ low, high)
-        far = jnp.where(even, high, high ^ low)
-        return (0, near, 0, 0, far, 0, 0)
-
-    block = (2, 1, 2, 2, 1, 32, tile)
-    shape = (2, 2, 2, 2, 2, 32, tile)
-    kernel = functools.partial(head_kernel, 5.0 * loss_scale, tiles)
     big = pltpu.VMEM((tiles, frames, tile), F32)
-    return pl.pallas_call(
-        kernel,
+    rows = pl.BlockSpec((width // 2, frames), lambda i: (0, 0))
+    return pl.pallas_call(
+        functools.partial(head_kernel, 5.0 * loss_scale, tiles),
+        grid=(2 * tiles,),
+        in_specs=[
+            pl.BlockSpec(memory_space=pltpu.SMEM),
+            pl.BlockSpec((frames, width), lambda i: (0, 0)),
+            pl.BlockSpec((frames, wide), lambda i: (0, 0)),
+            pl.BlockSpec((width, tile), lambda i: (0, i % tiles)),
+            pl.BlockSpec((wide, tile), lambda i: (0, jnp.minimum(i, tiles - 1))),
+        ],
+        out_specs=[
+            pl.BlockSpec((frames, tile), lambda i: (0, jnp.maximum(i - tiles, 0))),
+            pl.BlockSpec((frames, width), lambda i: (0, 0)),
+            rows,
+            rows,
+        ],
+        scratch_shapes=[
+            big,
+            big,
+            big,
+            pltpu.VMEM((2, frames, 128), F32),
+            pltpu.VMEM((width, frames), BF16),
+        ],
+        out_shape=[
+            jax.ShapeDtypeStruct((frames, scores), BF16),
+            jax.ShapeDtypeStruct((frames, width), F32),
+            jax.ShapeDtypeStruct((width // 2, frames), BF16),
+            jax.ShapeDtypeStruct((width // 2, frames), BF16),
+        ],
+        compiler_params=params("arbitrary"),
+        cost_estimate=pl.CostEstimate(
+            flops=2 * frames * scores * (2 * width + wide),
+            bytes_accessed=scores * (6 * width + 2 * wide),
+            transcendentals=4 * frames * scores,
+        ),
+        name="heads",
+    )(sc, hidden, teacher_in, head_weight, teacher_head_weight)
+
+
+def head_grad_kernel(sc_ref, ha_ref, hb_ref, ga_ref, gb_ref, out_ref, res_s):
+    half = res_s.shape[1] // 2
+    res_s[...] = dot(ha_ref[...], ga_ref[...]) + dot(hb_ref[...], gb_ref[...])
+    first = sc_ref[2] == 0
+    for nx, nz, fz in BITS:
+        for fx in range(2):
+            row = ((nz * 2 + fz) * 2 + (nx ^ fx)) * 32
+            rows = slice(row, row + 32)
+            value = res_s[rows, fx * half : (fx + 1) * half]
+            if nx != fx:
+                value = jnp.where(first, value, res_s[rows, nx * half : (nx + 1) * half])
+            out_ref[nx, 0, nz, fz, 0, :, fx * half : (fx + 1) * half] = encode(value)
+
+
+def head_grad(sc, h_mine, h_other, score_mine, score_other):
+    rows, frames = h_mine.shape
+    scores = score_mine.shape[1]
+    tile = scores // 4
+
+    def place(i, sc):
+        high, low = i // 2, i % 2
+        even = sc[2] == 0
+        return (0, jnp.where(even, high ^ low, high), 0, 0, jnp.where(even, high, high ^ low), 0, 0)
+
+    hidden = pl.BlockSpec((rows, frames), lambda i, sc: (0, 0))
+    score = pl.BlockSpec((frames, tile), lambda i, sc: (0, i))
+    return pl.pallas_call(
+        head_grad_kernel,
         grid_spec=pltpu.PrefetchScalarGridSpec(
             num_scalar_prefetch=1,
-            grid=(2 * tiles,),
-            in_specs=[
-                pl.BlockSpec((frames, width), lambda i, sc: (0, 0)),
-                pl.BlockSpec((frames, wide), lambda i, sc: (0, 0)),
-                pl.BlockSpec((width, tile), lambda i, sc: (0, i % tiles)),
-                pl.BlockSpec((wide, tile), lambda i, sc: (0, jnp.minimum(i, tiles - 1))),
-            ],
-            out_specs=[
-                pl.BlockSpec(block, lambda i, sc: place(i, sc[2])),
-                pl.BlockSpec(block, lambda i, sc: place(i, 1 - sc[2])),
-                pl.BlockSpec((frames, width), lambda i, sc: (0, 0)),
-            ],
-            scratch_shapes=[
-                big,
-                big,
-                big,
-                pltpu.VMEM((2, frames, 128), F32),
-                pltpu.VMEM((width, frames), BF16),
-                pltpu.VMEM((frames, tile), BF16),
-                pltpu.VMEM((width, tile), F32),
-            ],
-        ),
-        out_shape=[
-            jax.ShapeDtypeStruct(shape, F32),
-            jax.ShapeDtypeStruct(shape, BF16),
-            jax.ShapeDtypeStruct((frames, width), F32),
-        ],
+            grid=(4,),
+            in_specs=[hidden, hidden, score, score],
+            out_specs=pl.BlockSpec((2, 1, 2, 2, 1, 32, tile), place),
+            scratch_shapes=[pltpu.VMEM((rows, tile), F32)],
+        ),
+        out_shape=jax.ShapeDtypeStruct((2, 2, 2, 2, 2, 32, tile), BF16),
         compiler_params=params("arbitrary"),
         cost_estimate=pl.CostEstimate(
-            flops=2 * frames * scores * (3 * width + wide),
-            bytes_accessed=scores * (6 * width + 2 * wide),
-            transcendentals=4 * frames * scores,
-        ),
-        name="heads",
-    )(sc, hidden, teacher_in, head_weight, teacher_head_weight)
-
-
-def back_kernel(top, count, sc_ref, g4_ref, h_ref, pre_ref, w_ref, *refs):
-    *out_g, mine_ref, other_ref, g_s, pad_s, tap_s, ht_s, res_s = refs
+            flops=4 * rows * frames * scores,
+            bytes_accessed=4 * frames * scores + 2 * rows * scores,
+            transcendentals=0,
+        ),
+        name="head_grad",
+    )(sc, h_mine, h_other, score_mine, score_other)
+
+
+def back_kernel(sc_ref, g4_ref, h_ref, pre_ref, w_ref, send_ref, mine_ref, g_s, pad_s, tap_s, ht_s):
     step = pl.program_id(0)
     frames, width = g4_ref.shape
 
@@ -315,126 +342,138 @@
     pre = pre_ref[0]
     sigma = jax.nn.sigmoid(pre)
     g_pre = (g_act * sigma * (1.0 + pre * (1.0 - sigma))).astype(BF16)
-    pad_s[PAD : PAD + frames] = g_pre.astype(F32)
-    tap_s[1] = g_pre
-    for at in range(top, top - count, -1):
-
-        @pl.when(step == top - at)
-        def _():
-            reach = CLASSES * 2**at
-            tap_s[0] = pad_s[PAD + reach : PAD + reach + frames].astype(BF16)
-            tap_s[2] = pad_s[PAD - reach : PAD - reach + frames].astype(BF16)
-
+    send_ref[0, :2] = g_pre.reshape(2, frames // 2, width)
     ht_s[...] = h_ref[0].T
-    first = sc_ref[2] == 0
-    low = low_lanes((32, 128))
-    for tap in range(TAPS):
-        res_s[...] = dot(ht_s[...], tap_s[tap])
-        for nz, fz in ((0, 0), (0, 1), (1, 0), (1, 1)):
-            for ny, fy in ((0, 0), (0, 1), (1, 0), (1, 1)):
-                found = []
-                for core in range(2):
-                    zh, zl = high_low(core, nz, fz)
-                    yh, yl = high_low(core, ny, fy)
-                    cols = slice((yh * 2 + yl) * 128, (yh * 2 + yl + 1) * 128)
-                    rows = [((xl * 4 + zh * 2 + zl) * 2 + core) * 32 for xl in range(2)]
-                    a, b = (res_s[r : r + 32, cols] for r in rows)
-                    if core == 1:
-                        b = pltpu.roll(b, 64, 1)
-                    found.append((jnp.where(low, a, b), jnp.where(low, b, a)))
-                for nx in range(2):
-                    mine = jnp.where(first, found[0][nx], found[1][nx])
-                    other = jnp.where(first, found[1][nx], found[0][nx])
-                    mine_ref[nx, ny, nz, tap, fz, fy] = mine
-                    other_ref[nx, ny, nz, tap, fz, fy] = encode(other)
-
-    def through():
-        return (
+    split_rows(sc_ref[2], ht_s, mine_ref.at[0], send_ref.at[0, 2])
+
+    @pl.when(step < LAYERS - 1)
+    def _():
+        pad_s[PAD : PAD + frames] = g_pre.astype(F32)
+        for at in range(LAYERS - 1, 0, -1):
+
+            @pl.when(step == LAYERS - 1 - at)
+            def _():
+                reach = CLASSES * 2**at
+                tap_s[0] = pad_s[PAD + reach : PAD + reach + frames].astype(BF16)
+                tap_s[1] = pad_s[PAD - reach : PAD - reach + frames].astype(BF16)
+
+        g_s[...] = (
             g_act
             + dot_nt(tap_s[0], w_ref[0, 0])
-            + dot_nt(tap_s[1], w_ref[0, 1])
-            + dot_nt(tap_s[2], w_ref[0, 2])
+            + dot_nt(g_pre, w_ref[0, 1])
+            + dot_nt(tap_s[1], w_ref[0, 2])
         )
 
-    @pl.when(step < count - 1)
-    def _():
-        g_s[...] = through()
-
-    if out_g:
-
-        @pl.when(step == count - 1)
-        def _():
-            out_g[0][...] = through()
-
-
-def back(sc, g, saved, pre, weight, top, count):
+
+def back(sc, g, saved, pre, weight):
     frames, width = g.shape
-    more = top - count + 1 > 0
-    one = pl.BlockSpec((1, frames, width), lambda i: (top - i, 0, 0))
-    flat = pl.BlockSpec((frames, width), lambda i: (0, 0))
-    block = (2, 2, 2, TAPS, 2, 2, 32, width // 4)
-    shape = (2, 2, 2, count * TAPS, 2, 2, 32, width // 4)
-    out = pl.BlockSpec(block, lambda i: (0, 0, 0, count - 1 - i, 0, 0, 0, 0))
-    dots = 2 * count - (not more)
-    return pl.pallas_call(
-        functools.partial(back_kernel, top, count),
-        grid=(count,),
+
+    def at(*block):
+        return pl.BlockSpec((1, *block), lambda i: (LAYERS - 1 - i, *(0 for _ in block)))
+
+    return pl.pallas_call(
+        back_kernel,
+        grid=(LAYERS,),
         in_specs=[
             pl.BlockSpec(memory_space=pltpu.SMEM),
-            flat,
-            one,
-            one,
-            pl.BlockSpec((1, TAPS, width, width), lambda i: (top - i, 0, 0, 0)),
-        ],
-        out_specs=[flat] * more + [out, out],
-        out_shape=[jax.ShapeDtypeStruct((frames, width), F32)] * more
-        + [jax.ShapeDtypeStruct(shape, F32), jax.ShapeDtypeStruct(shape, BF16)],
+            pl.BlockSpec((frames, width), lambda i: (0, 0)),
+            at(frames, width),
+            at(frames, width),
+            pl.BlockSpec(
+                (1, TAPS, width, width), lambda i: (jnp.maximum(LAYERS - 1 - i, 1), 0, 0, 0)
+            ),
+        ],
+        out_specs=[at(3, frames // 2, width), at(width // 2, frames)],
+        out_shape=[
+            jax.ShapeDtypeStruct((LAYERS, 3, frames // 2, width), BF16),
+            jax.ShapeDtypeStruct((LAYERS, width // 2, frames), BF16),
+        ],
         scratch_shapes=[
             pltpu.VMEM((frames, width), F32),
             pltpu.VMEM((frames + 2 * PAD, width), F32),
-            pltpu.VMEM((TAPS, frames, width), BF16),
+            pltpu.VMEM((2, frames, width), BF16),
             pltpu.VMEM((width, frames), BF16),
-            pltpu.VMEM((width, width), F32),
         ],
         compiler_params=params("arbitrary"),
         cost_estimate=pl.CostEstimate(
-            flops=2 * dots * TAPS * frames * width * width,
-            bytes_accessed=count * (TAPS * width * width * 5 + frames * width * 6),
-            transcendentals=count * frames * width,
+            flops=2 * (LAYERS - 1) * TAPS * frames * width * width,
+            bytes_accessed=LAYERS * (TAPS * width * width * 2 + frames * width * 10),
+            transcendentals=LAYERS * frames * width,
         ),
         name="back",
     )(sc, g, saved, pre, weight)
 
 
-def pair_kernel(*refs):
-    *ins, out_ref = refs
-    at = 0
-    for mine, other in zip(ins[::2], ins[1::2]):
-        rows = mine.shape[1]
-        out_ref[0, at : at + rows] = encode(mine[0] + decode(other[0]))
-        at += rows
-
-
-def pair_sum(pieces):
-    lanes = pieces[0][0].shape[2]
-    rows = sum(mine.shape[1] for mine, _ in pieces)
-    specs = [
-        pl.BlockSpec((1, mine.shape[1], lanes), lambda i: (i, 0, 0))
-        for mine, _ in pieces
-        for _ in range(2)
-    ]
-    return pl.pallas_call(
-        pair_kernel,
-        grid=(8,),
-        in_specs=specs,
-        out_specs=pl.BlockSpec((1, rows, lanes), lambda i: (i, 0, 0)),
-        out_shape=jax.ShapeDtypeStruct((8, rows, lanes), BF16),
+def conv_grad_kernel(sc_ref, mine_ref, send_ref, got_ref, out_ref, pad_s, tap_s, res_s):
+    step = pl.program_id(0)
+    rows, frames = mine_ref.shape[1:]
+    width = send_ref.shape[3]
+
+    @pl.when(step == 0)
+    def _():
+        pad_s[...] = jnp.zeros_like(pad_s)
+
+    for side, ref in enumerate((send_ref, got_ref)):
+        g_pre = ref[0, :2].reshape(frames, width)
+        tap_s[1, side] = g_pre
+        pad_s[side, PAD : PAD + frames] = g_pre.astype(F32)
+    for at in range(LAYERS):
+
+        @pl.when(step == at)
+        def _():
+            reach = CLASSES * 2**at
+            for side in range(2):
+                tap_s[0, side] = pad_s[side, PAD + reach : PAD + reach + frames].astype(BF16)
+                tap_s[2, side] = pad_s[side, PAD - reach : PAD - reach + frames].astype(BF16)
+
+    core = sc_ref[2]
+    low = low_lanes((32, 128))
+    for tap in range(TAPS):
+        res_s[...] = dot(mine_ref[0], tap_s[tap, 0]) + dot(got_ref[0, 2], tap_s[tap, 1])
+        for nz, fz, ny in BITS:
+            for fy in range(2):
+                high = jnp.where(core == 0, fy, ny)
+                cols = pl.ds(pl.multiple_of((high * 2 + (ny ^ fy)) * 128, 128), 128)
+                row = (nz * 2 + fz) * 64
+                a = res_s[row : row + 32, cols]
+                b = pltpu.roll(res_s[row + 32 : row + 64, cols], 64 * core, 1)
+                out_ref[0, ny, nz, tap, fz, fy] = encode(jnp.where(low, a, b))
+                out_ref[1, ny, nz, tap, fz, fy] = encode(jnp.where(low, b, a))
+
+
+def conv_grad(sc, mine, send, got):
+    _, rows, frames = mine.shape
+    width = send.shape[3]
+
+    def at(*block):
+        return pl.BlockSpec((1, *block), lambda i: (i, *(0 for _ in block)))
+
+    return pl.pallas_call(
+        conv_grad_kernel,
+        grid=(LAYERS,),
+        in_specs=[
+            pl.BlockSpec(memory_space=pltpu.SMEM),
+            at(rows, frames),
+            at(3, frames // 2, width),
+            at(3, frames // 2, width),
+        ],
+        out_specs=pl.BlockSpec(
+            (2, 2, 2, TAPS, 2, 2, 32, width // 4), lambda i: (0, 0, 0, i, 0, 0, 0, 0)
+        ),
+        out_shape=jax.ShapeDtypeStruct((2, 2, 2, LAYERS * TAPS, 2, 2, 32, width // 4), BF16),
+        scratch_shapes=[
+            pltpu.VMEM((2, frames + 2 * PAD, width), F32),
+            pltpu.VMEM((TAPS, 2, frames, width), BF16),
+            pltpu.VMEM((rows, width), F32),
+        ],
         compiler_params=params("arbitrary"),
         cost_estimate=pl.CostEstimate(
-            flops=64 * rows * lanes, bytes_accessed=64 * rows * lanes, transcendentals=8 * rows * lanes
-        ),
-        name="pair_sum",
-    )(*[x for piece in pieces for x in piece])
+            flops=4 * LAYERS * TAPS * rows * frames * width,
+            bytes_accessed=LAYERS * (7 * rows * frames * 2 + TAPS * rows * width * 2),
+            transcendentals=0,
+        ),
+        name="conv_grad",
+    )(sc, mine, send, got)
 
 
 def total_of(ref, *at):
@@ -549,23 +588,19 @@
     teacher = exchange(teacher, frame_groups()).reshape(frames, -1)
 
     saved, pre, hidden = convolve(sc, student, conv_weight)
-    mine, other, g = heads(sc, hidden, teacher, head_weight, teacher_head_weight, loss_scale)
-    other = swap(other)
-    g, mine_hi, other_hi = back(sc, g, saved, pre, conv_weight, LAYERS - 1, 2)
-    other_hi = swap(other_hi)
-    mine, other, g = lax.optimization_barrier((mine, other, g))
-    shape = (8, 4 * 32, scores // 4)
-    near = pair_sum([(mine.reshape(shape), other.reshape(shape))])
-    near, g = lax.optimization_barrier((near, g))
-    head_got = exchange(near, near_groups())
-
-    mine_lo, other_lo = back(sc, g, saved, pre, conv_weight, LAYERS - 3, 2)
-    other_lo = swap(other_lo)
-    other_lo, head_got = lax.optimization_barrier((other_lo, head_got))
-    shape = (8, LAYERS * TAPS * 2 * 32, width // 4)
-    low = (mine_lo.reshape(shape), other_lo.reshape(shape))
-    high = (mine_hi.reshape(shape), other_hi.reshape(shape))
-    conv_got = exchange(pair_sum([low, high]), near_groups())
+    score, g, h_mine, h_other = heads(
+        sc, hidden, teacher, head_weight, teacher_head_weight, loss_scale
+    )
+    score_got, h_got = swap(score), swap(h_other)
+    send, mine = back(sc, g, saved, pre, conv_weight)
+    got = swap(send)
+    score_got, h_got, mine = lax.optimization_barrier((score_got, h_got, mine))
+    near = head_grad(sc, h_mine, h_got, score, score_got)
+    near, got = lax.optimization_barrier((near, got))
+    head_got = exchange(near.reshape(8, 4 * 32, scores // 4), near_groups())
+    near = conv_grad(sc, mine, send, got)
+    near, head_got = lax.optimization_barrier((near, head_got))
+    conv_got = exchange(near.reshape(8, LAYERS * TAPS * 4 * 32, width // 4), near_groups())
 
     far = head_far(head_got.reshape(8, 2, 2, 32, scores // 4))
     far = conv_far(conv_got.reshape(8, LAYERS * TAPS, 2, 2, 32, width // 4), far)

time: 166 us -> 163 us (0.982)
  Pallas kernels: 79.9 us -> 71 us
  waiting for transfers between devices: 41 us -> 47.6 us
    pallas_call x5 -> x4, Pallas kernels: 56.4 us -> 47.6 us  [the longest x1 18.5 us: heads(): pl.pallas_call(functools.partial(head_kernel, 5.0 * loss_scale, tiles), g...]
    all_to_all x4, waiting for transfers between devices: 36.3 us -> 42.2 us  [exchange(): return lax.all_to_all(x, AXES, 0, 0, tiled=True, axis_index_groups=groups)]
  transfers between devices with their start and end apart: 7 -> 7, of which waited for: 5 -> 5; matrix products, arithmetic and copies ran while one was open for 0% -> 0% of each run, Pallas kernels for 20% -> 27%
where the time goes in v2:
time: 163 us; the launch traced here: 162 us
  Pallas kernels  71 us (44%)
  waiting for transfers between devices  47.6 us (29%)
  starting transfers between devices  20.2 us (12%)
  blocking collectives  19.2 us (12%)
    all_to_all x4, waiting for transfers between devices, exchange(): return lax.all_to_all(x, AXES, 0, 0, tiled=True, axis_index_groups=groups)  42.2 us
    all_to_all x4, starting transfers between devices, exchange(): return lax.all_to_all(x, AXES, 0, 0, tiled=True, axis_index_groups=groups)  19.6 us
    all_to_all x1, blocking collectives, exchange(): return lax.all_to_all(x, AXES, 0, 0, tiled=True, axis_index_groups=groups)  19.2 us
    pallas_call x1, Pallas kernels, heads(): pl.pallas_call(functools.partial(head_kernel, 5.0 * loss_scale, tiles), g...  18.5 us
    pallas_call x1, Pallas kernels, back(): pl.pallas_call(back_kernel, grid=(LAYERS,), in_specs=[pl.BlockSpec(memory...  11.4 us
    pallas_call x1, Pallas kernels, conv_grad(): pl.pallas_call(conv_grad_kernel, grid=(LAYERS,), in_specs=[pl.BlockSpec(m...  9.38 us
    pallas_call x1, Pallas kernels, convolve(): pl.pallas_call(conv_kernel, grid=(LAYERS,), in_specs=[pl.BlockSpec(memory...  8.48 us
    pallas_call x1, Pallas kernels, head_grad(): pl.pallas_call(head_grad_kernel, grid_spec=pltpu.PrefetchScalarGridSpec(n...  8.36 us
  transfers between devices with their start and end apart: 7, of which 5 were waited for; matrix products, arithmetic and copies ran while one was open for 0% of the time, Pallas kernels for 27%

profile of v2, /device:TPU:0, one launch (start us, length us, event | category | flops | bytes accessed | tf_op | source)
XLA Modules:
  0.0 161.6 jit_solution(6422311987773535602)
XLA Ops:
  0.6 2.3 %regroup.2 = bf16[512,512]{1,0:T(8,128)(2,1)} custom-call(bf16[512,512]{1,0:T(8,128)(2,1)} %bitcast.18), custom_call_target="tpu_custom_call" | custom-call | tf_op jit(solution)/shard_map/regroup/pallas_call | solution.py:118
  2.9 7.0 %all-to-all-start = ((bf16[8,64,512]{2,1,0:T(8,128)(2,1)}), bf16[8,64,512]{2,1,0:T(8,128)(2,1)S(1)}, u32[]{:S(2)}, u32[]{:S(2)}) async-start(bf16[8,64,512]{2,1,0:T(8,128)(2,1)} %bitcast.15), calls=%async_computation | async-start | bytes 1048576 | tf_op jit(solution)/shard_map/all_to_all | solution.py:69
  9.9 2.6 %regroup.3 = bf16[512,768]{1,0:T(8,128)(2,1)} custom-call(bf16[512,768]{1,0:T(8,128)(2,1)} %bitcast.16), custom_call_target="tpu_custom_call" | custom-call | tf_op jit(solution)/shard_map/regroup/pallas_call | solution.py:118
  12.6 8.9 %all-to-all-done = bf16[8,64,512]{2,1,0:T(8,128)(2,1)S(1)} async-done(((bf16[8,64,512]{2,1,0:T(8,128)(2,1)}), bf16[8,64,512]{2,1,0:T(8,128)(2,1)S(1)}, u32[]{:S(2)}, u32[]{:S(2)}) %all-to-all-start) | async-done | bytes 524320 | tf_op jit(solution)/shard_map/all_to_all | solution.py:69
  21.5 0.0 copy-start.1
  21.5 3.5 %all-to-all-start.1 = ((bf16[8,64,768]{2,1,0:T(8,128)(2,1)}), bf16[8,64,768]{2,1,0:T(8,128)(2,1)S(1)}, u32[]{:S(2)}, u32[]{:S(2)}) async-start(bf16[8,64,768]{2,1,0:T(8,128)(2,1)} %bitcast.14), calls=%async_computation.1 | async-start | bytes 1572864 | tf_op jit(solution)/shard_map/all_to_all | solution.py:69
  25.7 0.6 pad_add_fusion.sc_ref
  26.3 0.0 copy-done.1
  26.3 8.5 %convolve.1 = (bf16[4,512,512]{2,1,0:T(8,128)(2,1)}, f32[4,512,512]{2,1,0:T(8,128)}, bf16[512,512]{1,0:T(8,128)(2,1)}) custom-call(s32[3]{0:T(128)} %pad_add_fusion.sc_ref, bf16[512,512]{1,0:T(8,128)(2,1)} %bitcast.19, bf16[4,3,512,512]{3,2,1,0:T(8,128)(2,1)} %w_ref.3), custom_call_target="tpu_custom_call" | custom-call | flops 3221225472 | bytes 12582912 | tf_op jit(solution)/shard_map/convolve/pallas_call | solution.py:158
  34.8 3.7 %all-to-all-done.1 = bf16[8,64,768]{2,1,0:T(8,128)(2,1)S(1)} async-done(((bf16[8,64,768]{2,1,0:T(8,128)(2,1)}), bf16[8,64,768]{2,1,0:T(8,128)(2,1)S(1)}, u32[]{:S(2)}, u32[]{:S(2)}) %all-to-all-start.1) | async-done | bytes 786464 | tf_op jit(solution)/shard_map/all_to_all | solution.py:69
  38.5 0.0 copy-start
  38.5 0.9 copy-done
  39.4 18.5 %heads.1 = (bf16[512,5120]{1,0:T(8,128)(2,1)}, f32[512,512]{1,0:T(8,128)}, bf16[256,512]{1,0:T(8,128)(2,1)}, bf16[256,512]{1,0:T(8,128)(2,1)}) custom-call(s32[3]{0:T(128)} %pad_add_fusion.sc_ref, bf16[512,512]{1,0:T(8,128)(2,1)} %get-tuple-element.18.h_ref, bf16[512,768]{1,0:T(8,128)(2,1)} %bitcast.17, bf16[512,5120]{1,0:T(8,128)(2,1)} %ws_ref.1, ...), custom_call_target="tpu_custom_call" | custom-call | flops 9395240960 | bytes 23592960 | tf_op jit(solution)/shard_map/heads/pallas_call | solution.py:247
  57.9 0.1 collective-permute-start
  58.0 0.0 copy-start.3
  58.0 11.4 %back.1 = (bf16[4,3,256,512]{3,2,1,0:T(8,128)(2,1)}, bf16[4,256,512]{2,1,0:T(8,128)(2,1)}) custom-call(s32[3]{0:T(128)} %pad_add_fusion.sc_ref, f32[512,512]{1,0:T(8,128)} %get-tuple-element.21.g4_ref, bf16[4,512,512]{2,1,0:T(8,128)(2,1)} %get-tuple-element.22.h_ref, f32[4,512,512]{2,1,0:T(8,128)} %get-tuple-element.23.pre_ref, bf16[4,3,512,512]{3,2,1,0:T(8,128)(2,1)} %w_ref.3), custom_call_target="tpu_custom_call" | custom-call | flops 2415919104 | bytes 16777216 | tf_op jit(solution)/shard_map/back/pallas_call | solution.py:374
  69.3 0.5 collective-permute-start.2
  69.8 0.0 copy-done.3
  69.8 0.1 collective-permute-start.1
  69.9 5.5 %collective-permute-done.1.hb_ref = bf16[256,512]{1,0:T(8,128)(2,1)S(1)} collective-permute-done((bf16[256,512]{1,0:T(8,128)(2,1)S(1)}, bf16[256,512]{1,0:T(8,128)(2,1)S(1)}, u32[]{:S(2)}, u32[]{:S(2)}) %collective-permute-start.1) | collective-permute-done | bytes 262176 | tf_op jit(solution)/shard_map/ppermute | solution.py:577
  75.4 0.0 copy-start.2
  75.4 0.0 collective-permute-done.gb_ref
  75.4 0.7 copy-done.2
  76.1 8.4 %head_grad.1 = bf16[2,2,2,2,2,32,1280]{6,5,4,3,2,1,0:T(8,128)(2,1)} custom-call(s32[3]{0:T(128)} %pad_add_fusion.sc_ref, bf16[256,512]{1,0:T(8,128)(2,1)} %get-tuple-element.27.ha_ref, bf16[256,512]{1,0:T(8,128)(2,1)} %copy-done.2, bf16[512,5120]{1,0:T(8,128)(2,1)} %get-tuple-element.19.ga_ref, bf16[512,5120]{1,0:T(8,128)(2,1)} %collective-permute-done.gb_ref), custom_call_target="tpu_custom_call" | custom-call | flops 2684354560 | bytes 13107200 | tf_op jit(solution)/shard_map/head_grad/pallas_call | solution.py:312
  84.4 0.0 collective-permute-done.2.got_ref
  84.4 4.6 %all-to-all-start.2 = ((bf16[8,128,1280]{2,1,0:T(8,128)(2,1)}), bf16[8,128,1280]{2,1,0:T(8,128)(2,1)}, u32[]{:S(2)}, u32[]{:S(2)}) async-start(bf16[8,128,1280]{2,1,0:T(8,128)(2,1)} %bitcast.12), calls=%async_computation.2 | async-start | bytes 5242880 | tf_op jit(solution)/shard_map/all_to_all | solution.py:69
  89.0 9.4 %conv_grad.1 = bf16[2,2,2,12,2,2,32,128]{7,6,5,4,3,2,1,0:T(8,128)(2,1)} custom-call(s32[3]{0:T(128)} %pad_add_fusion.sc_ref, bf16[4,256,512]{2,1,0:T(8,128)(2,1)} %get-tuple-element.25.mine_ref, bf16[4,3,256,512]{3,2,1,0:T(8,128)(2,1)} %get-tuple-element.26.send_ref, bf16[4,3,256,512]{3,2,1,0:T(8,128)(2,1)} %collective-permute-done.2.got_ref), custom_call_target="tpu_custom_call" | custom-call | flops 3221225472 | bytes 10485760 | tf_op jit(solution)/shard_map/conv_grad/pallas_call | solution.py:451
  98.4 9.9 %all-to-all-done.2 = bf16[8,128,1280]{2,1,0:T(8,128)(2,1)} async-done(((bf16[8,128,1280]{2,1,0:T(8,128)(2,1)}), bf16[8,128,1280]{2,1,0:T(8,128)(2,1)}, u32[]{:S(2)}, u32[]{:S(2)}) %all-to-all-start.2) | async-done | bytes 2621472 | tf_op jit(solution)/shard_map/all_to_all | solution.py:69
  108.3 4.5 %all-to-all-start.3 = ((bf16[8,1536,128]{2,1,0:T(8,128)(2,1)}), bf16[8,1536,128]{2,1,0:T(8,128)(2,1)}, u32[]{:S(2)}, u32[]{:S(2)}) async-start(bf16[8,1536,128]{2,1,0:T(8,128)(2,1)} %bitcast.13), calls=%async_computation.3 | async-start | bytes 6291456 | tf_op jit(solution)/shard_map/all_to_all | solution.py:69
  112.7 3.5 %head_far.1.head_ref = bf16[8,5,32,128]{3,2,1,0:T(8,128)(2,1)} custom-call(bf16[8,2,2,32,1280]{4,3,2,1,0:T(8,128)(2,1)} %bitcast.11.got_ref), custom_call_target="tpu_custom_call" | custom-call | flops 10485760 | bytes 3932160 | tf_op jit(solution)/shard_map/head_far/pallas_call | solution.py:496
  116.3 19.6 %all-to-all-done.3 = bf16[8,1536,128]{2,1,0:T(8,128)(2,1)} async-done(((bf16[8,1536,128]{2,1,0:T(8,128)(2,1)}), bf16[8,1536,128]{2,1,0:T(8,128)(2,1)}, u32[]{:S(2)}, u32[]{:S(2)}) %all-to-all-start.3) | async-done | bytes 3145760 | tf_op jit(solution)/shard_map/all_to_all | solution.py:69
  135.9 4.4 %conv_far.1 = bf16[8,11,32,128]{3,2,1,0:T(8,128)(2,1)} custom-call(bf16[8,12,2,2,32,128]{5,4,3,2,1,0:T(8,128)(2,1)} %bitcast.10.a_ref.b_ref, bf16[8,12,2,2,32,128]{5,4,3,2,1,0:T(8,128)(2,1)} %bitcast.10.a_ref.b_ref, bf16[8,5,32,128]{3,2,1,0:T(8,128)(2,1)} %head_far.1.head_ref), custom_call_target="tpu_custom_call" | custom-call | flops 12582912 | bytes 4718592 | tf_op jit(solution)/shard_map/conv_far/pallas_call | solution.py:533
  140.3 19.2 %all_to_all.25.got_ref = bf16[8,11,32,128]{3,2,1,0:T(8,128)(2,1)} all-to-all(bf16[8,11,32,128]{3,2,1,0:T(8,128)(2,1)} %conv_far.1), channel_id=1, replica_groups={{0,48,6,54,65,113,71,119},{16,32,22,38,81,97,87,103},{2,50,4,52,67,115,..., dimensions={0} | all-to-all | bytes 1441792 | tf_op jit(solution)/shard_map/all_to_all | solution.py:69
  159.5 2.0 %finish.1 = (f32[4,3,32,64]{3,2,1,0:T(8,128)}, f32[32,640]{1,0:T(8,128)}) custom-call(bf16[8,11,32,128]{3,2,1,0:T(8,128)(2,1)} %all_to_all.25.got_ref), custom_call_target="tpu_custom_call" | custom-call | tf_op jit(solution)/shard_map/finish/pallas_call | solution.py:563
Async XLA Ops:
  2.9 18.6 %all-to-all-start = ((bf16[8,64,512]{2,1,0:T(8,128)(2,1)}), bf16[8,64,512]{2,1,0:T(8,128)(2,1)S(1)}, u32[]{:S(2)}, u32[]{:S(2)}) async-start(bf16[8,64,512]{2,1,0:T(8,128)(2,1)} %bitcast.15), calls=%async_computation | async-start | bytes 1048576 | tf_op jit(solution)/shard_map/all_to_all | solution.py:69
  21.5 4.8 %copy-start.1 = (bf16[8,64,512]{2,1,0:T(8,128)(2,1)}, bf16[8,64,512]{2,1,0:T(8,128)(2,1)S(1)}, u32[]{:S(2)}) copy-start(bf16[8,64,512]{2,1,0:T(8,128)(2,1)S(1)} %all-to-all-done) | copy-start | bytes 1572868
  21.5 17.0 %all-to-all-start.1 = ((bf16[8,64,768]{2,1,0:T(8,128)(2,1)}), bf16[8,64,768]{2,1,0:T(8,128)(2,1)S(1)}, u32[]{:S(2)}, u32[]{:S(2)}) async-start(bf16[8,64,768]{2,1,0:T(8,128)(2,1)} %bitcast.14), calls=%async_computation.1 | async-start | bytes 1572864 | tf_op jit(solution)/shard_map/all_to_all | solution.py:69
  38.5 0.9 copy-start
  57.9 17.5 %collective-permute-start = (bf16[512,5120]{1,0:T(8,128)(2,1)}, bf16[512,5120]{1,0:T(8,128)(2,1)}, u32[]{:S(2)}, u32[]{:S(2)}) collective-permute-start(bf16[512,5120]{1,0:T(8,128)(2,1)} %get-tuple-element.19.ga_ref), channel_id=1, source_target_pairs={{0,8},{1,9},{2,10},{3,11},{4,12},{5,13},{6,14},{7,15},{8,0},{9,1},... | collective-permute-start | bytes 15728648 | tf_op jit(solution)/shard_map/ppermute | solution.py:577
  58.0 11.8 %copy-start.3 = (bf16[256,512]{1,0:T(8,128)(2,1)S(1)}, bf16[256,512]{1,0:T(8,128)(2,1)}, u32[]{:S(2)}) copy-start(bf16[256,512]{1,0:T(8,128)(2,1)} %get-tuple-element.20) | copy-start | bytes 786436
  69.3 15.1 %collective-permute-start.2 = (bf16[4,3,256,512]{3,2,1,0:T(8,128)(2,1)}, bf16[4,3,256,512]{3,2,1,0:T(8,128)(2,1)}, u32[]{:S(2)}, u32[]{:S(2)}) collective-permute-start(bf16[4,3,256,512]{3,2,1,0:T(8,128)(2,1)} %get-tuple-element.26.send_ref), channel_id=1, source_target_pairs={{0,8},{1,9},{2,10},{3,11},{4,12},{5,13},{6,14},{7,15},{8,0},{9,1},... | collective-permute-start | bytes 9437192 | tf_op jit(solution)/shard_map/ppermute | solution.py:577
  69.8 5.6 %collective-permute-start.1 = (bf16[256,512]{1,0:T(8,128)(2,1)S(1)}, bf16[256,512]{1,0:T(8,128)(2,1)S(1)}, u32[]{:S(2)}, u32[]{:S(2)}) collective-permute-start(bf16[256,512]{1,0:T(8,128)(2,1)S(1)} %copy-done.3), channel_id=1, source_target_pairs={{0,8},{1,9},{2,10},{3,11},{4,12},{5,13},{6,14},{7,15},{8,0},{9,1},... | collective-permute-start | bytes 786440 | tf_op jit(solution)/shard_map/ppermute | solution.py:577
  75.4 0.7 copy-start.2
  84.4 23.8 %all-to-all-start.2 = ((bf16[8,128,1280]{2,1,0:T(8,128)(2,1)}), bf16[8,128,1280]{2,1,0:T(8,128)(2,1)}, u32[]{:S(2)}, u32[]{:S(2)}) async-start(bf16[8,128,1280]{2,1,0:T(8,128)(2,1)} %bitcast.12), calls=%async_computation.2 | async-start | bytes 5242880 | tf_op jit(solution)/shard_map/all_to_all | solution.py:69
  108.3 27.6 %all-to-all-start.3 = ((bf16[8,1536,128]{2,1,0:T(8,128)(2,1)}), bf16[8,1536,128]{2,1,0:T(8,128)(2,1)}, u32[]{:S(2)}, u32[]{:S(2)}) async-start(bf16[8,1536,128]{2,1,0:T(8,128)(2,1)} %bitcast.13), calls=%async_computation.3 | async-start | bytes 6291456 | tf_op jit(solution)/shard_map/all_to_all | solution.py:69

commit v3 on v2

--- a/solution.py
+++ b/solution.py
@@ -124,7 +124,15 @@
     )(x)
 
 
-def conv_kernel(sc_ref, x_ref, w_ref, saved_ref, pre_ref, last_ref, pad_s, tap_s):
+def split_rows(core, ht_s, mine_ref, other_ref):
+    for ref, owner in ((mine_ref, core), (other_ref, 1 - core)):
+        for at, (nz, fz, xl) in enumerate(BITS):
+            high = jnp.where(owner == 0, fz, nz)
+            row = ((xl * 4 + high * 2 + (nz ^ fz)) * 2 + owner) * 32
+            ref[at * 32 : (at + 1) * 32] = ht_s[pl.ds(pl.multiple_of(row, 32), 32)]
+
+
+def conv_kernel(sc_ref, x_ref, w_ref, saved_ref, pre_ref, last_ref, mine_ref, other_ref, pad_s, tap_s, ht_s):
     layer = pl.program_id(0)
     frames = x_ref.shape[0]
 
@@ -147,14 +155,20 @@
     pre = dot(tap_s[0], w_ref[0, 0]) + dot(middle, w_ref[0, 1]) + dot(tap_s[1], w_ref[0, 2])
     pre_ref[0] = pre
     new = (frame_mask(sc_ref, frames) * (hidden + jax.nn.silu(pre))).astype(BF16)
-    last_ref[...] = new
     pad_s[PAD : PAD + frames] = new.astype(F32)
+
+    @pl.when(layer == LAYERS - 1)
+    def _():
+        last_ref[...] = new
+        ht_s[...] = new.T
+        split_rows(sc_ref[2], ht_s, mine_ref, other_ref)
 
 
 def convolve(sc, x, weight):
     frames, width = x.shape
     one = pl.BlockSpec((1, frames, width), lambda i: (i, 0, 0))
     flat = pl.BlockSpec((frames, width), lambda i: (0, 0))
+    rows = pl.BlockSpec((width // 2, frames), lambda i: (0, 0))
     return pl.pallas_call(
         conv_kernel,
         grid=(LAYERS,),
@@ -163,15 +177,18 @@
             flat,
             pl.BlockSpec((1, TAPS, width, width), lambda i: (i, 0, 0, 0)),
         ],
-        out_specs=[one, one, flat],
+        out_specs=[one, one, flat, rows, rows],
         out_shape=[
             jax.ShapeDtypeStruct((LAYERS, frames, width), BF16),
             jax.ShapeDtypeStruct((LAYERS, frames, width), F32),
             jax.ShapeDtypeStruct((frames, width), BF16),
+            jax.ShapeDtypeStruct((width // 2, frames), BF16),
+            jax.ShapeDtypeStruct((width // 2, frames), BF16),
         ],
         scratch_shapes=[
             pltpu.VMEM((frames + 2 * PAD, width), F32),
             pltpu.VMEM((2, frames, width), BF16),
+            pltpu.VMEM((width, frames), BF16),
         ],
         compiler_params=params("arbitrary"),
         cost_estimate=pl.CostEstimate(
@@ -183,16 +200,8 @@
     )(sc, x, weight)
 
 
-def split_rows(core, ht_s, mine_ref, other_ref):
-    for ref, owner in ((mine_ref, core), (other_ref, 1 - core)):
-        for at, (nz, fz, xl) in enumerate(BITS):
-            high = jnp.where(owner == 0, fz, nz)
-            row = ((xl * 4 + high * 2 + (nz ^ fz)) * 2 + owner) * 32
-            ref[at * 32 : (at + 1) * 32] = ht_s[pl.ds(pl.multiple_of(row, 32), 32)]
-
-
-def head_kernel(scale, tiles, sc_ref, h_ref, t_ref, ws_ref, wt_ref, score_ref, g_ref, mine_ref, other_ref,
-                sq_s, es_s, et_s, sum_s, ht_s):
+def head_kernel(scale, tiles, sc_ref, h_ref, t_ref, ws_ref, wt_ref, score_ref, g_ref,
+                sq_s, es_s, et_s, sum_s):
     step = pl.program_id(0)
     frames, width = h_ref.shape
     tile = ws_ref.shape[1]
@@ -221,8 +230,6 @@
         for i in range(2):
             inverse = factor / jnp.sum(sum_s[i], axis=1, keepdims=True)
             sum_s[i] = jnp.broadcast_to(inverse, (frames, 128))
-        ht_s[...] = h_ref[...].T
-        split_rows(sc_ref[2], ht_s, mine_ref, other_ref)
         g_ref[...] = jnp.zeros_like(g_ref)
 
     @pl.when(step >= tiles)
@@ -243,7 +250,6 @@
     tiles = 4
     tile = scores // tiles
     big = pltpu.VMEM((tiles, frames, tile), F32)
-    rows = pl.BlockSpec((width // 2, frames), lambda i: (0, 0))
     return pl.pallas_call(
         functools.partial(head_kernel, 5.0 * loss_scale, tiles),
         grid=(2 * tiles,),
@@ -257,21 +263,16 @@
         out_specs=[
             pl.BlockSpec((frames, tile), lambda i: (0, jnp.maximum(i - tiles, 0))),
             pl.BlockSpec((frames, width), lambda i: (0, 0)),
-            rows,
-            rows,
         ],
         scratch_shapes=[
             big,
             big,
             big,
             pltpu.VMEM((2, frames, 128), F32),
-            pltpu.VMEM((width, frames), BF16),
         ],
         out_shape=[
             jax.ShapeDtypeStruct((frames, scores), BF16),
             jax.ShapeDtypeStruct((frames, width), F32),
-            jax.ShapeDtypeStruct((width // 2, frames), BF16),
-            jax.ShapeDtypeStruct((width // 2, frames), BF16),
         ],
         compiler_params=params("arbitrary"),
         cost_estimate=pl.CostEstimate(
@@ -284,17 +285,20 @@
 
 
 def head_grad_kernel(sc_ref, ha_ref, hb_ref, ga_ref, gb_ref, out_ref, res_s):
-    half = res_s.shape[1] // 2
-    res_s[...] = dot(ha_ref[...], ga_ref[...]) + dot(hb_ref[...], gb_ref[...])
+    half = ga_ref.shape[1] // 2
     first = sc_ref[2] == 0
-    for nx, nz, fz in BITS:
-        for fx in range(2):
-            row = ((nz * 2 + fz) * 2 + (nx ^ fx)) * 32
-            rows = slice(row, row + 32)
-            value = res_s[rows, fx * half : (fx + 1) * half]
-            if nx != fx:
-                value = jnp.where(first, value, res_s[rows, nx * half : (nx + 1) * half])
-            out_ref[nx, 0, nz, fz, 0, :, fx * half : (fx + 1) * half] = encode(value)
+    for c in range(half // 128):
+        cols = [slice(x * half + c * 128, x * half + (c + 1) * 128) for x in range(2)]
+        ga, gb = (jnp.concatenate([ref[:, at] for at in cols], axis=1) for ref in (ga_ref, gb_ref))
+        res_s[c] = dot(ha_ref[...], ga) + dot(hb_ref[...], gb)
+        for nx, nz, fz in BITS:
+            for fx in range(2):
+                row = ((nz * 2 + fz) * 2 + (nx ^ fx)) * 32
+                rows = slice(row, row + 32)
+                value = res_s[c, rows, fx * 128 : (fx + 1) * 128]
+                if nx != fx:
+                    value = jnp.where(first, value, res_s[c, rows, nx * 128 : (nx + 1) * 128])
+                out_ref[nx, 0, nz, fz, 0, :, cols[fx]] = encode(value)
 
 
 def head_grad(sc, h_mine, h_other, score_mine, score_other):
@@ -316,7 +320,7 @@
             grid=(4,),
             in_specs=[hidden, hidden, score, score],
             out_specs=pl.BlockSpec((2, 1, 2, 2, 1, 32, tile), place),
-            scratch_shapes=[pltpu.VMEM((rows, tile), F32)],
+            scratch_shapes=[pltpu.VMEM((tile // 256, rows, 256), F32)],
         ),
         out_shape=jax.ShapeDtypeStruct((2, 2, 2, 2, 2, 32, tile), BF16),
         compiler_params=params("arbitrary"),
@@ -429,14 +433,14 @@
     core = sc_ref[2]
     low = low_lanes((32, 128))
     for tap in range(TAPS):
-        res_s[...] = dot(mine_ref[0], tap_s[tap, 0]) + dot(got_ref[0, 2], tap_s[tap, 1])
+        res_s[tap] = dot(mine_ref[0], tap_s[tap, 0]) + dot(got_ref[0, 2], tap_s[tap, 1])
         for nz, fz, ny in BITS:
             for fy in range(2):
                 high = jnp.where(core == 0, fy, ny)
                 cols = pl.ds(pl.multiple_of((high * 2 + (ny ^ fy)) * 128, 128), 128)
                 row = (nz * 2 + fz) * 64
-                a = res_s[row : row + 32, cols]
-                b = pltpu.roll(res_s[row + 32 : row + 64, cols], 64 * core, 1)
+                a = res_s[tap, row : row + 32, cols]
+                b = pltpu.roll(res_s[tap, row + 32 : row + 64, cols], 64 * core, 1)
                 out_ref[0, ny, nz, tap, fz, fy] = encode(jnp.where(low, a, b))
                 out_ref[1, ny, nz, tap, fz, fy] = encode(jnp.where(low, b, a))
 
@@ -464,7 +468,7 @@
         scratch_shapes=[
             pltpu.VMEM((2, frames + 2 * PAD, width), F32),
             pltpu.VMEM((TAPS, 2, frames, width), BF16),
-            pltpu.VMEM((rows, width), F32),
+            pltpu.VMEM((TAPS, rows, width), F32),
         ],
         compiler_params=params("arbitrary"),
         cost_estimate=pl.CostEstimate(
@@ -587,14 +591,13 @@
     teacher = regroup(teacher_rows[0]).reshape(TM, frames // TM, -1)
     teacher = exchange(teacher, frame_groups()).reshape(frames, -1)
 
-    saved, pre, hidden = convolve(sc, student, conv_weight)
-    score, g, h_mine, h_other = heads(
-        sc, hidden, teacher, head_weight, teacher_head_weight, loss_scale
-    )
-    score_got, h_got = swap(score), swap(h_other)
+    saved, pre, hidden, h_mine, h_other = convolve(sc, student, conv_weight)
+    h_got, hidden = lax.optimization_barrier((swap(h_other), hidden))
+    score, g = heads(sc, hidden, teacher, head_weight, teacher_head_weight, loss_scale)
+    score_got = swap(score)
     send, mine = back(sc, g, saved, pre, conv_weight)
     got = swap(send)
-    score_got, h_got, mine = lax.optimization_barrier((score_got, h_got, mine))
+    score_got, mine = lax.optimization_barrier((score_got, mine))
     near = head_grad(sc, h_mine, h_got, score, score_got)
     near, got = lax.optimization_barrier((near, got))
     head_got = exchange(near.reshape(8, 4 * 32, scores // 4), near_groups())

time: 163 us -> 159 us (0.975)
  waiting for transfers between devices: 47.6 us -> 41 us
  blocking collectives: 19.2 us -> 21.9 us
    ppermute x3, waiting for transfers between devices: 5.48 us -> 1.74 us  [swap(): return lax.ppermute(x, AXES, other_core())]
    all_to_all x4, waiting for transfers between devices: 42.2 us -> 39.3 us  [exchange(): return lax.all_to_all(x, AXES, 0, 0, tiled=True, axis_index_groups=groups)]
    all_to_all x1, blocking collectives: 19.2 us -> 21.9 us  [exchange(): return lax.all_to_all(x, AXES, 0, 0, tiled=True, axis_index_groups=groups)]
  transfers between devices with their start and end apart: 7 -> 7, of which waited for: 5 -> 5; matrix products, arithmetic and copies ran while one was open for 0% -> 0% of each run, Pallas kernels for 27% -> 28%
where the time goes in v3:
time: 159 us; the launch traced here: 158 us
  Pallas kernels  71.5 us (45%)
  waiting for transfers between devices  41 us (26%)
  blocking collectives  21.9 us (14%)
  starting transfers between devices  20.2 us (13%)
    all_to_all x4, waiting for transfers between devices, exchange(): return lax.all_to_all(x, AXES, 0, 0, tiled=True, axis_index_groups=groups)  39.3 us
    all_to_all x1, blocking collectives, exchange(): return lax.all_to_all(x, AXES, 0, 0, tiled=True, axis_index_groups=groups)  21.9 us
    all_to_all x4, starting transfers between devices, exchange(): return lax.all_to_all(x, AXES, 0, 0, tiled=True, axis_index_groups=groups)  19.6 us
    pallas_call x1, Pallas kernels, heads(): pl.pallas_call(functools.partial(head_kernel, 5.0 * loss_scale, tiles), g...  18.2 us
    pallas_call x1, Pallas kernels, back(): pl.pallas_call(back_kernel, grid=(LAYERS,), in_specs=[pl.BlockSpec(memory...  11.3 us
    pallas_call x1, Pallas kernels, conv_grad(): pl.pallas_call(conv_grad_kernel, grid=(LAYERS,), in_specs=[pl.BlockSpec(m...  9.6 us
    pallas_call x1, Pallas kernels, convolve(): pl.pallas_call(conv_kernel, grid=(LAYERS,), in_specs=[pl.BlockSpec(memory...  9.31 us
    pallas_call x1, Pallas kernels, head_grad(): pl.pallas_call(head_grad_kernel, grid_spec=pltpu.PrefetchScalarGridSpec(n...  8.25 us
  transfers between devices with their start and end apart: 7, of which 5 were waited for; matrix products, arithmetic and copies ran while one was open for 0% of the time, Pallas kernels for 28%

profile of v3, /device:TPU:0, one launch (start us, length us, event | category | flops | bytes accessed | tf_op | source)
XLA Modules:
  0.0 157.5 jit_solution(13612708374371236296)
XLA Ops:
  0.6 2.3 %regroup.2 = bf16[512,512]{1,0:T(8,128)(2,1)} custom-call(bf16[512,512]{1,0:T(8,128)(2,1)} %bitcast.18), custom_call_target="tpu_custom_call" | custom-call | tf_op jit(solution)/shard_map/regroup/pallas_call | solution.py:118
  2.9 7.0 %all-to-all-start = ((bf16[8,64,512]{2,1,0:T(8,128)(2,1)}), bf16[8,64,512]{2,1,0:T(8,128)(2,1)S(1)}, u32[]{:S(2)}, u32[]{:S(2)}) async-start(bf16[8,64,512]{2,1,0:T(8,128)(2,1)} %bitcast.15), calls=%async_computation | async-start | bytes 1048576 | tf_op jit(solution)/shard_map/all_to_all | solution.py:69
  9.9 2.6 %regroup.3 = bf16[512,768]{1,0:T(8,128)(2,1)} custom-call(bf16[512,768]{1,0:T(8,128)(2,1)} %bitcast.16), custom_call_target="tpu_custom_call" | custom-call | tf_op jit(solution)/shard_map/regroup/pallas_call | solution.py:118
  12.6 9.0 %all-to-all-done = bf16[8,64,512]{2,1,0:T(8,128)(2,1)S(1)} async-done(((bf16[8,64,512]{2,1,0:T(8,128)(2,1)}), bf16[8,64,512]{2,1,0:T(8,128)(2,1)S(1)}, u32[]{:S(2)}, u32[]{:S(2)}) %all-to-all-start) | async-done | bytes 524320 | tf_op jit(solution)/shard_map/all_to_all | solution.py:69
  21.5 0.0 copy-start.1
  21.5 3.5 %all-to-all-start.1 = ((bf16[8,64,768]{2,1,0:T(8,128)(2,1)}), bf16[8,64,768]{2,1,0:T(8,128)(2,1)S(1)}, u32[]{:S(2)}, u32[]{:S(2)}) async-start(bf16[8,64,768]{2,1,0:T(8,128)(2,1)} %bitcast.14), calls=%async_computation.1 | async-start | bytes 1572864 | tf_op jit(solution)/shard_map/all_to_all | solution.py:69
  25.7 0.6 pad_add_fusion.sc_ref
  26.4 0.0 copy-done.1
  26.4 9.3 %convolve.1 = (bf16[4,512,512]{2,1,0:T(8,128)(2,1)}, f32[4,512,512]{2,1,0:T(8,128)}, bf16[512,512]{1,0:T(8,128)(2,1)}, bf16[256,512]{1,0:T(8,128)(2,1)}, bf16[256,512]{1,0:T(8,128)(2,1)}) custom-call(s32[3]{0:T(128)} %pad_add_fusion.sc_ref, bf16[512,512]{1,0:T(8,128)(2,1)} %bitcast.19, bf16[4,3,512,512]{3,2,1,0:T(8,128)(2,1)} %w_ref.3), custom_call_target="tpu_custom_call" | custom-call | flops 3221225472 | bytes 12582912 | tf_op jit(solution)/shard_map/convolve/pallas_call | solution.py:172
  35.7 0.1 collective-permute-start
  35.8 1.7 %collective-permute-done.hb_ref = bf16[256,512]{1,0:T(8,128)(2,1)S(1)} collective-permute-done((bf16[256,512]{1,0:T(8,128)(2,1)}, bf16[256,512]{1,0:T(8,128)(2,1)S(1)}, u32[]{:S(2)}, u32[]{:S(2)}) %collective-permute-start) | collective-permute-done | bytes 262176 | tf_op jit(solution)/shard_map/ppermute | solution.py:581
  37.5 0.0 copy-start.2
  37.5 1.0 all-to-all-done.1
  38.5 0.0 copy-start
  38.5 0.9 copy-done
  39.4 18.2 %heads.1 = (bf16[512,5120]{1,0:T(8,128)(2,1)}, f32[512,512]{1,0:T(8,128)}) custom-call(s32[3]{0:T(128)} %pad_add_fusion.sc_ref, bf16[512,512]{1,0:T(8,128)(2,1)} %get-tuple-element.21.h_ref, bf16[512,768]{1,0:T(8,128)(2,1)} %bitcast.17, bf16[512,5120]{1,0:T(8,128)(2,1)} %ws_ref.1, bf16[768,5120]{1,0:T(8,128)(2,1)} %wt_ref.1), custom_call_target="tpu_custom_call" | custom-call | flops 9395240960 | bytes 23592960 | tf_op jit(solution)/shard_map/heads/pallas_call | solution.py:253
  57.6 0.0 copy-done.2
  57.6 0.1 collective-permute-start.1
  57.7 11.3 %back.1 = (bf16[4,3,256,512]{3,2,1,0:T(8,128)(2,1)}, bf16[4,256,512]{2,1,0:T(8,128)(2,1)}) custom-call(s32[3]{0:T(128)} %pad_add_fusion.sc_ref, f32[512,512]{1,0:T(8,128)} %get-tuple-element.23.g4_ref, bf16[4,512,512]{2,1,0:T(8,128)(2,1)} %get-tuple-element.24.h_ref, f32[4,512,512]{2,1,0:T(8,128)} %get-tuple-element.25.pre_ref, bf16[4,3,512,512]{3,2,1,0:T(8,128)(2,1)} %w_ref.3), custom_call_target="tpu_custom_call" | custom-call | flops 2415919104 | bytes 16777216 | tf_op jit(solution)/shard_map/back/pallas_call | solution.py:378
  69.0 0.5 collective-permute-start.2
  69.4 0.0 collective-permute-done.1.gb_ref
  69.4 8.3 %head_grad.1 = bf16[2,2,2,2,2,32,1280]{6,5,4,3,2,1,0:T(8,128)(2,1)} custom-call(s32[3]{0:T(128)} %pad_add_fusion.sc_ref, bf16[256,512]{1,0:T(8,128)(2,1)} %get-tuple-element.29.ha_ref, bf16[256,512]{1,0:T(8,128)(2,1)} %copy-done.2, bf16[512,5120]{1,0:T(8,128)(2,1)} %get-tuple-element.22.ga_ref, bf16[512,5120]{1,0:T(8,128)(2,1)} %collective-permute-done.1.gb_ref), custom_call_target="tpu_custom_call" | custom-call | flops 2684354560 | bytes 13107200 | tf_op jit(solution)/shard_map/head_grad/pallas_call | solution.py:316
  77.7 0.0 collective-permute-done.2.got_ref
  77.7 4.6 %all-to-all-start.2 = ((bf16[8,128,1280]{2,1,0:T(8,128)(2,1)}), bf16[8,128,1280]{2,1,0:T(8,128)(2,1)}, u32[]{:S(2)}, u32[]{:S(2)}) async-start(bf16[8,128,1280]{2,1,0:T(8,128)(2,1)} %bitcast.12), calls=%async_computation.2 | async-start | bytes 5242880 | tf_op jit(solution)/shard_map/all_to_all | solution.py:69
  82.3 9.6 %conv_grad.1 = bf16[2,2,2,12,2,2,32,128]{7,6,5,4,3,2,1,0:T(8,128)(2,1)} custom-call(s32[3]{0:T(128)} %pad_add_fusion.sc_ref, bf16[4,256,512]{2,1,0:T(8,128)(2,1)} %get-tuple-element.27.mine_ref, bf16[4,3,256,512]{3,2,1,0:T(8,128)(2,1)} %get-tuple-element.28.send_ref, bf16[4,3,256,512]{3,2,1,0:T(8,128)(2,1)} %collective-permute-done.2.got_ref), custom_call_target="tpu_custom_call" | custom-call | flops 3221225472 | bytes 10485760 | tf_op jit(solution)/shard_map/conv_grad/pallas_call | solution.py:455
  91.9 9.6 %all-to-all-done.2 = bf16[8,128,1280]{2,1,0:T(8,128)(2,1)} async-done(((bf16[8,128,1280]{2,1,0:T(8,128)(2,1)}), bf16[8,128,1280]{2,1,0:T(8,128)(2,1)}, u32[]{:S(2)}, u32[]{:S(2)}) %all-to-all-start.2) | async-done | bytes 2621472 | tf_op jit(solution)/shard_map/all_to_all | solution.py:69
  101.5 4.5 %all-to-all-start.3 = ((bf16[8,1536,128]{2,1,0:T(8,128)(2,1)}), bf16[8,1536,128]{2,1,0:T(8,128)(2,1)}, u32[]{:S(2)}, u32[]{:S(2)}) async-start(bf16[8,1536,128]{2,1,0:T(8,128)(2,1)} %bitcast.13), calls=%async_computation.3 | async-start | bytes 6291456 | tf_op jit(solution)/shard_map/all_to_all | solution.py:69
  106.0 3.5 %head_far.1.head_ref = bf16[8,5,32,128]{3,2,1,0:T(8,128)(2,1)} custom-call(bf16[8,2,2,32,1280]{4,3,2,1,0:T(8,128)(2,1)} %bitcast.11.got_ref), custom_call_target="tpu_custom_call" | custom-call | flops 10485760 | bytes 3932160 | tf_op jit(solution)/shard_map/head_far/pallas_call | solution.py:500
  109.5 19.6 %all-to-all-done.3 = bf16[8,1536,128]{2,1,0:T(8,128)(2,1)} async-done(((bf16[8,1536,128]{2,1,0:T(8,128)(2,1)}), bf16[8,1536,128]{2,1,0:T(8,128)(2,1)}, u32[]{:S(2)}, u32[]{:S(2)}) %all-to-all-start.3) | async-done | bytes 3145760 | tf_op jit(solution)/shard_map/all_to_all | solution.py:69
  129.1 4.4 %conv_far.1 = bf16[8,11,32,128]{3,2,1,0:T(8,128)(2,1)} custom-call(bf16[8,12,2,2,32,128]{5,4,3,2,1,0:T(8,128)(2,1)} %bitcast.10.a_ref.b_ref, bf16[8,12,2,2,32,128]{5,4,3,2,1,0:T(8,128)(2,1)} %bitcast.10.a_ref.b_ref, bf16[8,5,32,128]{3,2,1,0:T(8,128)(2,1)} %head_far.1.head_ref), custom_call_target="tpu_custom_call" | custom-call | flops 12582912 | bytes 4718592 | tf_op jit(solution)/shard_map/conv_far/pallas_call | solution.py:537
  133.6 21.9 %all_to_all.25.got_ref = bf16[8,11,32,128]{3,2,1,0:T(8,128)(2,1)} all-to-all(bf16[8,11,32,128]{3,2,1,0:T(8,128)(2,1)} %conv_far.1), channel_id=1, replica_groups={{0,48,6,54,65,113,71,119},{16,32,22,38,81,97,87,103},{2,50,4,52,67,115,..., dimensions={0} | all-to-all | bytes 1441792 | tf_op jit(solution)/shard_map/all_to_all | solution.py:69
  155.5 2.0 %finish.1 = (f32[4,3,32,64]{3,2,1,0:T(8,128)}, f32[32,640]{1,0:T(8,128)}) custom-call(bf16[8,11,32,128]{3,2,1,0:T(8,128)(2,1)} %all_to_all.25.got_ref), custom_call_target="tpu_custom_call" | custom-call | tf_op jit(solution)/shard_map/finish/pallas_call | solution.py:567
Async XLA Ops:
  2.9 18.6 %all-to-all-start = ((bf16[8,64,512]{2,1,0:T(8,128)(2,1)}), bf16[8,64,512]{2,1,0:T(8,128)(2,1)S(1)}, u32[]{:S(2)}, u32[]{:S(2)}) async-start(bf16[8,64,512]{2,1,0:T(8,128)(2,1)} %bitcast.15), calls=%async_computation | async-start | bytes 1048576 | tf_op jit(solution)/shard_map/all_to_all | solution.py:69
  21.5 4.8 %copy-start.1 = (bf16[8,64,512]{2,1,0:T(8,128)(2,1)}, bf16[8,64,512]{2,1,0:T(8,128)(2,1)S(1)}, u32[]{:S(2)}) copy-start(bf16[8,64,512]{2,1,0:T(8,128)(2,1)S(1)} %all-to-all-done) | copy-start | bytes 1572868
  21.5 17.0 %all-to-all-start.1 = ((bf16[8,64,768]{2,1,0:T(8,128)(2,1)}), bf16[8,64,768]{2,1,0:T(8,128)(2,1)S(1)}, u32[]{:S(2)}, u32[]{:S(2)}) async-start(bf16[8,64,768]{2,1,0:T(8,128)(2,1)} %bitcast.14), calls=%async_computation.1 | async-start | bytes 1572864 | tf_op jit(solution)/shard_map/all_to_all | solution.py:69
  35.7 1.8 %collective-permute-start = (bf16[256,512]{1,0:T(8,128)(2,1)}, bf16[256,512]{1,0:T(8,128)(2,1)S(1)}, u32[]{:S(2)}, u32[]{:S(2)}) collective-permute-start(bf16[256,512]{1,0:T(8,128)(2,1)} %get-tuple-element.19), channel_id=1, source_target_pairs={{0,8},{1,9},{2,10},{3,11},{4,12},{5,13},{6,14},{7,15},{8,0},{9,1},... | collective-permute-start | bytes 786440 | tf_op jit(solution)/shard_map/ppermute | solution.py:581
  37.5 20.1 %copy-start.2 = (bf16[256,512]{1,0:T(8,128)(2,1)}, bf16[256,512]{1,0:T(8,128)(2,1)S(1)}, u32[]{:S(2)}) copy-start(bf16[256,512]{1,0:T(8,128)(2,1)S(1)} %collective-permute-done.hb_ref) | copy-start | bytes 786436
  38.5 0.9 copy-start
  57.6 11.9 %collective-permute-start.1 = (bf16[512,5120]{1,0:T(8,128)(2,1)}, bf16[512,5120]{1,0:T(8,128)(2,1)}, u32[]{:S(2)}, u32[]{:S(2)}) collective-permute-start(bf16[512,5120]{1,0:T(8,128)(2,1)} %get-tuple-element.22.ga_ref), channel_id=1, source_target_pairs={{0,8},{1,9},{2,10},{3,11},{4,12},{5,13},{6,14},{7,15},{8,0},{9,1},... | collective-permute-start | bytes 15728648 | tf_op jit(solution)/shard_map/ppermute | solution.py:581
  69.0 8.7 %collective-permute-start.2 = (bf16[4,3,256,512]{3,2,1,0:T(8,128)(2,1)}, bf16[4,3,256,512]{3,2,1,0:T(8,128)(2,1)}, u32[]{:S(2)}, u32[]{:S(2)}) collective-permute-start(bf16[4,3,256,512]{3,2,1,0:T(8,128)(2,1)} %get-tuple-element.28.send_ref), channel_id=1, source_target_pairs={{0,8},{1,9},{2,10},{3,11},{4,12},{5,13},{6,14},{7,15},{8,0},{9,1},... | collective-permute-start | bytes 9437192 | tf_op jit(solution)/shard_map/ppermute | solution.py:581
  77.7 23.8 %all-to-all-start.2 = ((bf16[8,128,1280]{2,1,0:T(8,128)(2,1)}), bf16[8,128,1280]{2,1,0:T(8,128)(2,1)}, u32[]{:S(2)}, u32[]{:S(2)}) async-start(bf16[8,128,1280]{2,1,0:T(8,128)(2,1)} %bitcast.12), calls=%async_computation.2 | async-start | bytes 5242880 | tf_op jit(solution)/shard_map/all_to_all | solution.py:69
  101.5 27.6 %all-to-all-start.3 = ((bf16[8,1536,128]{2,1,0:T(8,128)(2,1)}), bf16[8,1536,128]{2,1,0:T(8,128)(2,1)}, u32[]{:S(2)}, u32[]{:S(2)}) async-start(bf16[8,1536,128]{2,1,0:T(8,128)(2,1)} %bitcast.13), calls=%async_computation.3 | async-start | bytes 6291456 | tf_op jit(solution)/shard_map/all_to_all | solution.py:69

commit v4 on v3

--- a/solution.py
+++ b/solution.py
@@ -90,8 +90,8 @@
     return lax.dot_general(a, b, (((1,), (1,)), ((), ())), preferred_element_type=F32)
 
 
-def params(*kinds):
-    return pltpu.CompilerParams(dimension_semantics=kinds, vmem_limit_bytes=62 * 1024 * 1024)
+def params(mib, *kinds):
+    return pltpu.CompilerParams(dimension_semantics=kinds, vmem_limit_bytes=mib * 1024 * 1024)
 
 
 def whole():
@@ -120,6 +120,7 @@
         out_shape=jax.ShapeDtypeStruct(x.shape, BF16),
         in_specs=[whole()],
         out_specs=whole(),
+        compiler_params=params(5),
         name="regroup",
     )(x)
 
@@ -190,7 +191,7 @@
             pltpu.VMEM((2, frames, width), BF16),
             pltpu.VMEM((width, frames), BF16),
         ],
-        compiler_params=params("arbitrary"),
+        compiler_params=params(14, "arbitrary"),
         cost_estimate=pl.CostEstimate(
             flops=2 * LAYERS * TAPS * frames * width * width,
             bytes_accessed=LAYERS * (TAPS * width * width * 2 + frames * width * 6),
@@ -274,7 +275,7 @@
             jax.ShapeDtypeStruct((frames, scores), BF16),
             jax.ShapeDtypeStruct((frames, width), F32),
         ],
-        compiler_params=params("arbitrary"),
+        compiler_params=params(48, "arbitrary"),
         cost_estimate=pl.CostEstimate(
             flops=2 * frames * scores * (2 * width + wide),
             bytes_accessed=scores * (6 * width + 2 * wide),
@@ -323,7 +324,7 @@
             scratch_shapes=[pltpu.VMEM((tile // 256, rows, 256), F32)],
         ),
         out_shape=jax.ShapeDtypeStruct((2, 2, 2, 2, 2, 32, tile), BF16),
-        compiler_params=params("arbitrary"),
+        compiler_params=params(13, "arbitrary"),
         cost_estimate=pl.CostEstimate(
             flops=4 * rows * frames * scores,
             bytes_accessed=4 * frames * scores + 2 * rows * scores,
@@ -398,7 +399,7 @@
             pltpu.VMEM((2, frames, width), BF16),
             pltpu.VMEM((width, frames), BF16),
         ],
-        compiler_params=params("arbitrary"),
+        compiler_params=params(16, "arbitrary"),
         cost_estimate=pl.CostEstimate(
             flops=2 * (LAYERS - 1) * TAPS * frames * width * width,
             bytes_accessed=LAYERS * (TAPS * width * width * 2 + frames * width * 10),
@@ -470,7 +471,7 @@
             pltpu.VMEM((TAPS, 2, frames, width), BF16),
             pltpu.VMEM((TAPS, rows, width), F32),
         ],
-        compiler_params=params("arbitrary"),
+        compiler_params=params(18, "arbitrary"),
         cost_estimate=pl.CostEstimate(
             flops=4 * LAYERS * TAPS * rows * frames * width,
             bytes_accessed=LAYERS * (7 * rows * frames * 2 + TAPS * rows * width * 2),
@@ -502,7 +503,7 @@
         out_shape=jax.ShapeDtypeStruct((8, tile // 256, 32, 128), BF16),
         in_specs=[whole()],
         out_specs=whole(),
-        compiler_params=params(),
+        compiler_params=params(8),
         cost_estimate=pl.CostEstimate(
             flops=8 * got.size, bytes_accessed=3 * got.size, transcendentals=got.size
         ),
@@ -544,7 +545,7 @@
             pl.BlockSpec(head.shape, lambda i: (0, 0, 0, 0)),
         ],
         out_specs=pl.BlockSpec(shape, lambda i: (0, 0, 0, 0)),
-        compiler_params=params("arbitrary"),
+        compiler_params=params(8, "arbitrary"),
         cost_estimate=pl.CostEstimate(
             flops=8 * got.size, bytes_accessed=3 * got.size, transcendentals=got.size
         ),
@@ -572,7 +573,7 @@
         ],
         in_specs=[whole()],
         out_specs=[whole(), whole()],
-        compiler_params=params(),
+        compiler_params=params(4),
         name="finish",
     )(got)
 

time: 159 us -> 154 us (0.969)
  local copies, waits for them, and re-layouts: 0.88 us -> 23.7 us
  Pallas kernels: 71.5 us -> 51.3 us
  waiting for transfers between devices: 41 us -> 35.5 us
    unnamed x6 -> x46, local copies, waits for them, and re-layouts: 0.88 us -> 23.7 us
    all_to_all x4, waiting for transfers between devices: 39.3 us -> 34 us  [exchange(): return lax.all_to_all(x, AXES, 0, 0, tiled=True, axis_index_groups=groups)]
    pallas_call x1, Pallas kernels: 9.31 us -> 5.95 us  [convolve(): pl.pallas_call(conv_kernel, grid=(LAYERS,), in_specs=[pl.BlockSpec(memory...]
    pallas_call x1, Pallas kernels: 8.25 us -> 5.06 us  [head_grad(): pl.pallas_call(head_grad_kernel, grid_spec=pltpu.PrefetchScalarGridSpec(n...]
    pallas_call x1, Pallas kernels: 11.3 us -> 8.22 us  [back(): pl.pallas_call(back_kernel, grid=(LAYERS,), in_specs=[pl.BlockSpec(memory...]
    pallas_call x1, Pallas kernels: 4.42 us -> 1.8 us  [conv_far(): pl.pallas_call(conv_far_kernel, grid=(steps,), out_shape=jax.ShapeDtypeSt...]
    pallas_call x1, Pallas kernels: 3.52 us -> 1.06 us  [head_far(): pl.pallas_call(head_far_kernel, out_shape=jax.ShapeDtypeStruct((8, tile /...]
    pallas_call x2, Pallas kernels: 4.91 us -> 2.74 us  [regroup(): pl.pallas_call(regroup_kernel, out_shape=jax.ShapeDtypeStruct(x.shape, BF...]
  transfers between devices with their start and end apart: 7 -> 7, of which waited for: 5 -> 4; matrix products, arithmetic and copies ran while one was open for 0% -> 0% of each run, Pallas kernels for 28% -> 19%
where the time goes in v4:
time: 154 us; the launch traced here: 153 us
  Pallas kernels  51.3 us (33%)
  waiting for transfers between devices  35.5 us (23%)
  local copies, waits for them, and re-layouts  23.7 us (15%)
  blocking collectives  21.6 us (14%)
  starting transfers between devices  19.4 us (13%)
    all_to_all x4, waiting for transfers between devices, exchange(): return lax.all_to_all(x, AXES, 0, 0, tiled=True, axis_index_groups=groups)  34 us
    unnamed x46, local copies, waits for them, and re-layouts  23.7 us
    all_to_all x1, blocking collectives, exchange(): return lax.all_to_all(x, AXES, 0, 0, tiled=True, axis_index_groups=groups)  21.6 us
    all_to_all x4, starting transfers between devices, exchange(): return lax.all_to_all(x, AXES, 0, 0, tiled=True, axis_index_groups=groups)  18.8 us
    pallas_call x1, Pallas kernels, heads(): pl.pallas_call(functools.partial(head_kernel, 5.0 * loss_scale, tiles), g...  17.7 us
    pallas_call x1, Pallas kernels, back(): pl.pallas_call(back_kernel, grid=(LAYERS,), in_specs=[pl.BlockSpec(memory...  8.22 us
    pallas_call x1, Pallas kernels, conv_grad(): pl.pallas_call(conv_grad_kernel, grid=(LAYERS,), in_specs=[pl.BlockSpec(m...  7.88 us
    pallas_call x1, Pallas kernels, convolve(): pl.pallas_call(conv_kernel, grid=(LAYERS,), in_specs=[pl.BlockSpec(memory...  5.95 us
  transfers between devices with their start and end apart: 7, of which 4 were waited for; matrix products, arithmetic and copies ran while one was open for 0% of the time, Pallas kernels for 19%

profile of v4, /device:TPU:0, one launch (start us, length us, event | category | flops | bytes accessed | tf_op | source)
XLA Modules:
  0.0 153.1 jit_solution(10725644393910472047)
XLA Ops:
  0.6 0.0 copy-start.8
  0.6 1.0 copy-done.8
  1.7 1.2 regroup.2
  2.9 7.0 %all-to-all-start = ((bf16[8,64,512]{2,1,0:T(8,128)(2,1)}), bf16[8,64,512]{2,1,0:T(8,128)(2,1)S(1)}, u32[]{:S(2)}, u32[]{:S(2)}) async-start(bf16[8,64,512]{2,1,0:T(8,128)(2,1)} %bitcast.3), calls=%async_computation | async-start | bytes 1048576 | tf_op jit(solution)/shard_map/all_to_all | solution.py:69
  9.9 0.0 copy-start.7
  9.9 1.1 copy-done.7
  11.1 1.5 regroup.3
  12.6 8.9 %all-to-all-done = bf16[8,64,512]{2,1,0:T(8,128)(2,1)S(1)} async-done(((bf16[8,64,512]{2,1,0:T(8,128)(2,1)}), bf16[8,64,512]{2,1,0:T(8,128)(2,1)S(1)}, u32[]{:S(2)}, u32[]{:S(2)}) %all-to-all-start) | async-done | bytes 524320 | tf_op jit(solution)/shard_map/all_to_all | solution.py:69
  21.5 3.5 %all-to-all-start.1 = ((bf16[8,64,768]{2,1,0:T(8,128)(2,1)}), bf16[8,64,768]{2,1,0:T(8,128)(2,1)S(1)}, u32[]{:S(2)}, u32[]{:S(2)}) async-start(bf16[8,64,768]{2,1,0:T(8,128)(2,1)} %bitcast.6), calls=%async_computation.1 | async-start | bytes 1572864 | tf_op jit(solution)/shard_map/all_to_all | solution.py:69
  25.7 0.1 pad_add_fusion.sc_ref
  25.8 0.0 copy-start.3
  25.8 2.8 %copy-done.3 = bf16[4,3,512,512]{3,2,1,0:T(8,128)(2,1)S(1)} copy-done((bf16[4,3,512,512]{3,2,1,0:T(8,128)(2,1)S(1)}, bf16[4,3,512,512]{3,2,1,0:T(8,128)(2,1)}, u32[]{:S(2)}) %copy-start.3) | copy-done | bytes 6291480
  28.6 6.0 %convolve.1 = (bf16[4,512,512]{2,1,0:T(8,128)(2,1)S(1)}, f32[4,512,512]{2,1,0:T(8,128)S(1)}, bf16[512,512]{1,0:T(8,128)(2,1)S(1)}, bf16[256,512]{1,0:T(8,128)(2,1)S(1)}, bf16[256,512]{1,0:T(8,128)(2,1)S(1)}) custom-call(s32[3]{0:T(128)S(1)} %pad_add_fusion.sc_ref, bf16[512,512]{1,0:T(8,128)(2,1)S(1)} %bitcast.24, bf16[4,3,512,512]{3,2,1,0:T(8,128)(2,1)S(1)} %copy-done.3), custom_call_target="tpu_custom_call" | custom-call | flops 3221225472 | bytes 12582912 | tf_op jit(solution)/shard_map/convolve/pallas_call | solution.py:173
  34.6 0.0 copy-start.4
  34.6 2.0 %copy-done.4 = f32[4,512,512]{2,1,0:T(8,128)} copy-done((f32[4,512,512]{2,1,0:T(8,128)}, f32[4,512,512]{2,1,0:T(8,128)S(1)}, u32[]{:S(2)}) %copy-start.4) | copy-done | bytes 4194328
  36.6 0.0 copy-start.9
  36.6 0.7 copy-done.9
  37.3 0.0 copy-start.17
  37.3 0.8 copy-done.17
  38.1 0.0 collective-permute-start
  38.1 1.5 %collective-permute-done.hb_ref = bf16[256,512]{1,0:T(8,128)(2,1)S(1)} collective-permute-done((bf16[256,512]{1,0:T(8,128)(2,1)S(1)}, bf16[256,512]{1,0:T(8,128)(2,1)S(1)}, u32[]{:S(2)}, u32[]{:S(2)}) %collective-permute-start) | collective-permute-done | bytes 262176 | tf_op jit(solution)/shard_map/ppermute | solution.py:582
  39.6 0.0 all-to-all-done.1
  39.6 0.0 slice-start
  39.6 0.0 copy-start.18
  39.6 1.2 copy-done.18
  40.8 0.0 slice-start.1
  40.8 0.0 copy-start.5
  40.8 17.7 %heads.1 = (bf16[512,5120]{1,0:T(8,128)(2,1)}, f32[512,512]{1,0:T(8,128)S(1)}) custom-call(s32[3]{0:T(128)S(1)} %pad_add_fusion.sc_ref, bf16[512,512]{1,0:T(8,128)(2,1)S(1)} %copy-done.18, bf16[512,768]{1,0:T(8,128)(2,1)S(1)} %bitcast.22, bf16[512,5120]{1,0:T(8,128)(2,1)} %ws_ref.1, bf16[768,5120]{1,0:T(8,128)(2,1)} %wt_ref.1), custom_call_target="tpu_custom_call" | custom-call | flops 9395240960 | bytes 23592960 | tf_op jit(solution)/shard_map/heads/pallas_call | solution.py:254
  58.5 0.1 collective-permute-start.1
  58.6 0.0 slice-done
  58.6 0.0 slice-done.1
  58.6 0.0 copy-done.5
  58.6 0.0 slice-start.3
  58.7 0.0 copy-start.10
  58.7 8.2 %back.1 = (bf16[4,3,256,512]{3,2,1,0:T(8,128)(2,1)S(1)}, bf16[4,256,512]{2,1,0:T(8,128)(2,1)S(1)}) custom-call(s32[3]{0:T(128)S(1)} %pad_add_fusion.sc_ref, f32[512,512]{1,0:T(8,128)S(1)} %get-tuple-element.23.g4_ref, bf16[4,512,512]{2,1,0:T(8,128)(2,1)S(1)} %get-tuple-element.24.h_ref, f32[4,512,512]{2,1,0:T(8,128)S(1)} %copy-done.5, ...), custom_call_target="tpu_custom_call" | custom-call | flops 2415919104 | bytes 16777216 | tf_op jit(solution)/shard_map/back/pallas_call | solution.py:379
  66.9 0.0 copy-start.15
  66.9 1.0 copy-done.15
  67.9 0.4 collective-permute-start.2
  68.3 0.0 collective-permute-done.1.gb_ref
  68.3 0.0 slice-done.2
  68.3 0.0 slice-done.3
  68.3 0.0 copy-done.10
  68.3 5.1 %head_grad.1 = bf16[2,2,2,2,2,32,1280]{6,5,4,3,2,1,0:T(8,128)(2,1)S(1)} custom-call(s32[3]{0:T(128)S(1)} %pad_add_fusion.sc_ref, bf16[256,512]{1,0:T(8,128)(2,1)S(1)} %copy-done.10, bf16[256,512]{1,0:T(8,128)(2,1)S(1)} %collective-permute-done.hb_ref, bf16[512,5120]{1,0:T(8,128)(2,1)S(1)} %bitcast.19, bf16[512,5120]{1,0:T(8,128)(2,1)S(1)} %collective-permute-done.1.gb_ref), custom_call_target="tpu_custom_call" | custom-call | flops 2684354560 | bytes 13107200 | tf_op jit(solution)/shard_map/head_grad/pallas_call | solution.py:317
  73.4 0.0 copy-done.11
  73.4 0.0 copy-start.2
  73.4 1.5 copy-done.2
  74.9 0.0 collective-permute-done.2.got_ref
  74.9 1.6 %copy-done.13 = bf16[4,3,256,512]{3,2,1,0:T(8,128)(2,1)} copy-done((bf16[4,3,256,512]{3,2,1,0:T(8,128)(2,1)}, bf16[4,3,256,512]{3,2,1,0:T(8,128)(2,1)S(1)}, u32[]{:S(2)}) %copy-start.13) | copy-done | bytes 3145752
  76.6 4.6 %all-to-all-start.2 = ((bf16[8,128,1280]{2,1,0:T(8,128)(2,1)}), bf16[8,128,1280]{2,1,0:T(8,128)(2,1)S(1)}, u32[]{:S(2)}, u32[]{:S(2)}) async-start(bf16[8,128,1280]{2,1,0:T(8,128)(2,1)} %bitcast.15), calls=%async_computation.2 | async-start | bytes 5242880 | tf_op jit(solution)/shard_map/all_to_all | solution.py:69
  81.1 1.9 %copy-done.12 = bf16[4,3,256,512]{3,2,1,0:T(8,128)(2,1)S(1)} copy-done((bf16[4,3,256,512]{3,2,1,0:T(8,128)(2,1)S(1)}, bf16[4,3,256,512]{3,2,1,0:T(8,128)(2,1)}, u32[]{:S(2)}) %copy-start.12) | copy-done | bytes 3145752
  83.0 1.9 %copy-done.14 = bf16[4,3,256,512]{3,2,1,0:T(8,128)(2,1)S(1)} copy-done((bf16[4,3,256,512]{3,2,1,0:T(8,128)(2,1)S(1)}, bf16[4,3,256,512]{3,2,1,0:T(8,128)(2,1)}, u32[]{:S(2)}) %copy-start.14) | copy-done | bytes 3145752
  84.9 1.2 copy-done.16
  86.1 7.9 %conv_grad.1 = bf16[2,2,2,12,2,2,32,128]{7,6,5,4,3,2,1,0:T(8,128)(2,1)S(1)} custom-call(s32[3]{0:T(128)S(1)} %pad_add_fusion.sc_ref, bf16[4,256,512]{2,1,0:T(8,128)(2,1)S(1)} %copy-done.16, bf16[4,3,256,512]{3,2,1,0:T(8,128)(2,1)S(1)} %copy-done.12, bf16[4,3,256,512]{3,2,1,0:T(8,128)(2,1)S(1)} %copy-done.14), custom_call_target="tpu_custom_call" | custom-call | flops 3221225472 | bytes 10485760 | tf_op jit(solution)/shard_map/conv_grad/pallas_call | solution.py:456
  94.0 0.0 copy-start.6
  94.0 1.6 %copy-done.6 = bf16[2,2,2,12,2,2,32,128]{7,6,5,4,3,2,1,0:T(8,128)(2,1)} copy-done((bf16[2,2,2,12,2,2,32,128]{7,6,5,4,3,2,1,0:T(8,128)(2,1)}, bf16[2,2,2,12,2,2,32,128]{7,6,5,4,3,2,1,0:T(8,128)(2,1)S(1)}, u32[]{:S(2)}) %copy-start.6) | copy-done | bytes 3145752
  95.7 4.9 %all-to-all-done.2 = bf16[8,128,1280]{2,1,0:T(8,128)(2,1)S(1)} async-done(((bf16[8,128,1280]{2,1,0:T(8,128)(2,1)}), bf16[8,128,1280]{2,1,0:T(8,128)(2,1)S(1)}, u32[]{:S(2)}, u32[]{:S(2)}) %all-to-all-start.2) | async-done | bytes 2621472 | tf_op jit(solution)/shard_map/all_to_all | solution.py:69
  100.6 1.5 copy-done
  102.1 3.7 %all-to-all-start.3 = ((bf16[8,1536,128]{2,1,0:T(8,128)(2,1)}), bf16[8,1536,128]{2,1,0:T(8,128)(2,1)S(1)}, u32[]{:S(2)}, u32[]{:S(2)}) async-start(bf16[8,1536,128]{2,1,0:T(8,128)(2,1)} %bitcast.20), calls=%async_computation.3 | async-start | bytes 6291456 | tf_op jit(solution)/shard_map/all_to_all | solution.py:69
  105.8 1.7 %copy-done.1 = bf16[8,128,1280]{2,1,0:T(8,128)(2,1)S(1)} copy-done((bf16[8,128,1280]{2,1,0:T(8,128)(2,1)S(1)}, bf16[8,128,1280]{2,1,0:T(8,128)(2,1)}, u32[]{:S(2)}) %copy-start.1) | copy-done | bytes 2621464
  107.5 1.1 head_far.1.head_ref
  108.6 20.1 %all-to-all-done.3 = bf16[8,1536,128]{2,1,0:T(8,128)(2,1)S(1)} async-done(((bf16[8,1536,128]{2,1,0:T(8,128)(2,1)}), bf16[8,1536,128]{2,1,0:T(8,128)(2,1)S(1)}, u32[]{:S(2)}, u32[]{:S(2)}) %all-to-all-start.3) | async-done | bytes 3145760 | tf_op jit(solution)/shard_map/all_to_all | solution.py:69
  128.7 1.8 %conv_far.1 = bf16[8,11,32,128]{3,2,1,0:T(8,128)(2,1)S(1)} custom-call(bf16[8,12,2,2,32,128]{5,4,3,2,1,0:T(8,128)(2,1)S(1)} %bitcast.12, bf16[8,12,2,2,32,128]{5,4,3,2,1,0:T(8,128)(2,1)S(1)} %bitcast.13, bf16[8,5,32,128]{3,2,1,0:T(8,128)(2,1)S(1)} %head_far.1.head_ref), custom_call_target="tpu_custom_call" | custom-call | flops 12582912 | bytes 4718592 | tf_op jit(solution)/shard_map/conv_far/pallas_call | solution.py:538
  130.5 21.6 %all_to_all.25.got_ref = bf16[8,11,32,128]{3,2,1,0:T(8,128)(2,1)S(1)} all-to-all(bf16[8,11,32,128]{3,2,1,0:T(8,128)(2,1)S(1)} %conv_far.1), channel_id=1, replica_groups={{0,48,6,54,65,113,71,119},{16,32,22,38,81,97,87,103},{2,50,4,52,67,115,..., dimensions={0} | all-to-all | bytes 1441792 | tf_op jit(solution)/shard_map/all_to_all | solution.py:69
  152.1 0.9 finish.1
  (10 shorter events, 0.0 us)
Async XLA Ops:
  0.6 1.0 copy-start.8
  2.9 18.6 %all-to-all-start = ((bf16[8,64,512]{2,1,0:T(8,128)(2,1)}), bf16[8,64,512]{2,1,0:T(8,128)(2,1)S(1)}, u32[]{:S(2)}, u32[]{:S(2)}) async-start(bf16[8,64,512]{2,1,0:T(8,128)(2,1)} %bitcast.3), calls=%async_computation | async-start | bytes 1048576 | tf_op jit(solution)/shard_map/all_to_all | solution.py:69
  9.9 1.1 copy-start.7
  21.5 18.1 %all-to-all-start.1 = ((bf16[8,64,768]{2,1,0:T(8,128)(2,1)}), bf16[8,64,768]{2,1,0:T(8,128)(2,1)S(1)}, u32[]{:S(2)}, u32[]{:S(2)}) async-start(bf16[8,64,768]{2,1,0:T(8,128)(2,1)} %bitcast.6), calls=%async_computation.1 | async-start | bytes 1572864 | tf_op jit(solution)/shard_map/all_to_all | solution.py:69
  25.8 2.8 %copy-start.3 = (bf16[4,3,512,512]{3,2,1,0:T(8,128)(2,1)S(1)}, bf16[4,3,512,512]{3,2,1,0:T(8,128)(2,1)}, u32[]{:S(2)}) copy-start(bf16[4,3,512,512]{3,2,1,0:T(8,128)(2,1)} %w_ref.3) | copy-start | bytes 18874372
  34.6 2.0 %copy-start.4 = (f32[4,512,512]{2,1,0:T(8,128)}, f32[4,512,512]{2,1,0:T(8,128)S(1)}, u32[]{:S(2)}) copy-start(f32[4,512,512]{2,1,0:T(8,128)S(1)} %get-tuple-element.25.pre_ref) | copy-start | bytes 12582916
  36.6 0.7 copy-start.9
  37.3 0.8 copy-start.17
  38.1 1.5 %collective-permute-start = (bf16[256,512]{1,0:T(8,128)(2,1)S(1)}, bf16[256,512]{1,0:T(8,128)(2,1)S(1)}, u32[]{:S(2)}, u32[]{:S(2)}) collective-permute-start(bf16[256,512]{1,0:T(8,128)(2,1)S(1)} %get-tuple-element.19), channel_id=1, source_target_pairs={{0,8},{1,9},{2,10},{3,11},{4,12},{5,13},{6,14},{7,15},{8,0},{9,1},... | collective-permute-start | bytes 786440 | tf_op jit(solution)/shard_map/ppermute | solution.py:582
  39.6 19.0 %slice-start = ((s8[6291456]{0:T(1024)(128)(4,1)}), s8[4194304]{0:T(1024)(128)(4,1)S(1)}, s32[]{:S(2)}) async-start(s8[6291456]{0:T(1024)(128)(4,1)} %bitcast.16), calls=%async_computation.5 | async-start | bytes 8388608
  39.6 1.2 copy-start.18
  40.8 17.8 %slice-start.1 = ((s8[6291456]{0:T(1024)(128)(4,1)}), s8[2097152]{0:T(1024)(128)(4,1)S(1)}, s32[]{:S(2)}) async-start(s8[6291456]{0:T(1024)(128)(4,1)} %bitcast.16), calls=%async_computation.6 | async-start | bytes 4194304
  40.8 17.8 %copy-start.5 = (f32[4,512,512]{2,1,0:T(8,128)S(1)}, f32[4,512,512]{2,1,0:T(8,128)}, u32[]{:S(2)}) copy-start(f32[4,512,512]{2,1,0:T(8,128)} %copy-done.4) | copy-start | bytes 12582916
  58.5 9.8 %collective-permute-start.1 = (bf16[512,5120]{1,0:T(8,128)(2,1)}, bf16[512,5120]{1,0:T(8,128)(2,1)S(1)}, u32[]{:S(2)}, u32[]{:S(2)}) collective-permute-start(bf16[512,5120]{1,0:T(8,128)(2,1)} %get-tuple-element.22.ga_ref), channel_id=1, source_target_pairs={{0,8},{1,9},{2,10},{3,11},{4,12},{5,13},{6,14},{7,15},{8,0},{9,1},... | collective-permute-start | bytes 15728648 | tf_op jit(solution)/shard_map/ppermute | solution.py:582
  58.6 9.7 %slice-start.2 = ((s8[5242880]{0:T(1024)(128)(4,1)}), s8[4194304]{0:T(1024)(128)(4,1)S(1)}, s32[]{:S(2)}) async-start(s8[5242880]{0:T(1024)(128)(4,1)} %bitcast.18), calls=%async_computation.7 | async-start | bytes 8388608
  58.6 9.6 %slice-start.3 = ((s8[5242880]{0:T(1024)(128)(4,1)}), s8[1048576]{0:T(1024)(128)(4,1)S(1)}, s32[]{:S(2)}) async-start(s8[5242880]{0:T(1024)(128)(4,1)} %bitcast.18), calls=%async_computation.8 | async-start | bytes 2097152
  58.7 9.6 %copy-start.10 = (bf16[256,512]{1,0:T(8,128)(2,1)S(1)}, bf16[256,512]{1,0:T(8,128)(2,1)}, u32[]{:S(2)}) copy-start(bf16[256,512]{1,0:T(8,128)(2,1)} %copy-done.9) | copy-start | bytes 786436
  66.9 1.0 copy-start.15
  67.9 5.5 %copy-start.11 = (bf16[4,3,256,512]{3,2,1,0:T(8,128)(2,1)}, bf16[4,3,256,512]{3,2,1,0:T(8,128)(2,1)S(1)}, u32[]{:S(2)}) copy-start(bf16[4,3,256,512]{3,2,1,0:T(8,128)(2,1)S(1)} %get-tuple-element.28.send_ref) | copy-start | bytes 9437188
  67.9 7.0 %collective-permute-start.2 = (bf16[4,3,256,512]{3,2,1,0:T(8,128)(2,1)S(1)}, bf16[4,3,256,512]{3,2,1,0:T(8,128)(2,1)S(1)}, u32[]{:S(2)}, u32[]{:S(2)}) collective-permute-start(bf16[4,3,256,512]{3,2,1,0:T(8,128)(2,1)S(1)} %get-tuple-element.28.send_ref), channel_id=1, source_target_pairs={{0,8},{1,9},{2,10},{3,11},{4,12},{5,13},{6,14},{7,15},{8,0},{9,1},... | collective-permute-start | bytes 9437192 | tf_op jit(solution)/shard_map/ppermute | solution.py:582
  73.4 1.5 %copy-start.2 = (bf16[2,2,2,2,2,32,1280]{6,5,4,3,2,1,0:T(8,128)(2,1)}, bf16[2,2,2,2,2,32,1280]{6,5,4,3,2,1,0:T(8,128)(2,1)S(1)}, u32[]{:S(2)}) copy-start(bf16[2,2,2,2,2,32,1280]{6,5,4,3,2,1,0:T(8,128)(2,1)S(1)} %head_grad.1) | copy-start | bytes 7864324
  74.9 1.6 %copy-start.13 = (bf16[4,3,256,512]{3,2,1,0:T(8,128)(2,1)}, bf16[4,3,256,512]{3,2,1,0:T(8,128)(2,1)S(1)}, u32[]{:S(2)}) copy-start(bf16[4,3,256,512]{3,2,1,0:T(8,128)(2,1)S(1)} %collective-permute-done.2.got_ref) | copy-start | bytes 9437188
  76.6 24.0 %all-to-all-start.2 = ((bf16[8,128,1280]{2,1,0:T(8,128)(2,1)}), bf16[8,128,1280]{2,1,0:T(8,128)(2,1)S(1)}, u32[]{:S(2)}, u32[]{:S(2)}) async-start(bf16[8,128,1280]{2,1,0:T(8,128)(2,1)} %bitcast.15), calls=%async_computation.2 | async-start | bytes 5242880 | tf_op jit(solution)/shard_map/all_to_all | solution.py:69
  81.1 1.9 %copy-start.12 = (bf16[4,3,256,512]{3,2,1,0:T(8,128)(2,1)S(1)}, bf16[4,3,256,512]{3,2,1,0:T(8,128)(2,1)}, u32[]{:S(2)}) copy-start(bf16[4,3,256,512]{3,2,1,0:T(8,128)(2,1)} %copy-done.11) | copy-start | bytes 9437188
  83.0 1.9 %copy-start.14 = (bf16[4,3,256,512]{3,2,1,0:T(8,128)(2,1)S(1)}, bf16[4,3,256,512]{3,2,1,0:T(8,128)(2,1)}, u32[]{:S(2)}) copy-start(bf16[4,3,256,512]{3,2,1,0:T(8,128)(2,1)} %copy-done.13) | copy-start | bytes 9437188
  84.9 1.2 copy-start.16
  94.0 1.6 %copy-start.6 = (bf16[2,2,2,12,2,2,32,128]{7,6,5,4,3,2,1,0:T(8,128)(2,1)}, bf16[2,2,2,12,2,2,32,128]{7,6,5,4,3,2,1,0:T(8,128)(2,1)S(1)}, u32[]{:S(2)}) copy-start(bf16[2,2,2,12,2,2,32,128]{7,6,5,4,3,2,1,0:T(8,128)(2,1)S(1)} %conv_grad.1) | copy-start | bytes 9437188
  100.6 1.5 copy-start
  102.1 26.6 %all-to-all-start.3 = ((bf16[8,1536,128]{2,1,0:T(8,128)(2,1)}), bf16[8,1536,128]{2,1,0:T(8,128)(2,1)S(1)}, u32[]{:S(2)}, u32[]{:S(2)}) async-start(bf16[8,1536,128]{2,1,0:T(8,128)(2,1)} %bitcast.20), calls=%async_computation.3 | async-start | bytes 6291456 | tf_op jit(solution)/shard_map/all_to_all | solution.py:69
  105.8 1.7 %copy-start.1 = (bf16[8,128,1280]{2,1,0:T(8,128)(2,1)S(1)}, bf16[8,128,1280]{2,1,0:T(8,128)(2,1)}, u32[]{:S(2)}) copy-start(bf16[8,128,1280]{2,1,0:T(8,128)(2,1)} %copy-done) | copy-start | bytes 7864324

commit v5 on v4

--- a/solution.py
+++ b/solution.py
@@ -98,6 +98,13 @@
     return pl.BlockSpec(memory_space=pltpu.VMEM)
 
 
+def in_hbm(x):
+    return pltpu.with_memory_space_constraint(x, pltpu.HBM)
+
+
+AFTER = pl.BlockSpec(memory_space=pl.ANY)
+
+
 def frame_mask(sc_ref, frames):
     row = lax.broadcasted_iota(jnp.int32, (frames, 1), 0)
     position = row // CLASSES * BASE_DILATION + sc_ref[1] * CLASSES + row % CLASSES
@@ -181,10 +188,10 @@
         out_specs=[one, one, flat, rows, rows],
         out_shape=[
             jax.ShapeDtypeStruct((LAYERS, frames, width), BF16),
-            jax.ShapeDtypeStruct((LAYERS, frames, width), F32),
-            jax.ShapeDtypeStruct((frames, width), BF16),
-            jax.ShapeDtypeStruct((width // 2, frames), BF16),
-            jax.ShapeDtypeStruct((width // 2, frames), BF16),
+            pltpu.HBM((LAYERS, frames, width), F32),
+            pltpu.HBM((frames, width), BF16),
+            pltpu.HBM((width // 2, frames), BF16),
+            pltpu.HBM((width // 2, frames), BF16),
         ],
         scratch_shapes=[
             pltpu.VMEM((frames + 2 * PAD, width), F32),
@@ -198,11 +205,11 @@
             transcendentals=LAYERS * frames * width,
         ),
         name="convolve",
-    )(sc, x, weight)
-
-
-def head_kernel(scale, tiles, sc_ref, h_ref, t_ref, ws_ref, wt_ref, score_ref, g_ref,
-                sq_s, es_s, et_s, sum_s):
+    )(sc, x, in_hbm(weight))
+
+
+def head_kernel(scale, tiles, sc_ref, h_ref, t_ref, ws_ref, wt_ref, _, score_ref, g_ref,
+                sq_s, et_s, sum_s):
     step = pl.program_id(0)
     frames, width = h_ref.shape
     tile = ws_ref.shape[1]
@@ -219,7 +226,6 @@
             squash = jnp.tanh(dot(h_ref[...], ws_ref[:, cols]))
             exp_s = jnp.exp(5.0 * squash)
             sq_s[step, :, cols] = squash
-            es_s[step, :, cols] = exp_s
             sum_s[0] += exp_s[:, :128] + exp_s[:, 128:]
             exp_t = jnp.exp(5.0 * jnp.tanh(dot(t_ref[...], wt_ref[:, cols])))
             et_s[step, :, cols] = exp_t
@@ -239,12 +245,12 @@
         for c in range(tile // 128):
             cols = slice(c * 128, (c + 1) * 128)
             squash = sq_s[at, :, cols]
-            p = es_s[at, :, cols] * sum_s[0] - et_s[at, :, cols] * sum_s[1]
+            p = jnp.exp(5.0 * squash) * sum_s[0] - et_s[at, :, cols] * sum_s[1]
             score_ref[:, cols] = (p * (1.0 - squash * squash)).astype(BF16)
         g_ref[...] += dot_nt(score_ref[...], ws_ref[...])
 
 
-def heads(sc, hidden, teacher_in, head_weight, teacher_head_weight, loss_scale):
+def heads(sc, hidden, teacher_in, head_weight, teacher_head_weight, after, loss_scale):
     frames, width = hidden.shape
     wide = teacher_in.shape[1]
     scores = head_weight.shape[1]
@@ -260,6 +266,7 @@
             pl.BlockSpec((frames, wide), lambda i: (0, 0)),
             pl.BlockSpec((width, tile), lambda i: (0, i % tiles)),
             pl.BlockSpec((wide, tile), lambda i: (0, jnp.minimum(i, tiles - 1))),
+            AFTER,
         ],
         out_specs=[
             pl.BlockSpec((frames, tile), lambda i: (0, jnp.maximum(i - tiles, 0))),
@@ -268,24 +275,23 @@
         scratch_shapes=[
             big,
             big,
-            big,
             pltpu.VMEM((2, frames, 128), F32),
         ],
         out_shape=[
             jax.ShapeDtypeStruct((frames, scores), BF16),
             jax.ShapeDtypeStruct((frames, width), F32),
         ],
-        compiler_params=params(48, "arbitrary"),
+        compiler_params=params(37, "arbitrary"),
         cost_estimate=pl.CostEstimate(
             flops=2 * frames * scores * (2 * width + wide),
             bytes_accessed=scores * (6 * width + 2 * wide),
             transcendentals=4 * frames * scores,
         ),
         name="heads",
-    )(sc, hidden, teacher_in, head_weight, teacher_head_weight)
-
-
-def head_grad_kernel(sc_ref, ha_ref, hb_ref, ga_ref, gb_ref, out_ref, res_s):
+    )(sc, hidden, teacher_in, in_hbm(head_weight), in_hbm(teacher_head_weight), after)
+
+
+def head_grad_kernel(sc_ref, ha_ref, hb_ref, ga_ref, gb_ref, _, out_ref, res_s):
     half = ga_ref.shape[1] // 2
     first = sc_ref[2] == 0
     for c in range(half // 128):
@@ -302,7 +308,7 @@
                 out_ref[nx, 0, nz, fz, 0, :, cols[fx]] = encode(value)
 
 
-def head_grad(sc, h_mine, h_other, score_mine, score_other):
+def head_grad(sc, h_mine, h_other, score_mine, score_other, after):
     rows, frames = h_mine.shape
     scores = score_mine.shape[1]
     tile = scores // 4
@@ -319,7 +325,7 @@
         grid_spec=pltpu.PrefetchScalarGridSpec(
             num_scalar_prefetch=1,
             grid=(4,),
-            in_specs=[hidden, hidden, score, score],
+            in_specs=[hidden, hidden, score, score, AFTER],
             out_specs=pl.BlockSpec((2, 1, 2, 2, 1, 32, tile), place),
             scratch_shapes=[pltpu.VMEM((tile // 256, rows, 256), F32)],
         ),
@@ -331,7 +337,7 @@
             transcendentals=0,
         ),
         name="head_grad",
-    )(sc, h_mine, h_other, score_mine, score_other)
+    )(sc, h_mine, h_other, score_mine, score_other, in_hbm(after))
 
 
 def back_kernel(sc_ref, g4_ref, h_ref, pre_ref, w_ref, send_ref, mine_ref, g_s, pad_s, tap_s, ht_s):
@@ -391,7 +397,7 @@
         out_specs=[at(3, frames // 2, width), at(width // 2, frames)],
         out_shape=[
             jax.ShapeDtypeStruct((LAYERS, 3, frames // 2, width), BF16),
-            jax.ShapeDtypeStruct((LAYERS, width // 2, frames), BF16),
+            pltpu.HBM((LAYERS, width // 2, frames), BF16),
         ],
         scratch_shapes=[
             pltpu.VMEM((frames, width), F32),
@@ -409,7 +415,7 @@
     )(sc, g, saved, pre, weight)
 
 
-def conv_grad_kernel(sc_ref, mine_ref, send_ref, got_ref, out_ref, pad_s, tap_s, res_s):
+def conv_grad_kernel(sc_ref, mine_ref, send_ref, got_ref, _, out_ref, pad_s, tap_s, res_s):
     step = pl.program_id(0)
     rows, frames = mine_ref.shape[1:]
     width = send_ref.shape[3]
@@ -446,7 +452,7 @@
                 out_ref[1, ny, nz, tap, fz, fy] = encode(jnp.where(low, b, a))
 
 
-def conv_grad(sc, mine, send, got):
+def conv_grad(sc, mine, send, got, after):
     _, rows, frames = mine.shape
     width = send.shape[3]
 
@@ -461,11 +467,12 @@
             at(rows, frames),
             at(3, frames // 2, width),
             at(3, frames // 2, width),
+            AFTER,
         ],
         out_specs=pl.BlockSpec(
             (2, 2, 2, TAPS, 2, 2, 32, width // 4), lambda i: (0, 0, 0, i, 0, 0, 0, 0)
         ),
-        out_shape=jax.ShapeDtypeStruct((2, 2, 2, LAYERS * TAPS, 2, 2, 32, width // 4), BF16),
+        out_shape=pltpu.HBM((2, 2, 2, LAYERS * TAPS, 2, 2, 32, width // 4), BF16),
         scratch_shapes=[
             pltpu.VMEM((2, frames + 2 * PAD, width), F32),
             pltpu.VMEM((TAPS, 2, frames, width), BF16),
@@ -478,7 +485,7 @@
             transcendentals=0,
         ),
         name="conv_grad",
-    )(sc, mine, send, got)
+    )(sc, mine, send, got, in_hbm(after))
 
 
 def total_of(ref, *at):
@@ -508,7 +515,7 @@
             flops=8 * got.size, bytes_accessed=3 * got.size, transcendentals=got.size
         ),
         name="head_far",
-    )(got)
+    )(in_hbm(got))
 
 
 def conv_far_kernel(a_ref, b_ref, head_ref, out_ref):
@@ -593,17 +600,16 @@
     teacher = exchange(teacher, frame_groups()).reshape(frames, -1)
 
     saved, pre, hidden, h_mine, h_other = convolve(sc, student, conv_weight)
-    h_got, hidden = lax.optimization_barrier((swap(h_other), hidden))
-    score, g = heads(sc, hidden, teacher, head_weight, teacher_head_weight, loss_scale)
+    h_got = swap(h_other)
+    score, g = heads(
+        sc, hidden, teacher, head_weight, teacher_head_weight, h_got, loss_scale
+    )
     score_got = swap(score)
     send, mine = back(sc, g, saved, pre, conv_weight)
     got = swap(send)
-    score_got, mine = lax.optimization_barrier((score_got, mine))
-    near = head_grad(sc, h_mine, h_got, score, score_got)
-    near, got = lax.optimization_barrier((near, got))
+    near = head_grad(sc, h_mine, h_got, score, score_got, mine)
     head_got = exchange(near.reshape(8, 4 * 32, scores // 4), near_groups())
-    near = conv_grad(sc, mine, send, got)
-    near, head_got = lax.optimization_barrier((near, head_got))
+    near = conv_grad(sc, mine, send, got, near)
     conv_got = exchange(near.reshape(8, LAYERS * TAPS * 4 * 32, width // 4), near_groups())
 
     far = head_far(head_got.reshape(8, 2, 2, 32, scores // 4))

time: 154 us -> 147 us (0.955)
  local copies, waits for them, and re-layouts: 23.7 us -> 3.38 us
  Pallas kernels: 51.3 us -> 58.9 us
  waiting for transfers between devices: 35.5 us -> 42.7 us
    unnamed x46 -> x16, local copies, waits for them, and re-layouts: 23.7 us -> 3.38 us
    all_to_all x4, waiting for transfers between devices: 34 us -> 42.7 us  [exchange(): return lax.all_to_all(x, AXES, 0, 0, tiled=True, axis_index_groups=groups)]
    pallas_call x1, Pallas kernels: 5.95 us -> 8.83 us  [convolve(): pl.pallas_call(conv_kernel, grid=(LAYERS,), in_specs=[pl.BlockSpec(memory...]
    pallas_call x1, Pallas kernels: 1.06 us -> 2.8 us  [head_far(): pl.pallas_call(head_far_kernel, out_shape=jax.ShapeDtypeStruct((8, tile /...]
    pallas_call x1, Pallas kernels: 7.88 us -> 9.5 us  [conv_grad(): pl.pallas_call(conv_grad_kernel, grid=(LAYERS,), in_specs=[pl.BlockSpec(m...]
  transfers between devices with their start and end apart: 7 -> 7, of which waited for: 4 -> 4; matrix products, arithmetic and copies ran while one was open for 0% -> 0% of each run, Pallas kernels for 19% -> 26%
where the time goes in v5:
time: 147 us
  Pallas kernels  58.9 us (40%)
  waiting for transfers between devices  42.7 us (29%)
  blocking collectives  20.5 us (14%)
  starting transfers between devices  19.5 us (13%)
  local copies, waits for them, and re-layouts  3.38 us (2%)
    all_to_all x4, waiting for transfers between devices, exchange(): return lax.all_to_all(x, AXES, 0, 0, tiled=True, axis_index_groups=groups)  42.7 us
    all_to_all x1, blocking collectives, exchange(): return lax.all_to_all(x, AXES, 0, 0, tiled=True, axis_index_groups=groups)  20.5 us
    all_to_all x4, starting transfers between devices, exchange(): return lax.all_to_all(x, AXES, 0, 0, tiled=True, axis_index_groups=groups)  19 us
    pallas_call x1, Pallas kernels, heads(): pl.pallas_call(functools.partial(head_kernel, 5.0 * loss_scale, tiles), g...  17.3 us
    pallas_call x1, Pallas kernels, conv_grad(): pl.pallas_call(conv_grad_kernel, grid=(LAYERS,), in_specs=[pl.BlockSpec(m...  9.5 us
    pallas_call x1, Pallas kernels, back(): pl.pallas_call(back_kernel, grid=(LAYERS,), in_specs=[pl.BlockSpec(memory...  9.29 us
    pallas_call x1, Pallas kernels, convolve(): pl.pallas_call(conv_kernel, grid=(LAYERS,), in_specs=[pl.BlockSpec(memory...  8.83 us
    pallas_call x1, Pallas kernels, head_grad(): pl.pallas_call(head_grad_kernel, grid_spec=pltpu.PrefetchScalarGridSpec(n...  5.73 us
  transfers between devices with their start and end apart: 7, of which 4 were waited for; matrix products, arithmetic and copies ran while one was open for 0% of the time, Pallas kernels for 26%

profile of v5, /device:TPU:0, one launch (start us, length us, event | category | flops | bytes accessed | tf_op | source)
XLA Modules:
  0.0 146.5 jit_solution(13633284520259901289)
XLA Ops:
  0.6 0.0 copy-start.3
  0.6 1.0 copy-done.3
  1.7 1.3 regroup.2
  2.9 7.0 %all-to-all-start = ((bf16[8,64,512]{2,1,0:T(8,128)(2,1)}), bf16[8,64,512]{2,1,0:T(8,128)(2,1)S(1)}, u32[]{:S(2)}, u32[]{:S(2)}) async-start(bf16[8,64,512]{2,1,0:T(8,128)(2,1)} %bitcast.3), calls=%async_computation | async-start | bytes 1048576 | tf_op jit(solution)/shard_map/all_to_all | solution.py:69
  9.9 0.0 copy-start.2
  9.9 1.1 copy-done.2
  11.1 1.5 %regroup.3 = bf16[512,768]{1,0:T(8,128)(2,1)} custom-call(bf16[512,768]{1,0:T(8,128)(2,1)S(1)} %bitcast.16), custom_call_target="tpu_custom_call" | custom-call | tf_op jit(solution)/shard_map/regroup/pallas_call | solution.py:125
  12.6 9.0 %all-to-all-done = bf16[8,64,512]{2,1,0:T(8,128)(2,1)S(1)} async-done(((bf16[8,64,512]{2,1,0:T(8,128)(2,1)}), bf16[8,64,512]{2,1,0:T(8,128)(2,1)S(1)}, u32[]{:S(2)}, u32[]{:S(2)}) %all-to-all-start) | async-done | bytes 524320 | tf_op jit(solution)/shard_map/all_to_all | solution.py:69
  21.5 3.5 %all-to-all-start.1 = ((bf16[8,64,768]{2,1,0:T(8,128)(2,1)}), bf16[8,64,768]{2,1,0:T(8,128)(2,1)S(1)}, u32[]{:S(2)}, u32[]{:S(2)}) async-start(bf16[8,64,768]{2,1,0:T(8,128)(2,1)} %bitcast.6), calls=%async_computation.1 | async-start | bytes 1572864 | tf_op jit(solution)/shard_map/all_to_all | solution.py:69
  25.7 0.1 pad_add_fusion.sc_ref
  25.8 8.8 %convolve.1 = (bf16[4,512,512]{2,1,0:T(8,128)(2,1)S(1)}, f32[4,512,512]{2,1,0:T(8,128)}, bf16[512,512]{1,0:T(8,128)(2,1)}, bf16[256,512]{1,0:T(8,128)(2,1)}, bf16[256,512]{1,0:T(8,128)(2,1)}) custom-call(s32[3]{0:T(128)S(1)} %pad_add_fusion.sc_ref, bf16[512,512]{1,0:T(8,128)(2,1)S(1)} %bitcast.19, bf16[4,3,512,512]{3,2,1,0:T(8,128)(2,1)} %w_ref.3), custom_call_target="tpu_custom_call" | custom-call | flops 3221225472 | bytes 12582912 | tf_op jit(solution)/shard_map/convolve/pallas_call | solution.py:180
  34.6 0.0 collective-permute-start
  34.7 3.8 %all-to-all-done.1 = bf16[8,64,768]{2,1,0:T(8,128)(2,1)S(1)} async-done(((bf16[8,64,768]{2,1,0:T(8,128)(2,1)}), bf16[8,64,768]{2,1,0:T(8,128)(2,1)S(1)}, u32[]{:S(2)}, u32[]{:S(2)}) %all-to-all-start.1) | async-done | bytes 786464 | tf_op jit(solution)/shard_map/all_to_all | solution.py:69
  38.5 0.0 collective-permute-done._.hb_ref
  38.5 0.0 slice-start
  38.5 0.0 copy-start.5
  38.5 1.2 copy-done.5
  39.7 0.0 slice-start.1
  39.7 0.0 copy-start.1
  39.7 17.3 %heads.1 = (bf16[512,5120]{1,0:T(8,128)(2,1)S(1)}, f32[512,512]{1,0:T(8,128)S(1)}) custom-call(s32[3]{0:T(128)S(1)} %pad_add_fusion.sc_ref, bf16[512,512]{1,0:T(8,128)(2,1)S(1)} %copy-done.5, bf16[512,768]{1,0:T(8,128)(2,1)S(1)} %bitcast.17, bf16[512,5120]{1,0:T(8,128)(2,1)} %ws_ref.1, bf16[768,5120]{1,0:T(8,128)(2,1)} %wt_ref.1, ...), custom_call_target="tpu_custom_call" | custom-call | flops 9395240960 | bytes 23592960 | tf_op jit(solution)/shard_map/heads/pallas_call | solution.py:260
  57.0 0.1 collective-permute-start.2
  57.1 0.0 slice-done
  57.1 0.0 slice-done.1
  57.1 0.0 copy-done.1
  57.2 0.0 copy-start.4
  57.2 9.3 %back.1 = (bf16[4,3,256,512]{3,2,1,0:T(8,128)(2,1)}, bf16[4,256,512]{2,1,0:T(8,128)(2,1)}) custom-call(s32[3]{0:T(128)S(1)} %pad_add_fusion.sc_ref, f32[512,512]{1,0:T(8,128)S(1)} %get-tuple-element.13.g4_ref, bf16[4,512,512]{2,1,0:T(8,128)(2,1)S(1)} %get-tuple-element.14.h_ref, f32[4,512,512]{2,1,0:T(8,128)S(1)} %copy-done.1, ...), custom_call_target="tpu_custom_call" | custom-call | flops 2415919104 | bytes 16777216 | tf_op jit(solution)/shard_map/back/pallas_call | solution.py:385
  66.5 0.5 collective-permute-start.1
  66.9 0.0 collective-permute-done.2.gb_ref
  66.9 0.0 copy-done.4
  66.9 5.7 %head_grad.1._ = bf16[2,2,2,2,2,32,1280]{6,5,4,3,2,1,0:T(8,128)(2,1)} custom-call(s32[3]{0:T(128)S(1)} %pad_add_fusion.sc_ref, bf16[256,512]{1,0:T(8,128)(2,1)S(1)} %copy-done.4, bf16[256,512]{1,0:T(8,128)(2,1)S(1)} %collective-permute-done._.hb_ref, bf16[512,5120]{1,0:T(8,128)(2,1)S(1)} %get-tuple-element.19.ga_ref, ...), custom_call_target="tpu_custom_call" | custom-call | flops 2684354560 | bytes 13107200 | tf_op jit(solution)/shard_map/head_grad/pallas_call | solution.py:323
  72.7 0.0 copy-start
  72.7 4.7 %all-to-all-start.3 = ((bf16[8,128,1280]{2,1,0:T(8,128)(2,1)}), bf16[8,128,1280]{2,1,0:T(8,128)(2,1)}, u32[]{:S(2)}, u32[]{:S(2)}) async-start(bf16[8,128,1280]{2,1,0:T(8,128)(2,1)} %bitcast.10), calls=%async_computation.3 | async-start | bytes 5242880 | tf_op jit(solution)/shard_map/all_to_all | solution.py:69
  77.4 0.0 collective-permute-done.1.got_ref
  77.4 0.0 copy-done
  77.4 9.5 %conv_grad.1 = bf16[2,2,2,12,2,2,32,128]{7,6,5,4,3,2,1,0:T(8,128)(2,1)} custom-call(s32[3]{0:T(128)S(1)} %pad_add_fusion.sc_ref, bf16[4,256,512]{2,1,0:T(8,128)(2,1)S(1)} %copy-done, bf16[4,3,256,512]{3,2,1,0:T(8,128)(2,1)} %get-tuple-element.17.send_ref, bf16[4,3,256,512]{3,2,1,0:T(8,128)(2,1)} %collective-permute-done.1.got_ref, ...), custom_call_target="tpu_custom_call" | custom-call | flops 3221225472 | bytes 10485760 | tf_op jit(solution)/shard_map/conv_grad/pallas_call | solution.py:462
  86.9 9.7 %all-to-all-done.3 = bf16[8,128,1280]{2,1,0:T(8,128)(2,1)} async-done(((bf16[8,128,1280]{2,1,0:T(8,128)(2,1)}), bf16[8,128,1280]{2,1,0:T(8,128)(2,1)}, u32[]{:S(2)}, u32[]{:S(2)}) %all-to-all-start.3) | async-done | bytes 2621472 | tf_op jit(solution)/shard_map/all_to_all | solution.py:69
  96.6 3.7 %all-to-all-start.2 = ((bf16[8,1536,128]{2,1,0:T(8,128)(2,1)}), bf16[8,1536,128]{2,1,0:T(8,128)(2,1)S(1)}, u32[]{:S(2)}, u32[]{:S(2)}) async-start(bf16[8,1536,128]{2,1,0:T(8,128)(2,1)} %bitcast.20), calls=%async_computation.2 | async-start | bytes 6291456 | tf_op jit(solution)/shard_map/all_to_all | solution.py:69
  100.3 2.8 %head_far.1.head_ref = bf16[8,5,32,128]{3,2,1,0:T(8,128)(2,1)S(1)} custom-call(bf16[8,2,2,32,1280]{4,3,2,1,0:T(8,128)(2,1)} %bitcast.11.got_ref), custom_call_target="tpu_custom_call" | custom-call | flops 10485760 | bytes 3932160 | tf_op jit(solution)/shard_map/head_far/pallas_call | solution.py:508
  103.1 20.1 %all-to-all-done.2 = bf16[8,1536,128]{2,1,0:T(8,128)(2,1)S(1)} async-done(((bf16[8,1536,128]{2,1,0:T(8,128)(2,1)}), bf16[8,1536,128]{2,1,0:T(8,128)(2,1)S(1)}, u32[]{:S(2)}, u32[]{:S(2)}) %all-to-all-start.2) | async-done | bytes 3145760 | tf_op jit(solution)/shard_map/all_to_all | solution.py:69
  123.3 1.8 %conv_far.1 = bf16[8,11,32,128]{3,2,1,0:T(8,128)(2,1)S(1)} custom-call(bf16[8,12,2,2,32,128]{5,4,3,2,1,0:T(8,128)(2,1)S(1)} %bitcast.12, bf16[8,12,2,2,32,128]{5,4,3,2,1,0:T(8,128)(2,1)S(1)} %bitcast.13, bf16[8,5,32,128]{3,2,1,0:T(8,128)(2,1)S(1)} %head_far.1.head_ref), custom_call_target="tpu_custom_call" | custom-call | flops 12582912 | bytes 4718592 | tf_op jit(solution)/shard_map/conv_far/pallas_call | solution.py:545
  125.1 20.5 %all_to_all.25.got_ref = bf16[8,11,32,128]{3,2,1,0:T(8,128)(2,1)S(1)} all-to-all(bf16[8,11,32,128]{3,2,1,0:T(8,128)(2,1)S(1)} %conv_far.1), channel_id=1, replica_groups={{0,48,6,54,65,113,71,119},{16,32,22,38,81,97,87,103},{2,50,4,52,67,115,..., dimensions={0} | all-to-all | bytes 1441792 | tf_op jit(solution)/shard_map/all_to_all | solution.py:69
  145.6 0.9 finish.1
  (1 shorter events, 0.0 us)
Async XLA Ops:
  0.6 1.0 copy-start.3
  2.9 18.6 %all-to-all-start = ((bf16[8,64,512]{2,1,0:T(8,128)(2,1)}), bf16[8,64,512]{2,1,0:T(8,128)(2,1)S(1)}, u32[]{:S(2)}, u32[]{:S(2)}) async-start(bf16[8,64,512]{2,1,0:T(8,128)(2,1)} %bitcast.3), calls=%async_computation | async-start | bytes 1048576 | tf_op jit(solution)/shard_map/all_to_all | solution.py:69
  9.9 1.1 copy-start.2
  21.5 17.0 %all-to-all-start.1 = ((bf16[8,64,768]{2,1,0:T(8,128)(2,1)}), bf16[8,64,768]{2,1,0:T(8,128)(2,1)S(1)}, u32[]{:S(2)}, u32[]{:S(2)}) async-start(bf16[8,64,768]{2,1,0:T(8,128)(2,1)} %bitcast.6), calls=%async_computation.1 | async-start | bytes 1572864 | tf_op jit(solution)/shard_map/all_to_all | solution.py:69
  34.6 3.9 %collective-permute-start = (bf16[256,512]{1,0:T(8,128)(2,1)}, bf16[256,512]{1,0:T(8,128)(2,1)S(1)}, u32[]{:S(2)}, u32[]{:S(2)}) collective-permute-start(bf16[256,512]{1,0:T(8,128)(2,1)} %get-tuple-element.12), channel_id=1, source_target_pairs={{0,8},{1,9},{2,10},{3,11},{4,12},{5,13},{6,14},{7,15},{8,0},{9,1},... | collective-permute-start | bytes 786440 | tf_op jit(solution)/shard_map/ppermute | solution.py:589
  38.5 18.6 %slice-start = ((s8[6291456]{0:T(1024)(128)(4,1)}), s8[4194304]{0:T(1024)(128)(4,1)S(1)}, s32[]{:S(2)}) async-start(s8[6291456]{0:T(1024)(128)(4,1)} %bitcast.14), calls=%async_computation.5 | async-start | bytes 8388608
  38.5 1.2 copy-start.5
  39.7 17.4 %slice-start.1 = ((s8[6291456]{0:T(1024)(128)(4,1)}), s8[2097152]{0:T(1024)(128)(4,1)S(1)}, s32[]{:S(2)}) async-start(s8[6291456]{0:T(1024)(128)(4,1)} %bitcast.14), calls=%async_computation.6 | async-start | bytes 4194304
  39.7 17.5 %copy-start.1 = (f32[4,512,512]{2,1,0:T(8,128)S(1)}, f32[4,512,512]{2,1,0:T(8,128)}, u32[]{:S(2)}) copy-start(f32[4,512,512]{2,1,0:T(8,128)} %get-tuple-element.15.pre_ref) | copy-start | bytes 12582916
  57.0 9.9 %collective-permute-start.2 = (bf16[512,5120]{1,0:T(8,128)(2,1)S(1)}, bf16[512,5120]{1,0:T(8,128)(2,1)S(1)}, u32[]{:S(2)}, u32[]{:S(2)}) collective-permute-start(bf16[512,5120]{1,0:T(8,128)(2,1)S(1)} %get-tuple-element.19.ga_ref), channel_id=1, source_target_pairs={{0,8},{1,9},{2,10},{3,11},{4,12},{5,13},{6,14},{7,15},{8,0},{9,1},... | collective-permute-start | bytes 15728648 | tf_op jit(solution)/shard_map/ppermute | solution.py:589
  57.2 9.8 %copy-start.4 = (bf16[256,512]{1,0:T(8,128)(2,1)S(1)}, bf16[256,512]{1,0:T(8,128)(2,1)}, u32[]{:S(2)}) copy-start(bf16[256,512]{1,0:T(8,128)(2,1)} %get-tuple-element.18.ha_ref) | copy-start | bytes 786436
  66.5 10.9 %collective-permute-start.1 = (bf16[4,3,256,512]{3,2,1,0:T(8,128)(2,1)}, bf16[4,3,256,512]{3,2,1,0:T(8,128)(2,1)}, u32[]{:S(2)}, u32[]{:S(2)}) collective-permute-start(bf16[4,3,256,512]{3,2,1,0:T(8,128)(2,1)} %get-tuple-element.17.send_ref), channel_id=1, source_target_pairs={{0,8},{1,9},{2,10},{3,11},{4,12},{5,13},{6,14},{7,15},{8,0},{9,1},... | collective-permute-start | bytes 9437192 | tf_op jit(solution)/shard_map/ppermute | solution.py:589
  72.7 4.7 %copy-start = (bf16[4,256,512]{2,1,0:T(8,128)(2,1)S(1)}, bf16[4,256,512]{2,1,0:T(8,128)(2,1)}, u32[]{:S(2)}) copy-start(bf16[4,256,512]{2,1,0:T(8,128)(2,1)} %get-tuple-element.16._.mine_ref) | copy-start | bytes 3145732
  72.7 24.0 %all-to-all-start.3 = ((bf16[8,128,1280]{2,1,0:T(8,128)(2,1)}), bf16[8,128,1280]{2,1,0:T(8,128)(2,1)}, u32[]{:S(2)}, u32[]{:S(2)}) async-start(bf16[8,128,1280]{2,1,0:T(8,128)(2,1)} %bitcast.10), calls=%async_computation.3 | async-start | bytes 5242880 | tf_op jit(solution)/shard_map/all_to_all | solution.py:69
  96.6 26.6 %all-to-all-start.2 = ((bf16[8,1536,128]{2,1,0:T(8,128)(2,1)}), bf16[8,1536,128]{2,1,0:T(8,128)(2,1)S(1)}, u32[]{:S(2)}, u32[]{:S(2)}) async-start(bf16[8,1536,128]{2,1,0:T(8,128)(2,1)} %bitcast.20), calls=%async_computation.2 | async-start | bytes 6291456 | tf_op jit(solution)/shard_map/all_to_all | solution.py:69

commit v6 on v5

--- a/solution.py
+++ b/solution.py
@@ -51,6 +51,11 @@
         return (v + core) % 4 // 2
 
     return groups_of(cube, near_of)
+
+
+def near_swap(x, bits):
+    pairs = [(group[i], group[i ^ bits]) for group in near_groups() for i in range(8)]
+    return lax.ppermute(x, AXES, pairs)
 
 
 def far_groups():
@@ -415,7 +420,8 @@
     )(sc, g, saved, pre, weight)
 
 
-def conv_grad_kernel(sc_ref, mine_ref, send_ref, got_ref, _, out_ref, pad_s, tap_s, res_s):
+def conv_grad_kernel(sc_ref, mine_ref, send_ref, got_ref, _, *refs):
+    outs, (pad_s, tap_s, res_s) = refs[:8], refs[8:]
     step = pl.program_id(0)
     rows, frames = mine_ref.shape[1:]
     width = send_ref.shape[3]
@@ -437,19 +443,21 @@
                 tap_s[0, side] = pad_s[side, PAD + reach : PAD + reach + frames].astype(BF16)
                 tap_s[2, side] = pad_s[side, PAD - reach : PAD - reach + frames].astype(BF16)
 
-    core = sc_ref[2]
-    low = low_lanes((32, 128))
+    core, mx, my, mz = (sc_ref[i] for i in range(2, 6))
+    side = lax.broadcasted_iota(jnp.int32, (32, 128), 1) // 64
+    straight, crossed = side == mx, side != mx
     for tap in range(TAPS):
         res_s[tap] = dot(mine_ref[0], tap_s[tap, 0]) + dot(got_ref[0, 2], tap_s[tap, 1])
-        for nz, fz, ny in BITS:
+        for dy, dz, fz in BITS:
             for fy in range(2):
+                ny, nz = my ^ dy, mz ^ dz
                 high = jnp.where(core == 0, fy, ny)
                 cols = pl.ds(pl.multiple_of((high * 2 + (ny ^ fy)) * 128, 128), 128)
-                row = (nz * 2 + fz) * 64
-                a = res_s[tap, row : row + 32, cols]
-                b = pltpu.roll(res_s[tap, row + 32 : row + 64, cols], 64 * core, 1)
-                out_ref[0, ny, nz, tap, fz, fy] = encode(jnp.where(low, a, b))
-                out_ref[1, ny, nz, tap, fz, fy] = encode(jnp.where(low, b, a))
+                row = pl.multiple_of((nz * 2 + fz) * 64, 64)
+                a = res_s[tap, pl.ds(row, 32), cols]
+                b = pltpu.roll(res_s[tap, pl.ds(row + 32, 32), cols], 64 * core, 1)
+                outs[dy * 2 + dz][tap, fz, fy] = encode(jnp.where(straight, a, b))
+                outs[4 + dy * 2 + dz][tap, fz, fy] = encode(jnp.where(crossed, a, b))
 
 
 def conv_grad(sc, mine, send, got, after):
@@ -459,6 +467,7 @@
     def at(*block):
         return pl.BlockSpec((1, *block), lambda i: (i, *(0 for _ in block)))
 
+    out = pl.BlockSpec((TAPS, 2, 2, 32, width // 4), lambda i: (i, 0, 0, 0, 0))
     return pl.pallas_call(
         conv_grad_kernel,
         grid=(LAYERS,),
@@ -469,10 +478,8 @@
             at(3, frames // 2, width),
             AFTER,
         ],
-        out_specs=pl.BlockSpec(
-            (2, 2, 2, TAPS, 2, 2, 32, width // 4), lambda i: (0, 0, 0, i, 0, 0, 0, 0)
-        ),
-        out_shape=pltpu.HBM((2, 2, 2, LAYERS * TAPS, 2, 2, 32, width // 4), BF16),
+        out_specs=[out] * 8,
+        out_shape=[jax.ShapeDtypeStruct((LAYERS * TAPS, 2, 2, 32, width // 4), BF16)] * 8,
         scratch_shapes=[
             pltpu.VMEM((2, frames + 2 * PAD, width), F32),
             pltpu.VMEM((TAPS, 2, frames, width), BF16),
@@ -518,9 +525,10 @@
     )(in_hbm(got))
 
 
-def conv_far_kernel(a_ref, b_ref, head_ref, out_ref):
+def conv_far_kernel(*refs):
+    first, second, (head_ref, out_ref) = refs[:8], refs[8:16], refs[16:]
     step = pl.program_id(0)
-    blocks, each = head_ref.shape[1], a_ref.shape[1]
+    blocks, each = head_ref.shape[1], first[0].shape[0]
     low = low_lanes((32, 128))
 
     @pl.when(step == 0)
@@ -531,8 +539,8 @@
         at = blocks + step * each + t
         for fz in range(2):
             for fy in range(2):
-                a = total_of(a_ref, t, fz, fy)
-                b = total_of(b_ref, t, fz, fy)
+                a = sum(decode(ref[t, fz, fy]) for ref in first)
+                b = sum(decode(ref[t, fz, fy]) for ref in second)
                 out_ref[fy * 2 + fz, at] = encode(jnp.where(low, a, pltpu.roll(b, 64, 1)))
                 out_ref[4 + fy * 2 + fz, at] = encode(jnp.where(low, pltpu.roll(a, 64, 1), b))
 
@@ -540,24 +548,23 @@
 def conv_far(got, head):
     half = LAYERS * TAPS // 2
     steps = 3
-    block = (8, half // steps, 2, 2, 32, 128)
+    block = (half // steps, 2, 2, 32, 128)
     shape = (8, head.shape[1] + half, 32, 128)
+    size = 8 * got[0].size
     return pl.pallas_call(
         conv_far_kernel,
         grid=(steps,),
         out_shape=jax.ShapeDtypeStruct(shape, BF16),
-        in_specs=[
-            pl.BlockSpec(block, lambda i: (0, i, 0, 0, 0, 0)),
-            pl.BlockSpec(block, lambda i: (0, i + steps, 0, 0, 0, 0)),
-            pl.BlockSpec(head.shape, lambda i: (0, 0, 0, 0)),
-        ],
+        in_specs=[pl.BlockSpec(block, lambda i: (i, 0, 0, 0, 0))] * 8
+        + [pl.BlockSpec(block, lambda i: (i + steps, 0, 0, 0, 0))] * 8
+        + [pl.BlockSpec(head.shape, lambda i: (0, 0, 0, 0))],
         out_specs=pl.BlockSpec(shape, lambda i: (0, 0, 0, 0)),
         compiler_params=params(8, "arbitrary"),
         cost_estimate=pl.CostEstimate(
-            flops=8 * got.size, bytes_accessed=3 * got.size, transcendentals=got.size
+            flops=8 * size, bytes_accessed=3 * size, transcendentals=size
         ),
         name="conv_far",
-    )(got, got, head)
+    )(*got, *got, head)
 
 
 def finish_kernel(got_ref, conv_ref, head_ref):
@@ -593,7 +600,15 @@
     _, frames, width = student_in.shape
     scores = head_weight.shape[1]
     loss_scale = scores / (3.0 * math.sqrt(READ * TM * frames))
-    sc = jnp.stack([valid[0], lax.axis_index("tm"), lax.axis_index("read") % 2])
+    read, tm = (lax.axis_index(axis) for axis in AXES)
+    core = read % 2
+    even = 1 - core
+    near_bits = (
+        tm % 2 ^ read // 8 * even,
+        tm // 4 ^ tm // 2 % 2 * even,
+        read // 4 % 2 ^ read // 2 % 2 * even,
+    )
+    sc = jnp.stack([valid[0], tm, core, *near_bits])
     regrouped = regroup(student_in[0]).reshape(TM, frames // TM, width)
     student = exchange(regrouped, frame_groups()).reshape(frames, width)
     teacher = regroup(teacher_rows[0]).reshape(TM, frames // TM, -1)
@@ -609,11 +624,11 @@
     got = swap(send)
     near = head_grad(sc, h_mine, h_got, score, score_got, mine)
     head_got = exchange(near.reshape(8, 4 * 32, scores // 4), near_groups())
-    near = conv_grad(sc, mine, send, got, near)
-    conv_got = exchange(near.reshape(8, LAYERS * TAPS * 4 * 32, width // 4), near_groups())
+    parts = conv_grad(sc, mine, send, got, near)
+    conv_got = [parts[0]] + [near_swap(parts[i], i) for i in range(1, 8)]
 
     far = head_far(head_got.reshape(8, 2, 2, 32, scores // 4))
-    far = conv_far(conv_got.reshape(8, LAYERS * TAPS, 2, 2, 32, width // 4), far)
+    far = conv_far(conv_got, far)
     return tuple(finish(exchange(far, far_groups()), scores))
 
 

time: 147 us -> 143 us (0.973); the launches traced: 147 us -> 140 us
  waiting for transfers between devices: 42.7 us -> 31.7 us
  starting transfers between devices: 19.5 us -> 24.7 us
    all_to_all x4 -> x3, waiting for transfers between devices: 42.7 us -> 12.7 us  [exchange(): return lax.all_to_all(x, AXES, 0, 0, tiled=True, axis_index_groups=groups)]
    ppermute x0 -> x7, waiting for transfers between devices: none -> 19 us  [near_swap(): return lax.ppermute(x, AXES, pairs)]
    ppermute x0 -> x7, starting transfers between devices: none -> 8.86 us  [near_swap(): return lax.ppermute(x, AXES, pairs)]
    all_to_all x4 -> x3, starting transfers between devices: 19 us -> 15.3 us  [exchange(): return lax.all_to_all(x, AXES, 0, 0, tiled=True, axis_index_groups=groups)]
  transfers between devices with their start and end apart: 7 -> 13, of which waited for: 4 -> 7; matrix products, arithmetic and copies ran while one was open for 0% -> 0% of each run, Pallas kernels for 26% -> 27%
where the time goes in v6:
time: 143 us; the launch traced here: 140 us
  Pallas kernels  58.4 us (41%)
  waiting for transfers between devices  31.7 us (22%)
  starting transfers between devices  24.7 us (17%)
  blocking collectives  20.5 us (14%)
  local copies, waits for them, and re-layouts  3.46 us (2%)
  between operations  1.51 us (1%)
    all_to_all x1, blocking collectives, exchange(): return lax.all_to_all(x, AXES, 0, 0, tiled=True, axis_index_groups=groups)  20.5 us
    ppermute x7, waiting for transfers between devices, near_swap(): return lax.ppermute(x, AXES, pairs)  19 us
    pallas_call x1, Pallas kernels, heads(): pl.pallas_call(functools.partial(head_kernel, 5.0 * loss_scale, tiles), g...  17.3 us
    all_to_all x3, starting transfers between devices, exchange(): return lax.all_to_all(x, AXES, 0, 0, tiled=True, axis_index_groups=groups)  15.3 us
    all_to_all x3, waiting for transfers between devices, exchange(): return lax.all_to_all(x, AXES, 0, 0, tiled=True, axis_index_groups=groups)  12.7 us
    pallas_call x1, Pallas kernels, back(): pl.pallas_call(back_kernel, grid=(LAYERS,), in_specs=[pl.BlockSpec(memory...  9.56 us
    ppermute x7, starting transfers between devices, near_swap(): return lax.ppermute(x, AXES, pairs)  8.86 us
    pallas_call x1, Pallas kernels, convolve(): pl.pallas_call(conv_kernel, grid=(LAYERS,), in_specs=[pl.BlockSpec(memory...  8.85 us
  transfers between devices with their start and end apart: 13, of which 7 were waited for; matrix products, arithmetic and copies ran while one was open for 0% of the time, Pallas kernels for 27%

profile of v6, /device:TPU:0, one launch (start us, length us, event | category | flops | bytes accessed | tf_op | source)
XLA Modules:
  0.0 140.3 jit_solution(3594406486738638029)
XLA Ops:
  0.6 0.0 copy-start.3
  0.6 1.0 copy-done.3
  1.7 1.3 regroup.2
  2.9 7.0 %all-to-all-start = ((bf16[8,64,512]{2,1,0:T(8,128)(2,1)}), bf16[8,64,512]{2,1,0:T(8,128)(2,1)S(1)}, u32[]{:S(2)}, u32[]{:S(2)}) async-start(bf16[8,64,512]{2,1,0:T(8,128)(2,1)} %bitcast.6), calls=%async_computation | async-start | bytes 1048576 | tf_op jit(solution)/shard_map/all_to_all | solution.py:74
  9.9 0.0 copy-start.2
  10.0 1.1 copy-done.2
  11.1 1.5 %regroup.3 = bf16[512,768]{1,0:T(8,128)(2,1)} custom-call(bf16[512,768]{1,0:T(8,128)(2,1)S(1)} %bitcast.15), custom_call_target="tpu_custom_call" | custom-call | tf_op jit(solution)/shard_map/regroup/pallas_call | solution.py:130
  12.6 9.0 %all-to-all-done = bf16[8,64,512]{2,1,0:T(8,128)(2,1)S(1)} async-done(((bf16[8,64,512]{2,1,0:T(8,128)(2,1)}), bf16[8,64,512]{2,1,0:T(8,128)(2,1)S(1)}, u32[]{:S(2)}, u32[]{:S(2)}) %all-to-all-start) | async-done | bytes 524320 | tf_op jit(solution)/shard_map/all_to_all | solution.py:74
  21.5 3.5 %all-to-all-start.1 = ((bf16[8,64,768]{2,1,0:T(8,128)(2,1)}), bf16[8,64,768]{2,1,0:T(8,128)(2,1)S(1)}, u32[]{:S(2)}, u32[]{:S(2)}) async-start(bf16[8,64,768]{2,1,0:T(8,128)(2,1)} %bitcast.9), calls=%async_computation.1 | async-start | bytes 1572864 | tf_op jit(solution)/shard_map/all_to_all | solution.py:74
  25.8 0.1 stack.23.sc_ref
  25.9 8.9 %convolve.1 = (bf16[4,512,512]{2,1,0:T(8,128)(2,1)S(1)}, f32[4,512,512]{2,1,0:T(8,128)}, bf16[512,512]{1,0:T(8,128)(2,1)}, bf16[256,512]{1,0:T(8,128)(2,1)}, bf16[256,512]{1,0:T(8,128)(2,1)}) custom-call(s32[6]{0:T(128)S(1)} %stack.23.sc_ref, bf16[512,512]{1,0:T(8,128)(2,1)S(1)} %bitcast.18, bf16[4,3,512,512]{3,2,1,0:T(8,128)(2,1)} %w_ref.3), custom_call_target="tpu_custom_call" | custom-call | flops 3221225472 | bytes 12582912 | tf_op jit(solution)/shard_map/convolve/pallas_call | solution.py:185
  34.8 0.0 collective-permute-start
  34.8 3.7 %all-to-all-done.1 = bf16[8,64,768]{2,1,0:T(8,128)(2,1)S(1)} async-done(((bf16[8,64,768]{2,1,0:T(8,128)(2,1)}), bf16[8,64,768]{2,1,0:T(8,128)(2,1)S(1)}, u32[]{:S(2)}, u32[]{:S(2)}) %all-to-all-start.1) | async-done | bytes 786464 | tf_op jit(solution)/shard_map/all_to_all | solution.py:74
  38.5 0.0 collective-permute-done._.hb_ref
  38.5 0.0 slice-start
  38.5 0.0 copy-start.5
  38.5 1.2 copy-done.5
  39.7 0.0 slice-start.1
  39.7 0.0 copy-start
  39.7 17.3 %heads.1 = (bf16[512,5120]{1,0:T(8,128)(2,1)S(1)}, f32[512,512]{1,0:T(8,128)S(1)}) custom-call(s32[6]{0:T(128)S(1)} %stack.23.sc_ref, bf16[512,512]{1,0:T(8,128)(2,1)S(1)} %copy-done.5, bf16[512,768]{1,0:T(8,128)(2,1)S(1)} %bitcast.16, bf16[512,5120]{1,0:T(8,128)(2,1)} %ws_ref.1, bf16[768,5120]{1,0:T(8,128)(2,1)} %wt_ref.1, ...), custom_call_target="tpu_custom_call" | custom-call | flops 9395240960 | bytes 23592960 | tf_op jit(solution)/shard_map/heads/pallas_call | solution.py:265
  57.1 0.1 collective-permute-start.2
  57.1 0.0 slice-done
  57.2 0.0 slice-done.1
  57.2 0.0 copy-done
  57.2 0.0 copy-start.4
  57.2 9.6 %back.1 = (bf16[4,3,256,512]{3,2,1,0:T(8,128)(2,1)}, bf16[4,256,512]{2,1,0:T(8,128)(2,1)}) custom-call(s32[6]{0:T(128)S(1)} %stack.23.sc_ref, f32[512,512]{1,0:T(8,128)S(1)} %get-tuple-element.21.g4_ref, bf16[4,512,512]{2,1,0:T(8,128)(2,1)S(1)} %get-tuple-element.22.h_ref, f32[4,512,512]{2,1,0:T(8,128)S(1)} %copy-done, bf16[4,3,512,512]{3,2,1,0:T(8,128)(2,1)S(1)} %bitcast.14), custom_call_target="tpu_custom_call" | custom-call | flops 2415919104 | bytes 16777216 | tf_op jit(solution)/shard_map/back/pallas_call | solution.py:390
  66.8 0.5 collective-permute-start.1
  67.2 0.0 collective-permute-done.2.gb_ref
  67.2 0.0 copy-done.4
  67.2 5.7 %head_grad.1._ = bf16[2,2,2,2,2,32,1280]{6,5,4,3,2,1,0:T(8,128)(2,1)} custom-call(s32[6]{0:T(128)S(1)} %stack.23.sc_ref, bf16[256,512]{1,0:T(8,128)(2,1)S(1)} %copy-done.4, bf16[256,512]{1,0:T(8,128)(2,1)S(1)} %collective-permute-done._.hb_ref, bf16[512,5120]{1,0:T(8,128)(2,1)S(1)} %get-tuple-element.27.ga_ref, ...), custom_call_target="tpu_custom_call" | custom-call | flops 2684354560 | bytes 13107200 | tf_op jit(solution)/shard_map/head_grad/pallas_call | solution.py:328
  73.0 0.0 copy-start.1
  73.0 4.7 %all-to-all-start.2 = ((bf16[8,128,1280]{2,1,0:T(8,128)(2,1)}), bf16[8,128,1280]{2,1,0:T(8,128)(2,1)}, u32[]{:S(2)}, u32[]{:S(2)}) async-start(bf16[8,128,1280]{2,1,0:T(8,128)(2,1)} %bitcast.11), calls=%async_computation.2 | async-start | bytes 5242880 | tf_op jit(solution)/shard_map/all_to_all | solution.py:74
  77.7 0.0 collective-permute-done.1.got_ref
  77.7 0.0 copy-done.1
  77.7 8.8 %conv_grad.1 = (bf16[12,2,2,32,128]{4,3,2,1,0:T(8,128)(2,1)S(1)}, bf16[12,2,2,32,128]{4,3,2,1,0:T(8,128)(2,1)S(1)}, bf16[12,2,2,32,128]{4,3,2,1,0:T(8,128)(2,1)S...) custom-call(s32[6]{0:T(128)S(1)} %stack.23.sc_ref, ...), custom_call_target="tpu_custom_call" | custom-call | flops 3221225472 | bytes 10485760 | tf_op jit(solution)/shard_map/conv_grad/pallas_call | solution.py:471
  86.6 1.9 %collective-permute-start.3 = (bf16[12,2,2,32,128]{4,3,2,1,0:T(8,128)(2,1)S(1)}, bf16[12,2,2,32,128]{4,3,2,1,0:T(8,128)(2,1)S(1)}, u32[]{:S(2)}, u32[]{:S(2)}) collective-permute-start(bf16[12,2,2,32,128]{4,3,2,1,0:T(8,128)(2,1)S(1)} %get-tuple-element.29), channel_id=1, source_target_pairs={{0,16},{16,0},{2,18},{18,2},{64,80},{80,64},{66,82},{82,66},{48,32... | collective-permute-start | bytes 1179656 | tf_op jit(solution)/shard_map/ppermute | solution.py:58
  88.5 1.3 collective-permute-start.4
  89.8 0.3 collective-permute-start.5
  90.1 1.7 %collective-permute-start.6 = (bf16[12,2,2,32,128]{4,3,2,1,0:T(8,128)(2,1)}, bf16[12,2,2,32,128]{4,3,2,1,0:T(8,128)(2,1)S(1)}, u32[]{:S(2)}, u32[]{:S(2)}) collective-permute-start(bf16[12,2,2,32,128]{4,3,2,1,0:T(8,128)(2,1)} %get-tuple-element.32), channel_id=1, source_target_pairs={{0,64},{16,80},{2,66},{18,82},{64,0},{80,16},{66,2},{82,18},{48,11... | collective-permute-start | bytes 1179656 | tf_op jit(solution)/shard_map/ppermute | solution.py:58
  91.8 1.6 %collective-permute-start.7 = (bf16[12,2,2,32,128]{4,3,2,1,0:T(8,128)(2,1)}, bf16[12,2,2,32,128]{4,3,2,1,0:T(8,128)(2,1)S(1)}, u32[]{:S(2)}, u32[]{:S(2)}) collective-permute-start(bf16[12,2,2,32,128]{4,3,2,1,0:T(8,128)(2,1)} %get-tuple-element.33), channel_id=1, source_target_pairs={{0,80},{16,64},{2,82},{18,66},{64,16},{80,0},{66,18},{82,2},{48,96... | collective-permute-start | bytes 1179656 | tf_op jit(solution)/shard_map/ppermute | solution.py:58
  93.4 6.9 %collective-permute-done.3.refs_1_.refs_9_ = bf16[12,2,2,32,128]{4,3,2,1,0:T(8,128)(2,1)S(1)} collective-permute-done((bf16[12,2,2,32,128]{4,3,2,1,0:T(8,128)(2,1)S(1)}, bf16[12,2,2,32,128]{4,3,2,1,0:T(8,128)(2,1)S(1)}, u32[]{:S(2)}, u32[]{:S(2)}) %collective-permute-start.3) | collective-permute-done | bytes 393248 | tf_op jit(solution)/shard_map/ppermute | solution.py:58
  100.3 1.5 %collective-permute-start.8 = (bf16[12,2,2,32,128]{4,3,2,1,0:T(8,128)(2,1)}, bf16[12,2,2,32,128]{4,3,2,1,0:T(8,128)(2,1)S(1)}, u32[]{:S(2)}, u32[]{:S(2)}) collective-permute-start(bf16[12,2,2,32,128]{4,3,2,1,0:T(8,128)(2,1)} %get-tuple-element.34), channel_id=1, source_target_pairs={{0,66},{16,82},{2,64},{18,80},{64,2},{80,18},{66,0},{82,16},{48,11... | collective-permute-start | bytes 1179656 | tf_op jit(solution)/shard_map/ppermute | solution.py:58
  101.8 0.0 collective-permute-done.4.refs_2_.refs_10_
  101.8 0.5 collective-permute-start.9
  102.3 0.0 all-to-all-done.2
  102.3 2.8 %head_far.1.refs_16_ = bf16[8,5,32,128]{3,2,1,0:T(8,128)(2,1)S(1)} custom-call(bf16[8,2,2,32,1280]{4,3,2,1,0:T(8,128)(2,1)} %bitcast.12.got_ref), custom_call_target="tpu_custom_call" | custom-call | flops 10485760 | bytes 3932160 | tf_op jit(solution)/shard_map/head_far/pallas_call | solution.py:515
  105.1 3.6 %collective-permute-done.5.refs_3_.refs_11_ = bf16[12,2,2,32,128]{4,3,2,1,0:T(8,128)(2,1)S(1)} collective-permute-done((bf16[12,2,2,32,128]{4,3,2,1,0:T(8,128)(2,1)}, bf16[12,2,2,32,128]{4,3,2,1,0:T(8,128)(2,1)S(1)}, u32[]{:S(2)}, u32[]{:S(2)}) %collective-permute-start.5) | collective-permute-done | bytes 393248 | tf_op jit(solution)/shard_map/ppermute | solution.py:58
  108.7 0.0 collective-permute-done.6.refs_4_.refs_12_
  108.8 0.1 collective-permute-done.7.refs_5_.refs_13_
  108.8 4.1 %collective-permute-done.8.refs_6_.refs_14_ = bf16[12,2,2,32,128]{4,3,2,1,0:T(8,128)(2,1)S(1)} collective-permute-done((bf16[12,2,2,32,128]{4,3,2,1,0:T(8,128)(2,1)}, bf16[12,2,2,32,128]{4,3,2,1,0:T(8,128)(2,1)S(1)}, u32[]{:S(2)}, u32[]{:S(2)}) %collective-permute-start.8) | collective-permute-done | bytes 393248 | tf_op jit(solution)/shard_map/ppermute | solution.py:58
  112.9 4.3 %collective-permute-done.9.refs_7_.refs_15_ = bf16[12,2,2,32,128]{4,3,2,1,0:T(8,128)(2,1)S(1)} collective-permute-done((bf16[12,2,2,32,128]{4,3,2,1,0:T(8,128)(2,1)}, bf16[12,2,2,32,128]{4,3,2,1,0:T(8,128)(2,1)S(1)}, u32[]{:S(2)}, u32[]{:S(2)}) %collective-permute-start.9) | collective-permute-done | bytes 393248 | tf_op jit(solution)/shard_map/ppermute | solution.py:58
  117.2 1.6 %conv_far.1 = bf16[8,11,32,128]{3,2,1,0:T(8,128)(2,1)S(1)} custom-call(bf16[12,2,2,32,128]{4,3,2,1,0:T(8,128)(2,1)S(1)} %get-tuple-element.28.refs_0_.refs_8_, bf16[12,2,2,32,128]{4,3,2,1,0:T(8,128)(2,1)S(1)} %collective-permute-done.3.refs_1_.refs_9_, bf16[12,2,2,32,128]{4,3,2,1,0:T(8,128)(2,1)S(1)} %collective-permute-done.4.refs_2_.refs_10_, ...), custom_call_target="tpu_custom_call" | custom-call | flops 12582912 | bytes 4718592 | tf_op jit(solution)/shard_map/conv_far/pallas_call | solution.py:554
  118.8 20.5 %all_to_all.20.got_ref = bf16[8,11,32,128]{3,2,1,0:T(8,128)(2,1)S(1)} all-to-all(bf16[8,11,32,128]{3,2,1,0:T(8,128)(2,1)S(1)} %conv_far.1), channel_id=1, replica_groups={{0,48,6,54,65,113,71,119},{16,32,22,38,81,97,87,103},{2,50,4,52,67,115,..., dimensions={0} | all-to-all | bytes 1441792 | tf_op jit(solution)/shard_map/all_to_all | solution.py:74
  139.3 0.9 finish.1
  (1 shorter events, 0.0 us)
Async XLA Ops:
  0.6 1.0 copy-start.3
  2.9 18.6 %all-to-all-start = ((bf16[8,64,512]{2,1,0:T(8,128)(2,1)}), bf16[8,64,512]{2,1,0:T(8,128)(2,1)S(1)}, u32[]{:S(2)}, u32[]{:S(2)}) async-start(bf16[8,64,512]{2,1,0:T(8,128)(2,1)} %bitcast.6), calls=%async_computation | async-start | bytes 1048576 | tf_op jit(solution)/shard_map/all_to_all | solution.py:74
  9.9 1.1 copy-start.2
  21.5 17.0 %all-to-all-start.1 = ((bf16[8,64,768]{2,1,0:T(8,128)(2,1)}), bf16[8,64,768]{2,1,0:T(8,128)(2,1)S(1)}, u32[]{:S(2)}, u32[]{:S(2)}) async-start(bf16[8,64,768]{2,1,0:T(8,128)(2,1)} %bitcast.9), calls=%async_computation.1 | async-start | bytes 1572864 | tf_op jit(solution)/shard_map/all_to_all | solution.py:74
  34.8 3.7 %collective-permute-start = (bf16[256,512]{1,0:T(8,128)(2,1)}, bf16[256,512]{1,0:T(8,128)(2,1)S(1)}, u32[]{:S(2)}, u32[]{:S(2)}) collective-permute-start(bf16[256,512]{1,0:T(8,128)(2,1)} %get-tuple-element.20), channel_id=1, source_target_pairs={{0,8},{1,9},{2,10},{3,11},{4,12},{5,13},{6,14},{7,15},{8,0},{9,1},... | collective-permute-start | bytes 786440 | tf_op jit(solution)/shard_map/ppermute | solution.py:596
  38.5 18.6 %slice-start = ((s8[6291456]{0:T(1024)(128)(4,1)}), s8[4194304]{0:T(1024)(128)(4,1)S(1)}, s32[]{:S(2)}) async-start(s8[6291456]{0:T(1024)(128)(4,1)} %bitcast.13), calls=%async_computation.4 | async-start | bytes 8388608
  38.5 1.2 copy-start.5
  39.7 17.5 %slice-start.1 = ((s8[6291456]{0:T(1024)(128)(4,1)}), s8[2097152]{0:T(1024)(128)(4,1)S(1)}, s32[]{:S(2)}) async-start(s8[6291456]{0:T(1024)(128)(4,1)} %bitcast.13), calls=%async_computation.5 | async-start | bytes 4194304
  39.7 17.5 %copy-start = (f32[4,512,512]{2,1,0:T(8,128)S(1)}, f32[4,512,512]{2,1,0:T(8,128)}, u32[]{:S(2)}) copy-start(f32[4,512,512]{2,1,0:T(8,128)} %get-tuple-element.23.pre_ref) | copy-start | bytes 12582916
  57.1 10.2 %collective-permute-start.2 = (bf16[512,5120]{1,0:T(8,128)(2,1)S(1)}, bf16[512,5120]{1,0:T(8,128)(2,1)S(1)}, u32[]{:S(2)}, u32[]{:S(2)}) collective-permute-start(bf16[512,5120]{1,0:T(8,128)(2,1)S(1)} %get-tuple-element.27.ga_ref), channel_id=1, source_target_pairs={{0,8},{1,9},{2,10},{3,11},{4,12},{5,13},{6,14},{7,15},{8,0},{9,1},... | collective-permute-start | bytes 15728648 | tf_op jit(solution)/shard_map/ppermute | solution.py:596
  57.2 10.0 %copy-start.4 = (bf16[256,512]{1,0:T(8,128)(2,1)S(1)}, bf16[256,512]{1,0:T(8,128)(2,1)}, u32[]{:S(2)}) copy-start(bf16[256,512]{1,0:T(8,128)(2,1)} %get-tuple-element.26.ha_ref) | copy-start | bytes 786436
  66.8 10.9 %collective-permute-start.1 = (bf16[4,3,256,512]{3,2,1,0:T(8,128)(2,1)}, bf16[4,3,256,512]{3,2,1,0:T(8,128)(2,1)}, u32[]{:S(2)}, u32[]{:S(2)}) collective-permute-start(bf16[4,3,256,512]{3,2,1,0:T(8,128)(2,1)} %get-tuple-element.25.send_ref), channel_id=1, source_target_pairs={{0,8},{1,9},{2,10},{3,11},{4,12},{5,13},{6,14},{7,15},{8,0},{9,1},... | collective-permute-start | bytes 9437192 | tf_op jit(solution)/shard_map/ppermute | solution.py:596
  73.0 4.8 %copy-start.1 = (bf16[4,256,512]{2,1,0:T(8,128)(2,1)S(1)}, bf16[4,256,512]{2,1,0:T(8,128)(2,1)}, u32[]{:S(2)}) copy-start(bf16[4,256,512]{2,1,0:T(8,128)(2,1)} %get-tuple-element.24._.mine_ref) | copy-start | bytes 3145732
  73.0 29.4 %all-to-all-start.2 = ((bf16[8,128,1280]{2,1,0:T(8,128)(2,1)}), bf16[8,128,1280]{2,1,0:T(8,128)(2,1)}, u32[]{:S(2)}, u32[]{:S(2)}) async-start(bf16[8,128,1280]{2,1,0:T(8,128)(2,1)} %bitcast.11), calls=%async_computation.2 | async-start | bytes 5242880 | tf_op jit(solution)/shard_map/all_to_all | solution.py:74
  86.6 13.8 %collective-permute-start.3 = (bf16[12,2,2,32,128]{4,3,2,1,0:T(8,128)(2,1)S(1)}, bf16[12,2,2,32,128]{4,3,2,1,0:T(8,128)(2,1)S(1)}, u32[]{:S(2)}, u32[]{:S(2)}) collective-permute-start(bf16[12,2,2,32,128]{4,3,2,1,0:T(8,128)(2,1)S(1)} %get-tuple-element.29), channel_id=1, source_target_pairs={{0,16},{16,0},{2,18},{18,2},{64,80},{80,64},{66,82},{82,66},{48,32... | collective-permute-start | bytes 1179656 | tf_op jit(solution)/shard_map/ppermute | solution.py:58
  88.5 13.3 %collective-permute-start.4 = (bf16[12,2,2,32,128]{4,3,2,1,0:T(8,128)(2,1)S(1)}, bf16[12,2,2,32,128]{4,3,2,1,0:T(8,128)(2,1)S(1)}, u32[]{:S(2)}, u32[]{:S(2)}) collective-permute-start(bf16[12,2,2,32,128]{4,3,2,1,0:T(8,128)(2,1)S(1)} %get-tuple-element.30), channel_id=1, source_target_pairs={{0,2},{16,18},{2,0},{18,16},{64,66},{80,82},{66,64},{82,80},{48,50... | collective-permute-start | bytes 1179656 | tf_op jit(solution)/shard_map/ppermute | solution.py:58
  89.8 19.0 %collective-permute-start.5 = (bf16[12,2,2,32,128]{4,3,2,1,0:T(8,128)(2,1)}, bf16[12,2,2,32,128]{4,3,2,1,0:T(8,128)(2,1)S(1)}, u32[]{:S(2)}, u32[]{:S(2)}) collective-permute-start(bf16[12,2,2,32,128]{4,3,2,1,0:T(8,128)(2,1)} %get-tuple-element.31), channel_id=1, source_target_pairs={{0,18},{16,2},{2,16},{18,0},{64,82},{80,66},{66,80},{82,64},{48,34... | collective-permute-start | bytes 1179656 | tf_op jit(solution)/shard_map/ppermute | solution.py:58
  90.1 18.6 %collective-permute-start.6 = (bf16[12,2,2,32,128]{4,3,2,1,0:T(8,128)(2,1)}, bf16[12,2,2,32,128]{4,3,2,1,0:T(8,128)(2,1)S(1)}, u32[]{:S(2)}, u32[]{:S(2)}) collective-permute-start(bf16[12,2,2,32,128]{4,3,2,1,0:T(8,128)(2,1)} %get-tuple-element.32), channel_id=1, source_target_pairs={{0,64},{16,80},{2,66},{18,82},{64,0},{80,16},{66,2},{82,18},{48,11... | collective-permute-start | bytes 1179656 | tf_op jit(solution)/shard_map/ppermute | solution.py:58
  91.8 17.0 %collective-permute-start.7 = (bf16[12,2,2,32,128]{4,3,2,1,0:T(8,128)(2,1)}, bf16[12,2,2,32,128]{4,3,2,1,0:T(8,128)(2,1)S(1)}, u32[]{:S(2)}, u32[]{:S(2)}) collective-permute-start(bf16[12,2,2,32,128]{4,3,2,1,0:T(8,128)(2,1)} %get-tuple-element.33), channel_id=1, source_target_pairs={{0,80},{16,64},{2,82},{18,66},{64,16},{80,0},{66,18},{82,2},{48,96... | collective-permute-start | bytes 1179656 | tf_op jit(solution)/shard_map/ppermute | solution.py:58
  100.3 12.6 %collective-permute-start.8 = (bf16[12,2,2,32,128]{4,3,2,1,0:T(8,128)(2,1)}, bf16[12,2,2,32,128]{4,3,2,1,0:T(8,128)(2,1)S(1)}, u32[]{:S(2)}, u32[]{:S(2)}) collective-permute-start(bf16[12,2,2,32,128]{4,3,2,1,0:T(8,128)(2,1)} %get-tuple-element.34), channel_id=1, source_target_pairs={{0,66},{16,82},{2,64},{18,80},{64,2},{80,18},{66,0},{82,16},{48,11... | collective-permute-start | bytes 1179656 | tf_op jit(solution)/shard_map/ppermute | solution.py:58
  101.8 15.4 %collective-permute-start.9 = (bf16[12,2,2,32,128]{4,3,2,1,0:T(8,128)(2,1)}, bf16[12,2,2,32,128]{4,3,2,1,0:T(8,128)(2,1)S(1)}, u32[]{:S(2)}, u32[]{:S(2)}) collective-permute-start(bf16[12,2,2,32,128]{4,3,2,1,0:T(8,128)(2,1)} %get-tuple-element.35), channel_id=1, source_target_pairs={{0,82},{16,66},{2,80},{18,64},{64,18},{80,2},{66,16},{82,0},{48,98... | collective-permute-start | bytes 1179656 | tf_op jit(solution)/shard_map/ppermute | solution.py:58

commit v7 on v6

--- a/solution.py
+++ b/solution.py
@@ -116,25 +116,33 @@
     return (position < sc_ref[0]).astype(F32)
 
 
-def regroup_kernel(x_ref, out_ref):
+def regroup_kernel(x_ref, out_ref, select_s):
     frames = x_ref.shape[0]
-    row = lax.broadcasted_iota(jnp.int32, (frames, frames), 0)
-    col = lax.broadcasted_iota(jnp.int32, (frames, frames), 1)
-    per = frames // TM
-    source = (row % per) // CLASSES * BASE_DILATION + row // per * CLASSES + row % CLASSES
-    select = jnp.where(col == source, 1.0, 0.0).astype(BF16)
-    out_ref[...] = dot(select, x_ref[...]).astype(BF16)
+
+    @pl.when(pl.program_id(0) == 0)
+    def _():
+        row = lax.broadcasted_iota(jnp.int32, (frames, frames), 0)
+        col = lax.broadcasted_iota(jnp.int32, (frames, frames), 1)
+        per = frames // TM
+        source = (row % per) // CLASSES * BASE_DILATION + row // per * CLASSES + row % CLASSES
+        select_s[...] = jnp.where(col == source, 1.0, 0.0).astype(BF16)
+
+    out_ref[...] = dot(select_s[...], x_ref[...]).astype(BF16)
 
 
 def regroup(x):
+    frames, width = x.shape
+    block = pl.BlockSpec((frames, 256), lambda i: (0, i))
     return pl.pallas_call(
         regroup_kernel,
+        grid=(width // 256,),
         out_shape=jax.ShapeDtypeStruct(x.shape, BF16),
-        in_specs=[whole()],
-        out_specs=whole(),
-        compiler_params=params(5),
+        in_specs=[block],
+        out_specs=block,
+        scratch_shapes=[pltpu.VMEM((frames, frames), BF16)],
+        compiler_params=params(5, "arbitrary"),
         name="regroup",
-    )(x)
+    )(in_hbm(x))
 
 
 def split_rows(core, ht_s, mine_ref, other_ref):
@@ -293,7 +301,7 @@
             transcendentals=4 * frames * scores,
         ),
         name="heads",
-    )(sc, hidden, teacher_in, in_hbm(head_weight), in_hbm(teacher_head_weight), after)
+    )(sc, in_hbm(hidden), teacher_in, in_hbm(head_weight), in_hbm(teacher_head_weight), after)
 
 
 def head_grad_kernel(sc_ref, ha_ref, hb_ref, ga_ref, gb_ref, _, out_ref, res_s):
@@ -625,7 +633,7 @@
     near = head_grad(sc, h_mine, h_got, score, score_got, mine)
     head_got = exchange(near.reshape(8, 4 * 32, scores // 4), near_groups())
     parts = conv_grad(sc, mine, send, got, near)
-    conv_got = [parts[0]] + [near_swap(parts[i], i) for i in range(1, 8)]
+    conv_got = [parts[0]] + [near_swap(parts[i], i) for i in (7, 3, 5, 6, 1, 2, 4)]
 
     far = head_far(head_got.reshape(8, 2, 2, 32, scores // 4))
     far = conv_far(conv_got, far)

time: 143 us -> 143 us (level); the launches traced: 140 us -> 142 us
  starting transfers between devices: 24.7 us -> 29.7 us
  Pallas kernels: 58.4 us -> 62 us
  local copies, waits for them, and re-layouts: 3.46 us -> 0.1 us
  waiting for transfers between devices: 31.7 us -> 28.4 us
    ppermute x7, starting transfers between devices: 8.86 us -> 13.9 us  [near_swap(): return lax.ppermute(x, AXES, pairs)]
    unnamed x16 -> x10, local copies, waits for them, and re-layouts: 3.38 us -> 0.02 us
    pallas_call x2, Pallas kernels: 2.76 us -> 6.03 us  [regroup(): pl.pallas_call(regroup_kernel, grid=(width // 256,), out_shape=jax.ShapeD...]
    ppermute x7, waiting for transfers between devices: 19 us -> 16.7 us  [near_swap(): return lax.ppermute(x, AXES, pairs)]
  transfers between devices with their start and end apart: 13 -> 13, of which waited for: 7 -> 5; matrix products, arithmetic and copies ran while one was open for 0% -> 0% of each run, Pallas kernels for 27% -> 28%
where the time goes in v7:
time: 143 us; the launch traced here: 142 us
  Pallas kernels  62 us (43%)
  starting transfers between devices  29.7 us (21%)
  waiting for transfers between devices  28.4 us (20%)
  blocking collectives  20.6 us (14%)
  between operations  1.53 us (1%)
    all_to_all x1, blocking collectives, exchange(): return lax.all_to_all(x, AXES, 0, 0, tiled=True, axis_index_groups=groups)  20.6 us
    pallas_call x1, Pallas kernels, heads(): pl.pallas_call(functools.partial(head_kernel, 5.0 * loss_scale, tiles), g...  17.6 us
    ppermute x7, waiting for transfers between devices, near_swap(): return lax.ppermute(x, AXES, pairs)  16.7 us
    all_to_all x3, starting transfers between devices, exchange(): return lax.all_to_all(x, AXES, 0, 0, tiled=True, axis_index_groups=groups)  15.3 us
    ppermute x7, starting transfers between devices, near_swap(): return lax.ppermute(x, AXES, pairs)  13.9 us
    all_to_all x3, waiting for transfers between devices, exchange(): return lax.all_to_all(x, AXES, 0, 0, tiled=True, axis_index_groups=groups)  11.8 us
    pallas_call x1, Pallas kernels, back(): pl.pallas_call(back_kernel, grid=(LAYERS,), in_specs=[pl.BlockSpec(memory...  9.55 us
    pallas_call x1, Pallas kernels, conv_grad(): pl.pallas_call(conv_grad_kernel, grid=(LAYERS,), in_specs=[pl.BlockSpec(m...  8.9 us
  transfers between devices with their start and end apart: 13, of which 5 were waited for; matrix products, arithmetic and copies ran while one was open for 0% of the time, Pallas kernels for 28%

profile of v7, /device:TPU:0, one launch (start us, length us, event | category | flops | bytes accessed | tf_op | source)
XLA Modules:
  0.0 142.4 jit_solution(10065835382917893056)
XLA Ops:
  0.6 2.5 %regroup.2 = bf16[512,512]{1,0:T(8,128)(2,1)} custom-call(bf16[512,512]{1,0:T(8,128)(2,1)} %bitcast.18), custom_call_target="tpu_custom_call" | custom-call | tf_op jit(solution)/shard_map/regroup/pallas_call | solution.py:136
  3.1 7.0 %all-to-all-start = ((bf16[8,64,512]{2,1,0:T(8,128)(2,1)}), bf16[8,64,512]{2,1,0:T(8,128)(2,1)S(1)}, u32[]{:S(2)}, u32[]{:S(2)}) async-start(bf16[8,64,512]{2,1,0:T(8,128)(2,1)} %bitcast.6), calls=%async_computation | async-start | bytes 1048576 | tf_op jit(solution)/shard_map/all_to_all | solution.py:74
  10.1 3.6 %regroup.3 = bf16[512,768]{1,0:T(8,128)(2,1)} custom-call(bf16[512,768]{1,0:T(8,128)(2,1)} %bitcast.17), custom_call_target="tpu_custom_call" | custom-call | tf_op jit(solution)/shard_map/regroup/pallas_call | solution.py:136
  13.7 8.0 %all-to-all-done = bf16[8,64,512]{2,1,0:T(8,128)(2,1)S(1)} async-done(((bf16[8,64,512]{2,1,0:T(8,128)(2,1)}), bf16[8,64,512]{2,1,0:T(8,128)(2,1)S(1)}, u32[]{:S(2)}, u32[]{:S(2)}) %all-to-all-start) | async-done | bytes 524320 | tf_op jit(solution)/shard_map/all_to_all | solution.py:74
  21.7 3.5 %all-to-all-start.1 = ((bf16[8,64,768]{2,1,0:T(8,128)(2,1)}), bf16[8,64,768]{2,1,0:T(8,128)(2,1)S(1)}, u32[]{:S(2)}, u32[]{:S(2)}) async-start(bf16[8,64,768]{2,1,0:T(8,128)(2,1)} %bitcast.9), calls=%async_computation.1 | async-start | bytes 1572864 | tf_op jit(solution)/shard_map/all_to_all | solution.py:74
  26.0 0.1 stack.23.sc_ref
  26.1 8.9 %convolve.1 = (bf16[4,512,512]{2,1,0:T(8,128)(2,1)S(1)}, f32[4,512,512]{2,1,0:T(8,128)}, bf16[512,512]{1,0:T(8,128)(2,1)}, bf16[256,512]{1,0:T(8,128)(2,1)}, bf16[256,512]{1,0:T(8,128)(2,1)}) custom-call(s32[6]{0:T(128)S(1)} %stack.23.sc_ref, bf16[512,512]{1,0:T(8,128)(2,1)S(1)} %bitcast.16, bf16[4,3,512,512]{3,2,1,0:T(8,128)(2,1)} %w_ref.3), custom_call_target="tpu_custom_call" | custom-call | flops 3221225472 | bytes 12582912 | tf_op jit(solution)/shard_map/convolve/pallas_call | solution.py:193
  35.0 0.0 collective-permute-start
  35.0 3.7 %all-to-all-done.1 = bf16[8,64,768]{2,1,0:T(8,128)(2,1)S(1)} async-done(((bf16[8,64,768]{2,1,0:T(8,128)(2,1)}), bf16[8,64,768]{2,1,0:T(8,128)(2,1)S(1)}, u32[]{:S(2)}, u32[]{:S(2)}) %all-to-all-start.1) | async-done | bytes 786464 | tf_op jit(solution)/shard_map/all_to_all | solution.py:74
  38.7 0.0 collective-permute-done._.hb_ref
  38.7 0.0 slice-start
  38.7 0.0 slice-start.1
  38.7 0.0 copy-start
  38.7 17.6 %heads.1 = (bf16[512,5120]{1,0:T(8,128)(2,1)S(1)}, f32[512,512]{1,0:T(8,128)S(1)}) custom-call(s32[6]{0:T(128)S(1)} %stack.23.sc_ref, bf16[512,512]{1,0:T(8,128)(2,1)} %get-tuple-element.19.h_ref, bf16[512,768]{1,0:T(8,128)(2,1)S(1)} %bitcast.15, bf16[512,5120]{1,0:T(8,128)(2,1)} %ws_ref.1, bf16[768,5120]{1,0:T(8,128)(2,1)} %wt_ref.1, ...), custom_call_target="tpu_custom_call" | custom-call | flops 9395240960 | bytes 23592960 | tf_op jit(solution)/shard_map/heads/pallas_call | solution.py:273
  56.3 0.1 collective-permute-start.2
  56.4 0.0 slice-done
  56.4 0.0 slice-done.1
  56.4 0.0 copy-done
  56.4 0.0 copy-start.2
  56.5 9.5 %back.1 = (bf16[4,3,256,512]{3,2,1,0:T(8,128)(2,1)}, bf16[4,256,512]{2,1,0:T(8,128)(2,1)}) custom-call(s32[6]{0:T(128)S(1)} %stack.23.sc_ref, f32[512,512]{1,0:T(8,128)S(1)} %get-tuple-element.21.g4_ref, bf16[4,512,512]{2,1,0:T(8,128)(2,1)S(1)} %get-tuple-element.22.h_ref, f32[4,512,512]{2,1,0:T(8,128)S(1)} %copy-done, bf16[4,3,512,512]{3,2,1,0:T(8,128)(2,1)S(1)} %bitcast.14), custom_call_target="tpu_custom_call" | custom-call | flops 2415919104 | bytes 16777216 | tf_op jit(solution)/shard_map/back/pallas_call | solution.py:398
  66.0 0.5 collective-permute-start.1
  66.5 0.0 collective-permute-done.2.gb_ref
  66.5 0.0 copy-done.2
  66.5 5.7 %head_grad.1._ = bf16[2,2,2,2,2,32,1280]{6,5,4,3,2,1,0:T(8,128)(2,1)} custom-call(s32[6]{0:T(128)S(1)} %stack.23.sc_ref, bf16[256,512]{1,0:T(8,128)(2,1)S(1)} %copy-done.2, bf16[256,512]{1,0:T(8,128)(2,1)S(1)} %collective-permute-done._.hb_ref, bf16[512,5120]{1,0:T(8,128)(2,1)S(1)} %get-tuple-element.27.ga_ref, ...), custom_call_target="tpu_custom_call" | custom-call | flops 2684354560 | bytes 13107200 | tf_op jit(solution)/shard_map/head_grad/pallas_call | solution.py:336
  72.2 0.0 copy-start.1
  72.2 4.7 %all-to-all-start.2 = ((bf16[8,128,1280]{2,1,0:T(8,128)(2,1)}), bf16[8,128,1280]{2,1,0:T(8,128)(2,1)}, u32[]{:S(2)}, u32[]{:S(2)}) async-start(bf16[8,128,1280]{2,1,0:T(8,128)(2,1)} %bitcast.11), calls=%async_computation.2 | async-start | bytes 5242880 | tf_op jit(solution)/shard_map/all_to_all | solution.py:74
  76.9 0.0 collective-permute-done.1.got_ref
  76.9 0.0 copy-done.1
  76.9 8.9 %conv_grad.1 = (bf16[12,2,2,32,128]{4,3,2,1,0:T(8,128)(2,1)S(1)}, bf16[12,2,2,32,128]{4,3,2,1,0:T(8,128)(2,1)}, bf16[12,2,2,32,128]{4,3,2,1,0:T(8,128)(2,1)}, bf...) custom-call(s32[6]{0:T(128)S(1)} %stack.23.sc_ref, ...), custom_call_target="tpu_custom_call" | custom-call | flops 3221225472 | bytes 10485760 | tf_op jit(solution)/shard_map/conv_grad/pallas_call | solution.py:479
  85.8 3.6 %collective-permute-start.3 = (bf16[12,2,2,32,128]{4,3,2,1,0:T(8,128)(2,1)S(1)}, bf16[12,2,2,32,128]{4,3,2,1,0:T(8,128)(2,1)S(1)}, u32[]{:S(2)}, u32[]{:S(2)}) collective-permute-start(bf16[12,2,2,32,128]{4,3,2,1,0:T(8,128)(2,1)S(1)} %get-tuple-element.29), channel_id=1, source_target_pairs={{0,82},{16,66},{2,80},{18,64},{64,18},{80,2},{66,16},{82,0},{48,98... | collective-permute-start | bytes 1179656 | tf_op jit(solution)/shard_map/ppermute | solution.py:58
  89.4 0.6 collective-permute-start.4
  90.0 1.6 %collective-permute-start.5 = (bf16[12,2,2,32,128]{4,3,2,1,0:T(8,128)(2,1)}, bf16[12,2,2,32,128]{4,3,2,1,0:T(8,128)(2,1)S(1)}, u32[]{:S(2)}, u32[]{:S(2)}) collective-permute-start(bf16[12,2,2,32,128]{4,3,2,1,0:T(8,128)(2,1)} %get-tuple-element.31), channel_id=1, source_target_pairs={{0,80},{16,64},{2,82},{18,66},{64,16},{80,0},{66,18},{82,2},{48,96... | collective-permute-start | bytes 1179656 | tf_op jit(solution)/shard_map/ppermute | solution.py:58
  91.6 2.2 %collective-permute-start.6 = (bf16[12,2,2,32,128]{4,3,2,1,0:T(8,128)(2,1)}, bf16[12,2,2,32,128]{4,3,2,1,0:T(8,128)(2,1)S(1)}, u32[]{:S(2)}, u32[]{:S(2)}) collective-permute-start(bf16[12,2,2,32,128]{4,3,2,1,0:T(8,128)(2,1)} %get-tuple-element.32), channel_id=1, source_target_pairs={{0,66},{16,82},{2,64},{18,80},{64,2},{80,18},{66,0},{82,16},{48,11... | collective-permute-start | bytes 1179656 | tf_op jit(solution)/shard_map/ppermute | solution.py:58
  93.8 0.6 collective-permute-start.7
  94.3 7.4 %collective-permute-done.3.refs_1_.refs_9_ = bf16[12,2,2,32,128]{4,3,2,1,0:T(8,128)(2,1)S(1)} collective-permute-done((bf16[12,2,2,32,128]{4,3,2,1,0:T(8,128)(2,1)S(1)}, bf16[12,2,2,32,128]{4,3,2,1,0:T(8,128)(2,1)S(1)}, u32[]{:S(2)}, u32[]{:S(2)}) %collective-permute-start.3) | collective-permute-done | bytes 393248 | tf_op jit(solution)/shard_map/ppermute | solution.py:58
  101.7 0.0 collective-permute-start.8
  101.7 6.2 %collective-permute-done.4.refs_2_.refs_10_ = bf16[12,2,2,32,128]{4,3,2,1,0:T(8,128)(2,1)S(1)} collective-permute-done((bf16[12,2,2,32,128]{4,3,2,1,0:T(8,128)(2,1)S(1)}, bf16[12,2,2,32,128]{4,3,2,1,0:T(8,128)(2,1)S(1)}, u32[]{:S(2)}, u32[]{:S(2)}) %collective-permute-start.4) | collective-permute-done | bytes 393248 | tf_op jit(solution)/shard_map/ppermute | solution.py:58
  107.9 5.4 %collective-permute-start.9 = (bf16[12,2,2,32,128]{4,3,2,1,0:T(8,128)(2,1)}, bf16[12,2,2,32,128]{4,3,2,1,0:T(8,128)(2,1)S(1)}, u32[]{:S(2)}, u32[]{:S(2)}) collective-permute-start(bf16[12,2,2,32,128]{4,3,2,1,0:T(8,128)(2,1)} %get-tuple-element.35), channel_id=1, source_target_pairs={{0,64},{16,80},{2,66},{18,82},{64,0},{80,16},{66,2},{82,18},{48,11... | collective-permute-start | bytes 1179656 | tf_op jit(solution)/shard_map/ppermute | solution.py:58
  113.3 0.0 all-to-all-done.2
  113.3 2.8 %head_far.1.refs_16_ = bf16[8,5,32,128]{3,2,1,0:T(8,128)(2,1)S(1)} custom-call(bf16[8,2,2,32,1280]{4,3,2,1,0:T(8,128)(2,1)} %bitcast.12.got_ref), custom_call_target="tpu_custom_call" | custom-call | flops 10485760 | bytes 3932160 | tf_op jit(solution)/shard_map/head_far/pallas_call | solution.py:523
  116.1 0.0 collective-permute-done.5.refs_3_.refs_11_
  116.1 0.0 collective-permute-done.6.refs_4_.refs_12_
  116.1 0.0 collective-permute-done.7.refs_5_.refs_13_
  116.1 0.0 collective-permute-done.8.refs_6_.refs_14_
  116.1 3.1 %collective-permute-done.9.refs_7_.refs_15_ = bf16[12,2,2,32,128]{4,3,2,1,0:T(8,128)(2,1)S(1)} collective-permute-done((bf16[12,2,2,32,128]{4,3,2,1,0:T(8,128)(2,1)}, bf16[12,2,2,32,128]{4,3,2,1,0:T(8,128)(2,1)S(1)}, u32[]{:S(2)}, u32[]{:S(2)}) %collective-permute-start.9) | collective-permute-done | bytes 393248 | tf_op jit(solution)/shard_map/ppermute | solution.py:58
  119.2 1.6 %conv_far.1 = bf16[8,11,32,128]{3,2,1,0:T(8,128)(2,1)S(1)} custom-call(bf16[12,2,2,32,128]{4,3,2,1,0:T(8,128)(2,1)S(1)} %get-tuple-element.28.refs_0_.refs_8_, bf16[12,2,2,32,128]{4,3,2,1,0:T(8,128)(2,1)S(1)} %collective-permute-done.3.refs_1_.refs_9_, bf16[12,2,2,32,128]{4,3,2,1,0:T(8,128)(2,1)S(1)} %collective-permute-done.4.refs_2_.refs_10_, ...), custom_call_target="tpu_custom_call" | custom-call | flops 12582912 | bytes 4718592 | tf_op jit(solution)/shard_map/conv_far/pallas_call | solution.py:562
  120.8 20.6 %all_to_all.20.got_ref = bf16[8,11,32,128]{3,2,1,0:T(8,128)(2,1)S(1)} all-to-all(bf16[8,11,32,128]{3,2,1,0:T(8,128)(2,1)S(1)} %conv_far.1), channel_id=1, replica_groups={{0,48,6,54,65,113,71,119},{16,32,22,38,81,97,87,103},{2,50,4,52,67,115,..., dimensions={0} | all-to-all | bytes 1441792 | tf_op jit(solution)/shard_map/all_to_all | solution.py:74
  141.4 0.9 finish.1
  (1 shorter events, 0.0 us)
Async XLA Ops:
  3.1 18.6 %all-to-all-start = ((bf16[8,64,512]{2,1,0:T(8,128)(2,1)}), bf16[8,64,512]{2,1,0:T(8,128)(2,1)S(1)}, u32[]{:S(2)}, u32[]{:S(2)}) async-start(bf16[8,64,512]{2,1,0:T(8,128)(2,1)} %bitcast.6), calls=%async_computation | async-start | bytes 1048576 | tf_op jit(solution)/shard_map/all_to_all | solution.py:74
  21.7 17.0 %all-to-all-start.1 = ((bf16[8,64,768]{2,1,0:T(8,128)(2,1)}), bf16[8,64,768]{2,1,0:T(8,128)(2,1)S(1)}, u32[]{:S(2)}, u32[]{:S(2)}) async-start(bf16[8,64,768]{2,1,0:T(8,128)(2,1)} %bitcast.9), calls=%async_computation.1 | async-start | bytes 1572864 | tf_op jit(solution)/shard_map/all_to_all | solution.py:74
  35.0 3.7 %collective-permute-start = (bf16[256,512]{1,0:T(8,128)(2,1)}, bf16[256,512]{1,0:T(8,128)(2,1)S(1)}, u32[]{:S(2)}, u32[]{:S(2)}) collective-permute-start(bf16[256,512]{1,0:T(8,128)(2,1)} %get-tuple-element.20), channel_id=1, source_target_pairs={{0,8},{1,9},{2,10},{3,11},{4,12},{5,13},{6,14},{7,15},{8,0},{9,1},... | collective-permute-start | bytes 786440 | tf_op jit(solution)/shard_map/ppermute | solution.py:604
  38.7 17.7 %slice-start = ((s8[6291456]{0:T(1024)(128)(4,1)}), s8[4194304]{0:T(1024)(128)(4,1)S(1)}, s32[]{:S(2)}) async-start(s8[6291456]{0:T(1024)(128)(4,1)} %bitcast.13), calls=%async_computation.4 | async-start | bytes 8388608
  38.7 17.7 %slice-start.1 = ((s8[6291456]{0:T(1024)(128)(4,1)}), s8[2097152]{0:T(1024)(128)(4,1)S(1)}, s32[]{:S(2)}) async-start(s8[6291456]{0:T(1024)(128)(4,1)} %bitcast.13), calls=%async_computation.5 | async-start | bytes 4194304
  38.7 17.7 %copy-start = (f32[4,512,512]{2,1,0:T(8,128)S(1)}, f32[4,512,512]{2,1,0:T(8,128)}, u32[]{:S(2)}) copy-start(f32[4,512,512]{2,1,0:T(8,128)} %get-tuple-element.23.pre_ref) | copy-start | bytes 12582916
  56.3 10.2 %collective-permute-start.2 = (bf16[512,5120]{1,0:T(8,128)(2,1)S(1)}, bf16[512,5120]{1,0:T(8,128)(2,1)S(1)}, u32[]{:S(2)}, u32[]{:S(2)}) collective-permute-start(bf16[512,5120]{1,0:T(8,128)(2,1)S(1)} %get-tuple-element.27.ga_ref), channel_id=1, source_target_pairs={{0,8},{1,9},{2,10},{3,11},{4,12},{5,13},{6,14},{7,15},{8,0},{9,1},... | collective-permute-start | bytes 15728648 | tf_op jit(solution)/shard_map/ppermute | solution.py:604
  56.4 10.0 %copy-start.2 = (bf16[256,512]{1,0:T(8,128)(2,1)S(1)}, bf16[256,512]{1,0:T(8,128)(2,1)}, u32[]{:S(2)}) copy-start(bf16[256,512]{1,0:T(8,128)(2,1)} %get-tuple-element.26.ha_ref) | copy-start | bytes 786436
  66.0 10.9 %collective-permute-start.1 = (bf16[4,3,256,512]{3,2,1,0:T(8,128)(2,1)}, bf16[4,3,256,512]{3,2,1,0:T(8,128)(2,1)}, u32[]{:S(2)}, u32[]{:S(2)}) collective-permute-start(bf16[4,3,256,512]{3,2,1,0:T(8,128)(2,1)} %get-tuple-element.25.send_ref), channel_id=1, source_target_pairs={{0,8},{1,9},{2,10},{3,11},{4,12},{5,13},{6,14},{7,15},{8,0},{9,1},... | collective-permute-start | bytes 9437192 | tf_op jit(solution)/shard_map/ppermute | solution.py:604
  72.2 4.7 %copy-start.1 = (bf16[4,256,512]{2,1,0:T(8,128)(2,1)S(1)}, bf16[4,256,512]{2,1,0:T(8,128)(2,1)}, u32[]{:S(2)}) copy-start(bf16[4,256,512]{2,1,0:T(8,128)(2,1)} %get-tuple-element.24._.mine_ref) | copy-start | bytes 3145732
  72.2 41.1 %all-to-all-start.2 = ((bf16[8,128,1280]{2,1,0:T(8,128)(2,1)}), bf16[8,128,1280]{2,1,0:T(8,128)(2,1)}, u32[]{:S(2)}, u32[]{:S(2)}) async-start(bf16[8,128,1280]{2,1,0:T(8,128)(2,1)} %bitcast.11), calls=%async_computation.2 | async-start | bytes 5242880 | tf_op jit(solution)/shard_map/all_to_all | solution.py:74
  85.8 15.9 %collective-permute-start.3 = (bf16[12,2,2,32,128]{4,3,2,1,0:T(8,128)(2,1)S(1)}, bf16[12,2,2,32,128]{4,3,2,1,0:T(8,128)(2,1)S(1)}, u32[]{:S(2)}, u32[]{:S(2)}) collective-permute-start(bf16[12,2,2,32,128]{4,3,2,1,0:T(8,128)(2,1)S(1)} %get-tuple-element.29), channel_id=1, source_target_pairs={{0,82},{16,66},{2,80},{18,64},{64,18},{80,2},{66,16},{82,0},{48,98... | collective-permute-start | bytes 1179656 | tf_op jit(solution)/shard_map/ppermute | solution.py:58
  89.4 18.5 %collective-permute-start.4 = (bf16[12,2,2,32,128]{4,3,2,1,0:T(8,128)(2,1)S(1)}, bf16[12,2,2,32,128]{4,3,2,1,0:T(8,128)(2,1)S(1)}, u32[]{:S(2)}, u32[]{:S(2)}) collective-permute-start(bf16[12,2,2,32,128]{4,3,2,1,0:T(8,128)(2,1)S(1)} %get-tuple-element.30), channel_id=1, source_target_pairs={{0,18},{16,2},{2,16},{18,0},{64,82},{80,66},{66,80},{82,64},{48,34... | collective-permute-start | bytes 1179656 | tf_op jit(solution)/shard_map/ppermute | solution.py:58
  90.0 26.1 %collective-permute-start.5 = (bf16[12,2,2,32,128]{4,3,2,1,0:T(8,128)(2,1)}, bf16[12,2,2,32,128]{4,3,2,1,0:T(8,128)(2,1)S(1)}, u32[]{:S(2)}, u32[]{:S(2)}) collective-permute-start(bf16[12,2,2,32,128]{4,3,2,1,0:T(8,128)(2,1)} %get-tuple-element.31), channel_id=1, source_target_pairs={{0,80},{16,64},{2,82},{18,66},{64,16},{80,0},{66,18},{82,2},{48,96... | collective-permute-start | bytes 1179656 | tf_op jit(solution)/shard_map/ppermute | solution.py:58
  91.6 24.5 %collective-permute-start.6 = (bf16[12,2,2,32,128]{4,3,2,1,0:T(8,128)(2,1)}, bf16[12,2,2,32,128]{4,3,2,1,0:T(8,128)(2,1)S(1)}, u32[]{:S(2)}, u32[]{:S(2)}) collective-permute-start(bf16[12,2,2,32,128]{4,3,2,1,0:T(8,128)(2,1)} %get-tuple-element.32), channel_id=1, source_target_pairs={{0,66},{16,82},{2,64},{18,80},{64,2},{80,18},{66,0},{82,16},{48,11... | collective-permute-start | bytes 1179656 | tf_op jit(solution)/shard_map/ppermute | solution.py:58
  93.8 22.3 %collective-permute-start.7 = (bf16[12,2,2,32,128]{4,3,2,1,0:T(8,128)(2,1)}, bf16[12,2,2,32,128]{4,3,2,1,0:T(8,128)(2,1)S(1)}, u32[]{:S(2)}, u32[]{:S(2)}) collective-permute-start(bf16[12,2,2,32,128]{4,3,2,1,0:T(8,128)(2,1)} %get-tuple-element.33), channel_id=1, source_target_pairs={{0,16},{16,0},{2,18},{18,2},{64,80},{80,64},{66,82},{82,66},{48,32... | collective-permute-start | bytes 1179656 | tf_op jit(solution)/shard_map/ppermute | solution.py:58
  101.7 14.4 %collective-permute-start.8 = (bf16[12,2,2,32,128]{4,3,2,1,0:T(8,128)(2,1)}, bf16[12,2,2,32,128]{4,3,2,1,0:T(8,128)(2,1)S(1)}, u32[]{:S(2)}, u32[]{:S(2)}) collective-permute-start(bf16[12,2,2,32,128]{4,3,2,1,0:T(8,128)(2,1)} %get-tuple-element.34), channel_id=1, source_target_pairs={{0,2},{16,18},{2,0},{18,16},{64,66},{80,82},{66,64},{82,80},{48,50... | collective-permute-start | bytes 1179656 | tf_op jit(solution)/shard_map/ppermute | solution.py:58
  107.9 11.3 %collective-permute-start.9 = (bf16[12,2,2,32,128]{4,3,2,1,0:T(8,128)(2,1)}, bf16[12,2,2,32,128]{4,3,2,1,0:T(8,128)(2,1)S(1)}, u32[]{:S(2)}, u32[]{:S(2)}) collective-permute-start(bf16[12,2,2,32,128]{4,3,2,1,0:T(8,128)(2,1)} %get-tuple-element.35), channel_id=1, source_target_pairs={{0,64},{16,80},{2,66},{18,82},{64,0},{80,16},{66,2},{82,18},{48,11... | collective-permute-start | bytes 1179656 | tf_op jit(solution)/shard_map/ppermute | solution.py:58

commit v8 on v6

--- a/solution.py
+++ b/solution.py
@@ -293,7 +293,7 @@
             transcendentals=4 * frames * scores,
         ),
         name="heads",
-    )(sc, hidden, teacher_in, in_hbm(head_weight), in_hbm(teacher_head_weight), after)
+    )(sc, in_hbm(hidden), teacher_in, in_hbm(head_weight), in_hbm(teacher_head_weight), after)
 
 
 def head_grad_kernel(sc_ref, ha_ref, hb_ref, ga_ref, gb_ref, _, out_ref, res_s):

time: 143 us -> 142 us (level)
    unnamed x16 -> x14, local copies, waits for them, and re-layouts: 3.38 us -> 2.18 us
where the time goes in v8:
time: 142 us; the launch traced here: 139 us
  Pallas kernels  58.7 us (41%)
  waiting for transfers between devices  31.6 us (22%)
  starting transfers between devices  24.7 us (17%)
  blocking collectives  20.5 us (14%)
  local copies, waits for them, and re-layouts  2.27 us (2%)
  between operations  1.51 us (1%)
    all_to_all x1, blocking collectives, exchange(): return lax.all_to_all(x, AXES, 0, 0, tiled=True, axis_index_groups=groups)  20.5 us
    ppermute x7, waiting for transfers between devices, near_swap(): return lax.ppermute(x, AXES, pairs)  19 us
    pallas_call x1, Pallas kernels, heads(): pl.pallas_call(functools.partial(head_kernel, 5.0 * loss_scale, tiles), g...  17.6 us
    all_to_all x3, starting transfers between devices, exchange(): return lax.all_to_all(x, AXES, 0, 0, tiled=True, axis_index_groups=groups)  15.3 us
    all_to_all x3, waiting for transfers between devices, exchange(): return lax.all_to_all(x, AXES, 0, 0, tiled=True, axis_index_groups=groups)  12.7 us
    pallas_call x1, Pallas kernels, back(): pl.pallas_call(back_kernel, grid=(LAYERS,), in_specs=[pl.BlockSpec(memory...  9.54 us
    pallas_call x1, Pallas kernels, conv_grad(): pl.pallas_call(conv_grad_kernel, grid=(LAYERS,), in_specs=[pl.BlockSpec(m...  8.87 us
    pallas_call x1, Pallas kernels, convolve(): pl.pallas_call(conv_kernel, grid=(LAYERS,), in_specs=[pl.BlockSpec(memory...  8.86 us
  transfers between devices with their start and end apart: 13, of which 7 were waited for; matrix products, arithmetic and copies ran while one was open for 0% of the time, Pallas kernels for 27%

profile of v8, /device:TPU:0, one launch (start us, length us, event | category | flops | bytes accessed | tf_op | source)
XLA Modules:
  0.0 139.3 jit_solution(5703439457721928946)
XLA Ops:
  0.6 0.0 copy-start.3
  0.6 1.0 copy-done.3
  1.7 1.3 regroup.2
  2.9 7.0 %all-to-all-start = ((bf16[8,64,512]{2,1,0:T(8,128)(2,1)}), bf16[8,64,512]{2,1,0:T(8,128)(2,1)S(1)}, u32[]{:S(2)}, u32[]{:S(2)}) async-start(bf16[8,64,512]{2,1,0:T(8,128)(2,1)} %bitcast.6), calls=%async_computation | async-start | bytes 1048576 | tf_op jit(solution)/shard_map/all_to_all | solution.py:74
  10.0 0.0 copy-start.2
  10.0 1.1 copy-done.2
  11.1 1.5 %regroup.3 = bf16[512,768]{1,0:T(8,128)(2,1)} custom-call(bf16[512,768]{1,0:T(8,128)(2,1)S(1)} %bitcast.15), custom_call_target="tpu_custom_call" | custom-call | tf_op jit(solution)/shard_map/regroup/pallas_call | solution.py:130
  12.6 9.0 %all-to-all-done = bf16[8,64,512]{2,1,0:T(8,128)(2,1)S(1)} async-done(((bf16[8,64,512]{2,1,0:T(8,128)(2,1)}), bf16[8,64,512]{2,1,0:T(8,128)(2,1)S(1)}, u32[]{:S(2)}, u32[]{:S(2)}) %all-to-all-start) | async-done | bytes 524320 | tf_op jit(solution)/shard_map/all_to_all | solution.py:74
  21.5 3.5 %all-to-all-start.1 = ((bf16[8,64,768]{2,1,0:T(8,128)(2,1)}), bf16[8,64,768]{2,1,0:T(8,128)(2,1)S(1)}, u32[]{:S(2)}, u32[]{:S(2)}) async-start(bf16[8,64,768]{2,1,0:T(8,128)(2,1)} %bitcast.9), calls=%async_computation.1 | async-start | bytes 1572864 | tf_op jit(solution)/shard_map/all_to_all | solution.py:74
  25.8 0.1 stack.23.sc_ref
  25.9 8.9 %convolve.1 = (bf16[4,512,512]{2,1,0:T(8,128)(2,1)S(1)}, f32[4,512,512]{2,1,0:T(8,128)}, bf16[512,512]{1,0:T(8,128)(2,1)}, bf16[256,512]{1,0:T(8,128)(2,1)}, bf16[256,512]{1,0:T(8,128)(2,1)}) custom-call(s32[6]{0:T(128)S(1)} %stack.23.sc_ref, bf16[512,512]{1,0:T(8,128)(2,1)S(1)} %bitcast.18, bf16[4,3,512,512]{3,2,1,0:T(8,128)(2,1)} %w_ref.3), custom_call_target="tpu_custom_call" | custom-call | flops 3221225472 | bytes 12582912 | tf_op jit(solution)/shard_map/convolve/pallas_call | solution.py:185
  34.8 0.0 collective-permute-start
  34.8 3.7 %all-to-all-done.1 = bf16[8,64,768]{2,1,0:T(8,128)(2,1)S(1)} async-done(((bf16[8,64,768]{2,1,0:T(8,128)(2,1)}), bf16[8,64,768]{2,1,0:T(8,128)(2,1)S(1)}, u32[]{:S(2)}, u32[]{:S(2)}) %all-to-all-start.1) | async-done | bytes 786464 | tf_op jit(solution)/shard_map/all_to_all | solution.py:74
  38.5 0.0 collective-permute-done._.hb_ref
  38.5 0.0 slice-start
  38.5 0.0 slice-start.1
  38.5 0.0 copy-start
  38.5 17.6 %heads.1 = (bf16[512,5120]{1,0:T(8,128)(2,1)S(1)}, f32[512,512]{1,0:T(8,128)S(1)}) custom-call(s32[6]{0:T(128)S(1)} %stack.23.sc_ref, bf16[512,512]{1,0:T(8,128)(2,1)} %get-tuple-element.19.h_ref, bf16[512,768]{1,0:T(8,128)(2,1)S(1)} %bitcast.16, bf16[512,5120]{1,0:T(8,128)(2,1)} %ws_ref.1, bf16[768,5120]{1,0:T(8,128)(2,1)} %wt_ref.1, ...), custom_call_target="tpu_custom_call" | custom-call | flops 9395240960 | bytes 23592960 | tf_op jit(solution)/shard_map/heads/pallas_call | solution.py:265
  56.1 0.1 collective-permute-start.2
  56.2 0.0 slice-done
  56.2 0.0 slice-done.1
  56.2 0.0 copy-done
  56.3 0.0 copy-start.4
  56.3 9.5 %back.1 = (bf16[4,3,256,512]{3,2,1,0:T(8,128)(2,1)}, bf16[4,256,512]{2,1,0:T(8,128)(2,1)}) custom-call(s32[6]{0:T(128)S(1)} %stack.23.sc_ref, f32[512,512]{1,0:T(8,128)S(1)} %get-tuple-element.21.g4_ref, bf16[4,512,512]{2,1,0:T(8,128)(2,1)S(1)} %get-tuple-element.22.h_ref, f32[4,512,512]{2,1,0:T(8,128)S(1)} %copy-done, bf16[4,3,512,512]{3,2,1,0:T(8,128)(2,1)S(1)} %bitcast.14), custom_call_target="tpu_custom_call" | custom-call | flops 2415919104 | bytes 16777216 | tf_op jit(solution)/shard_map/back/pallas_call | solution.py:390
  65.8 0.5 collective-permute-start.1
  66.3 0.0 collective-permute-done.2.gb_ref
  66.3 0.0 copy-done.4
  66.3 5.7 %head_grad.1._ = bf16[2,2,2,2,2,32,1280]{6,5,4,3,2,1,0:T(8,128)(2,1)} custom-call(s32[6]{0:T(128)S(1)} %stack.23.sc_ref, bf16[256,512]{1,0:T(8,128)(2,1)S(1)} %copy-done.4, bf16[256,512]{1,0:T(8,128)(2,1)S(1)} %collective-permute-done._.hb_ref, bf16[512,5120]{1,0:T(8,128)(2,1)S(1)} %get-tuple-element.27.ga_ref, ...), custom_call_target="tpu_custom_call" | custom-call | flops 2684354560 | bytes 13107200 | tf_op jit(solution)/shard_map/head_grad/pallas_call | solution.py:328
  72.0 0.0 copy-start.1
  72.0 4.7 %all-to-all-start.2 = ((bf16[8,128,1280]{2,1,0:T(8,128)(2,1)}), bf16[8,128,1280]{2,1,0:T(8,128)(2,1)}, u32[]{:S(2)}, u32[]{:S(2)}) async-start(bf16[8,128,1280]{2,1,0:T(8,128)(2,1)} %bitcast.11), calls=%async_computation.2 | async-start | bytes 5242880 | tf_op jit(solution)/shard_map/all_to_all | solution.py:74
  76.8 0.0 collective-permute-done.1.got_ref
  76.8 0.0 copy-done.1
  76.8 8.9 %conv_grad.1 = (bf16[12,2,2,32,128]{4,3,2,1,0:T(8,128)(2,1)S(1)}, bf16[12,2,2,32,128]{4,3,2,1,0:T(8,128)(2,1)S(1)}, bf16[12,2,2,32,128]{4,3,2,1,0:T(8,128)(2,1)S...) custom-call(s32[6]{0:T(128)S(1)} %stack.23.sc_ref, ...), custom_call_target="tpu_custom_call" | custom-call | flops 3221225472 | bytes 10485760 | tf_op jit(solution)/shard_map/conv_grad/pallas_call | solution.py:471
  85.6 1.9 %collective-permute-start.3 = (bf16[12,2,2,32,128]{4,3,2,1,0:T(8,128)(2,1)S(1)}, bf16[12,2,2,32,128]{4,3,2,1,0:T(8,128)(2,1)S(1)}, u32[]{:S(2)}, u32[]{:S(2)}) collective-permute-start(bf16[12,2,2,32,128]{4,3,2,1,0:T(8,128)(2,1)S(1)} %get-tuple-element.29), channel_id=1, source_target_pairs={{0,16},{16,0},{2,18},{18,2},{64,80},{80,64},{66,82},{82,66},{48,32... | collective-permute-start | bytes 1179656 | tf_op jit(solution)/shard_map/ppermute | solution.py:58
  87.6 1.3 collective-permute-start.4
  88.9 0.3 collective-permute-start.5
  89.2 1.7 %collective-permute-start.6 = (bf16[12,2,2,32,128]{4,3,2,1,0:T(8,128)(2,1)}, bf16[12,2,2,32,128]{4,3,2,1,0:T(8,128)(2,1)S(1)}, u32[]{:S(2)}, u32[]{:S(2)}) collective-permute-start(bf16[12,2,2,32,128]{4,3,2,1,0:T(8,128)(2,1)} %get-tuple-element.32), channel_id=1, source_target_pairs={{0,64},{16,80},{2,66},{18,82},{64,0},{80,16},{66,2},{82,18},{48,11... | collective-permute-start | bytes 1179656 | tf_op jit(solution)/shard_map/ppermute | solution.py:58
  90.9 1.6 %collective-permute-start.7 = (bf16[12,2,2,32,128]{4,3,2,1,0:T(8,128)(2,1)}, bf16[12,2,2,32,128]{4,3,2,1,0:T(8,128)(2,1)S(1)}, u32[]{:S(2)}, u32[]{:S(2)}) collective-permute-start(bf16[12,2,2,32,128]{4,3,2,1,0:T(8,128)(2,1)} %get-tuple-element.33), channel_id=1, source_target_pairs={{0,80},{16,64},{2,82},{18,66},{64,16},{80,0},{66,18},{82,2},{48,96... | collective-permute-start | bytes 1179656 | tf_op jit(solution)/shard_map/ppermute | solution.py:58
  92.5 6.9 %collective-permute-done.3.refs_1_.refs_9_ = bf16[12,2,2,32,128]{4,3,2,1,0:T(8,128)(2,1)S(1)} collective-permute-done((bf16[12,2,2,32,128]{4,3,2,1,0:T(8,128)(2,1)S(1)}, bf16[12,2,2,32,128]{4,3,2,1,0:T(8,128)(2,1)S(1)}, u32[]{:S(2)}, u32[]{:S(2)}) %collective-permute-start.3) | collective-permute-done | bytes 393248 | tf_op jit(solution)/shard_map/ppermute | solution.py:58
  99.4 1.5 %collective-permute-start.8 = (bf16[12,2,2,32,128]{4,3,2,1,0:T(8,128)(2,1)}, bf16[12,2,2,32,128]{4,3,2,1,0:T(8,128)(2,1)S(1)}, u32[]{:S(2)}, u32[]{:S(2)}) collective-permute-start(bf16[12,2,2,32,128]{4,3,2,1,0:T(8,128)(2,1)} %get-tuple-element.34), channel_id=1, source_target_pairs={{0,66},{16,82},{2,64},{18,80},{64,2},{80,18},{66,0},{82,16},{48,11... | collective-permute-start | bytes 1179656 | tf_op jit(solution)/shard_map/ppermute | solution.py:58
  100.9 0.0 collective-permute-done.4.refs_2_.refs_10_
  100.9 0.5 collective-permute-start.9
  101.4 0.0 all-to-all-done.2
  101.4 2.8 %head_far.1.refs_16_ = bf16[8,5,32,128]{3,2,1,0:T(8,128)(2,1)S(1)} custom-call(bf16[8,2,2,32,1280]{4,3,2,1,0:T(8,128)(2,1)} %bitcast.12.got_ref), custom_call_target="tpu_custom_call" | custom-call | flops 10485760 | bytes 3932160 | tf_op jit(solution)/shard_map/head_far/pallas_call | solution.py:515
  104.2 3.6 %collective-permute-done.5.refs_3_.refs_11_ = bf16[12,2,2,32,128]{4,3,2,1,0:T(8,128)(2,1)S(1)} collective-permute-done((bf16[12,2,2,32,128]{4,3,2,1,0:T(8,128)(2,1)}, bf16[12,2,2,32,128]{4,3,2,1,0:T(8,128)(2,1)S(1)}, u32[]{:S(2)}, u32[]{:S(2)}) %collective-permute-start.5) | collective-permute-done | bytes 393248 | tf_op jit(solution)/shard_map/ppermute | solution.py:58
  107.8 0.0 collective-permute-done.6.refs_4_.refs_12_
  107.8 0.1 collective-permute-done.7.refs_5_.refs_13_
  107.9 4.1 %collective-permute-done.8.refs_6_.refs_14_ = bf16[12,2,2,32,128]{4,3,2,1,0:T(8,128)(2,1)S(1)} collective-permute-done((bf16[12,2,2,32,128]{4,3,2,1,0:T(8,128)(2,1)}, bf16[12,2,2,32,128]{4,3,2,1,0:T(8,128)(2,1)S(1)}, u32[]{:S(2)}, u32[]{:S(2)}) %collective-permute-start.8) | collective-permute-done | bytes 393248 | tf_op jit(solution)/shard_map/ppermute | solution.py:58
  112.0 4.3 %collective-permute-done.9.refs_7_.refs_15_ = bf16[12,2,2,32,128]{4,3,2,1,0:T(8,128)(2,1)S(1)} collective-permute-done((bf16[12,2,2,32,128]{4,3,2,1,0:T(8,128)(2,1)}, bf16[12,2,2,32,128]{4,3,2,1,0:T(8,128)(2,1)S(1)}, u32[]{:S(2)}, u32[]{:S(2)}) %collective-permute-start.9) | collective-permute-done | bytes 393248 | tf_op jit(solution)/shard_map/ppermute | solution.py:58
  116.3 1.6 %conv_far.1 = bf16[8,11,32,128]{3,2,1,0:T(8,128)(2,1)S(1)} custom-call(bf16[12,2,2,32,128]{4,3,2,1,0:T(8,128)(2,1)S(1)} %get-tuple-element.28.refs_0_.refs_8_, bf16[12,2,2,32,128]{4,3,2,1,0:T(8,128)(2,1)S(1)} %collective-permute-done.3.refs_1_.refs_9_, bf16[12,2,2,32,128]{4,3,2,1,0:T(8,128)(2,1)S(1)} %collective-permute-done.4.refs_2_.refs_10_, ...), custom_call_target="tpu_custom_call" | custom-call | flops 12582912 | bytes 4718592 | tf_op jit(solution)/shard_map/conv_far/pallas_call | solution.py:554
  117.9 20.5 %all_to_all.20.got_ref = bf16[8,11,32,128]{3,2,1,0:T(8,128)(2,1)S(1)} all-to-all(bf16[8,11,32,128]{3,2,1,0:T(8,128)(2,1)S(1)} %conv_far.1), channel_id=1, replica_groups={{0,48,6,54,65,113,71,119},{16,32,22,38,81,97,87,103},{2,50,4,52,67,115,..., dimensions={0} | all-to-all | bytes 1441792 | tf_op jit(solution)/shard_map/all_to_all | solution.py:74
  138.4 0.9 finish.1
  (1 shorter events, 0.0 us)
Async XLA Ops:
  0.6 1.0 copy-start.3
  2.9 18.6 %all-to-all-start = ((bf16[8,64,512]{2,1,0:T(8,128)(2,1)}), bf16[8,64,512]{2,1,0:T(8,128)(2,1)S(1)}, u32[]{:S(2)}, u32[]{:S(2)}) async-start(bf16[8,64,512]{2,1,0:T(8,128)(2,1)} %bitcast.6), calls=%async_computation | async-start | bytes 1048576 | tf_op jit(solution)/shard_map/all_to_all | solution.py:74
  10.0 1.1 copy-start.2
  21.5 17.0 %all-to-all-start.1 = ((bf16[8,64,768]{2,1,0:T(8,128)(2,1)}), bf16[8,64,768]{2,1,0:T(8,128)(2,1)S(1)}, u32[]{:S(2)}, u32[]{:S(2)}) async-start(bf16[8,64,768]{2,1,0:T(8,128)(2,1)} %bitcast.9), calls=%async_computation.1 | async-start | bytes 1572864 | tf_op jit(solution)/shard_map/all_to_all | solution.py:74
  34.8 3.7 %collective-permute-start = (bf16[256,512]{1,0:T(8,128)(2,1)}, bf16[256,512]{1,0:T(8,128)(2,1)S(1)}, u32[]{:S(2)}, u32[]{:S(2)}) collective-permute-start(bf16[256,512]{1,0:T(8,128)(2,1)} %get-tuple-element.20), channel_id=1, source_target_pairs={{0,8},{1,9},{2,10},{3,11},{4,12},{5,13},{6,14},{7,15},{8,0},{9,1},... | collective-permute-start | bytes 786440 | tf_op jit(solution)/shard_map/ppermute | solution.py:596
  38.5 17.7 %slice-start = ((s8[6291456]{0:T(1024)(128)(4,1)}), s8[4194304]{0:T(1024)(128)(4,1)S(1)}, s32[]{:S(2)}) async-start(s8[6291456]{0:T(1024)(128)(4,1)} %bitcast.13), calls=%async_computation.4 | async-start | bytes 8388608
  38.5 17.7 %slice-start.1 = ((s8[6291456]{0:T(1024)(128)(4,1)}), s8[2097152]{0:T(1024)(128)(4,1)S(1)}, s32[]{:S(2)}) async-start(s8[6291456]{0:T(1024)(128)(4,1)} %bitcast.13), calls=%async_computation.5 | async-start | bytes 4194304
  38.5 17.7 %copy-start = (f32[4,512,512]{2,1,0:T(8,128)S(1)}, f32[4,512,512]{2,1,0:T(8,128)}, u32[]{:S(2)}) copy-start(f32[4,512,512]{2,1,0:T(8,128)} %get-tuple-element.23.pre_ref) | copy-start | bytes 12582916
  56.1 10.2 %collective-permute-start.2 = (bf16[512,5120]{1,0:T(8,128)(2,1)S(1)}, bf16[512,5120]{1,0:T(8,128)(2,1)S(1)}, u32[]{:S(2)}, u32[]{:S(2)}) collective-permute-start(bf16[512,5120]{1,0:T(8,128)(2,1)S(1)} %get-tuple-element.27.ga_ref), channel_id=1, source_target_pairs={{0,8},{1,9},{2,10},{3,11},{4,12},{5,13},{6,14},{7,15},{8,0},{9,1},... | collective-permute-start | bytes 15728648 | tf_op jit(solution)/shard_map/ppermute | solution.py:596
  56.3 10.0 %copy-start.4 = (bf16[256,512]{1,0:T(8,128)(2,1)S(1)}, bf16[256,512]{1,0:T(8,128)(2,1)}, u32[]{:S(2)}) copy-start(bf16[256,512]{1,0:T(8,128)(2,1)} %get-tuple-element.26.ha_ref) | copy-start | bytes 786436
  65.8 10.9 %collective-permute-start.1 = (bf16[4,3,256,512]{3,2,1,0:T(8,128)(2,1)}, bf16[4,3,256,512]{3,2,1,0:T(8,128)(2,1)}, u32[]{:S(2)}, u32[]{:S(2)}) collective-permute-start(bf16[4,3,256,512]{3,2,1,0:T(8,128)(2,1)} %get-tuple-element.25.send_ref), channel_id=1, source_target_pairs={{0,8},{1,9},{2,10},{3,11},{4,12},{5,13},{6,14},{7,15},{8,0},{9,1},... | collective-permute-start | bytes 9437192 | tf_op jit(solution)/shard_map/ppermute | solution.py:596
  72.0 4.8 %copy-start.1 = (bf16[4,256,512]{2,1,0:T(8,128)(2,1)S(1)}, bf16[4,256,512]{2,1,0:T(8,128)(2,1)}, u32[]{:S(2)}) copy-start(bf16[4,256,512]{2,1,0:T(8,128)(2,1)} %get-tuple-element.24._.mine_ref) | copy-start | bytes 3145732
  72.0 29.4 %all-to-all-start.2 = ((bf16[8,128,1280]{2,1,0:T(8,128)(2,1)}), bf16[8,128,1280]{2,1,0:T(8,128)(2,1)}, u32[]{:S(2)}, u32[]{:S(2)}) async-start(bf16[8,128,1280]{2,1,0:T(8,128)(2,1)} %bitcast.11), calls=%async_computation.2 | async-start | bytes 5242880 | tf_op jit(solution)/shard_map/all_to_all | solution.py:74
  85.6 13.8 %collective-permute-start.3 = (bf16[12,2,2,32,128]{4,3,2,1,0:T(8,128)(2,1)S(1)}, bf16[12,2,2,32,128]{4,3,2,1,0:T(8,128)(2,1)S(1)}, u32[]{:S(2)}, u32[]{:S(2)}) collective-permute-start(bf16[12,2,2,32,128]{4,3,2,1,0:T(8,128)(2,1)S(1)} %get-tuple-element.29), channel_id=1, source_target_pairs={{0,16},{16,0},{2,18},{18,2},{64,80},{80,64},{66,82},{82,66},{48,32... | collective-permute-start | bytes 1179656 | tf_op jit(solution)/shard_map/ppermute | solution.py:58
  87.6 13.3 %collective-permute-start.4 = (bf16[12,2,2,32,128]{4,3,2,1,0:T(8,128)(2,1)S(1)}, bf16[12,2,2,32,128]{4,3,2,1,0:T(8,128)(2,1)S(1)}, u32[]{:S(2)}, u32[]{:S(2)}) collective-permute-start(bf16[12,2,2,32,128]{4,3,2,1,0:T(8,128)(2,1)S(1)} %get-tuple-element.30), channel_id=1, source_target_pairs={{0,2},{16,18},{2,0},{18,16},{64,66},{80,82},{66,64},{82,80},{48,50... | collective-permute-start | bytes 1179656 | tf_op jit(solution)/shard_map/ppermute | solution.py:58
  88.9 18.9 %collective-permute-start.5 = (bf16[12,2,2,32,128]{4,3,2,1,0:T(8,128)(2,1)}, bf16[12,2,2,32,128]{4,3,2,1,0:T(8,128)(2,1)S(1)}, u32[]{:S(2)}, u32[]{:S(2)}) collective-permute-start(bf16[12,2,2,32,128]{4,3,2,1,0:T(8,128)(2,1)} %get-tuple-element.31), channel_id=1, source_target_pairs={{0,18},{16,2},{2,16},{18,0},{64,82},{80,66},{66,80},{82,64},{48,34... | collective-permute-start | bytes 1179656 | tf_op jit(solution)/shard_map/ppermute | solution.py:58
  89.2 18.6 %collective-permute-start.6 = (bf16[12,2,2,32,128]{4,3,2,1,0:T(8,128)(2,1)}, bf16[12,2,2,32,128]{4,3,2,1,0:T(8,128)(2,1)S(1)}, u32[]{:S(2)}, u32[]{:S(2)}) collective-permute-start(bf16[12,2,2,32,128]{4,3,2,1,0:T(8,128)(2,1)} %get-tuple-element.32), channel_id=1, source_target_pairs={{0,64},{16,80},{2,66},{18,82},{64,0},{80,16},{66,2},{82,18},{48,11... | collective-permute-start | bytes 1179656 | tf_op jit(solution)/shard_map/ppermute | solution.py:58
  90.9 17.0 %collective-permute-start.7 = (bf16[12,2,2,32,128]{4,3,2,1,0:T(8,128)(2,1)}, bf16[12,2,2,32,128]{4,3,2,1,0:T(8,128)(2,1)S(1)}, u32[]{:S(2)}, u32[]{:S(2)}) collective-permute-start(bf16[12,2,2,32,128]{4,3,2,1,0:T(8,128)(2,1)} %get-tuple-element.33), channel_id=1, source_target_pairs={{0,80},{16,64},{2,82},{18,66},{64,16},{80,0},{66,18},{82,2},{48,96... | collective-permute-start | bytes 1179656 | tf_op jit(solution)/shard_map/ppermute | solution.py:58
  99.4 12.6 %collective-permute-start.8 = (bf16[12,2,2,32,128]{4,3,2,1,0:T(8,128)(2,1)}, bf16[12,2,2,32,128]{4,3,2,1,0:T(8,128)(2,1)S(1)}, u32[]{:S(2)}, u32[]{:S(2)}) collective-permute-start(bf16[12,2,2,32,128]{4,3,2,1,0:T(8,128)(2,1)} %get-tuple-element.34), channel_id=1, source_target_pairs={{0,66},{16,82},{2,64},{18,80},{64,2},{80,18},{66,0},{82,16},{48,11... | collective-permute-start | bytes 1179656 | tf_op jit(solution)/shard_map/ppermute | solution.py:58
  100.9 15.4 %collective-permute-start.9 = (bf16[12,2,2,32,128]{4,3,2,1,0:T(8,128)(2,1)}, bf16[12,2,2,32,128]{4,3,2,1,0:T(8,128)(2,1)S(1)}, u32[]{:S(2)}, u32[]{:S(2)}) collective-permute-start(bf16[12,2,2,32,128]{4,3,2,1,0:T(8,128)(2,1)} %get-tuple-element.35), channel_id=1, source_target_pairs={{0,82},{16,66},{2,80},{18,64},{64,18},{80,2},{66,16},{82,0},{48,98... | collective-permute-start | bytes 1179656 | tf_op jit(solution)/shard_map/ppermute | solution.py:58

commit v9 on v8

--- a/solution.py
+++ b/solution.py
@@ -421,9 +421,9 @@
 
 
 def conv_grad_kernel(sc_ref, mine_ref, send_ref, got_ref, _, *refs):
-    outs, (pad_s, tap_s, res_s) = refs[:8], refs[8:]
+    outs, (pad_s, tap_s, left_s), results = refs[:8], refs[8:11], refs[11:]
     step = pl.program_id(0)
-    rows, frames = mine_ref.shape[1:]
+    frames = mine_ref.shape[2]
     width = send_ref.shape[3]
 
     @pl.when(step == 0)
@@ -432,30 +432,33 @@
 
     for side, ref in enumerate((send_ref, got_ref)):
         g_pre = ref[0, :2].reshape(frames, width)
-        tap_s[1, side] = g_pre
-        pad_s[side, PAD : PAD + frames] = g_pre.astype(F32)
+        tap_s[1, side * frames : (side + 1) * frames] = g_pre
+        pad_s[side, PAD : PAD + frames] = g_pre
     for at in range(LAYERS):
 
         @pl.when(step == at)
         def _():
             reach = CLASSES * 2**at
             for side in range(2):
-                tap_s[0, side] = pad_s[side, PAD + reach : PAD + reach + frames].astype(BF16)
-                tap_s[2, side] = pad_s[side, PAD - reach : PAD - reach + frames].astype(BF16)
+                rows = slice(side * frames, (side + 1) * frames)
+                tap_s[0, rows] = pad_s[side, PAD + reach : PAD + reach + frames]
+                tap_s[2, rows] = pad_s[side, PAD - reach : PAD - reach + frames]
 
     core, mx, my, mz = (sc_ref[i] for i in range(2, 6))
     side = lax.broadcasted_iota(jnp.int32, (32, 128), 1) // 64
     straight, crossed = side == mx, side != mx
-    for tap in range(TAPS):
-        res_s[tap] = dot(mine_ref[0], tap_s[tap, 0]) + dot(got_ref[0, 2], tap_s[tap, 1])
+    left_s[:, :frames] = mine_ref[0]
+    left_s[:, frames:] = got_ref[0, 2]
+    for tap, res_s in enumerate(results):
+        res_s[...] = dot(left_s[...], tap_s[tap])
         for dy, dz, fz in BITS:
             for fy in range(2):
                 ny, nz = my ^ dy, mz ^ dz
                 high = jnp.where(core == 0, fy, ny)
                 cols = pl.ds(pl.multiple_of((high * 2 + (ny ^ fy)) * 128, 128), 128)
                 row = pl.multiple_of((nz * 2 + fz) * 64, 64)
-                a = res_s[tap, pl.ds(row, 32), cols]
-                b = pltpu.roll(res_s[tap, pl.ds(row + 32, 32), cols], 64 * core, 1)
+                a = res_s[pl.ds(row, 32), cols]
+                b = pltpu.roll(res_s[pl.ds(row + 32, 32), cols], 64 * core, 1)
                 outs[dy * 2 + dz][tap, fz, fy] = encode(jnp.where(straight, a, b))
                 outs[4 + dy * 2 + dz][tap, fz, fy] = encode(jnp.where(crossed, a, b))
 
@@ -481,10 +484,11 @@
         out_specs=[out] * 8,
         out_shape=[jax.ShapeDtypeStruct((LAYERS * TAPS, 2, 2, 32, width // 4), BF16)] * 8,
         scratch_shapes=[
-            pltpu.VMEM((2, frames + 2 * PAD, width), F32),
-            pltpu.VMEM((TAPS, 2, frames, width), BF16),
-            pltpu.VMEM((TAPS, rows, width), F32),
-        ],
+            pltpu.VMEM((2, frames + 2 * PAD, width), BF16),
+            pltpu.VMEM((TAPS, 2 * frames, width), BF16),
+            pltpu.VMEM((rows, 2 * frames), BF16),
+        ]
+        + [pltpu.VMEM((rows, width), F32)] * TAPS,
         compiler_params=params(18, "arbitrary"),
         cost_estimate=pl.CostEstimate(
             flops=4 * LAYERS * TAPS * rows * frames * width,

time: 142 us -> 142 us (level)
  transfers between devices with their start and end apart: 13 -> 13, of which waited for: 7 -> 7; matrix products, arithmetic and copies ran while one was open for 0% -> 0% of each run, Pallas kernels for 27% -> 26%
where the time goes in v9:
time: 142 us; the launch traced here: 139 us
  Pallas kernels  58 us (41%)
  waiting for transfers between devices  31.7 us (22%)
  starting transfers between devices  25.3 us (18%)
  blocking collectives  20.5 us (14%)
  local copies, waits for them, and re-layouts  2.27 us (2%)
  between operations  1.51 us (1%)
    all_to_all x1, blocking collectives, exchange(): return lax.all_to_all(x, AXES, 0, 0, tiled=True, axis_index_groups=groups)  20.5 us
    ppermute x7, waiting for transfers between devices, near_swap(): return lax.ppermute(x, AXES, pairs)  19 us
    pallas_call x1, Pallas kernels, heads(): pl.pallas_call(functools.partial(head_kernel, 5.0 * loss_scale, tiles), g...  17.6 us
    all_to_all x3, starting transfers between devices, exchange(): return lax.all_to_all(x, AXES, 0, 0, tiled=True, axis_index_groups=groups)  15.3 us
    all_to_all x3, waiting for transfers between devices, exchange(): return lax.all_to_all(x, AXES, 0, 0, tiled=True, axis_index_groups=groups)  12.7 us
    pallas_call x1, Pallas kernels, back(): pl.pallas_call(back_kernel, grid=(LAYERS,), in_specs=[pl.BlockSpec(memory...  9.54 us
    ppermute x7, starting transfers between devices, near_swap(): return lax.ppermute(x, AXES, pairs)  9.48 us
    pallas_call x1, Pallas kernels, convolve(): pl.pallas_call(conv_kernel, grid=(LAYERS,), in_specs=[pl.BlockSpec(memory...  8.86 us
  transfers between devices with their start and end apart: 13, of which 7 were waited for; matrix products, arithmetic and copies ran while one was open for 0% of the time, Pallas kernels for 26%

profile of v9, /device:TPU:0, one launch (start us, length us, event | category | flops | bytes accessed | tf_op | source)
XLA Modules:
  0.0 139.3 jit_solution(8768286392521675574)
XLA Ops:
  0.6 0.0 copy-start.3
  0.6 1.0 copy-done.3
  1.7 1.3 regroup.2
  2.9 7.0 %all-to-all-start = ((bf16[8,64,512]{2,1,0:T(8,128)(2,1)}), bf16[8,64,512]{2,1,0:T(8,128)(2,1)S(1)}, u32[]{:S(2)}, u32[]{:S(2)}) async-start(bf16[8,64,512]{2,1,0:T(8,128)(2,1)} %bitcast.6), calls=%async_computation | async-start | bytes 1048576 | tf_op jit(solution)/shard_map/all_to_all | solution.py:74
  10.0 0.0 copy-start.2
  10.0 1.1 copy-done.2
  11.1 1.5 %regroup.3 = bf16[512,768]{1,0:T(8,128)(2,1)} custom-call(bf16[512,768]{1,0:T(8,128)(2,1)S(1)} %bitcast.15), custom_call_target="tpu_custom_call" | custom-call | tf_op jit(solution)/shard_map/regroup/pallas_call | solution.py:130
  12.6 9.0 %all-to-all-done = bf16[8,64,512]{2,1,0:T(8,128)(2,1)S(1)} async-done(((bf16[8,64,512]{2,1,0:T(8,128)(2,1)}), bf16[8,64,512]{2,1,0:T(8,128)(2,1)S(1)}, u32[]{:S(2)}, u32[]{:S(2)}) %all-to-all-start) | async-done | bytes 524320 | tf_op jit(solution)/shard_map/all_to_all | solution.py:74
  21.5 3.5 %all-to-all-start.1 = ((bf16[8,64,768]{2,1,0:T(8,128)(2,1)}), bf16[8,64,768]{2,1,0:T(8,128)(2,1)S(1)}, u32[]{:S(2)}, u32[]{:S(2)}) async-start(bf16[8,64,768]{2,1,0:T(8,128)(2,1)} %bitcast.9), calls=%async_computation.1 | async-start | bytes 1572864 | tf_op jit(solution)/shard_map/all_to_all | solution.py:74
  25.8 0.1 stack.23.sc_ref
  25.9 8.9 %convolve.1 = (bf16[4,512,512]{2,1,0:T(8,128)(2,1)S(1)}, f32[4,512,512]{2,1,0:T(8,128)}, bf16[512,512]{1,0:T(8,128)(2,1)}, bf16[256,512]{1,0:T(8,128)(2,1)}, bf16[256,512]{1,0:T(8,128)(2,1)}) custom-call(s32[6]{0:T(128)S(1)} %stack.23.sc_ref, bf16[512,512]{1,0:T(8,128)(2,1)S(1)} %bitcast.18, bf16[4,3,512,512]{3,2,1,0:T(8,128)(2,1)} %w_ref.3), custom_call_target="tpu_custom_call" | custom-call | flops 3221225472 | bytes 12582912 | tf_op jit(solution)/shard_map/convolve/pallas_call | solution.py:185
  34.8 0.0 collective-permute-start
  34.8 3.7 %all-to-all-done.1 = bf16[8,64,768]{2,1,0:T(8,128)(2,1)S(1)} async-done(((bf16[8,64,768]{2,1,0:T(8,128)(2,1)}), bf16[8,64,768]{2,1,0:T(8,128)(2,1)S(1)}, u32[]{:S(2)}, u32[]{:S(2)}) %all-to-all-start.1) | async-done | bytes 786464 | tf_op jit(solution)/shard_map/all_to_all | solution.py:74
  38.5 0.0 collective-permute-done._.hb_ref
  38.5 0.0 slice-start
  38.5 0.0 slice-start.1
  38.5 0.0 copy-start
  38.5 17.6 %heads.1 = (bf16[512,5120]{1,0:T(8,128)(2,1)S(1)}, f32[512,512]{1,0:T(8,128)S(1)}) custom-call(s32[6]{0:T(128)S(1)} %stack.23.sc_ref, bf16[512,512]{1,0:T(8,128)(2,1)} %get-tuple-element.19.h_ref, bf16[512,768]{1,0:T(8,128)(2,1)S(1)} %bitcast.16, bf16[512,5120]{1,0:T(8,128)(2,1)} %ws_ref.1, bf16[768,5120]{1,0:T(8,128)(2,1)} %wt_ref.1, ...), custom_call_target="tpu_custom_call" | custom-call | flops 9395240960 | bytes 23592960 | tf_op jit(solution)/shard_map/heads/pallas_call | solution.py:265
  56.1 0.1 collective-permute-start.2
  56.2 0.0 slice-done
  56.2 0.0 slice-done.1
  56.2 0.0 copy-done
  56.3 0.0 copy-start.4
  56.3 9.5 %back.1 = (bf16[4,3,256,512]{3,2,1,0:T(8,128)(2,1)}, bf16[4,256,512]{2,1,0:T(8,128)(2,1)}) custom-call(s32[6]{0:T(128)S(1)} %stack.23.sc_ref, f32[512,512]{1,0:T(8,128)S(1)} %get-tuple-element.21.g4_ref, bf16[4,512,512]{2,1,0:T(8,128)(2,1)S(1)} %get-tuple-element.22.h_ref, f32[4,512,512]{2,1,0:T(8,128)S(1)} %copy-done, bf16[4,3,512,512]{3,2,1,0:T(8,128)(2,1)S(1)} %bitcast.14), custom_call_target="tpu_custom_call" | custom-call | flops 2415919104 | bytes 16777216 | tf_op jit(solution)/shard_map/back/pallas_call | solution.py:390
  65.8 0.5 collective-permute-start.1
  66.3 0.0 collective-permute-done.2.gb_ref
  66.3 0.0 copy-done.4
  66.3 5.7 %head_grad.1._ = bf16[2,2,2,2,2,32,1280]{6,5,4,3,2,1,0:T(8,128)(2,1)} custom-call(s32[6]{0:T(128)S(1)} %stack.23.sc_ref, bf16[256,512]{1,0:T(8,128)(2,1)S(1)} %copy-done.4, bf16[256,512]{1,0:T(8,128)(2,1)S(1)} %collective-permute-done._.hb_ref, bf16[512,5120]{1,0:T(8,128)(2,1)S(1)} %get-tuple-element.27.ga_ref, ...), custom_call_target="tpu_custom_call" | custom-call | flops 2684354560 | bytes 13107200 | tf_op jit(solution)/shard_map/head_grad/pallas_call | solution.py:328
  72.0 0.0 copy-start.1
  72.0 4.7 %all-to-all-start.2 = ((bf16[8,128,1280]{2,1,0:T(8,128)(2,1)}), bf16[8,128,1280]{2,1,0:T(8,128)(2,1)}, u32[]{:S(2)}, u32[]{:S(2)}) async-start(bf16[8,128,1280]{2,1,0:T(8,128)(2,1)} %bitcast.11), calls=%async_computation.2 | async-start | bytes 5242880 | tf_op jit(solution)/shard_map/all_to_all | solution.py:74
  76.8 0.0 collective-permute-done.1.got_ref
  76.8 0.0 copy-done.1
  76.8 8.2 %conv_grad.1 = (bf16[12,2,2,32,128]{4,3,2,1,0:T(8,128)(2,1)S(1)}, bf16[12,2,2,32,128]{4,3,2,1,0:T(8,128)(2,1)S(1)}, bf16[12,2,2,32,128]{4,3,2,1,0:T(8,128)(2,1)S...) custom-call(s32[6]{0:T(128)S(1)} %stack.23.sc_ref, ...), custom_call_target="tpu_custom_call" | custom-call | flops 3221225472 | bytes 10485760 | tf_op jit(solution)/shard_map/conv_grad/pallas_call | solution.py:474
  85.0 1.9 %collective-permute-start.3 = (bf16[12,2,2,32,128]{4,3,2,1,0:T(8,128)(2,1)S(1)}, bf16[12,2,2,32,128]{4,3,2,1,0:T(8,128)(2,1)S(1)}, u32[]{:S(2)}, u32[]{:S(2)}) collective-permute-start(bf16[12,2,2,32,128]{4,3,2,1,0:T(8,128)(2,1)S(1)} %get-tuple-element.29), channel_id=1, source_target_pairs={{0,16},{16,0},{2,18},{18,2},{64,80},{80,64},{66,82},{82,66},{48,32... | collective-permute-start | bytes 1179656 | tf_op jit(solution)/shard_map/ppermute | solution.py:58
  86.9 1.3 collective-permute-start.4
  88.2 0.3 collective-permute-start.5
  88.5 1.7 %collective-permute-start.6 = (bf16[12,2,2,32,128]{4,3,2,1,0:T(8,128)(2,1)}, bf16[12,2,2,32,128]{4,3,2,1,0:T(8,128)(2,1)S(1)}, u32[]{:S(2)}, u32[]{:S(2)}) collective-permute-start(bf16[12,2,2,32,128]{4,3,2,1,0:T(8,128)(2,1)} %get-tuple-element.32), channel_id=1, source_target_pairs={{0,64},{16,80},{2,66},{18,82},{64,0},{80,16},{66,2},{82,18},{48,11... | collective-permute-start | bytes 1179656 | tf_op jit(solution)/shard_map/ppermute | solution.py:58
  90.2 1.6 %collective-permute-start.7 = (bf16[12,2,2,32,128]{4,3,2,1,0:T(8,128)(2,1)}, bf16[12,2,2,32,128]{4,3,2,1,0:T(8,128)(2,1)S(1)}, u32[]{:S(2)}, u32[]{:S(2)}) collective-permute-start(bf16[12,2,2,32,128]{4,3,2,1,0:T(8,128)(2,1)} %get-tuple-element.33), channel_id=1, source_target_pairs={{0,80},{16,64},{2,82},{18,66},{64,16},{80,0},{66,18},{82,2},{48,96... | collective-permute-start | bytes 1179656 | tf_op jit(solution)/shard_map/ppermute | solution.py:58
  91.9 6.9 %collective-permute-done.3.refs_1_.refs_9_ = bf16[12,2,2,32,128]{4,3,2,1,0:T(8,128)(2,1)S(1)} collective-permute-done((bf16[12,2,2,32,128]{4,3,2,1,0:T(8,128)(2,1)S(1)}, bf16[12,2,2,32,128]{4,3,2,1,0:T(8,128)(2,1)S(1)}, u32[]{:S(2)}, u32[]{:S(2)}) %collective-permute-start.3) | collective-permute-done | bytes 393248 | tf_op jit(solution)/shard_map/ppermute | solution.py:58
  98.8 2.1 %collective-permute-start.8 = (bf16[12,2,2,32,128]{4,3,2,1,0:T(8,128)(2,1)}, bf16[12,2,2,32,128]{4,3,2,1,0:T(8,128)(2,1)S(1)}, u32[]{:S(2)}, u32[]{:S(2)}) collective-permute-start(bf16[12,2,2,32,128]{4,3,2,1,0:T(8,128)(2,1)} %get-tuple-element.34), channel_id=1, source_target_pairs={{0,66},{16,82},{2,64},{18,80},{64,2},{80,18},{66,0},{82,16},{48,11... | collective-permute-start | bytes 1179656 | tf_op jit(solution)/shard_map/ppermute | solution.py:58
  100.9 0.0 collective-permute-done.4.refs_2_.refs_10_
  100.9 0.5 collective-permute-start.9
  101.4 0.0 all-to-all-done.2
  101.4 2.8 %head_far.1.refs_16_ = bf16[8,5,32,128]{3,2,1,0:T(8,128)(2,1)S(1)} custom-call(bf16[8,2,2,32,1280]{4,3,2,1,0:T(8,128)(2,1)} %bitcast.12.got_ref), custom_call_target="tpu_custom_call" | custom-call | flops 10485760 | bytes 3932160 | tf_op jit(solution)/shard_map/head_far/pallas_call | solution.py:519
  104.2 3.6 %collective-permute-done.5.refs_3_.refs_11_ = bf16[12,2,2,32,128]{4,3,2,1,0:T(8,128)(2,1)S(1)} collective-permute-done((bf16[12,2,2,32,128]{4,3,2,1,0:T(8,128)(2,1)}, bf16[12,2,2,32,128]{4,3,2,1,0:T(8,128)(2,1)S(1)}, u32[]{:S(2)}, u32[]{:S(2)}) %collective-permute-start.5) | collective-permute-done | bytes 393248 | tf_op jit(solution)/shard_map/ppermute | solution.py:58
  107.8 0.0 collective-permute-done.6.refs_4_.refs_12_
  107.8 0.1 collective-permute-done.7.refs_5_.refs_13_
  107.9 4.2 %collective-permute-done.8.refs_6_.refs_14_ = bf16[12,2,2,32,128]{4,3,2,1,0:T(8,128)(2,1)S(1)} collective-permute-done((bf16[12,2,2,32,128]{4,3,2,1,0:T(8,128)(2,1)}, bf16[12,2,2,32,128]{4,3,2,1,0:T(8,128)(2,1)S(1)}, u32[]{:S(2)}, u32[]{:S(2)}) %collective-permute-start.8) | collective-permute-done | bytes 393248 | tf_op jit(solution)/shard_map/ppermute | solution.py:58
  112.0 4.2 %collective-permute-done.9.refs_7_.refs_15_ = bf16[12,2,2,32,128]{4,3,2,1,0:T(8,128)(2,1)S(1)} collective-permute-done((bf16[12,2,2,32,128]{4,3,2,1,0:T(8,128)(2,1)}, bf16[12,2,2,32,128]{4,3,2,1,0:T(8,128)(2,1)S(1)}, u32[]{:S(2)}, u32[]{:S(2)}) %collective-permute-start.9) | collective-permute-done | bytes 393248 | tf_op jit(solution)/shard_map/ppermute | solution.py:58
  116.3 1.6 %conv_far.1 = bf16[8,11,32,128]{3,2,1,0:T(8,128)(2,1)S(1)} custom-call(bf16[12,2,2,32,128]{4,3,2,1,0:T(8,128)(2,1)S(1)} %get-tuple-element.28.refs_0_.refs_8_, bf16[12,2,2,32,128]{4,3,2,1,0:T(8,128)(2,1)S(1)} %collective-permute-done.3.refs_1_.refs_9_, bf16[12,2,2,32,128]{4,3,2,1,0:T(8,128)(2,1)S(1)} %collective-permute-done.4.refs_2_.refs_10_, ...), custom_call_target="tpu_custom_call" | custom-call | flops 12582912 | bytes 4718592 | tf_op jit(solution)/shard_map/conv_far/pallas_call | solution.py:558
  117.9 20.5 %all_to_all.20.got_ref = bf16[8,11,32,128]{3,2,1,0:T(8,128)(2,1)S(1)} all-to-all(bf16[8,11,32,128]{3,2,1,0:T(8,128)(2,1)S(1)} %conv_far.1), channel_id=1, replica_groups={{0,48,6,54,65,113,71,119},{16,32,22,38,81,97,87,103},{2,50,4,52,67,115,..., dimensions={0} | all-to-all | bytes 1441792 | tf_op jit(solution)/shard_map/all_to_all | solution.py:74
  138.4 0.9 finish.1
  (1 shorter events, 0.0 us)
Async XLA Ops:
  0.6 1.0 copy-start.3
  2.9 18.6 %all-to-all-start = ((bf16[8,64,512]{2,1,0:T(8,128)(2,1)}), bf16[8,64,512]{2,1,0:T(8,128)(2,1)S(1)}, u32[]{:S(2)}, u32[]{:S(2)}) async-start(bf16[8,64,512]{2,1,0:T(8,128)(2,1)} %bitcast.6), calls=%async_computation | async-start | bytes 1048576 | tf_op jit(solution)/shard_map/all_to_all | solution.py:74
  10.0 1.1 copy-start.2
  21.5 17.0 %all-to-all-start.1 = ((bf16[8,64,768]{2,1,0:T(8,128)(2,1)}), bf16[8,64,768]{2,1,0:T(8,128)(2,1)S(1)}, u32[]{:S(2)}, u32[]{:S(2)}) async-start(bf16[8,64,768]{2,1,0:T(8,128)(2,1)} %bitcast.9), calls=%async_computation.1 | async-start | bytes 1572864 | tf_op jit(solution)/shard_map/all_to_all | solution.py:74
  34.8 3.7 %collective-permute-start = (bf16[256,512]{1,0:T(8,128)(2,1)}, bf16[256,512]{1,0:T(8,128)(2,1)S(1)}, u32[]{:S(2)}, u32[]{:S(2)}) collective-permute-start(bf16[256,512]{1,0:T(8,128)(2,1)} %get-tuple-element.20), channel_id=1, source_target_pairs={{0,8},{1,9},{2,10},{3,11},{4,12},{5,13},{6,14},{7,15},{8,0},{9,1},... | collective-permute-start | bytes 786440 | tf_op jit(solution)/shard_map/ppermute | solution.py:600
  38.5 17.7 %slice-start = ((s8[6291456]{0:T(1024)(128)(4,1)}), s8[4194304]{0:T(1024)(128)(4,1)S(1)}, s32[]{:S(2)}) async-start(s8[6291456]{0:T(1024)(128)(4,1)} %bitcast.13), calls=%async_computation.4 | async-start | bytes 8388608
  38.5 17.7 %slice-start.1 = ((s8[6291456]{0:T(1024)(128)(4,1)}), s8[2097152]{0:T(1024)(128)(4,1)S(1)}, s32[]{:S(2)}) async-start(s8[6291456]{0:T(1024)(128)(4,1)} %bitcast.13), calls=%async_computation.5 | async-start | bytes 4194304
  38.5 17.7 %copy-start = (f32[4,512,512]{2,1,0:T(8,128)S(1)}, f32[4,512,512]{2,1,0:T(8,128)}, u32[]{:S(2)}) copy-start(f32[4,512,512]{2,1,0:T(8,128)} %get-tuple-element.23.pre_ref) | copy-start | bytes 12582916
  56.1 10.2 %collective-permute-start.2 = (bf16[512,5120]{1,0:T(8,128)(2,1)S(1)}, bf16[512,5120]{1,0:T(8,128)(2,1)S(1)}, u32[]{:S(2)}, u32[]{:S(2)}) collective-permute-start(bf16[512,5120]{1,0:T(8,128)(2,1)S(1)} %get-tuple-element.27.ga_ref), channel_id=1, source_target_pairs={{0,8},{1,9},{2,10},{3,11},{4,12},{5,13},{6,14},{7,15},{8,0},{9,1},... | collective-permute-start | bytes 15728648 | tf_op jit(solution)/shard_map/ppermute | solution.py:600
  56.3 10.0 %copy-start.4 = (bf16[256,512]{1,0:T(8,128)(2,1)S(1)}, bf16[256,512]{1,0:T(8,128)(2,1)}, u32[]{:S(2)}) copy-start(bf16[256,512]{1,0:T(8,128)(2,1)} %get-tuple-element.26.ha_ref) | copy-start | bytes 786436
  65.8 10.9 %collective-permute-start.1 = (bf16[4,3,256,512]{3,2,1,0:T(8,128)(2,1)}, bf16[4,3,256,512]{3,2,1,0:T(8,128)(2,1)}, u32[]{:S(2)}, u32[]{:S(2)}) collective-permute-start(bf16[4,3,256,512]{3,2,1,0:T(8,128)(2,1)} %get-tuple-element.25.send_ref), channel_id=1, source_target_pairs={{0,8},{1,9},{2,10},{3,11},{4,12},{5,13},{6,14},{7,15},{8,0},{9,1},... | collective-permute-start | bytes 9437192 | tf_op jit(solution)/shard_map/ppermute | solution.py:600
  72.0 4.8 %copy-start.1 = (bf16[4,256,512]{2,1,0:T(8,128)(2,1)S(1)}, bf16[4,256,512]{2,1,0:T(8,128)(2,1)}, u32[]{:S(2)}) copy-start(bf16[4,256,512]{2,1,0:T(8,128)(2,1)} %get-tuple-element.24._.mine_ref) | copy-start | bytes 3145732
  72.0 29.4 %all-to-all-start.2 = ((bf16[8,128,1280]{2,1,0:T(8,128)(2,1)}), bf16[8,128,1280]{2,1,0:T(8,128)(2,1)}, u32[]{:S(2)}, u32[]{:S(2)}) async-start(bf16[8,128,1280]{2,1,0:T(8,128)(2,1)} %bitcast.11), calls=%async_computation.2 | async-start | bytes 5242880 | tf_op jit(solution)/shard_map/all_to_all | solution.py:74
  85.0 13.8 %collective-permute-start.3 = (bf16[12,2,2,32,128]{4,3,2,1,0:T(8,128)(2,1)S(1)}, bf16[12,2,2,32,128]{4,3,2,1,0:T(8,128)(2,1)S(1)}, u32[]{:S(2)}, u32[]{:S(2)}) collective-permute-start(bf16[12,2,2,32,128]{4,3,2,1,0:T(8,128)(2,1)S(1)} %get-tuple-element.29), channel_id=1, source_target_pairs={{0,16},{16,0},{2,18},{18,2},{64,80},{80,64},{66,82},{82,66},{48,32... | collective-permute-start | bytes 1179656 | tf_op jit(solution)/shard_map/ppermute | solution.py:58
  86.9 13.9 %collective-permute-start.4 = (bf16[12,2,2,32,128]{4,3,2,1,0:T(8,128)(2,1)S(1)}, bf16[12,2,2,32,128]{4,3,2,1,0:T(8,128)(2,1)S(1)}, u32[]{:S(2)}, u32[]{:S(2)}) collective-permute-start(bf16[12,2,2,32,128]{4,3,2,1,0:T(8,128)(2,1)S(1)} %get-tuple-element.30), channel_id=1, source_target_pairs={{0,2},{16,18},{2,0},{18,16},{64,66},{80,82},{66,64},{82,80},{48,50... | collective-permute-start | bytes 1179656 | tf_op jit(solution)/shard_map/ppermute | solution.py:58
  88.2 19.6 %collective-permute-start.5 = (bf16[12,2,2,32,128]{4,3,2,1,0:T(8,128)(2,1)}, bf16[12,2,2,32,128]{4,3,2,1,0:T(8,128)(2,1)S(1)}, u32[]{:S(2)}, u32[]{:S(2)}) collective-permute-start(bf16[12,2,2,32,128]{4,3,2,1,0:T(8,128)(2,1)} %get-tuple-element.31), channel_id=1, source_target_pairs={{0,18},{16,2},{2,16},{18,0},{64,82},{80,66},{66,80},{82,64},{48,34... | collective-permute-start | bytes 1179656 | tf_op jit(solution)/shard_map/ppermute | solution.py:58
  88.5 19.2 %collective-permute-start.6 = (bf16[12,2,2,32,128]{4,3,2,1,0:T(8,128)(2,1)}, bf16[12,2,2,32,128]{4,3,2,1,0:T(8,128)(2,1)S(1)}, u32[]{:S(2)}, u32[]{:S(2)}) collective-permute-start(bf16[12,2,2,32,128]{4,3,2,1,0:T(8,128)(2,1)} %get-tuple-element.32), channel_id=1, source_target_pairs={{0,64},{16,80},{2,66},{18,82},{64,0},{80,16},{66,2},{82,18},{48,11... | collective-permute-start | bytes 1179656 | tf_op jit(solution)/shard_map/ppermute | solution.py:58
  90.2 17.6 %collective-permute-start.7 = (bf16[12,2,2,32,128]{4,3,2,1,0:T(8,128)(2,1)}, bf16[12,2,2,32,128]{4,3,2,1,0:T(8,128)(2,1)S(1)}, u32[]{:S(2)}, u32[]{:S(2)}) collective-permute-start(bf16[12,2,2,32,128]{4,3,2,1,0:T(8,128)(2,1)} %get-tuple-element.33), channel_id=1, source_target_pairs={{0,80},{16,64},{2,82},{18,66},{64,16},{80,0},{66,18},{82,2},{48,96... | collective-permute-start | bytes 1179656 | tf_op jit(solution)/shard_map/ppermute | solution.py:58
  98.8 13.3 %collective-permute-start.8 = (bf16[12,2,2,32,128]{4,3,2,1,0:T(8,128)(2,1)}, bf16[12,2,2,32,128]{4,3,2,1,0:T(8,128)(2,1)S(1)}, u32[]{:S(2)}, u32[]{:S(2)}) collective-permute-start(bf16[12,2,2,32,128]{4,3,2,1,0:T(8,128)(2,1)} %get-tuple-element.34), channel_id=1, source_target_pairs={{0,66},{16,82},{2,64},{18,80},{64,2},{80,18},{66,0},{82,16},{48,11... | collective-permute-start | bytes 1179656 | tf_op jit(solution)/shard_map/ppermute | solution.py:58
  100.9 15.4 %collective-permute-start.9 = (bf16[12,2,2,32,128]{4,3,2,1,0:T(8,128)(2,1)}, bf16[12,2,2,32,128]{4,3,2,1,0:T(8,128)(2,1)S(1)}, u32[]{:S(2)}, u32[]{:S(2)}) collective-permute-start(bf16[12,2,2,32,128]{4,3,2,1,0:T(8,128)(2,1)} %get-tuple-element.35), channel_id=1, source_target_pairs={{0,82},{16,66},{2,80},{18,64},{64,18},{80,2},{66,16},{82,0},{48,98... | collective-permute-start | bytes 1179656 | tf_op jit(solution)/shard_map/ppermute | solution.py:58

commit v10 on v9

--- a/solution.py
+++ b/solution.py
@@ -147,28 +147,28 @@
 
 def conv_kernel(sc_ref, x_ref, w_ref, saved_ref, pre_ref, last_ref, mine_ref, other_ref, pad_s, tap_s, ht_s):
     layer = pl.program_id(0)
-    frames = x_ref.shape[0]
+    frames, width = x_ref.shape
 
     @pl.when(layer == 0)
     def _():
         pad_s[...] = jnp.zeros_like(pad_s)
-        pad_s[PAD : PAD + frames] = x_ref[...].astype(F32)
+        pad_s[PAD : PAD + frames] = x_ref[...]
 
     for at in range(LAYERS):
 
         @pl.when(layer == at)
         def _():
             reach = CLASSES * 2**at
-            tap_s[0] = pad_s[PAD - reach : PAD - reach + frames].astype(BF16)
-            tap_s[1] = pad_s[PAD + reach : PAD + reach + frames].astype(BF16)
-
-    hidden = pad_s[PAD : PAD + frames]
-    middle = hidden.astype(BF16)
+            tap_s[:, :width] = pad_s[PAD - reach : PAD - reach + frames]
+            tap_s[:, 2 * width :] = pad_s[PAD + reach : PAD + reach + frames]
+
+    middle = pad_s[PAD : PAD + frames]
     saved_ref[0] = middle
-    pre = dot(tap_s[0], w_ref[0, 0]) + dot(middle, w_ref[0, 1]) + dot(tap_s[1], w_ref[0, 2])
+    tap_s[:, width : 2 * width] = middle
+    pre = dot(tap_s[...], w_ref[0].reshape(TAPS * width, width))
     pre_ref[0] = pre
-    new = (frame_mask(sc_ref, frames) * (hidden + jax.nn.silu(pre))).astype(BF16)
-    pad_s[PAD : PAD + frames] = new.astype(F32)
+    new = (frame_mask(sc_ref, frames) * (middle.astype(F32) + jax.nn.silu(pre))).astype(BF16)
+    pad_s[PAD : PAD + frames] = new
 
     @pl.when(layer == LAYERS - 1)
     def _():
@@ -199,8 +199,8 @@
             pltpu.HBM((width // 2, frames), BF16),
         ],
         scratch_shapes=[
-            pltpu.VMEM((frames + 2 * PAD, width), F32),
-            pltpu.VMEM((2, frames, width), BF16),
+            pltpu.VMEM((frames + 2 * PAD, width), BF16),
+            pltpu.VMEM((frames, TAPS * width), BF16),
             pltpu.VMEM((width, frames), BF16),
         ],
         compiler_params=params(14, "arbitrary"),
@@ -364,14 +364,14 @@
 
     @pl.when(step < LAYERS - 1)
     def _():
-        pad_s[PAD : PAD + frames] = g_pre.astype(F32)
+        pad_s[PAD : PAD + frames] = g_pre
         for at in range(LAYERS - 1, 0, -1):
 
             @pl.when(step == LAYERS - 1 - at)
             def _():
                 reach = CLASSES * 2**at
-                tap_s[0] = pad_s[PAD + reach : PAD + reach + frames].astype(BF16)
-                tap_s[1] = pad_s[PAD - reach : PAD - reach + frames].astype(BF16)
+                tap_s[0] = pad_s[PAD + reach : PAD + reach + frames]
+                tap_s[1] = pad_s[PAD - reach : PAD - reach + frames]
 
         g_s[...] = (
             g_act
@@ -406,7 +406,7 @@
         ],
         scratch_shapes=[
             pltpu.VMEM((frames, width), F32),
-            pltpu.VMEM((frames + 2 * PAD, width), F32),
+            pltpu.VMEM((frames + 2 * PAD, width), BF16),
             pltpu.VMEM((2, frames, width), BF16),
             pltpu.VMEM((width, frames), BF16),
         ],

time: 142 us -> 142 us (level)
  no operation moved by 1% of the time
where the time goes in v10:
time: 142 us; the launch traced here: 139 us
  Pallas kernels  57.8 us (41%)
  waiting for transfers between devices  31.7 us (22%)
  starting transfers between devices  25.3 us (18%)
  blocking collectives  20.5 us (14%)
  local copies, waits for them, and re-layouts  2.27 us (2%)
  between operations  1.51 us (1%)
    all_to_all x1, blocking collectives, exchange(): return lax.all_to_all(x, AXES, 0, 0, tiled=True, axis_index_groups=groups)  20.5 us
    ppermute x7, waiting for transfers between devices, near_swap(): return lax.ppermute(x, AXES, pairs)  19 us
    pallas_call x1, Pallas kernels, heads(): pl.pallas_call(functools.partial(head_kernel, 5.0 * loss_scale, tiles), g...  17.6 us
    all_to_all x3, starting transfers between devices, exchange(): return lax.all_to_all(x, AXES, 0, 0, tiled=True, axis_index_groups=groups)  15.3 us
    all_to_all x3, waiting for transfers between devices, exchange(): return lax.all_to_all(x, AXES, 0, 0, tiled=True, axis_index_groups=groups)  12.7 us
    ppermute x7, starting transfers between devices, near_swap(): return lax.ppermute(x, AXES, pairs)  9.48 us
    pallas_call x1, Pallas kernels, back(): pl.pallas_call(back_kernel, grid=(LAYERS,), in_specs=[pl.BlockSpec(memory...  9.35 us
    pallas_call x1, Pallas kernels, convolve(): pl.pallas_call(conv_kernel, grid=(LAYERS,), in_specs=[pl.BlockSpec(memory...  8.82 us
  transfers between devices with their start and end apart: 13, of which 7 were waited for; matrix products, arithmetic and copies ran while one was open for 0% of the time, Pallas kernels for 26%

profile of v10, /device:TPU:0, one launch (start us, length us, event | category | flops | bytes accessed | tf_op | source)
XLA Modules:
  0.0 139.1 jit_solution(6400314161204740181)
XLA Ops:
  0.6 0.0 copy-start.3
  0.6 1.0 copy-done.3
  1.7 1.3 regroup.2
  2.9 7.0 %all-to-all-start = ((bf16[8,64,512]{2,1,0:T(8,128)(2,1)}), bf16[8,64,512]{2,1,0:T(8,128)(2,1)S(1)}, u32[]{:S(2)}, u32[]{:S(2)}) async-start(bf16[8,64,512]{2,1,0:T(8,128)(2,1)} %bitcast.6), calls=%async_computation | async-start | bytes 1048576 | tf_op jit(solution)/shard_map/all_to_all | solution.py:74
  10.0 0.0 copy-start.2
  10.0 1.1 copy-done.2
  11.1 1.5 %regroup.3 = bf16[512,768]{1,0:T(8,128)(2,1)} custom-call(bf16[512,768]{1,0:T(8,128)(2,1)S(1)} %bitcast.15), custom_call_target="tpu_custom_call" | custom-call | tf_op jit(solution)/shard_map/regroup/pallas_call | solution.py:130
  12.6 9.0 %all-to-all-done = bf16[8,64,512]{2,1,0:T(8,128)(2,1)S(1)} async-done(((bf16[8,64,512]{2,1,0:T(8,128)(2,1)}), bf16[8,64,512]{2,1,0:T(8,128)(2,1)S(1)}, u32[]{:S(2)}, u32[]{:S(2)}) %all-to-all-start) | async-done | bytes 524320 | tf_op jit(solution)/shard_map/all_to_all | solution.py:74
  21.5 3.5 %all-to-all-start.1 = ((bf16[8,64,768]{2,1,0:T(8,128)(2,1)}), bf16[8,64,768]{2,1,0:T(8,128)(2,1)S(1)}, u32[]{:S(2)}, u32[]{:S(2)}) async-start(bf16[8,64,768]{2,1,0:T(8,128)(2,1)} %bitcast.9), calls=%async_computation.1 | async-start | bytes 1572864 | tf_op jit(solution)/shard_map/all_to_all | solution.py:74
  25.8 0.1 stack.23.sc_ref
  25.9 8.8 %convolve.1 = (bf16[4,512,512]{2,1,0:T(8,128)(2,1)S(1)}, f32[4,512,512]{2,1,0:T(8,128)}, bf16[512,512]{1,0:T(8,128)(2,1)}, bf16[256,512]{1,0:T(8,128)(2,1)}, bf16[256,512]{1,0:T(8,128)(2,1)}) custom-call(s32[6]{0:T(128)S(1)} %stack.23.sc_ref, bf16[512,512]{1,0:T(8,128)(2,1)S(1)} %bitcast.18, bf16[4,3,512,512]{3,2,1,0:T(8,128)(2,1)} %w_ref.3), custom_call_target="tpu_custom_call" | custom-call | flops 3221225472 | bytes 12582912 | tf_op jit(solution)/shard_map/convolve/pallas_call | solution.py:185
  34.7 0.0 collective-permute-start
  34.7 3.8 %all-to-all-done.1 = bf16[8,64,768]{2,1,0:T(8,128)(2,1)S(1)} async-done(((bf16[8,64,768]{2,1,0:T(8,128)(2,1)}), bf16[8,64,768]{2,1,0:T(8,128)(2,1)S(1)}, u32[]{:S(2)}, u32[]{:S(2)}) %all-to-all-start.1) | async-done | bytes 786464 | tf_op jit(solution)/shard_map/all_to_all | solution.py:74
  38.5 0.0 collective-permute-done._.hb_ref
  38.5 0.0 slice-start
  38.5 0.0 slice-start.1
  38.5 0.0 copy-start
  38.5 17.6 %heads.1 = (bf16[512,5120]{1,0:T(8,128)(2,1)S(1)}, f32[512,512]{1,0:T(8,128)S(1)}) custom-call(s32[6]{0:T(128)S(1)} %stack.23.sc_ref, bf16[512,512]{1,0:T(8,128)(2,1)} %get-tuple-element.19.h_ref, bf16[512,768]{1,0:T(8,128)(2,1)S(1)} %bitcast.16, bf16[512,5120]{1,0:T(8,128)(2,1)} %ws_ref.1, bf16[768,5120]{1,0:T(8,128)(2,1)} %wt_ref.1, ...), custom_call_target="tpu_custom_call" | custom-call | flops 9395240960 | bytes 23592960 | tf_op jit(solution)/shard_map/heads/pallas_call | solution.py:265
  56.1 0.1 collective-permute-start.2
  56.2 0.0 slice-done
  56.2 0.0 slice-done.1
  56.2 0.0 copy-done
  56.3 0.0 copy-start.4
  56.3 9.4 %back.1 = (bf16[4,3,256,512]{3,2,1,0:T(8,128)(2,1)}, bf16[4,256,512]{2,1,0:T(8,128)(2,1)}) custom-call(s32[6]{0:T(128)S(1)} %stack.23.sc_ref, f32[512,512]{1,0:T(8,128)S(1)} %get-tuple-element.21.g4_ref, bf16[4,512,512]{2,1,0:T(8,128)(2,1)S(1)} %get-tuple-element.22.h_ref, f32[4,512,512]{2,1,0:T(8,128)S(1)} %copy-done, bf16[4,3,512,512]{3,2,1,0:T(8,128)(2,1)S(1)} %bitcast.14), custom_call_target="tpu_custom_call" | custom-call | flops 2415919104 | bytes 16777216 | tf_op jit(solution)/shard_map/back/pallas_call | solution.py:390
  65.6 0.5 collective-permute-start.1
  66.1 0.0 collective-permute-done.2.gb_ref
  66.1 0.0 copy-done.4
  66.1 5.7 %head_grad.1._ = bf16[2,2,2,2,2,32,1280]{6,5,4,3,2,1,0:T(8,128)(2,1)} custom-call(s32[6]{0:T(128)S(1)} %stack.23.sc_ref, bf16[256,512]{1,0:T(8,128)(2,1)S(1)} %copy-done.4, bf16[256,512]{1,0:T(8,128)(2,1)S(1)} %collective-permute-done._.hb_ref, bf16[512,5120]{1,0:T(8,128)(2,1)S(1)} %get-tuple-element.27.ga_ref, ...), custom_call_target="tpu_custom_call" | custom-call | flops 2684354560 | bytes 13107200 | tf_op jit(solution)/shard_map/head_grad/pallas_call | solution.py:328
  71.8 0.0 copy-start.1
  71.8 4.7 %all-to-all-start.2 = ((bf16[8,128,1280]{2,1,0:T(8,128)(2,1)}), bf16[8,128,1280]{2,1,0:T(8,128)(2,1)}, u32[]{:S(2)}, u32[]{:S(2)}) async-start(bf16[8,128,1280]{2,1,0:T(8,128)(2,1)} %bitcast.11), calls=%async_computation.2 | async-start | bytes 5242880 | tf_op jit(solution)/shard_map/all_to_all | solution.py:74
  76.6 0.0 collective-permute-done.1.got_ref
  76.6 0.0 copy-done.1
  76.6 8.2 %conv_grad.1 = (bf16[12,2,2,32,128]{4,3,2,1,0:T(8,128)(2,1)S(1)}, bf16[12,2,2,32,128]{4,3,2,1,0:T(8,128)(2,1)S(1)}, bf16[12,2,2,32,128]{4,3,2,1,0:T(8,128)(2,1)S...) custom-call(s32[6]{0:T(128)S(1)} %stack.23.sc_ref, ...), custom_call_target="tpu_custom_call" | custom-call | flops 3221225472 | bytes 10485760 | tf_op jit(solution)/shard_map/conv_grad/pallas_call | solution.py:474
  84.8 1.9 %collective-permute-start.3 = (bf16[12,2,2,32,128]{4,3,2,1,0:T(8,128)(2,1)S(1)}, bf16[12,2,2,32,128]{4,3,2,1,0:T(8,128)(2,1)S(1)}, u32[]{:S(2)}, u32[]{:S(2)}) collective-permute-start(bf16[12,2,2,32,128]{4,3,2,1,0:T(8,128)(2,1)S(1)} %get-tuple-element.29), channel_id=1, source_target_pairs={{0,16},{16,0},{2,18},{18,2},{64,80},{80,64},{66,82},{82,66},{48,32... | collective-permute-start | bytes 1179656 | tf_op jit(solution)/shard_map/ppermute | solution.py:58
  86.7 1.3 collective-permute-start.4
  88.0 0.3 collective-permute-start.5
  88.3 1.7 %collective-permute-start.6 = (bf16[12,2,2,32,128]{4,3,2,1,0:T(8,128)(2,1)}, bf16[12,2,2,32,128]{4,3,2,1,0:T(8,128)(2,1)S(1)}, u32[]{:S(2)}, u32[]{:S(2)}) collective-permute-start(bf16[12,2,2,32,128]{4,3,2,1,0:T(8,128)(2,1)} %get-tuple-element.32), channel_id=1, source_target_pairs={{0,64},{16,80},{2,66},{18,82},{64,0},{80,16},{66,2},{82,18},{48,11... | collective-permute-start | bytes 1179656 | tf_op jit(solution)/shard_map/ppermute | solution.py:58
  90.1 1.6 %collective-permute-start.7 = (bf16[12,2,2,32,128]{4,3,2,1,0:T(8,128)(2,1)}, bf16[12,2,2,32,128]{4,3,2,1,0:T(8,128)(2,1)S(1)}, u32[]{:S(2)}, u32[]{:S(2)}) collective-permute-start(bf16[12,2,2,32,128]{4,3,2,1,0:T(8,128)(2,1)} %get-tuple-element.33), channel_id=1, source_target_pairs={{0,80},{16,64},{2,82},{18,66},{64,16},{80,0},{66,18},{82,2},{48,96... | collective-permute-start | bytes 1179656 | tf_op jit(solution)/shard_map/ppermute | solution.py:58
  91.7 6.9 %collective-permute-done.3.refs_1_.refs_9_ = bf16[12,2,2,32,128]{4,3,2,1,0:T(8,128)(2,1)S(1)} collective-permute-done((bf16[12,2,2,32,128]{4,3,2,1,0:T(8,128)(2,1)S(1)}, bf16[12,2,2,32,128]{4,3,2,1,0:T(8,128)(2,1)S(1)}, u32[]{:S(2)}, u32[]{:S(2)}) %collective-permute-start.3) | collective-permute-done | bytes 393248 | tf_op jit(solution)/shard_map/ppermute | solution.py:58
  98.6 2.1 %collective-permute-start.8 = (bf16[12,2,2,32,128]{4,3,2,1,0:T(8,128)(2,1)}, bf16[12,2,2,32,128]{4,3,2,1,0:T(8,128)(2,1)S(1)}, u32[]{:S(2)}, u32[]{:S(2)}) collective-permute-start(bf16[12,2,2,32,128]{4,3,2,1,0:T(8,128)(2,1)} %get-tuple-element.34), channel_id=1, source_target_pairs={{0,66},{16,82},{2,64},{18,80},{64,2},{80,18},{66,0},{82,16},{48,11... | collective-permute-start | bytes 1179656 | tf_op jit(solution)/shard_map/ppermute | solution.py:58
  100.7 0.0 collective-permute-done.4.refs_2_.refs_10_
  100.7 0.5 collective-permute-start.9
  101.2 0.0 all-to-all-done.2
  101.2 2.8 %head_far.1.refs_16_ = bf16[8,5,32,128]{3,2,1,0:T(8,128)(2,1)S(1)} custom-call(bf16[8,2,2,32,1280]{4,3,2,1,0:T(8,128)(2,1)} %bitcast.12.got_ref), custom_call_target="tpu_custom_call" | custom-call | flops 10485760 | bytes 3932160 | tf_op jit(solution)/shard_map/head_far/pallas_call | solution.py:519
  104.0 3.6 %collective-permute-done.5.refs_3_.refs_11_ = bf16[12,2,2,32,128]{4,3,2,1,0:T(8,128)(2,1)S(1)} collective-permute-done((bf16[12,2,2,32,128]{4,3,2,1,0:T(8,128)(2,1)}, bf16[12,2,2,32,128]{4,3,2,1,0:T(8,128)(2,1)S(1)}, u32[]{:S(2)}, u32[]{:S(2)}) %collective-permute-start.5) | collective-permute-done | bytes 393248 | tf_op jit(solution)/shard_map/ppermute | solution.py:58
  107.6 0.0 collective-permute-done.6.refs_4_.refs_12_
  107.6 0.1 collective-permute-done.7.refs_5_.refs_13_
  107.7 4.2 %collective-permute-done.8.refs_6_.refs_14_ = bf16[12,2,2,32,128]{4,3,2,1,0:T(8,128)(2,1)S(1)} collective-permute-done((bf16[12,2,2,32,128]{4,3,2,1,0:T(8,128)(2,1)}, bf16[12,2,2,32,128]{4,3,2,1,0:T(8,128)(2,1)S(1)}, u32[]{:S(2)}, u32[]{:S(2)}) %collective-permute-start.8) | collective-permute-done | bytes 393248 | tf_op jit(solution)/shard_map/ppermute | solution.py:58
  111.8 4.2 %collective-permute-done.9.refs_7_.refs_15_ = bf16[12,2,2,32,128]{4,3,2,1,0:T(8,128)(2,1)S(1)} collective-permute-done((bf16[12,2,2,32,128]{4,3,2,1,0:T(8,128)(2,1)}, bf16[12,2,2,32,128]{4,3,2,1,0:T(8,128)(2,1)S(1)}, u32[]{:S(2)}, u32[]{:S(2)}) %collective-permute-start.9) | collective-permute-done | bytes 393248 | tf_op jit(solution)/shard_map/ppermute | solution.py:58
  116.1 1.6 %conv_far.1 = bf16[8,11,32,128]{3,2,1,0:T(8,128)(2,1)S(1)} custom-call(bf16[12,2,2,32,128]{4,3,2,1,0:T(8,128)(2,1)S(1)} %get-tuple-element.28.refs_0_.refs_8_, bf16[12,2,2,32,128]{4,3,2,1,0:T(8,128)(2,1)S(1)} %collective-permute-done.3.refs_1_.refs_9_, bf16[12,2,2,32,128]{4,3,2,1,0:T(8,128)(2,1)S(1)} %collective-permute-done.4.refs_2_.refs_10_, ...), custom_call_target="tpu_custom_call" | custom-call | flops 12582912 | bytes 4718592 | tf_op jit(solution)/shard_map/conv_far/pallas_call | solution.py:558
  117.7 20.5 %all_to_all.20.got_ref = bf16[8,11,32,128]{3,2,1,0:T(8,128)(2,1)S(1)} all-to-all(bf16[8,11,32,128]{3,2,1,0:T(8,128)(2,1)S(1)} %conv_far.1), channel_id=1, replica_groups={{0,48,6,54,65,113,71,119},{16,32,22,38,81,97,87,103},{2,50,4,52,67,115,..., dimensions={0} | all-to-all | bytes 1441792 | tf_op jit(solution)/shard_map/all_to_all | solution.py:74
  138.2 0.9 finish.1
  (1 shorter events, 0.0 us)
Async XLA Ops:
  0.6 1.0 copy-start.3
  2.9 18.6 %all-to-all-start = ((bf16[8,64,512]{2,1,0:T(8,128)(2,1)}), bf16[8,64,512]{2,1,0:T(8,128)(2,1)S(1)}, u32[]{:S(2)}, u32[]{:S(2)}) async-start(bf16[8,64,512]{2,1,0:T(8,128)(2,1)} %bitcast.6), calls=%async_computation | async-start | bytes 1048576 | tf_op jit(solution)/shard_map/all_to_all | solution.py:74
  10.0 1.1 copy-start.2
  21.5 17.0 %all-to-all-start.1 = ((bf16[8,64,768]{2,1,0:T(8,128)(2,1)}), bf16[8,64,768]{2,1,0:T(8,128)(2,1)S(1)}, u32[]{:S(2)}, u32[]{:S(2)}) async-start(bf16[8,64,768]{2,1,0:T(8,128)(2,1)} %bitcast.9), calls=%async_computation.1 | async-start | bytes 1572864 | tf_op jit(solution)/shard_map/all_to_all | solution.py:74
  34.7 3.8 %collective-permute-start = (bf16[256,512]{1,0:T(8,128)(2,1)}, bf16[256,512]{1,0:T(8,128)(2,1)S(1)}, u32[]{:S(2)}, u32[]{:S(2)}) collective-permute-start(bf16[256,512]{1,0:T(8,128)(2,1)} %get-tuple-element.20), channel_id=1, source_target_pairs={{0,8},{1,9},{2,10},{3,11},{4,12},{5,13},{6,14},{7,15},{8,0},{9,1},... | collective-permute-start | bytes 786440 | tf_op jit(solution)/shard_map/ppermute | solution.py:600
  38.5 17.7 %slice-start = ((s8[6291456]{0:T(1024)(128)(4,1)}), s8[4194304]{0:T(1024)(128)(4,1)S(1)}, s32[]{:S(2)}) async-start(s8[6291456]{0:T(1024)(128)(4,1)} %bitcast.13), calls=%async_computation.4 | async-start | bytes 8388608
  38.5 17.7 %slice-start.1 = ((s8[6291456]{0:T(1024)(128)(4,1)}), s8[2097152]{0:T(1024)(128)(4,1)S(1)}, s32[]{:S(2)}) async-start(s8[6291456]{0:T(1024)(128)(4,1)} %bitcast.13), calls=%async_computation.5 | async-start | bytes 4194304
  38.5 17.7 %copy-start = (f32[4,512,512]{2,1,0:T(8,128)S(1)}, f32[4,512,512]{2,1,0:T(8,128)}, u32[]{:S(2)}) copy-start(f32[4,512,512]{2,1,0:T(8,128)} %get-tuple-element.23.pre_ref) | copy-start | bytes 12582916
  56.1 10.0 %collective-permute-start.2 = (bf16[512,5120]{1,0:T(8,128)(2,1)S(1)}, bf16[512,5120]{1,0:T(8,128)(2,1)S(1)}, u32[]{:S(2)}, u32[]{:S(2)}) collective-permute-start(bf16[512,5120]{1,0:T(8,128)(2,1)S(1)} %get-tuple-element.27.ga_ref), channel_id=1, source_target_pairs={{0,8},{1,9},{2,10},{3,11},{4,12},{5,13},{6,14},{7,15},{8,0},{9,1},... | collective-permute-start | bytes 15728648 | tf_op jit(solution)/shard_map/ppermute | solution.py:600
  56.3 9.8 %copy-start.4 = (bf16[256,512]{1,0:T(8,128)(2,1)S(1)}, bf16[256,512]{1,0:T(8,128)(2,1)}, u32[]{:S(2)}) copy-start(bf16[256,512]{1,0:T(8,128)(2,1)} %get-tuple-element.26.ha_ref) | copy-start | bytes 786436
  65.6 10.9 %collective-permute-start.1 = (bf16[4,3,256,512]{3,2,1,0:T(8,128)(2,1)}, bf16[4,3,256,512]{3,2,1,0:T(8,128)(2,1)}, u32[]{:S(2)}, u32[]{:S(2)}) collective-permute-start(bf16[4,3,256,512]{3,2,1,0:T(8,128)(2,1)} %get-tuple-element.25.send_ref), channel_id=1, source_target_pairs={{0,8},{1,9},{2,10},{3,11},{4,12},{5,13},{6,14},{7,15},{8,0},{9,1},... | collective-permute-start | bytes 9437192 | tf_op jit(solution)/shard_map/ppermute | solution.py:600
  71.8 4.8 %copy-start.1 = (bf16[4,256,512]{2,1,0:T(8,128)(2,1)S(1)}, bf16[4,256,512]{2,1,0:T(8,128)(2,1)}, u32[]{:S(2)}) copy-start(bf16[4,256,512]{2,1,0:T(8,128)(2,1)} %get-tuple-element.24._.mine_ref) | copy-start | bytes 3145732
  71.8 29.4 %all-to-all-start.2 = ((bf16[8,128,1280]{2,1,0:T(8,128)(2,1)}), bf16[8,128,1280]{2,1,0:T(8,128)(2,1)}, u32[]{:S(2)}, u32[]{:S(2)}) async-start(bf16[8,128,1280]{2,1,0:T(8,128)(2,1)} %bitcast.11), calls=%async_computation.2 | async-start | bytes 5242880 | tf_op jit(solution)/shard_map/all_to_all | solution.py:74
  84.8 13.8 %collective-permute-start.3 = (bf16[12,2,2,32,128]{4,3,2,1,0:T(8,128)(2,1)S(1)}, bf16[12,2,2,32,128]{4,3,2,1,0:T(8,128)(2,1)S(1)}, u32[]{:S(2)}, u32[]{:S(2)}) collective-permute-start(bf16[12,2,2,32,128]{4,3,2,1,0:T(8,128)(2,1)S(1)} %get-tuple-element.29), channel_id=1, source_target_pairs={{0,16},{16,0},{2,18},{18,2},{64,80},{80,64},{66,82},{82,66},{48,32... | collective-permute-start | bytes 1179656 | tf_op jit(solution)/shard_map/ppermute | solution.py:58
  86.7 13.9 %collective-permute-start.4 = (bf16[12,2,2,32,128]{4,3,2,1,0:T(8,128)(2,1)S(1)}, bf16[12,2,2,32,128]{4,3,2,1,0:T(8,128)(2,1)S(1)}, u32[]{:S(2)}, u32[]{:S(2)}) collective-permute-start(bf16[12,2,2,32,128]{4,3,2,1,0:T(8,128)(2,1)S(1)} %get-tuple-element.30), channel_id=1, source_target_pairs={{0,2},{16,18},{2,0},{18,16},{64,66},{80,82},{66,64},{82,80},{48,50... | collective-permute-start | bytes 1179656 | tf_op jit(solution)/shard_map/ppermute | solution.py:58
  88.0 19.6 %collective-permute-start.5 = (bf16[12,2,2,32,128]{4,3,2,1,0:T(8,128)(2,1)}, bf16[12,2,2,32,128]{4,3,2,1,0:T(8,128)(2,1)S(1)}, u32[]{:S(2)}, u32[]{:S(2)}) collective-permute-start(bf16[12,2,2,32,128]{4,3,2,1,0:T(8,128)(2,1)} %get-tuple-element.31), channel_id=1, source_target_pairs={{0,18},{16,2},{2,16},{18,0},{64,82},{80,66},{66,80},{82,64},{48,34... | collective-permute-start | bytes 1179656 | tf_op jit(solution)/shard_map/ppermute | solution.py:58
  88.3 19.2 %collective-permute-start.6 = (bf16[12,2,2,32,128]{4,3,2,1,0:T(8,128)(2,1)}, bf16[12,2,2,32,128]{4,3,2,1,0:T(8,128)(2,1)S(1)}, u32[]{:S(2)}, u32[]{:S(2)}) collective-permute-start(bf16[12,2,2,32,128]{4,3,2,1,0:T(8,128)(2,1)} %get-tuple-element.32), channel_id=1, source_target_pairs={{0,64},{16,80},{2,66},{18,82},{64,0},{80,16},{66,2},{82,18},{48,11... | collective-permute-start | bytes 1179656 | tf_op jit(solution)/shard_map/ppermute | solution.py:58
  90.1 17.6 %collective-permute-start.7 = (bf16[12,2,2,32,128]{4,3,2,1,0:T(8,128)(2,1)}, bf16[12,2,2,32,128]{4,3,2,1,0:T(8,128)(2,1)S(1)}, u32[]{:S(2)}, u32[]{:S(2)}) collective-permute-start(bf16[12,2,2,32,128]{4,3,2,1,0:T(8,128)(2,1)} %get-tuple-element.33), channel_id=1, source_target_pairs={{0,80},{16,64},{2,82},{18,66},{64,16},{80,0},{66,18},{82,2},{48,96... | collective-permute-start | bytes 1179656 | tf_op jit(solution)/shard_map/ppermute | solution.py:58
  98.6 13.3 %collective-permute-start.8 = (bf16[12,2,2,32,128]{4,3,2,1,0:T(8,128)(2,1)}, bf16[12,2,2,32,128]{4,3,2,1,0:T(8,128)(2,1)S(1)}, u32[]{:S(2)}, u32[]{:S(2)}) collective-permute-start(bf16[12,2,2,32,128]{4,3,2,1,0:T(8,128)(2,1)} %get-tuple-element.34), channel_id=1, source_target_pairs={{0,66},{16,82},{2,64},{18,80},{64,2},{80,18},{66,0},{82,16},{48,11... | collective-permute-start | bytes 1179656 | tf_op jit(solution)/shard_map/ppermute | solution.py:58
  100.7 15.4 %collective-permute-start.9 = (bf16[12,2,2,32,128]{4,3,2,1,0:T(8,128)(2,1)}, bf16[12,2,2,32,128]{4,3,2,1,0:T(8,128)(2,1)S(1)}, u32[]{:S(2)}, u32[]{:S(2)}) collective-permute-start(bf16[12,2,2,32,128]{4,3,2,1,0:T(8,128)(2,1)} %get-tuple-element.35), channel_id=1, source_target_pairs={{0,82},{16,66},{2,80},{18,64},{64,18},{80,2},{66,16},{82,0},{48,98... | collective-permute-start | bytes 1179656 | tf_op jit(solution)/shard_map/ppermute | solution.py:58

commit v11 on v9

--- a/solution.py
+++ b/solution.py
@@ -629,7 +629,7 @@
     near = head_grad(sc, h_mine, h_got, score, score_got, mine)
     head_got = exchange(near.reshape(8, 4 * 32, scores // 4), near_groups())
     parts = conv_grad(sc, mine, send, got, near)
-    conv_got = [parts[0]] + [near_swap(parts[i], i) for i in range(1, 8)]
+    conv_got = [parts[0]] + [near_swap(parts[i], i) for i in (1, 2, 7, 6, 5, 3, 4)]
 
     far = head_far(head_got.reshape(8, 2, 2, 32, scores // 4))
     far = conv_far(conv_got, far)

time: 142 us -> 140 us (0.986); the launches traced: 139 us -> 140 us
  starting transfers between devices: 25.3 us -> 27.4 us
  waiting for transfers between devices: 31.7 us -> 29.9 us
    ppermute x7, starting transfers between devices: 9.48 us -> 11.6 us  [near_swap(): return lax.ppermute(x, AXES, pairs)]
    ppermute x7, waiting for transfers between devices: 19 us -> 17.3 us  [near_swap(): return lax.ppermute(x, AXES, pairs)]
  transfers between devices with their start and end apart: 13 -> 13, of which waited for: 7 -> 5; matrix products, arithmetic and copies ran while one was open for 0% -> 0% of each run, Pallas kernels for 26% -> 26%
where the time goes in v11:
time: 140 us
  Pallas kernels  58 us (41%)
  waiting for transfers between devices  29.9 us (21%)
  starting transfers between devices  27.4 us (20%)
  blocking collectives  20.6 us (15%)
  local copies, waits for them, and re-layouts  2.27 us (2%)
  between operations  1.54 us (1%)
    all_to_all x1, blocking collectives, exchange(): return lax.all_to_all(x, AXES, 0, 0, tiled=True, axis_index_groups=groups)  20.6 us
    pallas_call x1, Pallas kernels, heads(): pl.pallas_call(functools.partial(head_kernel, 5.0 * loss_scale, tiles), g...  17.6 us
    ppermute x7, waiting for transfers between devices, near_swap(): return lax.ppermute(x, AXES, pairs)  17.3 us
    all_to_all x3, starting transfers between devices, exchange(): return lax.all_to_all(x, AXES, 0, 0, tiled=True, axis_index_groups=groups)  15.3 us
    all_to_all x3, waiting for transfers between devices, exchange(): return lax.all_to_all(x, AXES, 0, 0, tiled=True, axis_index_groups=groups)  12.7 us
    ppermute x7, starting transfers between devices, near_swap(): return lax.ppermute(x, AXES, pairs)  11.6 us
    pallas_call x1, Pallas kernels, back(): pl.pallas_call(back_kernel, grid=(LAYERS,), in_specs=[pl.BlockSpec(memory...  9.54 us
    pallas_call x1, Pallas kernels, convolve(): pl.pallas_call(conv_kernel, grid=(LAYERS,), in_specs=[pl.BlockSpec(memory...  8.86 us
  transfers between devices with their start and end apart: 13, of which 5 were waited for; matrix products, arithmetic and copies ran while one was open for 0% of the time, Pallas kernels for 26%

profile of v11, /device:TPU:0, one launch (start us, length us, event | category | flops | bytes accessed | tf_op | source)
XLA Modules:
  0.0 139.8 jit_solution(13283541641460941254)
XLA Ops:
  0.6 0.0 copy-start.3
  0.6 1.0 copy-done.3
  1.7 1.3 regroup.2
  2.9 7.0 %all-to-all-start = ((bf16[8,64,512]{2,1,0:T(8,128)(2,1)}), bf16[8,64,512]{2,1,0:T(8,128)(2,1)S(1)}, u32[]{:S(2)}, u32[]{:S(2)}) async-start(bf16[8,64,512]{2,1,0:T(8,128)(2,1)} %bitcast.6), calls=%async_computation | async-start | bytes 1048576 | tf_op jit(solution)/shard_map/all_to_all | solution.py:74
  10.0 0.0 copy-start.2
  10.0 1.1 copy-done.2
  11.1 1.5 %regroup.3 = bf16[512,768]{1,0:T(8,128)(2,1)} custom-call(bf16[512,768]{1,0:T(8,128)(2,1)S(1)} %bitcast.15), custom_call_target="tpu_custom_call" | custom-call | tf_op jit(solution)/shard_map/regroup/pallas_call | solution.py:130
  12.6 9.0 %all-to-all-done = bf16[8,64,512]{2,1,0:T(8,128)(2,1)S(1)} async-done(((bf16[8,64,512]{2,1,0:T(8,128)(2,1)}), bf16[8,64,512]{2,1,0:T(8,128)(2,1)S(1)}, u32[]{:S(2)}, u32[]{:S(2)}) %all-to-all-start) | async-done | bytes 524320 | tf_op jit(solution)/shard_map/all_to_all | solution.py:74
  21.5 3.5 %all-to-all-start.1 = ((bf16[8,64,768]{2,1,0:T(8,128)(2,1)}), bf16[8,64,768]{2,1,0:T(8,128)(2,1)S(1)}, u32[]{:S(2)}, u32[]{:S(2)}) async-start(bf16[8,64,768]{2,1,0:T(8,128)(2,1)} %bitcast.9), calls=%async_computation.1 | async-start | bytes 1572864 | tf_op jit(solution)/shard_map/all_to_all | solution.py:74
  25.8 0.1 stack.23.sc_ref
  25.9 8.9 %convolve.1 = (bf16[4,512,512]{2,1,0:T(8,128)(2,1)S(1)}, f32[4,512,512]{2,1,0:T(8,128)}, bf16[512,512]{1,0:T(8,128)(2,1)}, bf16[256,512]{1,0:T(8,128)(2,1)}, bf16[256,512]{1,0:T(8,128)(2,1)}) custom-call(s32[6]{0:T(128)S(1)} %stack.23.sc_ref, bf16[512,512]{1,0:T(8,128)(2,1)S(1)} %bitcast.18, bf16[4,3,512,512]{3,2,1,0:T(8,128)(2,1)} %w_ref.3), custom_call_target="tpu_custom_call" | custom-call | flops 3221225472 | bytes 12582912 | tf_op jit(solution)/shard_map/convolve/pallas_call | solution.py:185
  34.8 0.0 collective-permute-start
  34.8 3.7 %all-to-all-done.1 = bf16[8,64,768]{2,1,0:T(8,128)(2,1)S(1)} async-done(((bf16[8,64,768]{2,1,0:T(8,128)(2,1)}), bf16[8,64,768]{2,1,0:T(8,128)(2,1)S(1)}, u32[]{:S(2)}, u32[]{:S(2)}) %all-to-all-start.1) | async-done | bytes 786464 | tf_op jit(solution)/shard_map/all_to_all | solution.py:74
  38.5 0.0 collective-permute-done._.hb_ref
  38.5 0.0 slice-start
  38.5 0.0 slice-start.1
  38.5 0.0 copy-start
  38.5 17.6 %heads.1 = (bf16[512,5120]{1,0:T(8,128)(2,1)S(1)}, f32[512,512]{1,0:T(8,128)S(1)}) custom-call(s32[6]{0:T(128)S(1)} %stack.23.sc_ref, bf16[512,512]{1,0:T(8,128)(2,1)} %get-tuple-element.19.h_ref, bf16[512,768]{1,0:T(8,128)(2,1)S(1)} %bitcast.16, bf16[512,5120]{1,0:T(8,128)(2,1)} %ws_ref.1, bf16[768,5120]{1,0:T(8,128)(2,1)} %wt_ref.1, ...), custom_call_target="tpu_custom_call" | custom-call | flops 9395240960 | bytes 23592960 | tf_op jit(solution)/shard_map/heads/pallas_call | solution.py:265
  56.1 0.1 collective-permute-start.2
  56.2 0.0 slice-done
  56.2 0.0 slice-done.1
  56.2 0.0 copy-done
  56.3 0.0 copy-start.4
  56.3 9.5 %back.1 = (bf16[4,3,256,512]{3,2,1,0:T(8,128)(2,1)}, bf16[4,256,512]{2,1,0:T(8,128)(2,1)}) custom-call(s32[6]{0:T(128)S(1)} %stack.23.sc_ref, f32[512,512]{1,0:T(8,128)S(1)} %get-tuple-element.21.g4_ref, bf16[4,512,512]{2,1,0:T(8,128)(2,1)S(1)} %get-tuple-element.22.h_ref, f32[4,512,512]{2,1,0:T(8,128)S(1)} %copy-done, bf16[4,3,512,512]{3,2,1,0:T(8,128)(2,1)S(1)} %bitcast.14), custom_call_target="tpu_custom_call" | custom-call | flops 2415919104 | bytes 16777216 | tf_op jit(solution)/shard_map/back/pallas_call | solution.py:390
  65.8 0.5 collective-permute-start.1
  66.3 0.0 collective-permute-done.2.gb_ref
  66.3 0.0 copy-done.4
  66.3 5.7 %head_grad.1._ = bf16[2,2,2,2,2,32,1280]{6,5,4,3,2,1,0:T(8,128)(2,1)} custom-call(s32[6]{0:T(128)S(1)} %stack.23.sc_ref, bf16[256,512]{1,0:T(8,128)(2,1)S(1)} %copy-done.4, bf16[256,512]{1,0:T(8,128)(2,1)S(1)} %collective-permute-done._.hb_ref, bf16[512,5120]{1,0:T(8,128)(2,1)S(1)} %get-tuple-element.27.ga_ref, ...), custom_call_target="tpu_custom_call" | custom-call | flops 2684354560 | bytes 13107200 | tf_op jit(solution)/shard_map/head_grad/pallas_call | solution.py:328
  72.0 0.0 copy-start.1
  72.0 4.7 %all-to-all-start.2 = ((bf16[8,128,1280]{2,1,0:T(8,128)(2,1)}), bf16[8,128,1280]{2,1,0:T(8,128)(2,1)}, u32[]{:S(2)}, u32[]{:S(2)}) async-start(bf16[8,128,1280]{2,1,0:T(8,128)(2,1)} %bitcast.11), calls=%async_computation.2 | async-start | bytes 5242880 | tf_op jit(solution)/shard_map/all_to_all | solution.py:74
  76.8 0.0 collective-permute-done.1.got_ref
  76.8 0.0 copy-done.1
  76.8 8.2 %conv_grad.1 = (bf16[12,2,2,32,128]{4,3,2,1,0:T(8,128)(2,1)S(1)}, bf16[12,2,2,32,128]{4,3,2,1,0:T(8,128)(2,1)S(1)}, bf16[12,2,2,32,128]{4,3,2,1,0:T(8,128)(2,1)S...) custom-call(s32[6]{0:T(128)S(1)} %stack.23.sc_ref, ...), custom_call_target="tpu_custom_call" | custom-call | flops 3221225472 | bytes 10485760 | tf_op jit(solution)/shard_map/conv_grad/pallas_call | solution.py:474
  85.0 1.9 %collective-permute-start.3 = (bf16[12,2,2,32,128]{4,3,2,1,0:T(8,128)(2,1)S(1)}, bf16[12,2,2,32,128]{4,3,2,1,0:T(8,128)(2,1)S(1)}, u32[]{:S(2)}, u32[]{:S(2)}) collective-permute-start(bf16[12,2,2,32,128]{4,3,2,1,0:T(8,128)(2,1)S(1)} %get-tuple-element.29), channel_id=1, source_target_pairs={{0,16},{16,0},{2,18},{18,2},{64,80},{80,64},{66,82},{82,66},{48,32... | collective-permute-start | bytes 1179656 | tf_op jit(solution)/shard_map/ppermute | solution.py:58
  86.9 1.3 collective-permute-start.4
  88.2 1.5 %collective-permute-start.5 = (bf16[12,2,2,32,128]{4,3,2,1,0:T(8,128)(2,1)}, bf16[12,2,2,32,128]{4,3,2,1,0:T(8,128)(2,1)S(1)}, u32[]{:S(2)}, u32[]{:S(2)}) collective-permute-start(bf16[12,2,2,32,128]{4,3,2,1,0:T(8,128)(2,1)} %get-tuple-element.31), channel_id=1, source_target_pairs={{0,82},{16,66},{2,80},{18,64},{64,18},{80,2},{66,16},{82,0},{48,98... | collective-permute-start | bytes 1179656 | tf_op jit(solution)/shard_map/ppermute | solution.py:58
  89.7 1.4 %collective-permute-start.6 = (bf16[12,2,2,32,128]{4,3,2,1,0:T(8,128)(2,1)}, bf16[12,2,2,32,128]{4,3,2,1,0:T(8,128)(2,1)S(1)}, u32[]{:S(2)}, u32[]{:S(2)}) collective-permute-start(bf16[12,2,2,32,128]{4,3,2,1,0:T(8,128)(2,1)} %get-tuple-element.32), channel_id=1, source_target_pairs={{0,66},{16,82},{2,64},{18,80},{64,2},{80,18},{66,0},{82,16},{48,11... | collective-permute-start | bytes 1179656 | tf_op jit(solution)/shard_map/ppermute | solution.py:58
  91.1 2.4 %collective-permute-start.7 = (bf16[12,2,2,32,128]{4,3,2,1,0:T(8,128)(2,1)}, bf16[12,2,2,32,128]{4,3,2,1,0:T(8,128)(2,1)S(1)}, u32[]{:S(2)}, u32[]{:S(2)}) collective-permute-start(bf16[12,2,2,32,128]{4,3,2,1,0:T(8,128)(2,1)} %get-tuple-element.33), channel_id=1, source_target_pairs={{0,80},{16,64},{2,82},{18,66},{64,16},{80,0},{66,18},{82,2},{48,96... | collective-permute-start | bytes 1179656 | tf_op jit(solution)/shard_map/ppermute | solution.py:58
  93.5 9.5 %collective-permute-done.3.refs_1_.refs_9_ = bf16[12,2,2,32,128]{4,3,2,1,0:T(8,128)(2,1)S(1)} collective-permute-done((bf16[12,2,2,32,128]{4,3,2,1,0:T(8,128)(2,1)S(1)}, bf16[12,2,2,32,128]{4,3,2,1,0:T(8,128)(2,1)S(1)}, u32[]{:S(2)}, u32[]{:S(2)}) %collective-permute-start.3) | collective-permute-done | bytes 393248 | tf_op jit(solution)/shard_map/ppermute | solution.py:58
  103.0 0.9 collective-permute-start.8
  103.8 4.7 %collective-permute-done.4.refs_2_.refs_10_ = bf16[12,2,2,32,128]{4,3,2,1,0:T(8,128)(2,1)S(1)} collective-permute-done((bf16[12,2,2,32,128]{4,3,2,1,0:T(8,128)(2,1)S(1)}, bf16[12,2,2,32,128]{4,3,2,1,0:T(8,128)(2,1)S(1)}, u32[]{:S(2)}, u32[]{:S(2)}) %collective-permute-start.4) | collective-permute-done | bytes 393248 | tf_op jit(solution)/shard_map/ppermute | solution.py:58
  108.5 2.2 %collective-permute-start.9 = (bf16[12,2,2,32,128]{4,3,2,1,0:T(8,128)(2,1)}, bf16[12,2,2,32,128]{4,3,2,1,0:T(8,128)(2,1)S(1)}, u32[]{:S(2)}, u32[]{:S(2)}) collective-permute-start(bf16[12,2,2,32,128]{4,3,2,1,0:T(8,128)(2,1)} %get-tuple-element.35), channel_id=1, source_target_pairs={{0,64},{16,80},{2,66},{18,82},{64,0},{80,16},{66,2},{82,18},{48,11... | collective-permute-start | bytes 1179656 | tf_op jit(solution)/shard_map/ppermute | solution.py:58
  110.7 0.0 all-to-all-done.2
  110.7 2.8 %head_far.1.refs_16_ = bf16[8,5,32,128]{3,2,1,0:T(8,128)(2,1)S(1)} custom-call(bf16[8,2,2,32,1280]{4,3,2,1,0:T(8,128)(2,1)} %bitcast.12.got_ref), custom_call_target="tpu_custom_call" | custom-call | flops 10485760 | bytes 3932160 | tf_op jit(solution)/shard_map/head_far/pallas_call | solution.py:519
  113.5 0.0 collective-permute-done.5.refs_3_.refs_11_
  113.5 0.0 collective-permute-done.6.refs_4_.refs_12_
  113.5 0.0 collective-permute-done.7.refs_5_.refs_13_
  113.5 0.0 collective-permute-done.8.refs_6_.refs_14_
  113.5 3.1 %collective-permute-done.9.refs_7_.refs_15_ = bf16[12,2,2,32,128]{4,3,2,1,0:T(8,128)(2,1)S(1)} collective-permute-done((bf16[12,2,2,32,128]{4,3,2,1,0:T(8,128)(2,1)}, bf16[12,2,2,32,128]{4,3,2,1,0:T(8,128)(2,1)S(1)}, u32[]{:S(2)}, u32[]{:S(2)}) %collective-permute-start.9) | collective-permute-done | bytes 393248 | tf_op jit(solution)/shard_map/ppermute | solution.py:58
  116.6 1.6 %conv_far.1 = bf16[8,11,32,128]{3,2,1,0:T(8,128)(2,1)S(1)} custom-call(bf16[12,2,2,32,128]{4,3,2,1,0:T(8,128)(2,1)S(1)} %get-tuple-element.28.refs_0_.refs_8_, bf16[12,2,2,32,128]{4,3,2,1,0:T(8,128)(2,1)S(1)} %collective-permute-done.3.refs_1_.refs_9_, bf16[12,2,2,32,128]{4,3,2,1,0:T(8,128)(2,1)S(1)} %collective-permute-done.4.refs_2_.refs_10_, ...), custom_call_target="tpu_custom_call" | custom-call | flops 12582912 | bytes 4718592 | tf_op jit(solution)/shard_map/conv_far/pallas_call | solution.py:558
  118.2 20.6 %all_to_all.20.got_ref = bf16[8,11,32,128]{3,2,1,0:T(8,128)(2,1)S(1)} all-to-all(bf16[8,11,32,128]{3,2,1,0:T(8,128)(2,1)S(1)} %conv_far.1), channel_id=1, replica_groups={{0,48,6,54,65,113,71,119},{16,32,22,38,81,97,87,103},{2,50,4,52,67,115,..., dimensions={0} | all-to-all | bytes 1441792 | tf_op jit(solution)/shard_map/all_to_all | solution.py:74
  138.8 0.9 finish.1
  (1 shorter events, 0.0 us)
Async XLA Ops:
  0.6 1.0 copy-start.3
  2.9 18.6 %all-to-all-start = ((bf16[8,64,512]{2,1,0:T(8,128)(2,1)}), bf16[8,64,512]{2,1,0:T(8,128)(2,1)S(1)}, u32[]{:S(2)}, u32[]{:S(2)}) async-start(bf16[8,64,512]{2,1,0:T(8,128)(2,1)} %bitcast.6), calls=%async_computation | async-start | bytes 1048576 | tf_op jit(solution)/shard_map/all_to_all | solution.py:74
  10.0 1.1 copy-start.2
  21.5 17.0 %all-to-all-start.1 = ((bf16[8,64,768]{2,1,0:T(8,128)(2,1)}), bf16[8,64,768]{2,1,0:T(8,128)(2,1)S(1)}, u32[]{:S(2)}, u32[]{:S(2)}) async-start(bf16[8,64,768]{2,1,0:T(8,128)(2,1)} %bitcast.9), calls=%async_computation.1 | async-start | bytes 1572864 | tf_op jit(solution)/shard_map/all_to_all | solution.py:74
  34.8 3.7 %collective-permute-start = (bf16[256,512]{1,0:T(8,128)(2,1)}, bf16[256,512]{1,0:T(8,128)(2,1)S(1)}, u32[]{:S(2)}, u32[]{:S(2)}) collective-permute-start(bf16[256,512]{1,0:T(8,128)(2,1)} %get-tuple-element.20), channel_id=1, source_target_pairs={{0,8},{1,9},{2,10},{3,11},{4,12},{5,13},{6,14},{7,15},{8,0},{9,1},... | collective-permute-start | bytes 786440 | tf_op jit(solution)/shard_map/ppermute | solution.py:600
  38.5 17.7 %slice-start = ((s8[6291456]{0:T(1024)(128)(4,1)}), s8[4194304]{0:T(1024)(128)(4,1)S(1)}, s32[]{:S(2)}) async-start(s8[6291456]{0:T(1024)(128)(4,1)} %bitcast.13), calls=%async_computation.4 | async-start | bytes 8388608
  38.5 17.7 %slice-start.1 = ((s8[6291456]{0:T(1024)(128)(4,1)}), s8[2097152]{0:T(1024)(128)(4,1)S(1)}, s32[]{:S(2)}) async-start(s8[6291456]{0:T(1024)(128)(4,1)} %bitcast.13), calls=%async_computation.5 | async-start | bytes 4194304
  38.5 17.7 %copy-start = (f32[4,512,512]{2,1,0:T(8,128)S(1)}, f32[4,512,512]{2,1,0:T(8,128)}, u32[]{:S(2)}) copy-start(f32[4,512,512]{2,1,0:T(8,128)} %get-tuple-element.23.pre_ref) | copy-start | bytes 12582916
  56.1 10.2 %collective-permute-start.2 = (bf16[512,5120]{1,0:T(8,128)(2,1)S(1)}, bf16[512,5120]{1,0:T(8,128)(2,1)S(1)}, u32[]{:S(2)}, u32[]{:S(2)}) collective-permute-start(bf16[512,5120]{1,0:T(8,128)(2,1)S(1)} %get-tuple-element.27.ga_ref), channel_id=1, source_target_pairs={{0,8},{1,9},{2,10},{3,11},{4,12},{5,13},{6,14},{7,15},{8,0},{9,1},... | collective-permute-start | bytes 15728648 | tf_op jit(solution)/shard_map/ppermute | solution.py:600
  56.3 10.0 %copy-start.4 = (bf16[256,512]{1,0:T(8,128)(2,1)S(1)}, bf16[256,512]{1,0:T(8,128)(2,1)}, u32[]{:S(2)}) copy-start(bf16[256,512]{1,0:T(8,128)(2,1)} %get-tuple-element.26.ha_ref) | copy-start | bytes 786436
  65.8 10.9 %collective-permute-start.1 = (bf16[4,3,256,512]{3,2,1,0:T(8,128)(2,1)}, bf16[4,3,256,512]{3,2,1,0:T(8,128)(2,1)}, u32[]{:S(2)}, u32[]{:S(2)}) collective-permute-start(bf16[4,3,256,512]{3,2,1,0:T(8,128)(2,1)} %get-tuple-element.25.send_ref), channel_id=1, source_target_pairs={{0,8},{1,9},{2,10},{3,11},{4,12},{5,13},{6,14},{7,15},{8,0},{9,1},... | collective-permute-start | bytes 9437192 | tf_op jit(solution)/shard_map/ppermute | solution.py:600
  72.0 4.8 %copy-start.1 = (bf16[4,256,512]{2,1,0:T(8,128)(2,1)S(1)}, bf16[4,256,512]{2,1,0:T(8,128)(2,1)}, u32[]{:S(2)}) copy-start(bf16[4,256,512]{2,1,0:T(8,128)(2,1)} %get-tuple-element.24._.mine_ref) | copy-start | bytes 3145732
  72.0 38.7 %all-to-all-start.2 = ((bf16[8,128,1280]{2,1,0:T(8,128)(2,1)}), bf16[8,128,1280]{2,1,0:T(8,128)(2,1)}, u32[]{:S(2)}, u32[]{:S(2)}) async-start(bf16[8,128,1280]{2,1,0:T(8,128)(2,1)} %bitcast.11), calls=%async_computation.2 | async-start | bytes 5242880 | tf_op jit(solution)/shard_map/all_to_all | solution.py:74
  85.0 18.0 %collective-permute-start.3 = (bf16[12,2,2,32,128]{4,3,2,1,0:T(8,128)(2,1)S(1)}, bf16[12,2,2,32,128]{4,3,2,1,0:T(8,128)(2,1)S(1)}, u32[]{:S(2)}, u32[]{:S(2)}) collective-permute-start(bf16[12,2,2,32,128]{4,3,2,1,0:T(8,128)(2,1)S(1)} %get-tuple-element.29), channel_id=1, source_target_pairs={{0,16},{16,0},{2,18},{18,2},{64,80},{80,64},{66,82},{82,66},{48,32... | collective-permute-start | bytes 1179656 | tf_op jit(solution)/shard_map/ppermute | solution.py:58
  86.9 21.6 %collective-permute-start.4 = (bf16[12,2,2,32,128]{4,3,2,1,0:T(8,128)(2,1)S(1)}, bf16[12,2,2,32,128]{4,3,2,1,0:T(8,128)(2,1)S(1)}, u32[]{:S(2)}, u32[]{:S(2)}) collective-permute-start(bf16[12,2,2,32,128]{4,3,2,1,0:T(8,128)(2,1)S(1)} %get-tuple-element.30), channel_id=1, source_target_pairs={{0,2},{16,18},{2,0},{18,16},{64,66},{80,82},{66,64},{82,80},{48,50... | collective-permute-start | bytes 1179656 | tf_op jit(solution)/shard_map/ppermute | solution.py:58
  88.2 25.3 %collective-permute-start.5 = (bf16[12,2,2,32,128]{4,3,2,1,0:T(8,128)(2,1)}, bf16[12,2,2,32,128]{4,3,2,1,0:T(8,128)(2,1)S(1)}, u32[]{:S(2)}, u32[]{:S(2)}) collective-permute-start(bf16[12,2,2,32,128]{4,3,2,1,0:T(8,128)(2,1)} %get-tuple-element.31), channel_id=1, source_target_pairs={{0,82},{16,66},{2,80},{18,64},{64,18},{80,2},{66,16},{82,0},{48,98... | collective-permute-start | bytes 1179656 | tf_op jit(solution)/shard_map/ppermute | solution.py:58
  89.7 23.8 %collective-permute-start.6 = (bf16[12,2,2,32,128]{4,3,2,1,0:T(8,128)(2,1)}, bf16[12,2,2,32,128]{4,3,2,1,0:T(8,128)(2,1)S(1)}, u32[]{:S(2)}, u32[]{:S(2)}) collective-permute-start(bf16[12,2,2,32,128]{4,3,2,1,0:T(8,128)(2,1)} %get-tuple-element.32), channel_id=1, source_target_pairs={{0,66},{16,82},{2,64},{18,80},{64,2},{80,18},{66,0},{82,16},{48,11... | collective-permute-start | bytes 1179656 | tf_op jit(solution)/shard_map/ppermute | solution.py:58
  91.1 22.4 %collective-permute-start.7 = (bf16[12,2,2,32,128]{4,3,2,1,0:T(8,128)(2,1)}, bf16[12,2,2,32,128]{4,3,2,1,0:T(8,128)(2,1)S(1)}, u32[]{:S(2)}, u32[]{:S(2)}) collective-permute-start(bf16[12,2,2,32,128]{4,3,2,1,0:T(8,128)(2,1)} %get-tuple-element.33), channel_id=1, source_target_pairs={{0,80},{16,64},{2,82},{18,66},{64,16},{80,0},{66,18},{82,2},{48,96... | collective-permute-start | bytes 1179656 | tf_op jit(solution)/shard_map/ppermute | solution.py:58
  103.0 10.5 %collective-permute-start.8 = (bf16[12,2,2,32,128]{4,3,2,1,0:T(8,128)(2,1)}, bf16[12,2,2,32,128]{4,3,2,1,0:T(8,128)(2,1)S(1)}, u32[]{:S(2)}, u32[]{:S(2)}) collective-permute-start(bf16[12,2,2,32,128]{4,3,2,1,0:T(8,128)(2,1)} %get-tuple-element.34), channel_id=1, source_target_pairs={{0,18},{16,2},{2,16},{18,0},{64,82},{80,66},{66,80},{82,64},{48,34... | collective-permute-start | bytes 1179656 | tf_op jit(solution)/shard_map/ppermute | solution.py:58
  108.5 8.1 %collective-permute-start.9 = (bf16[12,2,2,32,128]{4,3,2,1,0:T(8,128)(2,1)}, bf16[12,2,2,32,128]{4,3,2,1,0:T(8,128)(2,1)S(1)}, u32[]{:S(2)}, u32[]{:S(2)}) collective-permute-start(bf16[12,2,2,32,128]{4,3,2,1,0:T(8,128)(2,1)} %get-tuple-element.35), channel_id=1, source_target_pairs={{0,64},{16,80},{2,66},{18,82},{64,0},{80,16},{66,2},{82,18},{48,11... | collective-permute-start | bytes 1179656 | tf_op jit(solution)/shard_map/ppermute | solution.py:58

commit v12 on v10

--- a/solution.py
+++ b/solution.py
@@ -629,7 +629,7 @@
     near = head_grad(sc, h_mine, h_got, score, score_got, mine)
     head_got = exchange(near.reshape(8, 4 * 32, scores // 4), near_groups())
     parts = conv_grad(sc, mine, send, got, near)
-    conv_got = [parts[0]] + [near_swap(parts[i], i) for i in range(1, 8)]
+    conv_got = [parts[0]] + [near_swap(parts[i], i) for i in (1, 2, 7, 6, 5, 3, 4)]
 
     far = head_far(head_got.reshape(8, 2, 2, 32, scores // 4))
     far = conv_far(conv_got, far)

time: 142 us -> 140 us (0.986); the launches traced: 139 us -> 140 us
  starting transfers between devices: 25.3 us -> 27.4 us
  waiting for transfers between devices: 31.7 us -> 30 us
    ppermute x7, starting transfers between devices: 9.48 us -> 11.6 us  [near_swap(): return lax.ppermute(x, AXES, pairs)]
    ppermute x7, waiting for transfers between devices: 19 us -> 17.3 us  [near_swap(): return lax.ppermute(x, AXES, pairs)]
  transfers between devices with their start and end apart: 13 -> 13, of which waited for: 7 -> 5; matrix products, arithmetic and copies ran while one was open for 0% -> 0% of each run, Pallas kernels for 26% -> 26%
where the time goes in v12:
time: 140 us
  Pallas kernels  57.8 us (41%)
  waiting for transfers between devices  30 us (21%)
  starting transfers between devices  27.4 us (20%)
  blocking collectives  20.5 us (15%)
  local copies, waits for them, and re-layouts  2.27 us (2%)
  between operations  1.54 us (1%)
    all_to_all x1, blocking collectives, exchange(): return lax.all_to_all(x, AXES, 0, 0, tiled=True, axis_index_groups=groups)  20.5 us
    pallas_call x1, Pallas kernels, heads(): pl.pallas_call(functools.partial(head_kernel, 5.0 * loss_scale, tiles), g...  17.6 us
    ppermute x7, waiting for transfers between devices, near_swap(): return lax.ppermute(x, AXES, pairs)  17.3 us
    all_to_all x3, starting transfers between devices, exchange(): return lax.all_to_all(x, AXES, 0, 0, tiled=True, axis_index_groups=groups)  15.3 us
    all_to_all x3, waiting for transfers between devices, exchange(): return lax.all_to_all(x, AXES, 0, 0, tiled=True, axis_index_groups=groups)  12.7 us
    ppermute x7, starting transfers between devices, near_swap(): return lax.ppermute(x, AXES, pairs)  11.6 us
    pallas_call x1, Pallas kernels, back(): pl.pallas_call(back_kernel, grid=(LAYERS,), in_specs=[pl.BlockSpec(memory...  9.35 us
    pallas_call x1, Pallas kernels, convolve(): pl.pallas_call(conv_kernel, grid=(LAYERS,), in_specs=[pl.BlockSpec(memory...  8.82 us
  transfers between devices with their start and end apart: 13, of which 5 were waited for; matrix products, arithmetic and copies ran while one was open for 0% of the time, Pallas kernels for 26%

profile of v12, /device:TPU:0, one launch (start us, length us, event | category | flops | bytes accessed | tf_op | source)
XLA Modules:
  0.0 139.5 jit_solution(12001005977130438917)
XLA Ops:
  0.6 0.0 copy-start.3
  0.6 1.0 copy-done.3
  1.7 1.3 regroup.2
  2.9 7.0 %all-to-all-start = ((bf16[8,64,512]{2,1,0:T(8,128)(2,1)}), bf16[8,64,512]{2,1,0:T(8,128)(2,1)S(1)}, u32[]{:S(2)}, u32[]{:S(2)}) async-start(bf16[8,64,512]{2,1,0:T(8,128)(2,1)} %bitcast.6), calls=%async_computation | async-start | bytes 1048576 | tf_op jit(solution)/shard_map/all_to_all | solution.py:74
  10.0 0.0 copy-start.2
  10.0 1.1 copy-done.2
  11.1 1.5 %regroup.3 = bf16[512,768]{1,0:T(8,128)(2,1)} custom-call(bf16[512,768]{1,0:T(8,128)(2,1)S(1)} %bitcast.15), custom_call_target="tpu_custom_call" | custom-call | tf_op jit(solution)/shard_map/regroup/pallas_call | solution.py:130
  12.6 9.0 %all-to-all-done = bf16[8,64,512]{2,1,0:T(8,128)(2,1)S(1)} async-done(((bf16[8,64,512]{2,1,0:T(8,128)(2,1)}), bf16[8,64,512]{2,1,0:T(8,128)(2,1)S(1)}, u32[]{:S(2)}, u32[]{:S(2)}) %all-to-all-start) | async-done | bytes 524320 | tf_op jit(solution)/shard_map/all_to_all | solution.py:74
  21.5 3.5 %all-to-all-start.1 = ((bf16[8,64,768]{2,1,0:T(8,128)(2,1)}), bf16[8,64,768]{2,1,0:T(8,128)(2,1)S(1)}, u32[]{:S(2)}, u32[]{:S(2)}) async-start(bf16[8,64,768]{2,1,0:T(8,128)(2,1)} %bitcast.9), calls=%async_computation.1 | async-start | bytes 1572864 | tf_op jit(solution)/shard_map/all_to_all | solution.py:74
  25.8 0.1 stack.23.sc_ref
  25.9 8.8 %convolve.1 = (bf16[4,512,512]{2,1,0:T(8,128)(2,1)S(1)}, f32[4,512,512]{2,1,0:T(8,128)}, bf16[512,512]{1,0:T(8,128)(2,1)}, bf16[256,512]{1,0:T(8,128)(2,1)}, bf16[256,512]{1,0:T(8,128)(2,1)}) custom-call(s32[6]{0:T(128)S(1)} %stack.23.sc_ref, bf16[512,512]{1,0:T(8,128)(2,1)S(1)} %bitcast.18, bf16[4,3,512,512]{3,2,1,0:T(8,128)(2,1)} %w_ref.3), custom_call_target="tpu_custom_call" | custom-call | flops 3221225472 | bytes 12582912 | tf_op jit(solution)/shard_map/convolve/pallas_call | solution.py:185
  34.7 0.0 collective-permute-start
  34.7 3.8 %all-to-all-done.1 = bf16[8,64,768]{2,1,0:T(8,128)(2,1)S(1)} async-done(((bf16[8,64,768]{2,1,0:T(8,128)(2,1)}), bf16[8,64,768]{2,1,0:T(8,128)(2,1)S(1)}, u32[]{:S(2)}, u32[]{:S(2)}) %all-to-all-start.1) | async-done | bytes 786464 | tf_op jit(solution)/shard_map/all_to_all | solution.py:74
  38.5 0.0 collective-permute-done._.hb_ref
  38.5 0.0 slice-start
  38.5 0.0 slice-start.1
  38.5 0.0 copy-start
  38.5 17.6 %heads.1 = (bf16[512,5120]{1,0:T(8,128)(2,1)S(1)}, f32[512,512]{1,0:T(8,128)S(1)}) custom-call(s32[6]{0:T(128)S(1)} %stack.23.sc_ref, bf16[512,512]{1,0:T(8,128)(2,1)} %get-tuple-element.19.h_ref, bf16[512,768]{1,0:T(8,128)(2,1)S(1)} %bitcast.16, bf16[512,5120]{1,0:T(8,128)(2,1)} %ws_ref.1, bf16[768,5120]{1,0:T(8,128)(2,1)} %wt_ref.1, ...), custom_call_target="tpu_custom_call" | custom-call | flops 9395240960 | bytes 23592960 | tf_op jit(solution)/shard_map/heads/pallas_call | solution.py:265
  56.1 0.1 collective-permute-start.2
  56.2 0.0 slice-done
  56.2 0.0 slice-done.1
  56.2 0.0 copy-done
  56.3 0.0 copy-start.4
  56.3 9.4 %back.1 = (bf16[4,3,256,512]{3,2,1,0:T(8,128)(2,1)}, bf16[4,256,512]{2,1,0:T(8,128)(2,1)}) custom-call(s32[6]{0:T(128)S(1)} %stack.23.sc_ref, f32[512,512]{1,0:T(8,128)S(1)} %get-tuple-element.21.g4_ref, bf16[4,512,512]{2,1,0:T(8,128)(2,1)S(1)} %get-tuple-element.22.h_ref, f32[4,512,512]{2,1,0:T(8,128)S(1)} %copy-done, bf16[4,3,512,512]{3,2,1,0:T(8,128)(2,1)S(1)} %bitcast.14), custom_call_target="tpu_custom_call" | custom-call | flops 2415919104 | bytes 16777216 | tf_op jit(solution)/shard_map/back/pallas_call | solution.py:390
  65.6 0.5 collective-permute-start.1
  66.1 0.0 collective-permute-done.2.gb_ref
  66.1 0.0 copy-done.4
  66.1 5.7 %head_grad.1._ = bf16[2,2,2,2,2,32,1280]{6,5,4,3,2,1,0:T(8,128)(2,1)} custom-call(s32[6]{0:T(128)S(1)} %stack.23.sc_ref, bf16[256,512]{1,0:T(8,128)(2,1)S(1)} %copy-done.4, bf16[256,512]{1,0:T(8,128)(2,1)S(1)} %collective-permute-done._.hb_ref, bf16[512,5120]{1,0:T(8,128)(2,1)S(1)} %get-tuple-element.27.ga_ref, ...), custom_call_target="tpu_custom_call" | custom-call | flops 2684354560 | bytes 13107200 | tf_op jit(solution)/shard_map/head_grad/pallas_call | solution.py:328
  71.8 0.0 copy-start.1
  71.8 4.7 %all-to-all-start.2 = ((bf16[8,128,1280]{2,1,0:T(8,128)(2,1)}), bf16[8,128,1280]{2,1,0:T(8,128)(2,1)}, u32[]{:S(2)}, u32[]{:S(2)}) async-start(bf16[8,128,1280]{2,1,0:T(8,128)(2,1)} %bitcast.11), calls=%async_computation.2 | async-start | bytes 5242880 | tf_op jit(solution)/shard_map/all_to_all | solution.py:74
  76.6 0.0 collective-permute-done.1.got_ref
  76.6 0.0 copy-done.1
  76.6 8.2 %conv_grad.1 = (bf16[12,2,2,32,128]{4,3,2,1,0:T(8,128)(2,1)S(1)}, bf16[12,2,2,32,128]{4,3,2,1,0:T(8,128)(2,1)S(1)}, bf16[12,2,2,32,128]{4,3,2,1,0:T(8,128)(2,1)S...) custom-call(s32[6]{0:T(128)S(1)} %stack.23.sc_ref, ...), custom_call_target="tpu_custom_call" | custom-call | flops 3221225472 | bytes 10485760 | tf_op jit(solution)/shard_map/conv_grad/pallas_call | solution.py:474
  84.8 1.9 %collective-permute-start.3 = (bf16[12,2,2,32,128]{4,3,2,1,0:T(8,128)(2,1)S(1)}, bf16[12,2,2,32,128]{4,3,2,1,0:T(8,128)(2,1)S(1)}, u32[]{:S(2)}, u32[]{:S(2)}) collective-permute-start(bf16[12,2,2,32,128]{4,3,2,1,0:T(8,128)(2,1)S(1)} %get-tuple-element.29), channel_id=1, source_target_pairs={{0,16},{16,0},{2,18},{18,2},{64,80},{80,64},{66,82},{82,66},{48,32... | collective-permute-start | bytes 1179656 | tf_op jit(solution)/shard_map/ppermute | solution.py:58
  86.7 1.3 collective-permute-start.4
  88.0 1.5 %collective-permute-start.5 = (bf16[12,2,2,32,128]{4,3,2,1,0:T(8,128)(2,1)}, bf16[12,2,2,32,128]{4,3,2,1,0:T(8,128)(2,1)S(1)}, u32[]{:S(2)}, u32[]{:S(2)}) collective-permute-start(bf16[12,2,2,32,128]{4,3,2,1,0:T(8,128)(2,1)} %get-tuple-element.31), channel_id=1, source_target_pairs={{0,82},{16,66},{2,80},{18,64},{64,18},{80,2},{66,16},{82,0},{48,98... | collective-permute-start | bytes 1179656 | tf_op jit(solution)/shard_map/ppermute | solution.py:58
  89.5 1.4 %collective-permute-start.6 = (bf16[12,2,2,32,128]{4,3,2,1,0:T(8,128)(2,1)}, bf16[12,2,2,32,128]{4,3,2,1,0:T(8,128)(2,1)S(1)}, u32[]{:S(2)}, u32[]{:S(2)}) collective-permute-start(bf16[12,2,2,32,128]{4,3,2,1,0:T(8,128)(2,1)} %get-tuple-element.32), channel_id=1, source_target_pairs={{0,66},{16,82},{2,64},{18,80},{64,2},{80,18},{66,0},{82,16},{48,11... | collective-permute-start | bytes 1179656 | tf_op jit(solution)/shard_map/ppermute | solution.py:58
  90.9 2.4 %collective-permute-start.7 = (bf16[12,2,2,32,128]{4,3,2,1,0:T(8,128)(2,1)}, bf16[12,2,2,32,128]{4,3,2,1,0:T(8,128)(2,1)S(1)}, u32[]{:S(2)}, u32[]{:S(2)}) collective-permute-start(bf16[12,2,2,32,128]{4,3,2,1,0:T(8,128)(2,1)} %get-tuple-element.33), channel_id=1, source_target_pairs={{0,80},{16,64},{2,82},{18,66},{64,16},{80,0},{66,18},{82,2},{48,96... | collective-permute-start | bytes 1179656 | tf_op jit(solution)/shard_map/ppermute | solution.py:58
  93.3 9.5 %collective-permute-done.3.refs_1_.refs_9_ = bf16[12,2,2,32,128]{4,3,2,1,0:T(8,128)(2,1)S(1)} collective-permute-done((bf16[12,2,2,32,128]{4,3,2,1,0:T(8,128)(2,1)S(1)}, bf16[12,2,2,32,128]{4,3,2,1,0:T(8,128)(2,1)S(1)}, u32[]{:S(2)}, u32[]{:S(2)}) %collective-permute-start.3) | collective-permute-done | bytes 393248 | tf_op jit(solution)/shard_map/ppermute | solution.py:58
  102.8 0.9 collective-permute-start.8
  103.6 4.7 %collective-permute-done.4.refs_2_.refs_10_ = bf16[12,2,2,32,128]{4,3,2,1,0:T(8,128)(2,1)S(1)} collective-permute-done((bf16[12,2,2,32,128]{4,3,2,1,0:T(8,128)(2,1)S(1)}, bf16[12,2,2,32,128]{4,3,2,1,0:T(8,128)(2,1)S(1)}, u32[]{:S(2)}, u32[]{:S(2)}) %collective-permute-start.4) | collective-permute-done | bytes 393248 | tf_op jit(solution)/shard_map/ppermute | solution.py:58
  108.3 2.2 %collective-permute-start.9 = (bf16[12,2,2,32,128]{4,3,2,1,0:T(8,128)(2,1)}, bf16[12,2,2,32,128]{4,3,2,1,0:T(8,128)(2,1)S(1)}, u32[]{:S(2)}, u32[]{:S(2)}) collective-permute-start(bf16[12,2,2,32,128]{4,3,2,1,0:T(8,128)(2,1)} %get-tuple-element.35), channel_id=1, source_target_pairs={{0,64},{16,80},{2,66},{18,82},{64,0},{80,16},{66,2},{82,18},{48,11... | collective-permute-start | bytes 1179656 | tf_op jit(solution)/shard_map/ppermute | solution.py:58
  110.5 0.0 all-to-all-done.2
  110.5 2.8 %head_far.1.refs_16_ = bf16[8,5,32,128]{3,2,1,0:T(8,128)(2,1)S(1)} custom-call(bf16[8,2,2,32,1280]{4,3,2,1,0:T(8,128)(2,1)} %bitcast.12.got_ref), custom_call_target="tpu_custom_call" | custom-call | flops 10485760 | bytes 3932160 | tf_op jit(solution)/shard_map/head_far/pallas_call | solution.py:519
  113.3 0.0 collective-permute-done.5.refs_3_.refs_11_
  113.3 0.0 collective-permute-done.6.refs_4_.refs_12_
  113.3 0.0 collective-permute-done.7.refs_5_.refs_13_
  113.3 0.0 collective-permute-done.8.refs_6_.refs_14_
  113.3 3.1 %collective-permute-done.9.refs_7_.refs_15_ = bf16[12,2,2,32,128]{4,3,2,1,0:T(8,128)(2,1)S(1)} collective-permute-done((bf16[12,2,2,32,128]{4,3,2,1,0:T(8,128)(2,1)}, bf16[12,2,2,32,128]{4,3,2,1,0:T(8,128)(2,1)S(1)}, u32[]{:S(2)}, u32[]{:S(2)}) %collective-permute-start.9) | collective-permute-done | bytes 393248 | tf_op jit(solution)/shard_map/ppermute | solution.py:58
  116.5 1.6 %conv_far.1 = bf16[8,11,32,128]{3,2,1,0:T(8,128)(2,1)S(1)} custom-call(bf16[12,2,2,32,128]{4,3,2,1,0:T(8,128)(2,1)S(1)} %get-tuple-element.28.refs_0_.refs_8_, bf16[12,2,2,32,128]{4,3,2,1,0:T(8,128)(2,1)S(1)} %collective-permute-done.3.refs_1_.refs_9_, bf16[12,2,2,32,128]{4,3,2,1,0:T(8,128)(2,1)S(1)} %collective-permute-done.4.refs_2_.refs_10_, ...), custom_call_target="tpu_custom_call" | custom-call | flops 12582912 | bytes 4718592 | tf_op jit(solution)/shard_map/conv_far/pallas_call | solution.py:558
  118.0 20.5 %all_to_all.20.got_ref = bf16[8,11,32,128]{3,2,1,0:T(8,128)(2,1)S(1)} all-to-all(bf16[8,11,32,128]{3,2,1,0:T(8,128)(2,1)S(1)} %conv_far.1), channel_id=1, replica_groups={{0,48,6,54,65,113,71,119},{16,32,22,38,81,97,87,103},{2,50,4,52,67,115,..., dimensions={0} | all-to-all | bytes 1441792 | tf_op jit(solution)/shard_map/all_to_all | solution.py:74
  138.6 0.9 finish.1
  (1 shorter events, 0.0 us)
Async XLA Ops:
  0.6 1.0 copy-start.3
  2.9 18.6 %all-to-all-start = ((bf16[8,64,512]{2,1,0:T(8,128)(2,1)}), bf16[8,64,512]{2,1,0:T(8,128)(2,1)S(1)}, u32[]{:S(2)}, u32[]{:S(2)}) async-start(bf16[8,64,512]{2,1,0:T(8,128)(2,1)} %bitcast.6), calls=%async_computation | async-start | bytes 1048576 | tf_op jit(solution)/shard_map/all_to_all | solution.py:74
  10.0 1.1 copy-start.2
  21.5 17.0 %all-to-all-start.1 = ((bf16[8,64,768]{2,1,0:T(8,128)(2,1)}), bf16[8,64,768]{2,1,0:T(8,128)(2,1)S(1)}, u32[]{:S(2)}, u32[]{:S(2)}) async-start(bf16[8,64,768]{2,1,0:T(8,128)(2,1)} %bitcast.9), calls=%async_computation.1 | async-start | bytes 1572864 | tf_op jit(solution)/shard_map/all_to_all | solution.py:74
  34.7 3.8 %collective-permute-start = (bf16[256,512]{1,0:T(8,128)(2,1)}, bf16[256,512]{1,0:T(8,128)(2,1)S(1)}, u32[]{:S(2)}, u32[]{:S(2)}) collective-permute-start(bf16[256,512]{1,0:T(8,128)(2,1)} %get-tuple-element.20), channel_id=1, source_target_pairs={{0,8},{1,9},{2,10},{3,11},{4,12},{5,13},{6,14},{7,15},{8,0},{9,1},... | collective-permute-start | bytes 786440 | tf_op jit(solution)/shard_map/ppermute | solution.py:600
  38.5 17.7 %slice-start = ((s8[6291456]{0:T(1024)(128)(4,1)}), s8[4194304]{0:T(1024)(128)(4,1)S(1)}, s32[]{:S(2)}) async-start(s8[6291456]{0:T(1024)(128)(4,1)} %bitcast.13), calls=%async_computation.4 | async-start | bytes 8388608
  38.5 17.7 %slice-start.1 = ((s8[6291456]{0:T(1024)(128)(4,1)}), s8[2097152]{0:T(1024)(128)(4,1)S(1)}, s32[]{:S(2)}) async-start(s8[6291456]{0:T(1024)(128)(4,1)} %bitcast.13), calls=%async_computation.5 | async-start | bytes 4194304
  38.5 17.7 %copy-start = (f32[4,512,512]{2,1,0:T(8,128)S(1)}, f32[4,512,512]{2,1,0:T(8,128)}, u32[]{:S(2)}) copy-start(f32[4,512,512]{2,1,0:T(8,128)} %get-tuple-element.23.pre_ref) | copy-start | bytes 12582916
  56.1 10.0 %collective-permute-start.2 = (bf16[512,5120]{1,0:T(8,128)(2,1)S(1)}, bf16[512,5120]{1,0:T(8,128)(2,1)S(1)}, u32[]{:S(2)}, u32[]{:S(2)}) collective-permute-start(bf16[512,5120]{1,0:T(8,128)(2,1)S(1)} %get-tuple-element.27.ga_ref), channel_id=1, source_target_pairs={{0,8},{1,9},{2,10},{3,11},{4,12},{5,13},{6,14},{7,15},{8,0},{9,1},... | collective-permute-start | bytes 15728648 | tf_op jit(solution)/shard_map/ppermute | solution.py:600
  56.3 9.8 %copy-start.4 = (bf16[256,512]{1,0:T(8,128)(2,1)S(1)}, bf16[256,512]{1,0:T(8,128)(2,1)}, u32[]{:S(2)}) copy-start(bf16[256,512]{1,0:T(8,128)(2,1)} %get-tuple-element.26.ha_ref) | copy-start | bytes 786436
  65.6 10.9 %collective-permute-start.1 = (bf16[4,3,256,512]{3,2,1,0:T(8,128)(2,1)}, bf16[4,3,256,512]{3,2,1,0:T(8,128)(2,1)}, u32[]{:S(2)}, u32[]{:S(2)}) collective-permute-start(bf16[4,3,256,512]{3,2,1,0:T(8,128)(2,1)} %get-tuple-element.25.send_ref), channel_id=1, source_target_pairs={{0,8},{1,9},{2,10},{3,11},{4,12},{5,13},{6,14},{7,15},{8,0},{9,1},... | collective-permute-start | bytes 9437192 | tf_op jit(solution)/shard_map/ppermute | solution.py:600
  71.8 4.8 %copy-start.1 = (bf16[4,256,512]{2,1,0:T(8,128)(2,1)S(1)}, bf16[4,256,512]{2,1,0:T(8,128)(2,1)}, u32[]{:S(2)}) copy-start(bf16[4,256,512]{2,1,0:T(8,128)(2,1)} %get-tuple-element.24._.mine_ref) | copy-start | bytes 3145732
  71.8 38.7 %all-to-all-start.2 = ((bf16[8,128,1280]{2,1,0:T(8,128)(2,1)}), bf16[8,128,1280]{2,1,0:T(8,128)(2,1)}, u32[]{:S(2)}, u32[]{:S(2)}) async-start(bf16[8,128,1280]{2,1,0:T(8,128)(2,1)} %bitcast.11), calls=%async_computation.2 | async-start | bytes 5242880 | tf_op jit(solution)/shard_map/all_to_all | solution.py:74
  84.8 18.0 %collective-permute-start.3 = (bf16[12,2,2,32,128]{4,3,2,1,0:T(8,128)(2,1)S(1)}, bf16[12,2,2,32,128]{4,3,2,1,0:T(8,128)(2,1)S(1)}, u32[]{:S(2)}, u32[]{:S(2)}) collective-permute-start(bf16[12,2,2,32,128]{4,3,2,1,0:T(8,128)(2,1)S(1)} %get-tuple-element.29), channel_id=1, source_target_pairs={{0,16},{16,0},{2,18},{18,2},{64,80},{80,64},{66,82},{82,66},{48,32... | collective-permute-start | bytes 1179656 | tf_op jit(solution)/shard_map/ppermute | solution.py:58
  86.7 21.6 %collective-permute-start.4 = (bf16[12,2,2,32,128]{4,3,2,1,0:T(8,128)(2,1)S(1)}, bf16[12,2,2,32,128]{4,3,2,1,0:T(8,128)(2,1)S(1)}, u32[]{:S(2)}, u32[]{:S(2)}) collective-permute-start(bf16[12,2,2,32,128]{4,3,2,1,0:T(8,128)(2,1)S(1)} %get-tuple-element.30), channel_id=1, source_target_pairs={{0,2},{16,18},{2,0},{18,16},{64,66},{80,82},{66,64},{82,80},{48,50... | collective-permute-start | bytes 1179656 | tf_op jit(solution)/shard_map/ppermute | solution.py:58
  88.0 25.3 %collective-permute-start.5 = (bf16[12,2,2,32,128]{4,3,2,1,0:T(8,128)(2,1)}, bf16[12,2,2,32,128]{4,3,2,1,0:T(8,128)(2,1)S(1)}, u32[]{:S(2)}, u32[]{:S(2)}) collective-permute-start(bf16[12,2,2,32,128]{4,3,2,1,0:T(8,128)(2,1)} %get-tuple-element.31), channel_id=1, source_target_pairs={{0,82},{16,66},{2,80},{18,64},{64,18},{80,2},{66,16},{82,0},{48,98... | collective-permute-start | bytes 1179656 | tf_op jit(solution)/shard_map/ppermute | solution.py:58
  89.5 23.8 %collective-permute-start.6 = (bf16[12,2,2,32,128]{4,3,2,1,0:T(8,128)(2,1)}, bf16[12,2,2,32,128]{4,3,2,1,0:T(8,128)(2,1)S(1)}, u32[]{:S(2)}, u32[]{:S(2)}) collective-permute-start(bf16[12,2,2,32,128]{4,3,2,1,0:T(8,128)(2,1)} %get-tuple-element.32), channel_id=1, source_target_pairs={{0,66},{16,82},{2,64},{18,80},{64,2},{80,18},{66,0},{82,16},{48,11... | collective-permute-start | bytes 1179656 | tf_op jit(solution)/shard_map/ppermute | solution.py:58
  90.9 22.4 %collective-permute-start.7 = (bf16[12,2,2,32,128]{4,3,2,1,0:T(8,128)(2,1)}, bf16[12,2,2,32,128]{4,3,2,1,0:T(8,128)(2,1)S(1)}, u32[]{:S(2)}, u32[]{:S(2)}) collective-permute-start(bf16[12,2,2,32,128]{4,3,2,1,0:T(8,128)(2,1)} %get-tuple-element.33), channel_id=1, source_target_pairs={{0,80},{16,64},{2,82},{18,66},{64,16},{80,0},{66,18},{82,2},{48,96... | collective-permute-start | bytes 1179656 | tf_op jit(solution)/shard_map/ppermute | solution.py:58
  102.8 10.5 %collective-permute-start.8 = (bf16[12,2,2,32,128]{4,3,2,1,0:T(8,128)(2,1)}, bf16[12,2,2,32,128]{4,3,2,1,0:T(8,128)(2,1)S(1)}, u32[]{:S(2)}, u32[]{:S(2)}) collective-permute-start(bf16[12,2,2,32,128]{4,3,2,1,0:T(8,128)(2,1)} %get-tuple-element.34), channel_id=1, source_target_pairs={{0,18},{16,2},{2,16},{18,0},{64,82},{80,66},{66,80},{82,64},{48,34... | collective-permute-start | bytes 1179656 | tf_op jit(solution)/shard_map/ppermute | solution.py:58
  108.3 8.1 %collective-permute-start.9 = (bf16[12,2,2,32,128]{4,3,2,1,0:T(8,128)(2,1)}, bf16[12,2,2,32,128]{4,3,2,1,0:T(8,128)(2,1)S(1)}, u32[]{:S(2)}, u32[]{:S(2)}) collective-permute-start(bf16[12,2,2,32,128]{4,3,2,1,0:T(8,128)(2,1)} %get-tuple-element.35), channel_id=1, source_target_pairs={{0,64},{16,80},{2,66},{18,82},{64,0},{80,16},{66,2},{82,18},{48,11... | collective-permute-start | bytes 1179656 | tf_op jit(solution)/shard_map/ppermute | solution.py:58
